TPU v7x, 128 devices: a whole 4x4x4 slice. The times are simulated.
128 devices in a mesh: dx: 8 (over x, core), dy: 16 (over y, z).
Axes of the slice: x: 4, y: 4, z: 4, core: 2. Of those that a mesh axis runs over, the one named last changes fastest.
Arguments:
- positions: float32 [3, 262144], P(None, ('dx', 'dy')), may hold values from -6 to 6
- masses: float32 [262144], P(('dx', 'dy')), may hold values from 0.003 to 0.03
- centers: float32 [3, 131072], P(None, ('dx', 'dy')), may hold values from -3 to 3
- radii: float32 [131072], P(('dx', 'dy')), may hold values from 0.6 to 1.8
- pair_block: int32 [262144], P(('dx', 'dy')), may hold values from 0 to 15
- pair_halo: int32 [262144], P(('dx', 'dy')), may hold values from -1 to 1023, as said below
Outputs:
- centers_out: float32 [3, 131072], P(None, ('dx', 'dy'))
- radii_out: float32 [131072], P(('dx', 'dy'))
- profile: float32 [16, 131072], P(None, ('dx', 'dy'))
Inputs may be any that keep to these rules, and one draw needn't show every extreme that they name: `pair_halo`: for each domain and each owner, the 16 slots hold the live halo indices first and then -1; in every draw some owner receives 16 live slots from every domain.
All inputs are finite; a program needn't handle non-finite values.
Results may differ from a plain program's by a relative error of at most 0.0003.
Values sent between devices are 32-bit elements; how exact they have to be, the bound alone decides.
No kernel may reach another device: no remote copies, remote signals or barrier semaphores. Data moves between devices by JAX's collectives and lax.ppermute only.
A program may use at most 64 MiB of HBM per device.

v0:
```python
import jax
import jax.numpy as jnp
from jax import lax
from jax.sharding import PartitionSpec as P

SHELLS = 16
BLOCK = 128
GROUP = 4
ITERS = 2


def slot_terms(points, weights, center, radius, live):
    offset = points - center[:, :, None]
    dist = jnp.sqrt(jnp.sum(offset * offset, axis=0))
    scaled = dist * (SHELLS / 2.0 / radius)[:, None]
    middles = jnp.arange(SHELLS, dtype=jnp.float32) + 0.5
    tent = jnp.maximum(0.0, 1.0 - jnp.abs(scaled[None] - middles[:, None, None]))
    massed = weights * live[:, None]
    shells = jnp.sum(tent * massed[None], axis=2)
    inner = jnp.clip(SHELLS / 2.0 - scaled, 0.0, 1.0) * massed
    total = jnp.sum(inner, axis=1)
    moment = jnp.sum(offset * inner[None], axis=2)
    return jnp.concatenate([shells, total[None], moment], axis=0)


def advance(centers, radii, sums):
    profile = jnp.cumsum(sums[:SHELLS], axis=0)
    enclosed = profile[SHELLS // 2 - 1]
    ratio = (1.0 + enclosed) / (1.0 + radii * radii * radii)
    new_radii = radii * ratio ** (1.0 / 3.0)
    new_centers = centers + sums[SHELLS + 1 :] / jnp.maximum(sums[SHELLS], 1.0)
    return (new_centers, new_radii, profile)


def body(positions, masses, centers, radii, pair_block, pair_halo):
    devices = lax.axis_size(("dx", "dy"))
    halo_dev = radii.shape[0]
    block_count = masses.shape[0] // BLOCK
    slots = pair_halo.shape[0] // devices
    points = positions.reshape(3, block_count, BLOCK)
    weights = masses.reshape(block_count, BLOCK)
    slot_blocks = pair_block.reshape(devices, slots)
    slot_halos = pair_halo.reshape(devices, slots)
    live_grid = slot_halos >= 0
    wanted = lax.all_to_all(pair_halo, ("dx", "dy"), split_axis=0, concat_axis=0, tiled=True)
    safe_wanted = jnp.maximum(wanted, 0)
    segment = jnp.where(wanted >= 0, wanted, halo_dev)
    group_count = slots // GROUP
    width = SHELLS + 4
    profile = None
    for step in range(ITERS):
        state = jnp.concatenate([centers, radii[None]], axis=0)
        asked = jnp.take(state, safe_wanted, axis=1)
        slot_state = lax.all_to_all(asked, ("dx", "dy"), split_axis=1, concat_axis=1, tiled=True)
        state_grid = slot_state.reshape(4, devices, slots)

        def one_group(group, buffer):
            start = group * GROUP
            blocks_here = lax.dynamic_slice_in_dim(slot_blocks, start, GROUP, 1).reshape(-1)
            state_here = lax.dynamic_slice_in_dim(state_grid, start, GROUP, 2).reshape(4, -1)
            live_here = lax.dynamic_slice_in_dim(live_grid, start, GROUP, 1).reshape(-1)
            pts = jnp.take(points, blocks_here, axis=1)
            wts = jnp.take(weights, blocks_here, axis=0)
            terms = slot_terms(
                pts, wts, state_here[:3], state_here[3], live_here.astype(jnp.float32)
            )
            return lax.dynamic_update_slice_in_dim(
                buffer, terms.reshape(width, devices, GROUP), start, 2
            )

        partial_value = lax.fori_loop(
            0, group_count, one_group, jnp.zeros((width, devices, slots), jnp.float32)
        )
        arrived = lax.all_to_all(
            partial_value.reshape(width, -1), ("dx", "dy"), split_axis=1, concat_axis=1, tiled=True
        )
        sums = jax.ops.segment_sum(arrived.T, segment, num_segments=halo_dev + 1)[:halo_dev].T
        centers, radii, profile = advance(centers, radii, sums)
    return (centers, radii, profile)


def solution(mesh):
    in_specs = (
        P(None, ("dx", "dy")),
        P(("dx", "dy")),
        P(None, ("dx", "dy")),
        P(("dx", "dy")),
        P(("dx", "dy")),
        P(("dx", "dy")),
    )
    out_specs = (P(None, ("dx", "dy")), P(("dx", "dy")), P(None, ("dx", "dy")))
    return jax.shard_map(body, mesh=mesh, in_specs=in_specs, out_specs=out_specs, check_vma=False)
```

profile of v0, /device:TPU:1, one launch (start us, length us, event | category | flops | bytes accessed | tf_op | source)
XLA Modules:
  0.0 240.8 jit_solution(9236727377475748480)
XLA Ops:
  0.6 1.4 all_to_all.32
  2.0 11.5 %all-to-all-start = ((s32[128,16,1]{1,2,0:T(1,128)}), s32[128,16,1]{1,2,0:T(1,128)S(1)}, u32[]{:S(2)}, u32[]{:S(2)}) async-start(s32[128,16,1]{1,2,0:T(1,128)} %bitcast.8), calls=%async_computation | async-start | bytes 131072 | tf_op jit(solution)/shard_map/all_to_all | solution.py:45
  14.5 8.5 %all-to-all-done = s32[128,16,1]{1,2,0:T(1,128)S(1)} async-done(((s32[128,16,1]{1,2,0:T(1,128)}), s32[128,16,1]{1,2,0:T(1,128)S(1)}, u32[]{:S(2)}, u32[]{:S(2)}) %all-to-all-start) | async-done | bytes 8224 | tf_op jit(solution)/shard_map/all_to_all | solution.py:45
  23.6 1.0 maximum_reduce_fusion
  24.7 5.5 %gather_fusion.4 = f32[2048,4]{1,0:T(8,128)S(1)} fusion(f32[4,1024]{0,1:T(8,128)S(1)} %copy.118, s32[2048]{0:T(1024)S(1)} %fusion.4), kind=kCustom, calls=%fused_computation.clone | custom fusion | bytes 73728 | tf_op jit(solution)/shard_map/jit(_take)/gather | solution.py:53
  30.5 1.5 copy.119
  32.0 4.5 %all-to-all-start.1 = ((f32[4,128,16]{2,0,1:T(4,128)}), f32[4,128,16]{2,0,1:T(4,128)S(1)}, u32[]{:S(2)}, u32[]{:S(2)}) async-start(f32[4,128,16]{2,0,1:T(4,128)} %copy.119), calls=%async_computation.1 | async-start | bytes 524288 | tf_op jit(solution)/shard_map/all_to_all | solution.py:54
  36.8 11.0 %all-to-all-done.1 = f32[4,128,16]{2,0,1:T(4,128)S(1)} async-done(((f32[4,128,16]{2,0,1:T(4,128)}), f32[4,128,16]{2,0,1:T(4,128)S(1)}, u32[]{:S(2)}, u32[]{:S(2)}) %all-to-all-start.1) | async-done | bytes 32800 | tf_op jit(solution)/shard_map/all_to_all | solution.py:54
  47.8 53.5 %while.26 = (s32[]{:T(128)}, f32[20,128,16]{1,2,0:T(8,128)S(1)}, s32[128,16]{1,0:T(8,128)S(1)}, f32[3,16,128]{2,0,1:T(4,128)S(1)}, f32[4,128,16]{2,0,1:T(4,128)S...) while((s32[]{:T(128)}, f32[20,128,16]{1,2,0:T(8,128)S(1)}, ...), condition=%wide.region_5.9_spmd, body=%wide.region_0.8_spmd.sunk | while | flops 8274455 | bytes 6390599 | solution.py:71
  48.1 2.1 gather_fusion
  50.4 0.9 copy.162
  51.3 3.0 %multiply_reduce_fusion.12 = f32[512,128]{1,0:T(8,128)S(1)} fusion(f32[512,3,128]{2,1,0:T(4,128)S(1)} %gather_fusion, f32[3,512]{0,1:T(8,128)S(1)} %bitcast.77, pred[512]{0:T(512)(128)(4,1)S(1)} %compare_and_fusion.5), kind=kLoop, calls=%fused_computation.11.clone.1 | loop fusion | flops 720896 | bytes 1055232 | tf_op jit(solution)/shard_map/while/body/eval_jaxpr/reduce_sum | solution.py:14
  54.2 1.0 gather_fusion.1
  56.2 1.2 multiply_reduce_fusion.14
  57.7 3.2 %multiply_reduce_fusion.13 = f32[3,512]{0,1:T(8,128)S(1)} fusion(f32[512,3,128]{2,1,0:T(4,128)S(1)} %gather_fusion, f32[512,128]{1,0:T(8,128)S(1)} %get-tuple-element.437, f32[3,512]{0,1:T(8,128)S(1)} %bitcast.78, pred[512]{0:T(512)(128)(4,1)S(1)} %compare_and_fusion.5), kind=kLoop, calls=%fused_computation.10.clone.1 | loop fusion | flops 784896 | bytes 1061376 | tf_op jit(solution)/shard_map/while/body/eval_jaxpr/reduce_sum | solution.py:22
  61.5 2.1 gather_fusion
  63.8 0.9 copy.162
  64.7 3.0 %multiply_reduce_fusion.12 = f32[512,128]{1,0:T(8,128)S(1)} fusion(f32[512,3,128]{2,1,0:T(4,128)S(1)} %gather_fusion, f32[3,512]{0,1:T(8,128)S(1)} %bitcast.77, pred[512]{0:T(512)(128)(4,1)S(1)} %compare_and_fusion.5), kind=kLoop, calls=%fused_computation.11.clone.1 | loop fusion | flops 720896 | bytes 1055232 | tf_op jit(solution)/shard_map/while/body/eval_jaxpr/reduce_sum | solution.py:14
  67.6 1.0 gather_fusion.1
  69.6 1.2 multiply_reduce_fusion.14
  71.0 3.2 %multiply_reduce_fusion.13 = f32[3,512]{0,1:T(8,128)S(1)} fusion(f32[512,3,128]{2,1,0:T(4,128)S(1)} %gather_fusion, f32[512,128]{1,0:T(8,128)S(1)} %get-tuple-element.437, f32[3,512]{0,1:T(8,128)S(1)} %bitcast.78, pred[512]{0:T(512)(128)(4,1)S(1)} %compare_and_fusion.5), kind=kLoop, calls=%fused_computation.10.clone.1 | loop fusion | flops 784896 | bytes 1061376 | tf_op jit(solution)/shard_map/while/body/eval_jaxpr/reduce_sum | solution.py:22
  74.9 2.1 gather_fusion
  78.0 3.0 %multiply_reduce_fusion.12 = f32[512,128]{1,0:T(8,128)S(1)} fusion(f32[512,3,128]{2,1,0:T(4,128)S(1)} %gather_fusion, f32[3,512]{0,1:T(8,128)S(1)} %bitcast.77, pred[512]{0:T(512)(128)(4,1)S(1)} %compare_and_fusion.5), kind=kLoop, calls=%fused_computation.11.clone.1 | loop fusion | flops 720896 | bytes 1055232 | tf_op jit(solution)/shard_map/while/body/eval_jaxpr/reduce_sum | solution.py:14
  81.0 1.0 gather_fusion.1
  83.0 1.2 multiply_reduce_fusion.14
  84.4 3.2 %multiply_reduce_fusion.13 = f32[3,512]{0,1:T(8,128)S(1)} fusion(f32[512,3,128]{2,1,0:T(4,128)S(1)} %gather_fusion, f32[512,128]{1,0:T(8,128)S(1)} %get-tuple-element.437, f32[3,512]{0,1:T(8,128)S(1)} %bitcast.78, pred[512]{0:T(512)(128)(4,1)S(1)} %compare_and_fusion.5), kind=kLoop, calls=%fused_computation.10.clone.1 | loop fusion | flops 784896 | bytes 1061376 | tf_op jit(solution)/shard_map/while/body/eval_jaxpr/reduce_sum | solution.py:22
  88.2 2.1 gather_fusion
  91.4 3.0 %multiply_reduce_fusion.12 = f32[512,128]{1,0:T(8,128)S(1)} fusion(f32[512,3,128]{2,1,0:T(4,128)S(1)} %gather_fusion, f32[3,512]{0,1:T(8,128)S(1)} %bitcast.77, pred[512]{0:T(512)(128)(4,1)S(1)} %compare_and_fusion.5), kind=kLoop, calls=%fused_computation.11.clone.1 | loop fusion | flops 720896 | bytes 1055232 | tf_op jit(solution)/shard_map/while/body/eval_jaxpr/reduce_sum | solution.py:14
  94.4 1.0 gather_fusion.1
  96.4 1.2 multiply_reduce_fusion.14
  97.8 3.2 %multiply_reduce_fusion.13 = f32[3,512]{0,1:T(8,128)S(1)} fusion(f32[512,3,128]{2,1,0:T(4,128)S(1)} %gather_fusion, f32[512,128]{1,0:T(8,128)S(1)} %get-tuple-element.437, f32[3,512]{0,1:T(8,128)S(1)} %bitcast.78, pred[512]{0:T(512)(128)(4,1)S(1)} %compare_and_fusion.5), kind=kLoop, calls=%fused_computation.10.clone.1 | loop fusion | flops 784896 | bytes 1061376 | tf_op jit(solution)/shard_map/while/body/eval_jaxpr/reduce_sum | solution.py:22
  101.9 1.5 reshape.331
  103.4 4.2 %all-to-all-start.2 = ((f32[128,1,320]{2,1,0:T(1,128)}), f32[128,1,320]{2,1,0:T(1,128)S(1)}, u32[]{:S(2)}, u32[]{:S(2)}) async-start(f32[128,1,320]{2,1,0:T(1,128)} %reshape.331), calls=%async_computation.2 | async-start | bytes 393216 | tf_op jit(solution)/shard_map/all_to_all | solution.py:74
  107.6 10.6 %all-to-all-done.2 = f32[128,1,320]{2,1,0:T(1,128)S(1)} async-done(((f32[128,1,320]{2,1,0:T(1,128)}), f32[128,1,320]{2,1,0:T(1,128)S(1)}, u32[]{:S(2)}, u32[]{:S(2)}) %all-to-all-start.2) | async-done | bytes 163872 | tf_op jit(solution)/shard_map/all_to_all | solution.py:74
  118.7 1.1 reduce.9
  120.5 11.8 %scatter_custom_fusion = f32[1025,20]{1,0:T(8,128)S(1)} fusion(s32[2048]{0:T(1024)S(1)} %bitcast.105, f32[2048,20]{1,0:T(8,128)S(1)} %bitcast.92, f32[]{:T(128)} %constant.152.clone.1), kind=kCustom, calls=%fused_computation.46 | custom fusion | flops 40960 | bytes 82004 | tf_op jit(solution)/shard_map/scatter-add | solution.py:77
  133.3 5.5 %gather_fusion.5 = f32[2048,4]{1,0:T(8,128)S(1)} fusion(f32[4,1024]{0,1:T(8,128)S(1)} %copy.125, s32[2048]{0:T(1024)S(1)} %fusion.4), kind=kCustom, calls=%fused_computation.3.clone | custom fusion | bytes 73728 | tf_op jit(solution)/shard_map/jit(_take)/gather | solution.py:53
  139.1 1.5 copy.126
  140.6 4.3 %all-to-all-start.3 = ((f32[4,128,16]{2,0,1:T(4,128)}), f32[4,128,16]{2,0,1:T(4,128)S(1)}, u32[]{:S(2)}, u32[]{:S(2)}) async-start(f32[4,128,16]{2,0,1:T(4,128)} %copy.126), calls=%async_computation.3 | async-start | bytes 524288 | tf_op jit(solution)/shard_map/all_to_all | solution.py:54
  144.9 11.3 %all-to-all-done.3 = f32[4,128,16]{2,0,1:T(4,128)S(1)} async-done(((f32[4,128,16]{2,0,1:T(4,128)}), f32[4,128,16]{2,0,1:T(4,128)S(1)}, u32[]{:S(2)}, u32[]{:S(2)}) %all-to-all-start.3) | async-done | bytes 32800 | tf_op jit(solution)/shard_map/all_to_all | solution.py:54
  156.2 53.5 %while.27 = (s32[]{:T(128)}, f32[20,128,16]{1,2,0:T(8,128)S(1)}, s32[128,16]{1,0:T(8,128)S(1)}, f32[3,16,128]{2,0,1:T(4,128)S(1)}, f32[4,128,16]{2,0,1:T(4,128)S...) while((s32[]{:T(128)}, f32[20,128,16]{1,2,0:T(8,128)S(1)}, ...), condition=%wide.region_13.17_spmd, body=%wide.region_8.0_spmd.sunk | while | flops 8274455 | bytes 6390599 | solution.py:71
  156.4 2.1 gather_fusion.2
  159.6 3.0 %multiply_reduce_fusion.15 = f32[512,128]{1,0:T(8,128)S(1)} fusion(f32[512,3,128]{2,1,0:T(4,128)S(1)} %gather_fusion.2, f32[3,512]{0,1:T(8,128)S(1)} %bitcast.79, pred[512]{0:T(512)(128)(4,1)S(1)} %compare_and_fusion.6), kind=kLoop, calls=%fused_computation.28.clone.1 | loop fusion | flops 720896 | bytes 1055232 | tf_op jit(solution)/shard_map/while/body/eval_jaxpr/reduce_sum | solution.py:14
  162.6 1.0 gather_fusion.3
  164.6 1.2 multiply_reduce_fusion.17
  166.0 3.2 %multiply_reduce_fusion.16 = f32[3,512]{0,1:T(8,128)S(1)} fusion(f32[512,3,128]{2,1,0:T(4,128)S(1)} %gather_fusion.2, f32[512,128]{1,0:T(8,128)S(1)} %get-tuple-element.448, f32[3,512]{0,1:T(8,128)S(1)} %bitcast.80, pred[512]{0:T(512)(128)(4,1)S(1)} %compare_and_fusion.6), kind=kLoop, calls=%fused_computation.27.clone.1 | loop fusion | flops 784896 | bytes 1061376 | tf_op jit(solution)/shard_map/while/body/eval_jaxpr/reduce_sum | solution.py:22
  169.8 2.1 gather_fusion.2
  173.0 3.0 %multiply_reduce_fusion.15 = f32[512,128]{1,0:T(8,128)S(1)} fusion(f32[512,3,128]{2,1,0:T(4,128)S(1)} %gather_fusion.2, f32[3,512]{0,1:T(8,128)S(1)} %bitcast.79, pred[512]{0:T(512)(128)(4,1)S(1)} %compare_and_fusion.6), kind=kLoop, calls=%fused_computation.28.clone.1 | loop fusion | flops 720896 | bytes 1055232 | tf_op jit(solution)/shard_map/while/body/eval_jaxpr/reduce_sum | solution.py:14
  176.0 1.0 gather_fusion.3
  177.9 1.2 multiply_reduce_fusion.17
  179.4 3.2 %multiply_reduce_fusion.16 = f32[3,512]{0,1:T(8,128)S(1)} fusion(f32[512,3,128]{2,1,0:T(4,128)S(1)} %gather_fusion.2, f32[512,128]{1,0:T(8,128)S(1)} %get-tuple-element.448, f32[3,512]{0,1:T(8,128)S(1)} %bitcast.80, pred[512]{0:T(512)(128)(4,1)S(1)} %compare_and_fusion.6), kind=kLoop, calls=%fused_computation.27.clone.1 | loop fusion | flops 784896 | bytes 1061376 | tf_op jit(solution)/shard_map/while/body/eval_jaxpr/reduce_sum | solution.py:22
  183.2 2.1 gather_fusion.2
  186.4 3.0 %multiply_reduce_fusion.15 = f32[512,128]{1,0:T(8,128)S(1)} fusion(f32[512,3,128]{2,1,0:T(4,128)S(1)} %gather_fusion.2, f32[3,512]{0,1:T(8,128)S(1)} %bitcast.79, pred[512]{0:T(512)(128)(4,1)S(1)} %compare_and_fusion.6), kind=kLoop, calls=%fused_computation.28.clone.1 | loop fusion | flops 720896 | bytes 1055232 | tf_op jit(solution)/shard_map/while/body/eval_jaxpr/reduce_sum | solution.py:14
  189.4 1.0 gather_fusion.3
  191.3 1.2 multiply_reduce_fusion.17
  192.8 3.2 %multiply_reduce_fusion.16 = f32[3,512]{0,1:T(8,128)S(1)} fusion(f32[512,3,128]{2,1,0:T(4,128)S(1)} %gather_fusion.2, f32[512,128]{1,0:T(8,128)S(1)} %get-tuple-element.448, f32[3,512]{0,1:T(8,128)S(1)} %bitcast.80, pred[512]{0:T(512)(128)(4,1)S(1)} %compare_and_fusion.6), kind=kLoop, calls=%fused_computation.27.clone.1 | loop fusion | flops 784896 | bytes 1061376 | tf_op jit(solution)/shard_map/while/body/eval_jaxpr/reduce_sum | solution.py:22
  196.6 2.1 gather_fusion.2
  199.8 3.0 %multiply_reduce_fusion.15 = f32[512,128]{1,0:T(8,128)S(1)} fusion(f32[512,3,128]{2,1,0:T(4,128)S(1)} %gather_fusion.2, f32[3,512]{0,1:T(8,128)S(1)} %bitcast.79, pred[512]{0:T(512)(128)(4,1)S(1)} %compare_and_fusion.6), kind=kLoop, calls=%fused_computation.28.clone.1 | loop fusion | flops 720896 | bytes 1055232 | tf_op jit(solution)/shard_map/while/body/eval_jaxpr/reduce_sum | solution.py:14
  202.7 1.0 gather_fusion.3
  204.7 1.2 multiply_reduce_fusion.17
  206.2 3.2 %multiply_reduce_fusion.16 = f32[3,512]{0,1:T(8,128)S(1)} fusion(f32[512,3,128]{2,1,0:T(4,128)S(1)} %gather_fusion.2, f32[512,128]{1,0:T(8,128)S(1)} %get-tuple-element.448, f32[3,512]{0,1:T(8,128)S(1)} %bitcast.80, pred[512]{0:T(512)(128)(4,1)S(1)} %compare_and_fusion.6), kind=kLoop, calls=%fused_computation.27.clone.1 | loop fusion | flops 784896 | bytes 1061376 | tf_op jit(solution)/shard_map/while/body/eval_jaxpr/reduce_sum | solution.py:22
  211.1 14.6 %all_to_all.48 = f32[128,1,320]{2,1,0:T(1,128)S(1)} all-to-all(f32[128,1,320]{2,1,0:T(1,128)S(1)} %reshape.333), channel_id=1, replica_groups=mesh['dx'=8,'dy'=16] {'dx','dy'}, dimensions={0} | all-to-all | bytes 327680 | tf_op jit(solution)/shard_map/all_to_all | solution.py:74
  225.7 1.1 reduce.10
  227.4 11.8 %scatter_custom_fusion.1 = f32[1025,20]{1,0:T(8,128)S(1)} fusion(s32[2048]{0:T(1024)S(1)} %bitcast.106, f32[2048,20]{1,0:T(8,128)S(1)} %bitcast.91, f32[]{:T(128)} %constant.152.clone.1), kind=kCustom, calls=%fused_computation.44 | custom fusion | flops 40960 | bytes 82004 | tf_op jit(solution)/shard_map/scatter-add | solution.py:77
  (211 shorter events, 29.0 us)
Async XLA Ops:
  2.0 21.0 %all-to-all-start = ((s32[128,16,1]{1,2,0:T(1,128)}), s32[128,16,1]{1,2,0:T(1,128)S(1)}, u32[]{:S(2)}, u32[]{:S(2)}) async-start(s32[128,16,1]{1,2,0:T(1,128)} %bitcast.8), calls=%async_computation | async-start | bytes 131072 | tf_op jit(solution)/shard_map/all_to_all | solution.py:45
  30.5 6.1 %copy-start.4 = (s32[2048]{0:T(1024)S(1)}, s32[2048]{0:T(1024)}, u32[]{:S(2)}) copy-start(s32[2048]{0:T(1024)} %param.21) | copy-start | bytes 24580
  30.5 6.1 %copy-start.6 = (s32[2048]{0:T(1024)S(1)}, s32[2048]{0:T(1024)}, u32[]{:S(2)}) copy-start(s32[2048]{0:T(1024)} %param.20) | copy-start | bytes 24580
  30.5 17.3 %copy-start = (f32[2048]{0:T(1024)S(1)}, f32[2048]{0:T(1024)}, u32[]{:S(2)}) copy-start(f32[2048]{0:T(1024)} %param.17) | copy-start | bytes 24580
  30.5 17.3 %copy-start.1 = (f32[3,2048]{1,0:T(4,128)S(1)}, f32[3,2048]{1,0:T(4,128)}, u32[]{:S(2)}) copy-start(f32[3,2048]{1,0:T(4,128)} %param.16) | copy-start | bytes 73732
  32.0 15.8 %all-to-all-start.1 = ((f32[4,128,16]{2,0,1:T(4,128)}), f32[4,128,16]{2,0,1:T(4,128)S(1)}, u32[]{:S(2)}, u32[]{:S(2)}) async-start(f32[4,128,16]{2,0,1:T(4,128)} %copy.119), calls=%async_computation.1 | async-start | bytes 524288 | tf_op jit(solution)/shard_map/all_to_all | solution.py:54
  103.4 14.8 %all-to-all-start.2 = ((f32[128,1,320]{2,1,0:T(1,128)}), f32[128,1,320]{2,1,0:T(1,128)S(1)}, u32[]{:S(2)}, u32[]{:S(2)}) async-start(f32[128,1,320]{2,1,0:T(1,128)} %reshape.331), calls=%async_computation.2 | async-start | bytes 393216 | tf_op jit(solution)/shard_map/all_to_all | solution.py:74
  120.5 12.1 %copy-start.3 = (f32[3,1024]{1,0:T(4,128)S(1)}, f32[3,1024]{1,0:T(4,128)}, u32[]{:S(2)}) copy-start(f32[3,1024]{1,0:T(4,128)} %param.18) | copy-start | bytes 36868
  132.3 0.7 copy-start.5
  140.6 15.6 %all-to-all-start.3 = ((f32[4,128,16]{2,0,1:T(4,128)}), f32[4,128,16]{2,0,1:T(4,128)S(1)}, u32[]{:S(2)}, u32[]{:S(2)}) async-start(f32[4,128,16]{2,0,1:T(4,128)} %copy.126), calls=%async_computation.3 | async-start | bytes 524288 | tf_op jit(solution)/shard_map/all_to_all | solution.py:54
  240.2 0.7 copy-start.2
where the time goes:
time: 241 us
  other arithmetic  93.1 us (39%)
  local copies, waits for them, and re-layouts  65.2 us (27%)
  waiting for transfers between devices  41.4 us (17%)
  starting transfers between devices  24.5 us (10%)
  blocking collectives  14.6 us (6%)
    reduce_sum x8, other arithmetic, slot_terms(): moment = jnp.sum(offset * inner[None], axis=2)  25.6 us
    reduce_sum x8, other arithmetic, slot_terms(): dist = jnp.sqrt(jnp.sum(offset * offset, axis=0))  23.6 us
    scatter-add x2, other arithmetic, body(): jax.ops.segment_sum(arrived.T, segment, num_segments=halo_dev + 1)  23.6 us
    all_to_all x2, waiting for transfers between devices, body(): lax.all_to_all(asked, ('dx', 'dy'), split_axis=1, concat_axis=1, tiled=True)  22.3 us
    gather x8, local copies, waits for them, and re-layouts, one_group(): pts = jnp.take(points, blocks_here, axis=1)  16.6 us
    all_to_all x1, blocking collectives, body(): lax.all_to_all(partial_value.reshape(width, -1), ('dx', 'dy'), split_axis...  14.6 us
    all_to_all x1, starting transfers between devices, body(): lax.all_to_all(pair_halo, ('dx', 'dy'), split_axis=0, concat_axis=0, tile...  11.5 us
    gather x2, local copies, waits for them, and re-layouts, body(): asked = jnp.take(state, safe_wanted, axis=1)  10.9 us
  transfers between devices with their start and end apart: 4, of which 4 were waited for; matrix products, arithmetic and copies ran while one was open for 0% of the time, Pallas kernels for 0%

commit v1 on v0

v1 whole, which is shorter than its diff:
```python
import jax
import jax.numpy as jnp
from jax import lax
from jax.experimental import pallas as pl
from jax.experimental.pallas import tpu as pltpu
from jax.sharding import PartitionSpec as P

SHELLS = 16
BLOCK = 128
ITERS = 2
LANES = 128
ROWS = 24
AXES = ("dx", "dy")


def split(value, terms):
    parts = []
    for _ in range(terms):
        part = value.astype(jnp.bfloat16)
        parts.append(part)
        value = value - part.astype(jnp.float32)
    return parts


def kernel(particles, asked, centers, radii, centers_out, radii_out, profile_out, wide, one_hot, points, slot_state, partial):
    domains, _, blocks, _ = particles.shape
    halos = radii.shape[1]
    slots = asked.shape[2]
    tiles = slot_state.shape[0]
    group = LANES // slots

    lane = lax.broadcasted_iota(jnp.int32, (group, LANES), 1)
    own = lane // slots == lax.broadcasted_iota(jnp.int32, (group, LANES), 0)
    rows = []
    for which in range(2):
        wide[...] = jnp.zeros_like(wide)
        wide[:, :slots] = asked[which].astype(jnp.float32)
        row = wide[...]
        shift = slots
        while shift < LANES:
            row = row + pltpu.roll(row, shift, 1)
            shift *= 2
        rows.append([jnp.sum(jnp.where(own, row[t * group : (t + 1) * group], 0.0), axis=0, keepdims=True) for t in range(tiles)])
    halo_rows, block_rows = rows

    halo_index = lax.broadcasted_iota(jnp.int32, (halos, LANES), 0).astype(jnp.float32)
    for t in range(tiles):
        hit = halo_index == halo_rows[t]
        one_hot[:, t * LANES : (t + 1) * LANES] = jnp.where(hit, 1.0, 0.0).astype(jnp.bfloat16)

    count = group * blocks
    block_index = lax.broadcasted_iota(jnp.int32, (count, LANES), 0).astype(jnp.float32)
    first = (lax.broadcasted_iota(jnp.int32, (1, LANES), 1) // slots * blocks).astype(jnp.float32)
    for t in range(tiles):
        hit = block_index == block_rows[t] + first
        pick = jnp.where(hit, 1.0, 0.0).astype(jnp.bfloat16)
        for c in range(4):
            chosen = particles[t * group : (t + 1) * group, c].reshape(count, BLOCK).T
            high, low = split(chosen, 2)
            points[t, c] = jnp.dot(high, pick, preferred_element_type=jnp.float32) + jnp.dot(
                low, pick, preferred_element_type=jnp.float32
            )

    center = centers[...]
    radius = radii[...]
    partial[...] = jnp.zeros_like(partial)
    for step in range(ITERS):
        state = jnp.concatenate([center, radius], axis=0)
        stacked = jnp.concatenate([s.astype(jnp.float32) for s in split(state, 3)] + [jnp.zeros_like(state)], axis=0)
        got = jnp.dot(stacked.astype(jnp.bfloat16), one_hot[...], preferred_element_type=jnp.float32)
        got = got[0:4] + got[4:8] + got[8:12]
        for t in range(tiles):
            slot_state[t, 0:4] = got[:, t * LANES : (t + 1) * LANES]

        def one_tile(t, carry):
            mine = slot_state[t]
            cx, cy, cz, rad = mine[0:1], mine[1:2], mine[2:3], mine[3:4]
            scale = (SHELLS / 2.0) / jnp.where(rad > 0.0, rad, 1.0)
            ramps = [None] * (SHELLS + 1)
            inner = [None] * 4

            def add(sums, k, value):
                sums[k] = value if sums[k] is None else sums[k] + value

            for p in range(0, BLOCK, 8):
                x = points[t, 0, p : p + 8] - cx
                y = points[t, 1, p : p + 8] - cy
                z = points[t, 2, p : p + 8] - cz
                mass = points[t, 3, p : p + 8]
                scaled = jnp.sqrt(x * x + y * y + z * z) * scale
                half = mass * 0.5
                reach = half - mass * scaled
                for k in range(SHELLS + 1):
                    add(ramps, k, jnp.maximum(reach, 0.0))
                    if k == SHELLS // 2 - 1:
                        weight = jnp.maximum(jnp.minimum(reach + half, mass), 0.0)
                    reach = reach + mass
                add(inner, 0, weight)
                add(inner, 1, weight * x)
                add(inner, 2, weight * y)
                add(inner, 3, weight * z)
            for k in range(SHELLS):
                cumulative = ramps[k + 1] - ramps[k] - ramps[0]
                partial[t, k : k + 1] = jnp.sum(cumulative, axis=0, keepdims=True)
            for k in range(4):
                partial[t, SHELLS + k : SHELLS + k + 1] = jnp.sum(inner[k], axis=0, keepdims=True)
            return carry

        lax.fori_loop(0, tiles, one_tile, 0)
        terms = jnp.concatenate([partial[t] for t in range(tiles)], axis=1)
        high, low = split(terms, 2)
        across = (((1,), (1,)), ((), ()))
        sums = lax.dot_general(high, one_hot[...], across, preferred_element_type=jnp.float32) + lax.dot_general(
            low, one_hot[...], across, preferred_element_type=jnp.float32
        )
        profile = sums[:SHELLS]
        enclosed = profile[SHELLS // 2 - 1 : SHELLS // 2]
        ratio = (1.0 + enclosed) / (1.0 + radius * radius * radius)
        radius = radius * jnp.exp(jnp.log(ratio) * (1.0 / 3.0))
        center = center + sums[SHELLS + 1 : SHELLS + 4] / jnp.maximum(sums[SHELLS : SHELLS + 1], 1.0)
    centers_out[...] = center
    radii_out[...] = radius
    profile_out[...] = profile


def body(positions, masses, centers, radii, pair_block, pair_halo):
    devices = lax.axis_size(AXES)
    halos = radii.shape[0]
    blocks = masses.shape[0] // BLOCK
    slots = pair_halo.shape[0] // devices
    tiles = devices * slots // LANES
    mine = jnp.concatenate([positions, masses[None]], axis=0).reshape(4 * blocks, BLOCK)
    for axis in reversed(AXES):
        mine = lax.all_gather(mine, axis, axis=0, tiled=True)
    particles = mine.reshape(devices, 4, blocks, BLOCK)
    pairs = jnp.stack([pair_halo.reshape(devices, slots), pair_block.reshape(devices, slots)])
    asked = lax.all_to_all(pairs, AXES, split_axis=1, concat_axis=1, tiled=True)
    centers, radii, profile = pl.pallas_call(
        kernel,
        out_shape=(
            jax.ShapeDtypeStruct((3, halos), jnp.float32),
            jax.ShapeDtypeStruct((1, halos), jnp.float32),
            jax.ShapeDtypeStruct((SHELLS, halos), jnp.float32),
        ),
        scratch_shapes=[
            pltpu.VMEM((devices, LANES), jnp.float32),
            pltpu.VMEM((halos, devices * slots), jnp.bfloat16),
            pltpu.VMEM((tiles, 4, BLOCK, LANES), jnp.float32),
            pltpu.VMEM((tiles, 8, LANES), jnp.float32),
            pltpu.VMEM((tiles, ROWS, LANES), jnp.float32),
        ],
        compiler_params=pltpu.CompilerParams(vmem_limit_bytes=48 * 2**20),
    )(particles, asked, centers, radii[None])
    return (centers, radii[0], profile)


def solution(mesh):
    in_specs = (
        P(None, AXES),
        P(AXES),
        P(None, AXES),
        P(AXES),
        P(AXES),
        P(AXES),
    )
    out_specs = (P(None, AXES), P(AXES), P(None, AXES))
    return jax.shard_map(body, mesh=mesh, in_specs=in_specs, out_specs=out_specs, check_vma=False)
```

time: 241 us -> 96 us (0.40)
  other arithmetic: 93.1 us -> 0.81 us
  local copies, waits for them, and re-layouts: 65.2 us -> 5.27 us
  blocking collectives: 14.6 us -> 46.7 us
  waiting for transfers between devices: 41.4 us -> 12.3 us
  starting transfers between devices: 24.5 us -> 0.04 us
  Pallas kernels: 0 us -> 16.3 us
  between operations: 1.01 us -> 14.1 us
    reduce_sum x32 -> x0, other arithmetic: 62 us -> none  [the longest x8 25.6 us: slot_terms(): moment = jnp.sum(offset * inner[None], axis=2)]
    all_to_all x4 -> x0, waiting for transfers between devices: 41.4 us -> none  [the longest x2 22.3 us: body(): lax.all_to_all(asked, ('dx', 'dy'), split_axis=1, concat_axis=1, tiled=True)]
    gather x18 -> x0, local copies, waits for them, and re-layouts: 35.8 us -> none  [the longest x8 16.6 us: one_group(): pts = jnp.take(points, blocks_here, axis=1)]
    all_to_all x4 -> x0, starting transfers between devices: 24.5 us -> none  [the longest x1 11.5 us: body(): lax.all_to_all(pair_halo, ('dx', 'dy'), split_axis=0, concat_axis=0, tile...]
    scatter-add x2 -> x0, other arithmetic: 23.6 us -> none  [body(): jax.ops.segment_sum(arrived.T, segment, num_segments=halo_dev + 1)]
    all_gather x0 -> x1, blocking collectives: none -> 23.3 us  [body(): mine = lax.all_gather(mine, axis, axis=0, tiled=True)]
    pallas_call x0 -> x1, Pallas kernels: none -> 16.3 us  [body(): pl.pallas_call(kernel, out_shape=(jax.ShapeDtypeStruct((3, halos), jnp.fl...]
    all_gather x0 -> x1, waiting for transfers between devices: none -> 12.3 us  [body(): mine = lax.all_gather(mine, axis, axis=0, tiled=True)]
  transfers between devices with their start and end apart: 4 -> 1, of which waited for: 4 -> 1; matrix products, arithmetic and copies ran while one was open for 0% -> 2% of each run, Pallas kernels for 0% -> 0%
where the time goes in v1:
time: 96 us; the launch traced here: 95.6 us
  blocking collectives  46.7 us (49%)
  Pallas kernels  16.3 us (17%)
  between operations  14.1 us (15%)
  waiting for transfers between devices  12.3 us (13%)
  local copies, waits for them, and re-layouts  5.27 us (5%)
    all_to_all x1, blocking collectives, body(): asked = lax.all_to_all(pairs, AXES, split_axis=1, concat_axis=1, tiled=True)  23.5 us
    all_gather x1, blocking collectives, body(): mine = lax.all_gather(mine, axis, axis=0, tiled=True)  23.3 us
    pallas_call x1, Pallas kernels, body(): pl.pallas_call(kernel, out_shape=(jax.ShapeDtypeStruct((3, halos), jnp.fl...  16.3 us
    all_gather x1, waiting for transfers between devices, body(): mine = lax.all_gather(mine, axis, axis=0, tiled=True)  12.3 us
    unnamed x6, local copies, waits for them, and re-layouts  3.59 us
  transfers between devices with their start and end apart: 1, of which 1 were waited for; matrix products, arithmetic and copies ran while one was open for 2% of the time, Pallas kernels for 0%

profile of v1, /device:TPU:1, one launch (start us, length us, event | category | flops | bytes accessed | tf_op | source)
XLA Modules:
  0.0 95.6 jit_solution(7755551397634515862)
XLA Ops:
  7.2 0.0 all-gather.2.cloned.1.call-start
  7.2 0.8 pad_maximum_fusion
  8.0 23.3 %all_gather.6 = f32[1024,128]{1,0:T(8,128)} all-gather(f32[64,128]{1,0:T(8,128)S(1)} %reshape.12), channel_id=1, replica_groups=mesh['dx'=8,'dy'=16] {'dy'}, dimensions={0}, use_global_device_ids=true | all-gather | bytes 557056 | tf_op jit(solution)/shard_map/all_gather | solution.py:134
  31.3 0.0 all-gather.2.cloned.1.call-update
  31.3 0.8 stack_reshape.6
  32.1 0.8 stack_reshape.7
  32.9 0.1 copy.13
  33.0 23.5 %all_to_all.5 = s32[2,128,16]{2,0,1:T(2,128)S(1)} all-to-all(s32[2,128,16]{2,0,1:T(2,128)S(1)} %copy.13), channel_id=1, replica_groups=mesh['dx'=8,'dy'=16] {'dx','dy'}, dimensions={1} | all-to-all | bytes 32768 | tf_op jit(solution)/shard_map/all_to_all | solution.py:137
  56.5 12.3 %all-gather.2.cloned.1.call-done = f32[8192,128]{1,0:T(8,128)} async-done(((f32[1024,128]{1,0:T(8,128)}), f32[8192,128]{1,0:T(8,128)}) %all-gather.2.cloned.1.call-update) | async-done | bytes 4194320 | tf_op jit(solution)/shard_map/all_gather | solution.py:134
  68.8 0.0 copy-start
  68.8 2.2 %copy-done = f32[8192,128]{1,0:T(8,128)S(1)} copy-done((f32[8192,128]{1,0:T(8,128)S(1)}, f32[8192,128]{1,0:T(8,128)}, u32[]{:S(2)}) %copy-start) | copy-done | bytes 4194328
  71.0 0.0 copy-start.1
  71.0 0.7 copy-done.1
  71.7 0.0 copy-start.2
  71.7 0.7 copy-done.2
  72.4 16.3 %shard_map.85 = (f32[3,1024]{1,0:T(4,128)}, f32[1,1024]{1,0:T(1,128)}, f32[16,1024]{1,0:T(8,128)}) custom-call(f32[128,4,16,128]{3,2,1,0:T(8,128)S(1)} %bitcast.4, s32[2,128,16]{2,1,0:T(8,128)S(1)} %copy.14.asked, f32[3,1024]{1,0:T(4,128)S(1)} %copy-done.1, f32[1,1024]{1,0:T(1,128)S(1)} %bitcast.5), custom_call_target="tpu_custom_call" | custom-call | tf_op jit(solution)/shard_map/pallas_call | solution.py:138
  (3 shorter events, 0.0 us)
Async XLA Ops:
  7.2 61.7 %all-gather.2.cloned.1.call-start = ((), (), s32[]{:S(2)}) async-start(), calls=%async_computation.1 | async-start | bytes 4718592 | tf_op jit(solution)/shard_map/all_gather | solution.py:134
  68.8 2.2 %copy-start = (f32[8192,128]{1,0:T(8,128)S(1)}, f32[8192,128]{1,0:T(8,128)}, u32[]{:S(2)}) copy-start(f32[8192,128]{1,0:T(8,128)} %all-gather.2.cloned.1.call-done) | copy-start | bytes 12582916
  71.0 0.7 copy-start.1
  71.7 0.7 copy-start.2
Sparse Core Ops, SparseCore 0:
  31.4 37.3 all-gather.1

commit v2 on v1

--- a/solution.py
+++ b/solution.py
@@ -3,14 +3,14 @@
 from jax import lax
 from jax.experimental import pallas as pl
 from jax.experimental.pallas import tpu as pltpu
-from jax.sharding import PartitionSpec as P
+from jax.sharding import Mesh, PartitionSpec as P
 
 SHELLS = 16
 BLOCK = 128
 ITERS = 2
 LANES = 128
 ROWS = 24
-AXES = ("dx", "dy")
+AXES = ("x", "core", "y", "z")
 
 
 def split(value, terms):
@@ -22,20 +22,24 @@
     return parts
 
 
-def kernel(particles, asked, centers, radii, centers_out, radii_out, profile_out, wide, one_hot, points, slot_state, partial):
-    domains, _, blocks, _ = particles.shape
+def kernel(order, asked, centers, radii, *refs):
+    particles, (centers_out, radii_out, profile_out, wide, one_hot, points, slot_state, partial) = refs[:-8], refs[-8:]
+    chunk, _, blocks, _ = particles[0].shape
     halos = radii.shape[1]
-    slots = asked.shape[2]
+    slots = asked.shape[1] // 2
     tiles = slot_state.shape[0]
     group = LANES // slots
+    chunk_tiles = chunk // group
 
     lane = lax.broadcasted_iota(jnp.int32, (group, LANES), 1)
     own = lane // slots == lax.broadcasted_iota(jnp.int32, (group, LANES), 0)
     rows = []
+    wide[...] = jnp.zeros_like(wide)
+    for d in range(wide.shape[0]):
+        wide[d : d + 1, : 2 * slots] = asked[pl.ds(order[d], 1)].astype(jnp.float32)
+    lanes = lax.broadcasted_iota(jnp.int32, wide.shape, 1)
     for which in range(2):
-        wide[...] = jnp.zeros_like(wide)
-        wide[:, :slots] = asked[which].astype(jnp.float32)
-        row = wide[...]
+        row = jnp.where(lanes // slots == which, wide[...], 0.0)
         shift = slots
         while shift < LANES:
             row = row + pltpu.roll(row, shift, 1)
@@ -55,7 +59,7 @@
         hit = block_index == block_rows[t] + first
         pick = jnp.where(hit, 1.0, 0.0).astype(jnp.bfloat16)
         for c in range(4):
-            chosen = particles[t * group : (t + 1) * group, c].reshape(count, BLOCK).T
+            chosen = particles[t // chunk_tiles][t % chunk_tiles * group : (t % chunk_tiles + 1) * group, c].reshape(count, BLOCK).T
             high, low = split(chosen, 2)
             points[t, c] = jnp.dot(high, pick, preferred_element_type=jnp.float32) + jnp.dot(
                 low, pick, preferred_element_type=jnp.float32
@@ -123,20 +127,37 @@
     profile_out[...] = profile
 
 
+def shifted(value, axis):
+    size = lax.axis_size(axis)
+    return [value] + [lax.ppermute(value, axis, [(i, (i + k) % size) for i in range(size)]) for k in range(1, size)]
+
+
+def sources():
+    index = jnp.zeros((1,), jnp.int32)
+    for axis, stride in (("x", 32), ("core", 16), ("y", 4), ("z", 1)):
+        size = lax.axis_size(axis)
+        here = (lax.axis_index(axis) - jnp.arange(size, dtype=jnp.int32)) % size * stride
+        index = (index[:, None] + here[None, :]).reshape(-1)
+    return index
+
+
 def body(positions, masses, centers, radii, pair_block, pair_halo):
     devices = lax.axis_size(AXES)
     halos = radii.shape[0]
     blocks = masses.shape[0] // BLOCK
     slots = pair_halo.shape[0] // devices
     tiles = devices * slots // LANES
-    mine = jnp.concatenate([positions, masses[None]], axis=0).reshape(4 * blocks, BLOCK)
-    for axis in reversed(AXES):
-        mine = lax.all_gather(mine, axis, axis=0, tiled=True)
-    particles = mine.reshape(devices, 4, blocks, BLOCK)
-    pairs = jnp.stack([pair_halo.reshape(devices, slots), pair_block.reshape(devices, slots)])
-    asked = lax.all_to_all(pairs, AXES, split_axis=1, concat_axis=1, tiled=True)
+    pairs = jnp.concatenate([pair_halo.reshape(devices, slots), pair_block.reshape(devices, slots)], axis=1)
+    plane = jnp.concatenate([positions, masses[None]], axis=0).reshape(1, 4, blocks, BLOCK)
+    for axis in ("z", "y"):
+        plane = jnp.concatenate(shifted(plane, axis), axis=0)
+    plane, pairs = lax.optimization_barrier((plane, pairs))
+    chunks = [part for slab in shifted(plane, "x") for part in shifted(slab, "core")]
+    asked = lax.all_to_all(pairs, AXES, split_axis=0, concat_axis=0, tiled=True)
+    vmem = pl.BlockSpec(memory_space=pltpu.VMEM)
     centers, radii, profile = pl.pallas_call(
         kernel,
+        in_specs=[pl.BlockSpec(memory_space=pltpu.SMEM)] + [vmem] * (3 + len(chunks)),
         out_shape=(
             jax.ShapeDtypeStruct((3, halos), jnp.float32),
             jax.ShapeDtypeStruct((1, halos), jnp.float32),
@@ -150,11 +171,12 @@
             pltpu.VMEM((tiles, ROWS, LANES), jnp.float32),
         ],
         compiler_params=pltpu.CompilerParams(vmem_limit_bytes=48 * 2**20),
-    )(particles, asked, centers, radii[None])
+    )(sources(), asked, centers, radii[None], *chunks)
     return (centers, radii[0], profile)
 
 
 def solution(mesh):
+    chips = Mesh(mesh.devices.reshape(4, 2, 4, 4), AXES)
     in_specs = (
         P(None, AXES),
         P(AXES),
@@ -164,4 +186,4 @@
         P(AXES),
     )
     out_specs = (P(None, AXES), P(AXES), P(None, AXES))
-    return jax.shard_map(body, mesh=mesh, in_specs=in_specs, out_specs=out_specs, check_vma=False)
+    return jax.shard_map(body, mesh=chips, in_specs=in_specs, out_specs=out_specs, check_vma=False)

time: 96 us -> 81.9 us (0.85)
  blocking collectives: 46.7 us -> 0 us
  starting transfers between devices: 0.04 us -> 39 us
  between operations: 14.1 us -> 0.78 us
  waiting for transfers between devices: 12.3 us -> 21.2 us
  local copies, waits for them, and re-layouts: 5.27 us -> 2.72 us
  Pallas kernels: 16.3 us -> 17.5 us
    ppermute x0 -> x13, starting transfers between devices: none -> 34.6 us  [shifted(): lax.ppermute(value, axis, [(i, (i + k) % size) for i in range(size)])]
    all_to_all x1 -> x0, blocking collectives: 23.5 us -> none  [body(): asked = lax.all_to_all(pairs, AXES, split_axis=1, concat_axis=1, tiled=True)]
    all_gather x1 -> x0, blocking collectives: 23.3 us -> none  [body(): mine = lax.all_gather(mine, axis, axis=0, tiled=True)]
    all_gather x1 -> x0, waiting for transfers between devices: 12.3 us -> none  [body(): mine = lax.all_gather(mine, axis, axis=0, tiled=True)]
    ppermute x0 -> x13, waiting for transfers between devices: none -> 11.9 us  [shifted(): lax.ppermute(value, axis, [(i, (i + k) % size) for i in range(size)])]
    all_to_all x0 -> x1, waiting for transfers between devices: none -> 9.31 us  [body(): asked = lax.all_to_all(pairs, AXES, split_axis=0, concat_axis=0, tiled=True)]
    all_to_all x0 -> x1, starting transfers between devices: none -> 4.47 us  [body(): asked = lax.all_to_all(pairs, AXES, split_axis=0, concat_axis=0, tiled=True)]
    unnamed x6 -> x16, local copies, waits for them, and re-layouts: 3.59 us -> 1.46 us
  transfers between devices with their start and end apart: 1 -> 14, of which waited for: 1 -> 5; matrix products, arithmetic and copies ran while one was open for 2% -> 2% of each run, Pallas kernels for 0% -> 0%
where the time goes in v2:
time: 81.9 us; the launch traced here: 81.6 us
  starting transfers between devices  39 us (48%)
  waiting for transfers between devices  21.2 us (26%)
  Pallas kernels  17.5 us (21%)
  local copies, waits for them, and re-layouts  2.72 us (3%)
    ppermute x13, starting transfers between devices, shifted(): lax.ppermute(value, axis, [(i, (i + k) % size) for i in range(size)])  34.6 us
    pallas_call x1, Pallas kernels, body(): pl.pallas_call(kernel, in_specs=[pl.BlockSpec(memory_space=pltpu.SMEM)] +...  17.5 us
    ppermute x13, waiting for transfers between devices, shifted(): lax.ppermute(value, axis, [(i, (i + k) % size) for i in range(size)])  11.9 us
    all_to_all x1, waiting for transfers between devices, body(): asked = lax.all_to_all(pairs, AXES, split_axis=0, concat_axis=0, tiled=True)  9.31 us
    all_to_all x1, starting transfers between devices, body(): asked = lax.all_to_all(pairs, AXES, split_axis=0, concat_axis=0, tiled=True)  4.47 us
  transfers between devices with their start and end apart: 14, of which 5 were waited for; matrix products, arithmetic and copies ran while one was open for 2% of the time, Pallas kernels for 0%

profile of v2, /device:TPU:1, one launch (start us, length us, event | category | flops | bytes accessed | tf_op | source)
XLA Modules:
  0.0 81.6 jit_solution(144519688779460276)
XLA Ops:
  0.6 0.0 copy-start.2
  0.6 0.8 copy.14
  1.4 0.0 copy-done.2
  1.4 0.0 copy-start.3
  1.4 4.5 %collective-permute-start.1 = (f32[1,4,16,128]{3,2,1,0:T(8,128)S(1)}, f32[1,4,16,128]{3,2,1,0:T(8,128)S(1)}, u32[]{:S(2)}, u32[]{:S(2)}) collective-permute-start(f32[1,4,16,128]{3,2,1,0:T(8,128)S(1)} %get-tuple-element.13), channel_id=1, source_target_pairs={{0,2},{1,3},{2,0},{3,1},{4,6},{5,7},{6,4},{7,5},{8,10},{9,11},{10,... | collective-permute-start | bytes 98312 | tf_op jit(solution)/shard_map/ppermute | solution.py:132
  5.9 0.7 collective-permute-start
  6.7 1.9 %collective-permute-start.2 = (f32[1,4,16,128]{3,2,1,0:T(8,128)S(1)}, f32[1,4,16,128]{3,2,1,0:T(8,128)S(1)}, u32[]{:S(2)}, u32[]{:S(2)}) collective-permute-start(f32[1,4,16,128]{3,2,1,0:T(8,128)S(1)} %get-tuple-element.13), channel_id=1, source_target_pairs={{0,3},{1,0},{2,1},{3,2},{4,7},{5,4},{6,5},{7,6},{8,11},{9,8},{10,9... | collective-permute-start | bytes 98312 | tf_op jit(solution)/shard_map/ppermute | solution.py:132
  8.6 0.0 copy-done.3
  8.6 0.1 reshape.114
  8.7 0.0 copy-start.4
  8.7 0.1 copy.10
  8.8 0.6 copy-done.4
  9.4 0.1 reshape.113
  9.5 0.1 copy.9
  9.5 0.0 collective-permute-done.1
  9.5 0.4 collective-permute-done
  9.9 0.0 collective-permute-done.2
  9.9 2.8 %collective-permute-start.5 = (f32[4,4,16,128]{3,2,1,0:T(8,128)S(1)}, f32[4,4,16,128]{3,2,1,0:T(8,128)S(1)}, u32[]{:S(2)}, u32[]{:S(2)}) collective-permute-start(f32[4,4,16,128]{3,2,1,0:T(8,128)S(1)} %pad_maximum_fusion), channel_id=1, source_target_pairs={{0,12},{4,0},{8,4},{12,8},{1,13},{5,1},{9,5},{13,9},{2,14},{6,2},{... | collective-permute-start | bytes 393224 | tf_op jit(solution)/shard_map/ppermute | solution.py:132
  12.7 0.3 collective-permute-start.4
  13.1 0.7 collective-permute-start.3
  13.8 5.7 %collective-permute-done.3 = f32[4,4,16,128]{3,2,1,0:T(8,128)S(1)} collective-permute-done((f32[4,4,16,128]{3,2,1,0:T(8,128)S(1)}, f32[4,4,16,128]{3,2,1,0:T(8,128)S(1)}, u32[]{:S(2)}, u32[]{:S(2)}) %collective-permute-start.3) | collective-permute-done | bytes 131104 | tf_op jit(solution)/shard_map/ppermute | solution.py:132
  19.5 0.0 collective-permute-done.4
  19.5 0.0 collective-permute-done.5
  19.5 2.5 %collective-permute-start.11 = (f32[16,4,16,128]{3,2,1,0:T(8,128)S(1)}, f32[16,4,16,128]{3,2,1,0:T(8,128)S(1)}, u32[]{:S(2)}, u32[]{:S(2)}) collective-permute-start(f32[16,4,16,128]{3,2,1,0:T(8,128)S(1)} %constant_dynamic-update-slice_fusion.refs_0_), channel_id=1, source_target_pairs={{0,96},{32,0},{64,32},{96,64},{1,97},{33,1},{65,33},{97,65},{2,98}... | collective-permute-start | bytes 1572872 | tf_op jit(solution)/shard_map/ppermute | solution.py:132
  22.1 0.5 collective-permute-start.9
  22.6 0.6 collective-permute-start.7
  23.2 0.1 broadcast_add_fusion.2
  23.3 0.1 add.98
  23.4 4.4 %collective-permute-start.6 = (f32[16,4,16,128]{3,2,1,0:T(8,128)S(1)}, f32[16,4,16,128]{3,2,1,0:T(8,128)S(1)}, u32[]{:S(2)}, u32[]{:S(2)}) collective-permute-start(f32[16,4,16,128]{3,2,1,0:T(8,128)S(1)} %constant_dynamic-update-slice_fusion.refs_0_), channel_id=1, source_target_pairs={{0,16},{16,0},{1,17},{17,1},{2,18},{18,2},{3,19},{19,3},{4,20},{20... | collective-permute-start | bytes 1572872 | tf_op jit(solution)/shard_map/ppermute | solution.py:132
  27.8 2.7 %collective-permute-done.11.refs_6_ = f32[16,4,16,128]{3,2,1,0:T(8,128)S(1)} collective-permute-done((f32[16,4,16,128]{3,2,1,0:T(8,128)S(1)}, f32[16,4,16,128]{3,2,1,0:T(8,128)S(1)}, u32[]{:S(2)}, u32[]{:S(2)}) %collective-permute-start.11) | collective-permute-done | bytes 524320 | tf_op jit(solution)/shard_map/ppermute | solution.py:132
  30.5 14.9 %collective-permute-start.12 = (f32[16,4,16,128]{3,2,1,0:T(8,128)S(1)}, f32[16,4,16,128]{3,2,1,0:T(8,128)S(1)}, u32[]{:S(2)}, u32[]{:S(2)}) collective-permute-start(f32[16,4,16,128]{3,2,1,0:T(8,128)S(1)} %collective-permute-done.11.refs_6_), channel_id=1, source_target_pairs={{0,16},{16,0},{1,17},{17,1},{2,18},{18,2},{3,19},{19,3},{4,20},{20... | collective-permute-start | bytes 1572872 | tf_op jit(solution)/shard_map/ppermute | solution.py:132
  45.5 0.0 collective-permute-done.9.refs_4_
  45.5 0.0 collective-permute-start.10
  45.5 3.2 %collective-permute-done.7.refs_2_ = f32[16,4,16,128]{3,2,1,0:T(8,128)S(1)} collective-permute-done((f32[16,4,16,128]{3,2,1,0:T(8,128)S(1)}, f32[16,4,16,128]{3,2,1,0:T(8,128)S(1)}, u32[]{:S(2)}, u32[]{:S(2)}) %collective-permute-start.7) | collective-permute-done | bytes 524320 | tf_op jit(solution)/shard_map/ppermute | solution.py:132
  48.7 0.5 collective-permute-start.8
  49.2 0.1 broadcast_add_fusion.1
  49.2 0.1 add.103
  49.3 0.7 copy.11
  50.0 4.5 %all-to-all-start = ((s32[128,1,32]{2,1,0:T(1,128)}), s32[128,1,32]{2,1,0:T(1,128)S(1)}, u32[]{:S(2)}, u32[]{:S(2)}) async-start(s32[128,1,32]{2,1,0:T(1,128)} %bitcast.1), calls=%async_computation | async-start | bytes 131072 | tf_op jit(solution)/shard_map/all_to_all | solution.py:156
  54.5 0.0 copy-start
  54.5 0.1 broadcast_add_fusion
  54.6 0.0 copy-start.1
  54.6 0.1 add.108.order
  54.7 9.3 %all-to-all-done = s32[128,1,32]{2,1,0:T(1,128)S(1)} async-done(((s32[128,1,32]{2,1,0:T(1,128)}), s32[128,1,32]{2,1,0:T(1,128)S(1)}, u32[]{:S(2)}, u32[]{:S(2)}) %all-to-all-start) | async-done | bytes 16416 | tf_op jit(solution)/shard_map/all_to_all | solution.py:156
  64.0 0.0 collective-permute-done.6.refs_1_
  64.0 0.0 collective-permute-done.12.refs_7_
  64.0 0.0 collective-permute-done.10.refs_5_
  64.0 0.0 collective-permute-done.8.refs_3_
  64.0 0.0 copy-done
  64.1 0.0 copy-done.1
  64.1 17.5 %shard_map.85 = (f32[3,1024]{1,0:T(4,128)}, f32[1,1024]{1,0:T(1,128)}, f32[16,1024]{1,0:T(8,128)}) custom-call(s32[128]{0:T(128)S(1)} %add.108.order, s32[128,32]{1,0:T(8,128)S(1)} %bitcast.10, f32[3,1024]{1,0:T(4,128)S(1)} %copy-done, f32[1,1024]{1,0:T(1,128)S(1)} %bitcast.11, f32[16,4,16,128]{3,2,1,0:T(8,128)S(1)} %constant_dynamic-update-slice_fusion.refs_0_, ...), custom_call_target="tpu_custom_call" | custom-call | tf_op jit(solution)/shard_map/pallas_call | solution.py:158
  (13 shorter events, 0.1 us)
Async XLA Ops:
  0.6 0.8 copy-start.2
  1.4 7.2 %copy-start.3 = (s32[2048]{0:T(1024)S(1)}, s32[2048]{0:T(1024)}, u32[]{:S(2)}) copy-start(s32[2048]{0:T(1024)} %param.10) | copy-start | bytes 24580
  1.4 8.1 %collective-permute-start.1 = (f32[1,4,16,128]{3,2,1,0:T(8,128)S(1)}, f32[1,4,16,128]{3,2,1,0:T(8,128)S(1)}, u32[]{:S(2)}, u32[]{:S(2)}) collective-permute-start(f32[1,4,16,128]{3,2,1,0:T(8,128)S(1)} %get-tuple-element.13), channel_id=1, source_target_pairs={{0,2},{1,3},{2,0},{3,1},{4,6},{5,7},{6,4},{7,5},{8,10},{9,11},{10,... | collective-permute-start | bytes 98312 | tf_op jit(solution)/shard_map/ppermute | solution.py:132
  5.9 4.0 %collective-permute-start = (f32[1,4,16,128]{3,2,1,0:T(8,128)S(1)}, f32[1,4,16,128]{3,2,1,0:T(8,128)S(1)}, u32[]{:S(2)}, u32[]{:S(2)}) collective-permute-start(f32[1,4,16,128]{3,2,1,0:T(8,128)S(1)} %get-tuple-element.13), channel_id=1, source_target_pairs={{0,1},{1,2},{2,3},{3,0},{4,5},{5,6},{6,7},{7,4},{8,9},{9,10},{10,1... | collective-permute-start | bytes 98312 | tf_op jit(solution)/shard_map/ppermute | solution.py:132
  6.7 3.2 %collective-permute-start.2 = (f32[1,4,16,128]{3,2,1,0:T(8,128)S(1)}, f32[1,4,16,128]{3,2,1,0:T(8,128)S(1)}, u32[]{:S(2)}, u32[]{:S(2)}) collective-permute-start(f32[1,4,16,128]{3,2,1,0:T(8,128)S(1)} %get-tuple-element.13), channel_id=1, source_target_pairs={{0,3},{1,0},{2,1},{3,2},{4,7},{5,4},{6,5},{7,6},{8,11},{9,8},{10,9... | collective-permute-start | bytes 98312 | tf_op jit(solution)/shard_map/ppermute | solution.py:132
  8.7 0.7 copy-start.4
  9.9 9.6 %collective-permute-start.5 = (f32[4,4,16,128]{3,2,1,0:T(8,128)S(1)}, f32[4,4,16,128]{3,2,1,0:T(8,128)S(1)}, u32[]{:S(2)}, u32[]{:S(2)}) collective-permute-start(f32[4,4,16,128]{3,2,1,0:T(8,128)S(1)} %pad_maximum_fusion), channel_id=1, source_target_pairs={{0,12},{4,0},{8,4},{12,8},{1,13},{5,1},{9,5},{13,9},{2,14},{6,2},{... | collective-permute-start | bytes 393224 | tf_op jit(solution)/shard_map/ppermute | solution.py:132
  12.7 6.7 %collective-permute-start.4 = (f32[4,4,16,128]{3,2,1,0:T(8,128)S(1)}, f32[4,4,16,128]{3,2,1,0:T(8,128)S(1)}, u32[]{:S(2)}, u32[]{:S(2)}) collective-permute-start(f32[4,4,16,128]{3,2,1,0:T(8,128)S(1)} %pad_maximum_fusion), channel_id=1, source_target_pairs={{0,8},{4,12},{8,0},{12,4},{1,9},{5,13},{9,1},{13,5},{2,10},{6,14},... | collective-permute-start | bytes 393224 | tf_op jit(solution)/shard_map/ppermute | solution.py:132
  13.1 6.4 %collective-permute-start.3 = (f32[4,4,16,128]{3,2,1,0:T(8,128)S(1)}, f32[4,4,16,128]{3,2,1,0:T(8,128)S(1)}, u32[]{:S(2)}, u32[]{:S(2)}) collective-permute-start(f32[4,4,16,128]{3,2,1,0:T(8,128)S(1)} %pad_maximum_fusion), channel_id=1, source_target_pairs={{0,4},{4,8},{8,12},{12,0},{1,5},{5,9},{9,13},{13,1},{2,6},{6,10},{... | collective-permute-start | bytes 393224 | tf_op jit(solution)/shard_map/ppermute | solution.py:132
  19.5 11.0 %collective-permute-start.11 = (f32[16,4,16,128]{3,2,1,0:T(8,128)S(1)}, f32[16,4,16,128]{3,2,1,0:T(8,128)S(1)}, u32[]{:S(2)}, u32[]{:S(2)}) collective-permute-start(f32[16,4,16,128]{3,2,1,0:T(8,128)S(1)} %constant_dynamic-update-slice_fusion.refs_0_), channel_id=1, source_target_pairs={{0,96},{32,0},{64,32},{96,64},{1,97},{33,1},{65,33},{97,65},{2,98}... | collective-permute-start | bytes 1572872 | tf_op jit(solution)/shard_map/ppermute | solution.py:132
  22.1 23.4 %collective-permute-start.9 = (f32[16,4,16,128]{3,2,1,0:T(8,128)S(1)}, f32[16,4,16,128]{3,2,1,0:T(8,128)S(1)}, u32[]{:S(2)}, u32[]{:S(2)}) collective-permute-start(f32[16,4,16,128]{3,2,1,0:T(8,128)S(1)} %constant_dynamic-update-slice_fusion.refs_0_), channel_id=1, source_target_pairs={{0,64},{32,96},{64,0},{96,32},{1,65},{33,97},{65,1},{97,33},{2,66}... | collective-permute-start | bytes 1572872 | tf_op jit(solution)/shard_map/ppermute | solution.py:132
  22.6 26.1 %collective-permute-start.7 = (f32[16,4,16,128]{3,2,1,0:T(8,128)S(1)}, f32[16,4,16,128]{3,2,1,0:T(8,128)S(1)}, u32[]{:S(2)}, u32[]{:S(2)}) collective-permute-start(f32[16,4,16,128]{3,2,1,0:T(8,128)S(1)} %constant_dynamic-update-slice_fusion.refs_0_), channel_id=1, source_target_pairs={{0,32},{32,64},{64,96},{96,0},{1,33},{33,65},{65,97},{97,1},{2,34}... | collective-permute-start | bytes 1572872 | tf_op jit(solution)/shard_map/ppermute | solution.py:132
  23.4 40.6 %collective-permute-start.6 = (f32[16,4,16,128]{3,2,1,0:T(8,128)S(1)}, f32[16,4,16,128]{3,2,1,0:T(8,128)S(1)}, u32[]{:S(2)}, u32[]{:S(2)}) collective-permute-start(f32[16,4,16,128]{3,2,1,0:T(8,128)S(1)} %constant_dynamic-update-slice_fusion.refs_0_), channel_id=1, source_target_pairs={{0,16},{16,0},{1,17},{17,1},{2,18},{18,2},{3,19},{19,3},{4,20},{20... | collective-permute-start | bytes 1572872 | tf_op jit(solution)/shard_map/ppermute | solution.py:132
  30.5 33.5 %collective-permute-start.12 = (f32[16,4,16,128]{3,2,1,0:T(8,128)S(1)}, f32[16,4,16,128]{3,2,1,0:T(8,128)S(1)}, u32[]{:S(2)}, u32[]{:S(2)}) collective-permute-start(f32[16,4,16,128]{3,2,1,0:T(8,128)S(1)} %collective-permute-done.11.refs_6_), channel_id=1, source_target_pairs={{0,16},{16,0},{1,17},{17,1},{2,18},{18,2},{3,19},{19,3},{4,20},{20... | collective-permute-start | bytes 1572872 | tf_op jit(solution)/shard_map/ppermute | solution.py:132
  45.5 18.6 %collective-permute-start.10 = (f32[16,4,16,128]{3,2,1,0:T(8,128)S(1)}, f32[16,4,16,128]{3,2,1,0:T(8,128)}, u32[]{:S(2)}, u32[]{:S(2)}) collective-permute-start(f32[16,4,16,128]{3,2,1,0:T(8,128)S(1)} %collective-permute-done.9.refs_4_), channel_id=1, source_target_pairs={{0,16},{16,0},{1,17},{17,1},{2,18},{18,2},{3,19},{19,3},{4,20},{20... | collective-permute-start | bytes 1572872 | tf_op jit(solution)/shard_map/ppermute | solution.py:132
  48.7 15.4 %collective-permute-start.8 = (f32[16,4,16,128]{3,2,1,0:T(8,128)S(1)}, f32[16,4,16,128]{3,2,1,0:T(8,128)}, u32[]{:S(2)}, u32[]{:S(2)}) collective-permute-start(f32[16,4,16,128]{3,2,1,0:T(8,128)S(1)} %collective-permute-done.7.refs_2_), channel_id=1, source_target_pairs={{0,16},{16,0},{1,17},{17,1},{2,18},{18,2},{3,19},{19,3},{4,20},{20... | collective-permute-start | bytes 1572872 | tf_op jit(solution)/shard_map/ppermute | solution.py:132
  50.0 14.0 %all-to-all-start = ((s32[128,1,32]{2,1,0:T(1,128)}), s32[128,1,32]{2,1,0:T(1,128)S(1)}, u32[]{:S(2)}, u32[]{:S(2)}) async-start(s32[128,1,32]{2,1,0:T(1,128)} %bitcast.1), calls=%async_computation | async-start | bytes 131072 | tf_op jit(solution)/shard_map/all_to_all | solution.py:156
  54.5 9.5 %copy-start = (f32[3,1024]{1,0:T(4,128)S(1)}, f32[3,1024]{1,0:T(4,128)}, u32[]{:S(2)}) copy-start(f32[3,1024]{1,0:T(4,128)} %centers.1) | copy-start | bytes 36868
  54.6 9.5 %copy-start.1 = (f32[1024]{0:T(1024)S(1)}, f32[1024]{0:T(1024)}, u32[]{:S(2)}) copy-start(f32[1024]{0:T(1024)} %param.9) | copy-start | bytes 12292

commit v3 on v2

v3 whole, which is shorter than its diff:
```python
import functools

import jax
import jax.numpy as jnp
from jax import lax
from jax.experimental import pallas as pl
from jax.experimental.pallas import tpu as pltpu
from jax.sharding import Mesh, PartitionSpec as P

SHELLS = 16
BLOCK = 128
LANES = 128
ROWS = 24
AXES = ("x", "core", "y", "z")
VMEM = pl.BlockSpec(memory_space=pltpu.VMEM)
PARAMS = pltpu.CompilerParams(vmem_limit_bytes=16 * 2**20)


def f32(*shape):
    return jax.ShapeDtypeStruct(shape, jnp.float32)


def split(value, terms):
    parts = []
    for _ in range(terms):
        part = value.astype(jnp.bfloat16)
        parts.append(part)
        value = value - part.astype(jnp.float32)
    return parts


def gather_state(center, radius, one_hot):
    state = jnp.concatenate([center, radius], axis=0)
    stacked = jnp.concatenate([s.astype(jnp.float32) for s in split(state, 3)] + [jnp.zeros_like(state)], axis=0)
    got = jnp.dot(stacked.astype(jnp.bfloat16), one_hot, preferred_element_type=jnp.float32)
    return got[0:4] + got[4:8] + got[8:12]


def prepare(blocks, order, asked, centers, radii, one_hot, slot_state, wide):
    halos = radii.shape[1]
    slots = asked.shape[1] // 2
    tiles = slot_state.shape[0]
    group = LANES // slots
    wide[...] = jnp.zeros_like(wide)
    for d in range(wide.shape[0]):
        wide[d : d + 1, : 2 * slots] = asked[pl.ds(order[d], 1)].astype(jnp.float32)
    lane = lax.broadcasted_iota(jnp.int32, (group, LANES), 1)
    own = lane // slots == lax.broadcasted_iota(jnp.int32, (group, LANES), 0)
    lanes = lax.broadcasted_iota(jnp.int32, wide.shape, 1)
    rows = []
    for which in range(2):
        row = jnp.where(lanes // slots == which, wide[...], 0.0)
        shift = slots
        while shift < LANES:
            row = row + pltpu.roll(row, shift, 1)
            shift *= 2
        rows.append([jnp.sum(jnp.where(own, row[t * group : (t + 1) * group], 0.0), axis=0, keepdims=True) for t in range(tiles)])
    halo_rows, block_rows = rows
    halo_index = lax.broadcasted_iota(jnp.int32, (halos, LANES), 0).astype(jnp.float32)
    first = (lax.broadcasted_iota(jnp.int32, (1, LANES), 1) // slots * blocks).astype(jnp.float32)
    for t in range(tiles):
        hit = halo_index == halo_rows[t]
        one_hot[:, t * LANES : (t + 1) * LANES] = jnp.where(hit, 1.0, 0.0).astype(jnp.bfloat16)
    got = gather_state(centers[...], radii[...], one_hot[...])
    for t in range(tiles):
        slot_state[t] = jnp.concatenate(
            [got[:, t * LANES : (t + 1) * LANES], block_rows[t] + first, jnp.zeros((3, LANES), jnp.float32)], axis=0
        )


def tile_sums(mine, points, t, out, o):
    cx, cy, cz, rad = mine[0:1], mine[1:2], mine[2:3], mine[3:4]
    scale = (SHELLS / 2.0) / jnp.where(rad > 0.0, rad, 1.0)
    ramps = [None] * (SHELLS + 1)
    inner = [None] * 4

    def add(sums, k, value):
        sums[k] = value if sums[k] is None else sums[k] + value

    for p in range(0, BLOCK, 8):
        x = points[t, 0, p : p + 8] - cx
        y = points[t, 1, p : p + 8] - cy
        z = points[t, 2, p : p + 8] - cz
        mass = points[t, 3, p : p + 8]
        scaled = jnp.sqrt(x * x + y * y + z * z) * scale
        half = mass * 0.5
        reach = half - mass * scaled
        for k in range(SHELLS + 1):
            add(ramps, k, jnp.maximum(reach, 0.0))
            if k == SHELLS // 2 - 1:
                weight = jnp.maximum(jnp.minimum(reach + half, mass), 0.0)
            reach = reach + mass
        add(inner, 0, weight)
        add(inner, 1, weight * x)
        add(inner, 2, weight * y)
        add(inner, 3, weight * z)
    for k in range(SHELLS):
        cumulative = ramps[k + 1] - ramps[k] - ramps[0]
        out[o, k : k + 1] = jnp.sum(cumulative, axis=0, keepdims=True)
    for k in range(4):
        out[o, SHELLS + k : SHELLS + k + 1] = jnp.sum(inner[k], axis=0, keepdims=True)


def first_pass(offset, group, slot_state, *refs):
    chunks, (points, partial) = refs[:-2], refs[-2:]
    chunk, _, blocks, _ = chunks[0].shape
    count = group * blocks
    tiles = chunk // group
    block_index = lax.broadcasted_iota(jnp.int32, (count, LANES), 0).astype(jnp.float32)
    partial[...] = jnp.zeros_like(partial)
    for t in range(tiles * len(chunks)):
        hit = block_index == slot_state[offset + t, 4:5]
        pick = jnp.where(hit, 1.0, 0.0).astype(jnp.bfloat16)
        at = t % tiles * group
        for c in range(4):
            chosen = chunks[t // tiles][at : at + group, c].reshape(count, BLOCK).T
            high, low = split(chosen, 2)
            points[t, c] = jnp.dot(high, pick, preferred_element_type=jnp.float32) + jnp.dot(
                low, pick, preferred_element_type=jnp.float32
            )

    def one_tile(t, carry):
        tile_sums(slot_state[offset + t], points, t, partial, t)
        return carry

    lax.fori_loop(0, tiles * len(chunks), one_tile, 0)


def finish(slabs, one_hot, centers, radii, *refs):
    points, partials = refs[:slabs], refs[slabs : 2 * slabs]
    centers_out, radii_out, profile_out, slot_state, partial = refs[2 * slabs :]
    tiles = slot_state.shape[0]
    each = tiles // slabs

    def advance(center, radius, terms):
        high, low = split(terms, 2)
        across = (((1,), (1,)), ((), ()))
        sums = lax.dot_general(high, one_hot[...], across, preferred_element_type=jnp.float32) + lax.dot_general(
            low, one_hot[...], across, preferred_element_type=jnp.float32
        )
        profile = sums[:SHELLS]
        enclosed = profile[SHELLS // 2 - 1 : SHELLS // 2]
        ratio = (1.0 + enclosed) / (1.0 + radius * radius * radius)
        radius = radius * jnp.exp(jnp.log(ratio) * (1.0 / 3.0))
        center = center + sums[SHELLS + 1 : SHELLS + 4] / jnp.maximum(sums[SHELLS : SHELLS + 1], 1.0)
        return center, radius, profile

    terms = jnp.concatenate([partials[t // each][t % each] for t in range(tiles)], axis=1)
    center, radius, _ = advance(centers[...], radii[...], terms)
    got = gather_state(center, radius, one_hot[...])
    for t in range(tiles):
        slot_state[t, 0:4] = got[:, t * LANES : (t + 1) * LANES]
    partial[...] = jnp.zeros_like(partial)
    for slab in range(slabs):

        def one_tile(t, carry):
            tile_sums(slot_state[slab * each + t], points[slab], t, partial, slab * each + t)
            return carry

        lax.fori_loop(0, each, one_tile, 0)
    terms = jnp.concatenate([partial[t] for t in range(tiles)], axis=1)
    center, radius, profile = advance(center, radius, terms)
    centers_out[...] = center
    radii_out[...] = radius
    profile_out[...] = profile


def shifted(value, axis):
    size = lax.axis_size(axis)
    return [value] + [lax.ppermute(value, axis, [(i, (i + k) % size) for i in range(size)]) for k in range(1, size)]


def sources():
    index = jnp.zeros((1,), jnp.int32)
    for axis, stride in (("x", 32), ("core", 16), ("y", 4), ("z", 1)):
        size = lax.axis_size(axis)
        here = (lax.axis_index(axis) - jnp.arange(size, dtype=jnp.int32)) % size * stride
        index = (index[:, None] + here[None, :]).reshape(-1)
    return index


def body(positions, masses, centers, radii, pair_block, pair_halo):
    devices = lax.axis_size(AXES)
    halos = radii.shape[0]
    blocks = masses.shape[0] // BLOCK
    slots = pair_halo.shape[0] // devices
    tiles = devices * slots // LANES
    pairs = jnp.concatenate([pair_halo.reshape(devices, slots), pair_block.reshape(devices, slots)], axis=1)
    plane = jnp.concatenate([positions, masses[None]], axis=0).reshape(1, 4, blocks, BLOCK)
    order = sources()
    for axis in ("z", "y"):
        plane = jnp.concatenate(shifted(plane, axis), axis=0)
    plane, pairs, order = lax.optimization_barrier((plane, pairs, order))
    slabs = shifted(plane, "x")
    asked = lax.all_to_all(pairs, AXES, split_axis=0, concat_axis=0, tiled=True)
    radii = radii[None]
    one_hot, slot_state = pl.pallas_call(
        functools.partial(prepare, blocks),
        in_specs=[pl.BlockSpec(memory_space=pltpu.SMEM), VMEM, VMEM, VMEM],
        out_specs=[VMEM] * 2,
        out_shape=(jax.ShapeDtypeStruct((halos, devices * slots), jnp.bfloat16), f32(tiles, 8, LANES)),
        scratch_shapes=[pltpu.VMEM((devices, LANES), jnp.float32)],
        compiler_params=PARAMS,
    )(order, asked, centers, radii)
    each = tiles // len(slabs)
    points, partials = [], []
    for i, slab in enumerate(slabs):
        if i:
            slab, _ = lax.optimization_barrier((slab, partials[0]))
        got = pl.pallas_call(
            functools.partial(first_pass, i * each, LANES // slots),
            in_specs=[VMEM] * 3,
            out_specs=[VMEM] * 2,
            out_shape=(f32(each, 4, BLOCK, LANES), f32(each, ROWS, LANES)),
            compiler_params=PARAMS,
        )(slot_state, *shifted(slab, "core"))
        points.append(got[0])
        partials.append(got[1])
    centers, radii, profile = pl.pallas_call(
        functools.partial(finish, len(slabs)),
        in_specs=[VMEM] * (3 + 2 * len(slabs)),
        out_specs=[VMEM] * 3,
        out_shape=(f32(3, halos), f32(1, halos), f32(SHELLS, halos)),
        scratch_shapes=[pltpu.VMEM((tiles, 8, LANES), jnp.float32), pltpu.VMEM((tiles, ROWS, LANES), jnp.float32)],
        compiler_params=PARAMS,
    )(one_hot, centers, radii, *points, *partials)
    return (centers, radii[0], profile)


def solution(mesh):
    chips = Mesh(mesh.devices.reshape(4, 2, 4, 4), AXES)
    in_specs = (
        P(None, AXES),
        P(AXES),
        P(None, AXES),
        P(AXES),
        P(AXES),
        P(AXES),
    )
    out_specs = (P(None, AXES), P(AXES), P(None, AXES))
    return jax.shard_map(body, mesh=chips, in_specs=in_specs, out_specs=out_specs, check_vma=False)
```

time: 81.9 us -> 78.4 us (0.957)
  blocking collectives: 0 us -> 27.5 us
  starting transfers between devices: 39 us -> 17.5 us
  waiting for transfers between devices: 21.2 us -> 8.7 us
  local copies, waits for them, and re-layouts: 2.72 us -> 4.3 us
  other arithmetic: 0.28 us -> 1.68 us
    all_to_all x0 -> x1, blocking collectives: none -> 27.5 us  [body(): asked = lax.all_to_all(pairs, AXES, split_axis=0, concat_axis=0, tiled=True)]
    ppermute x13, starting transfers between devices: 34.6 us -> 17.5 us  [shifted(): lax.ppermute(value, axis, [(i, (i + k) % size) for i in range(size)])]
    all_to_all x1 -> x0, waiting for transfers between devices: 9.31 us -> none  [body(): asked = lax.all_to_all(pairs, AXES, split_axis=0, concat_axis=0, tiled=True)]
    all_to_all x1 -> x0, starting transfers between devices: 4.47 us -> none  [body(): asked = lax.all_to_all(pairs, AXES, split_axis=0, concat_axis=0, tiled=True)]
    ppermute x13, waiting for transfers between devices: 11.9 us -> 8.7 us  [shifted(): lax.ppermute(value, axis, [(i, (i + k) % size) for i in range(size)])]
    unnamed x16 -> x14, local copies, waits for them, and re-layouts: 1.46 us -> 2.22 us
    pallas_call x1 -> x6, Pallas kernels: 17.5 us -> 17.4 us  [the longest x1 9.66 us: body(): pl.pallas_call(functools.partial(finish, len(slabs)), in_specs=[VMEM] * (...]
  transfers between devices with their start and end apart: 14 -> 13, of which waited for: 5 -> 2; matrix products, arithmetic and copies ran while one was open for 2% -> 3% of each run, Pallas kernels for 0% -> 8%
where the time goes in v3:
time: 78.4 us; the launch traced here: 77.9 us
  blocking collectives  27.5 us (35%)
  starting transfers between devices  17.5 us (22%)
  Pallas kernels  17.4 us (22%)
  waiting for transfers between devices  8.7 us (11%)
  local copies, waits for them, and re-layouts  4.3 us (5%)
  other arithmetic  1.68 us (2%)
  between operations  0.86 us (1%)
    all_to_all x1, blocking collectives, body(): asked = lax.all_to_all(pairs, AXES, split_axis=0, concat_axis=0, tiled=True)  27.5 us
    ppermute x13, starting transfers between devices, shifted(): lax.ppermute(value, axis, [(i, (i + k) % size) for i in range(size)])  17.5 us
    pallas_call x1, Pallas kernels, body(): pl.pallas_call(functools.partial(finish, len(slabs)), in_specs=[VMEM] * (...  9.66 us
    ppermute x13, waiting for transfers between devices, shifted(): lax.ppermute(value, axis, [(i, (i + k) % size) for i in range(size)])  8.7 us
    pallas_call x4, Pallas kernels, body(): pl.pallas_call(functools.partial(first_pass, i * each, LANES // slots), i...  5.29 us
    pallas_call x1, Pallas kernels, body(): pl.pallas_call(functools.partial(prepare, blocks), in_specs=[pl.BlockSpec...  2.4 us
    unnamed x14, local copies, waits for them, and re-layouts  2.22 us
  transfers between devices with their start and end apart: 13, of which 2 were waited for; matrix products, arithmetic and copies ran while one was open for 3% of the time, Pallas kernels for 8%

profile of v3, /device:TPU:1, one launch (start us, length us, event | category | flops | bytes accessed | tf_op | source)
XLA Modules:
  0.0 77.9 jit_solution(7002830222239923491)
XLA Ops:
  0.6 0.0 copy-start.1
  0.6 0.0 copy-start.3
  0.7 0.8 copy.14
  1.4 0.7 pad_maximum_fusion.1
  2.1 4.4 %collective-permute-start.1 = (f32[1,4,16,128]{3,2,1,0:T(8,128)S(1)}, f32[1,4,16,128]{3,2,1,0:T(8,128)S(1)}, u32[]{:S(2)}, u32[]{:S(2)}) collective-permute-start(f32[1,4,16,128]{3,2,1,0:T(8,128)S(1)} %get-tuple-element.41), channel_id=1, source_target_pairs={{0,2},{1,3},{2,0},{3,1},{4,6},{5,7},{6,4},{7,5},{8,10},{9,11},{10,... | collective-permute-start | bytes 98312 | tf_op jit(solution)/shard_map/ppermute | solution.py:170
  6.6 0.7 collective-permute-start
  7.3 1.9 %collective-permute-start.2 = (f32[1,4,16,128]{3,2,1,0:T(8,128)S(1)}, f32[1,4,16,128]{3,2,1,0:T(8,128)S(1)}, u32[]{:S(2)}, u32[]{:S(2)}) collective-permute-start(f32[1,4,16,128]{3,2,1,0:T(8,128)S(1)} %get-tuple-element.41), channel_id=1, source_target_pairs={{0,3},{1,0},{2,1},{3,2},{4,7},{5,4},{6,5},{7,6},{8,11},{9,8},{10,9... | collective-permute-start | bytes 98312 | tf_op jit(solution)/shard_map/ppermute | solution.py:170
  9.3 0.1 broadcast_add_fusion.2
  9.4 0.1 add.98
  9.4 0.1 broadcast_add_fusion.1
  9.5 0.1 add.103
  9.6 0.8 reshape.114
  10.4 0.1 copy.10
  10.4 0.8 %reshape.113 = s32[128,16]{1,0:T(8,128)S(1)} reshape(s32[2048]{0:T(1024)} %param.11) | data formatting | bytes 16384 | tf_op jit(solution)/shard_map/reshape | solution.py:188
  11.2 0.1 copy.9
  11.3 0.1 broadcast_add_fusion
  11.4 0.1 add.108.order
  11.5 0.0 collective-permute-done.1
  11.5 0.0 collective-permute-done
  11.5 0.0 collective-permute-done.2
  11.5 0.7 pad_maximum_fusion
  12.2 2.8 %collective-permute-start.5 = (f32[4,4,16,128]{3,2,1,0:T(8,128)S(1)}, f32[4,4,16,128]{3,2,1,0:T(8,128)S(1)}, u32[]{:S(2)}, u32[]{:S(2)}) collective-permute-start(f32[4,4,16,128]{3,2,1,0:T(8,128)S(1)} %pad_maximum_fusion), channel_id=1, source_target_pairs={{0,12},{4,0},{8,4},{12,8},{1,13},{5,1},{9,5},{13,9},{2,14},{6,2},{... | collective-permute-start | bytes 393224 | tf_op jit(solution)/shard_map/ppermute | solution.py:170
  15.0 0.3 collective-permute-start.4
  15.4 0.7 collective-permute-start.3
  16.1 7.6 %collective-permute-done.3 = f32[4,4,16,128]{3,2,1,0:T(8,128)S(1)} collective-permute-done((f32[4,4,16,128]{3,2,1,0:T(8,128)S(1)}, f32[4,4,16,128]{3,2,1,0:T(8,128)S(1)}, u32[]{:S(2)}, u32[]{:S(2)}) %collective-permute-start.3) | collective-permute-done | bytes 131104 | tf_op jit(solution)/shard_map/ppermute | solution.py:170
  23.8 0.0 collective-permute-done.4
  23.8 0.0 collective-permute-done.5
  23.8 1.6 %collective-permute-start.6 = (f32[16,4,16,128]{3,2,1,0:T(8,128)S(1)}, f32[16,4,16,128]{3,2,1,0:T(8,128)S(1)}, u32[]{:S(2)}, u32[]{:S(2)}) collective-permute-start(f32[16,4,16,128]{3,2,1,0:T(8,128)S(1)} %constant_dynamic-update-slice_fusion.refs_0_), channel_id=1, source_target_pairs={{0,16},{16,0},{1,17},{17,1},{2,18},{18,2},{3,19},{19,3},{4,20},{20... | collective-permute-start | bytes 1572872 | tf_op jit(solution)/shard_map/ppermute | solution.py:170
  25.4 2.5 %collective-permute-start.11 = (f32[16,4,16,128]{3,2,1,0:T(8,128)S(1)}, f32[16,4,16,128]{3,2,1,0:T(8,128)S(1)}, u32[]{:S(2)}, u32[]{:S(2)}) collective-permute-start(f32[16,4,16,128]{3,2,1,0:T(8,128)S(1)} %constant_dynamic-update-slice_fusion.refs_0_), channel_id=1, source_target_pairs={{0,96},{32,0},{64,32},{96,64},{1,97},{33,1},{65,33},{97,65},{2,98}... | collective-permute-start | bytes 1572872 | tf_op jit(solution)/shard_map/ppermute | solution.py:170
  27.9 0.5 collective-permute-start.9
  28.4 0.6 collective-permute-start.7
  29.0 0.1 copy.11
  29.1 27.5 %all_to_all.11 = s32[128,1,32]{2,1,0:T(1,128)S(1)} all-to-all(s32[128,1,32]{2,1,0:T(1,128)S(1)} %bitcast.13), channel_id=1, replica_groups=mesh['x'=4,'core'=2,'y'=4,'z'=4] {'x','core','y','z'}, dimensions={0} | all-to-all | bytes 32768 | tf_op jit(solution)/shard_map/all_to_all | solution.py:195
  56.7 0.0 copy-start
  56.7 0.7 copy-done
  57.4 0.0 copy-start.2
  57.4 0.7 copy-done.2
  58.1 2.4 %shard_map.85 = (bf16[1024,2048]{1,0:T(8,128)(2,1)S(1)}, f32[16,8,128]{2,1,0:T(8,128)S(1)}) custom-call(s32[128]{0:T(128)S(1)} %add.108.order, s32[128,32]{1,0:T(8,128)S(1)} %bitcast.10, f32[3,1024]{1,0:T(4,128)S(1)} %copy-done, f32[1,1024]{1,0:T(1,128)S(1)} %bitcast.11), custom_call_target="tpu_custom_call" | custom-call | tf_op jit(solution)/shard_map/pallas_call | solution.py:197
  60.5 0.0 collective-permute-done.6.refs_1_
  60.5 1.3 %shard_map.86 = (f32[4,4,128,128]{3,2,1,0:T(8,128)S(1)}, f32[4,24,128]{2,1,0:T(8,128)S(1)}) custom-call(f32[16,8,128]{2,1,0:T(8,128)S(1)} %get-tuple-element.25.slot_state, f32[16,4,16,128]{3,2,1,0:T(8,128)S(1)} %constant_dynamic-update-slice_fusion.refs_0_, f32[16,4,16,128]{3,2,1,0:T(8,128)S(1)} %collective-permute-done.6.refs_1_), custom_call_target="tpu_custom_call" | custom-call | tf_op jit(solution)/shard_map/pallas_call | solution.py:210
  61.8 0.0 collective-permute-done.11.refs_0_
  61.8 0.0 collective-permute-done.9.refs_0_
  61.8 0.0 collective-permute-done.7.refs_0_
  61.8 0.9 %collective-permute-start.8 = (f32[16,4,16,128]{3,2,1,0:T(8,128)S(1)}, f32[16,4,16,128]{3,2,1,0:T(8,128)S(1)}, u32[]{:S(2)}, u32[]{:S(2)}) collective-permute-start(f32[16,4,16,128]{3,2,1,0:T(8,128)S(1)} %collective-permute-done.7.refs_0_), channel_id=1, source_target_pairs={{0,16},{16,0},{1,17},{17,1},{2,18},{18,2},{3,19},{19,3},{4,20},{20... | collective-permute-start | bytes 1572872 | tf_op jit(solution)/shard_map/ppermute | solution.py:170
  62.7 0.1 collective-permute-start.10
  62.8 0.4 collective-permute-start.12
  63.2 1.0 %collective-permute-done.8.refs_1_ = f32[16,4,16,128]{3,2,1,0:T(8,128)S(1)} collective-permute-done((f32[16,4,16,128]{3,2,1,0:T(8,128)S(1)}, f32[16,4,16,128]{3,2,1,0:T(8,128)S(1)}, u32[]{:S(2)}, u32[]{:S(2)}) %collective-permute-start.8) | collective-permute-done | bytes 524320 | tf_op jit(solution)/shard_map/ppermute | solution.py:170
  64.2 1.3 %shard_map.87 = (f32[4,4,128,128]{3,2,1,0:T(8,128)S(1)}, f32[4,24,128]{2,1,0:T(8,128)S(1)}) custom-call(f32[16,8,128]{2,1,0:T(8,128)S(1)} %get-tuple-element.25.slot_state, f32[16,4,16,128]{3,2,1,0:T(8,128)S(1)} %collective-permute-done.7.refs_0_, f32[16,4,16,128]{3,2,1,0:T(8,128)S(1)} %collective-permute-done.8.refs_1_), custom_call_target="tpu_custom_call" | custom-call | tf_op jit(solution)/shard_map/pallas_call | solution.py:210
  65.6 0.0 collective-permute-done.10.refs_1_
  65.6 1.3 %shard_map.88 = (f32[4,4,128,128]{3,2,1,0:T(8,128)S(1)}, f32[4,24,128]{2,1,0:T(8,128)S(1)}) custom-call(f32[16,8,128]{2,1,0:T(8,128)S(1)} %get-tuple-element.25.slot_state, f32[16,4,16,128]{3,2,1,0:T(8,128)S(1)} %collective-permute-done.9.refs_0_, f32[16,4,16,128]{3,2,1,0:T(8,128)S(1)} %collective-permute-done.10.refs_1_), custom_call_target="tpu_custom_call" | custom-call | tf_op jit(solution)/shard_map/pallas_call | solution.py:210
  66.9 0.0 collective-permute-done.12.refs_1_
  66.9 1.3 %shard_map.89 = (f32[4,4,128,128]{3,2,1,0:T(8,128)S(1)}, f32[4,24,128]{2,1,0:T(8,128)S(1)}) custom-call(f32[16,8,128]{2,1,0:T(8,128)S(1)} %get-tuple-element.25.slot_state, f32[16,4,16,128]{3,2,1,0:T(8,128)S(1)} %collective-permute-done.11.refs_0_, f32[16,4,16,128]{3,2,1,0:T(8,128)S(1)} %collective-permute-done.12.refs_1_), custom_call_target="tpu_custom_call" | custom-call | tf_op jit(solution)/shard_map/pallas_call | solution.py:210
  68.3 0.0 copy-done.1
  68.3 0.0 copy-done.3
  68.3 9.7 %shard_map.90 = (f32[3,1024]{1,0:T(4,128)}, f32[1,1024]{1,0:T(1,128)}, f32[16,1024]{1,0:T(8,128)}) custom-call(bf16[1024,2048]{1,0:T(8,128)(2,1)S(1)} %get-tuple-element.24.one_hot, f32[3,1024]{1,0:T(4,128)S(1)} %copy-done.1, f32[1,1024]{1,0:T(1,128)S(1)} %bitcast.12, f32[4,4,128,128]{3,2,1,0:T(8,128)S(1)} %get-tuple-element.27.refs_0_, ...), custom_call_target="tpu_custom_call" | custom-call | tf_op jit(solution)/shard_map/pallas_call | solution.py:219
  (11 shorter events, 0.1 us)
Async XLA Ops:
  0.6 67.6 %copy-start.1 = (f32[3,1024]{1,0:T(4,128)S(1)}, f32[3,1024]{1,0:T(4,128)}, u32[]{:S(2)}) copy-start(f32[3,1024]{1,0:T(4,128)} %centers.3) | copy-start | bytes 36868
  0.6 67.6 %copy-start.3 = (f32[1024]{0:T(1024)S(1)}, f32[1024]{0:T(1024)}, u32[]{:S(2)}) copy-start(f32[1024]{0:T(1024)} %param.9) | copy-start | bytes 12292
  2.1 9.4 %collective-permute-start.1 = (f32[1,4,16,128]{3,2,1,0:T(8,128)S(1)}, f32[1,4,16,128]{3,2,1,0:T(8,128)S(1)}, u32[]{:S(2)}, u32[]{:S(2)}) collective-permute-start(f32[1,4,16,128]{3,2,1,0:T(8,128)S(1)} %get-tuple-element.41), channel_id=1, source_target_pairs={{0,2},{1,3},{2,0},{3,1},{4,6},{5,7},{6,4},{7,5},{8,10},{9,11},{10,... | collective-permute-start | bytes 98312 | tf_op jit(solution)/shard_map/ppermute | solution.py:170
  6.6 5.0 %collective-permute-start = (f32[1,4,16,128]{3,2,1,0:T(8,128)S(1)}, f32[1,4,16,128]{3,2,1,0:T(8,128)S(1)}, u32[]{:S(2)}, u32[]{:S(2)}) collective-permute-start(f32[1,4,16,128]{3,2,1,0:T(8,128)S(1)} %get-tuple-element.41), channel_id=1, source_target_pairs={{0,1},{1,2},{2,3},{3,0},{4,5},{5,6},{6,7},{7,4},{8,9},{9,10},{10,1... | collective-permute-start | bytes 98312 | tf_op jit(solution)/shard_map/ppermute | solution.py:170
  7.3 4.2 %collective-permute-start.2 = (f32[1,4,16,128]{3,2,1,0:T(8,128)S(1)}, f32[1,4,16,128]{3,2,1,0:T(8,128)S(1)}, u32[]{:S(2)}, u32[]{:S(2)}) collective-permute-start(f32[1,4,16,128]{3,2,1,0:T(8,128)S(1)} %get-tuple-element.41), channel_id=1, source_target_pairs={{0,3},{1,0},{2,1},{3,2},{4,7},{5,4},{6,5},{7,6},{8,11},{9,8},{10,9... | collective-permute-start | bytes 98312 | tf_op jit(solution)/shard_map/ppermute | solution.py:170
  12.2 11.6 %collective-permute-start.5 = (f32[4,4,16,128]{3,2,1,0:T(8,128)S(1)}, f32[4,4,16,128]{3,2,1,0:T(8,128)S(1)}, u32[]{:S(2)}, u32[]{:S(2)}) collective-permute-start(f32[4,4,16,128]{3,2,1,0:T(8,128)S(1)} %pad_maximum_fusion), channel_id=1, source_target_pairs={{0,12},{4,0},{8,4},{12,8},{1,13},{5,1},{9,5},{13,9},{2,14},{6,2},{... | collective-permute-start | bytes 393224 | tf_op jit(solution)/shard_map/ppermute | solution.py:170
  15.0 8.7 %collective-permute-start.4 = (f32[4,4,16,128]{3,2,1,0:T(8,128)S(1)}, f32[4,4,16,128]{3,2,1,0:T(8,128)S(1)}, u32[]{:S(2)}, u32[]{:S(2)}) collective-permute-start(f32[4,4,16,128]{3,2,1,0:T(8,128)S(1)} %pad_maximum_fusion), channel_id=1, source_target_pairs={{0,8},{4,12},{8,0},{12,4},{1,9},{5,13},{9,1},{13,5},{2,10},{6,14},... | collective-permute-start | bytes 393224 | tf_op jit(solution)/shard_map/ppermute | solution.py:170
  15.4 8.4 %collective-permute-start.3 = (f32[4,4,16,128]{3,2,1,0:T(8,128)S(1)}, f32[4,4,16,128]{3,2,1,0:T(8,128)S(1)}, u32[]{:S(2)}, u32[]{:S(2)}) collective-permute-start(f32[4,4,16,128]{3,2,1,0:T(8,128)S(1)} %pad_maximum_fusion), channel_id=1, source_target_pairs={{0,4},{4,8},{8,12},{12,0},{1,5},{5,9},{9,13},{13,1},{2,6},{6,10},{... | collective-permute-start | bytes 393224 | tf_op jit(solution)/shard_map/ppermute | solution.py:170
  23.8 36.6 %collective-permute-start.6 = (f32[16,4,16,128]{3,2,1,0:T(8,128)S(1)}, f32[16,4,16,128]{3,2,1,0:T(8,128)S(1)}, u32[]{:S(2)}, u32[]{:S(2)}) collective-permute-start(f32[16,4,16,128]{3,2,1,0:T(8,128)S(1)} %constant_dynamic-update-slice_fusion.refs_0_), channel_id=1, source_target_pairs={{0,16},{16,0},{1,17},{17,1},{2,18},{18,2},{3,19},{19,3},{4,20},{20... | collective-permute-start | bytes 1572872 | tf_op jit(solution)/shard_map/ppermute | solution.py:170
  25.4 36.4 %collective-permute-start.11 = (f32[16,4,16,128]{3,2,1,0:T(8,128)S(1)}, f32[16,4,16,128]{3,2,1,0:T(8,128)S(1)}, u32[]{:S(2)}, u32[]{:S(2)}) collective-permute-start(f32[16,4,16,128]{3,2,1,0:T(8,128)S(1)} %constant_dynamic-update-slice_fusion.refs_0_), channel_id=1, source_target_pairs={{0,96},{32,0},{64,32},{96,64},{1,97},{33,1},{65,33},{97,65},{2,98}... | collective-permute-start | bytes 1572872 | tf_op jit(solution)/shard_map/ppermute | solution.py:170
  27.9 33.9 %collective-permute-start.9 = (f32[16,4,16,128]{3,2,1,0:T(8,128)S(1)}, f32[16,4,16,128]{3,2,1,0:T(8,128)S(1)}, u32[]{:S(2)}, u32[]{:S(2)}) collective-permute-start(f32[16,4,16,128]{3,2,1,0:T(8,128)S(1)} %constant_dynamic-update-slice_fusion.refs_0_), channel_id=1, source_target_pairs={{0,64},{32,96},{64,0},{96,32},{1,65},{33,97},{65,1},{97,33},{2,66}... | collective-permute-start | bytes 1572872 | tf_op jit(solution)/shard_map/ppermute | solution.py:170
  28.4 33.4 %collective-permute-start.7 = (f32[16,4,16,128]{3,2,1,0:T(8,128)S(1)}, f32[16,4,16,128]{3,2,1,0:T(8,128)S(1)}, u32[]{:S(2)}, u32[]{:S(2)}) collective-permute-start(f32[16,4,16,128]{3,2,1,0:T(8,128)S(1)} %constant_dynamic-update-slice_fusion.refs_0_), channel_id=1, source_target_pairs={{0,32},{32,64},{64,96},{96,0},{1,33},{33,65},{65,97},{97,1},{2,34}... | collective-permute-start | bytes 1572872 | tf_op jit(solution)/shard_map/ppermute | solution.py:170
  56.7 0.7 copy-start
  57.4 0.7 copy-start.2
  61.8 2.4 %collective-permute-start.8 = (f32[16,4,16,128]{3,2,1,0:T(8,128)S(1)}, f32[16,4,16,128]{3,2,1,0:T(8,128)S(1)}, u32[]{:S(2)}, u32[]{:S(2)}) collective-permute-start(f32[16,4,16,128]{3,2,1,0:T(8,128)S(1)} %collective-permute-done.7.refs_0_), channel_id=1, source_target_pairs={{0,16},{16,0},{1,17},{17,1},{2,18},{18,2},{3,19},{19,3},{4,20},{20... | collective-permute-start | bytes 1572872 | tf_op jit(solution)/shard_map/ppermute | solution.py:170
  62.7 2.9 %collective-permute-start.10 = (f32[16,4,16,128]{3,2,1,0:T(8,128)S(1)}, f32[16,4,16,128]{3,2,1,0:T(8,128)S(1)}, u32[]{:S(2)}, u32[]{:S(2)}) collective-permute-start(f32[16,4,16,128]{3,2,1,0:T(8,128)S(1)} %collective-permute-done.9.refs_0_), channel_id=1, source_target_pairs={{0,16},{16,0},{1,17},{17,1},{2,18},{18,2},{3,19},{19,3},{4,20},{20... | collective-permute-start | bytes 1572872 | tf_op jit(solution)/shard_map/ppermute | solution.py:170
  62.8 4.1 %collective-permute-start.12 = (f32[16,4,16,128]{3,2,1,0:T(8,128)S(1)}, f32[16,4,16,128]{3,2,1,0:T(8,128)S(1)}, u32[]{:S(2)}, u32[]{:S(2)}) collective-permute-start(f32[16,4,16,128]{3,2,1,0:T(8,128)S(1)} %collective-permute-done.11.refs_0_), channel_id=1, source_target_pairs={{0,16},{16,0},{1,17},{17,1},{2,18},{18,2},{3,19},{19,3},{4,20},{20... | collective-permute-start | bytes 1572872 | tf_op jit(solution)/shard_map/ppermute | solution.py:170

commit v4 on v3

--- a/solution.py
+++ b/solution.py
@@ -36,20 +36,19 @@
     return got[0:4] + got[4:8] + got[8:12]
 
 
-def prepare(blocks, order, asked, centers, radii, one_hot, slot_state, wide):
+def prepare(blocks, slots, order, asked, centers, radii, one_hot, halo_hot, slot_state, wide):
     halos = radii.shape[1]
-    slots = asked.shape[1] // 2
+    domains = wide.shape[0]
     tiles = slot_state.shape[0]
     group = LANES // slots
-    wide[...] = jnp.zeros_like(wide)
-    for d in range(wide.shape[0]):
-        wide[d : d + 1, : 2 * slots] = asked[pl.ds(order[d], 1)].astype(jnp.float32)
+    for d in range(domains):
+        wide[d : d + 1] = asked[pl.ds(order[d], 1)].astype(jnp.float32)
     lane = lax.broadcasted_iota(jnp.int32, (group, LANES), 1)
     own = lane // slots == lax.broadcasted_iota(jnp.int32, (group, LANES), 0)
-    lanes = lax.broadcasted_iota(jnp.int32, wide.shape, 1)
+    here = lax.broadcasted_iota(jnp.int32, (domains, LANES), 1) // slots == order[domains]
     rows = []
     for which in range(2):
-        row = jnp.where(lanes // slots == which, wide[...], 0.0)
+        row = jnp.where(here, wide[:, which * LANES : (which + 1) * LANES], 0.0)
         shift = slots
         while shift < LANES:
             row = row + pltpu.roll(row, shift, 1)
@@ -61,6 +60,12 @@
     for t in range(tiles):
         hit = halo_index == halo_rows[t]
         one_hot[:, t * LANES : (t + 1) * LANES] = jnp.where(hit, 1.0, 0.0).astype(jnp.bfloat16)
+    across = lax.broadcasted_iota(jnp.int32, (LANES, halos), 1).astype(jnp.float32)
+    for t in range(tiles):
+        column = jnp.broadcast_to(halo_rows[t], (LANES, LANES)).T
+        for h in range(0, halos, LANES):
+            hit = across[:, h : h + LANES] == column
+            halo_hot[t * LANES : (t + 1) * LANES, h : h + LANES] = jnp.where(hit, 1.0, 0.0).astype(jnp.bfloat16)
     got = gather_state(centers[...], radii[...], one_hot[...])
     for t in range(tiles):
         slot_state[t] = jnp.concatenate(
@@ -126,18 +131,17 @@
     lax.fori_loop(0, tiles * len(chunks), one_tile, 0)
 
 
-def finish(slabs, one_hot, centers, radii, *refs):
+def finish(slabs, one_hot, halo_hot, centers, radii, *refs):
     points, partials = refs[:slabs], refs[slabs : 2 * slabs]
     centers_out, radii_out, profile_out, slot_state, partial = refs[2 * slabs :]
     tiles = slot_state.shape[0]
     each = tiles // slabs
 
     def advance(center, radius, terms):
-        high, low = split(terms, 2)
-        across = (((1,), (1,)), ((), ()))
-        sums = lax.dot_general(high, one_hot[...], across, preferred_element_type=jnp.float32) + lax.dot_general(
-            low, one_hot[...], across, preferred_element_type=jnp.float32
-        )
+        high, low = [part.astype(jnp.float32) for part in split(terms, 2)]
+        both = jnp.concatenate([high, low], axis=0).astype(jnp.bfloat16)
+        sums = jnp.dot(both, halo_hot[...], preferred_element_type=jnp.float32)
+        sums = sums[:ROWS] + sums[ROWS:]
         profile = sums[:SHELLS]
         enclosed = profile[SHELLS // 2 - 1 : SHELLS // 2]
         ratio = (1.0 + enclosed) / (1.0 + radius * radius * radius)
@@ -185,21 +189,27 @@
     blocks = masses.shape[0] // BLOCK
     slots = pair_halo.shape[0] // devices
     tiles = devices * slots // LANES
-    pairs = jnp.concatenate([pair_halo.reshape(devices, slots), pair_block.reshape(devices, slots)], axis=1)
+    group = LANES // slots
+    pairs = jnp.concatenate([pair_halo.reshape(tiles, LANES), pair_block.reshape(tiles, LANES)], axis=1)
+    pairs = jnp.broadcast_to(pairs[:, None], (tiles, group, 2 * LANES)).reshape(devices, 2 * LANES)
+    asked = lax.all_to_all(pairs, AXES, split_axis=0, concat_axis=0, tiled=True)
     plane = jnp.concatenate([positions, masses[None]], axis=0).reshape(1, 4, blocks, BLOCK)
-    order = sources()
+    order = jnp.concatenate([sources(), lax.axis_index(AXES)[None] % group])
     for axis in ("z", "y"):
         plane = jnp.concatenate(shifted(plane, axis), axis=0)
-    plane, pairs, order = lax.optimization_barrier((plane, pairs, order))
+    plane, asked, order = lax.optimization_barrier((plane, asked, order))
     slabs = shifted(plane, "x")
-    asked = lax.all_to_all(pairs, AXES, split_axis=0, concat_axis=0, tiled=True)
     radii = radii[None]
-    one_hot, slot_state = pl.pallas_call(
-        functools.partial(prepare, blocks),
+    one_hot, halo_hot, slot_state = pl.pallas_call(
+        functools.partial(prepare, blocks, slots),
         in_specs=[pl.BlockSpec(memory_space=pltpu.SMEM), VMEM, VMEM, VMEM],
-        out_specs=[VMEM] * 2,
-        out_shape=(jax.ShapeDtypeStruct((halos, devices * slots), jnp.bfloat16), f32(tiles, 8, LANES)),
-        scratch_shapes=[pltpu.VMEM((devices, LANES), jnp.float32)],
+        out_specs=[VMEM] * 3,
+        out_shape=(
+            jax.ShapeDtypeStruct((halos, devices * slots), jnp.bfloat16),
+            jax.ShapeDtypeStruct((devices * slots, halos), jnp.bfloat16),
+            f32(tiles, 8, LANES),
+        ),
+        scratch_shapes=[pltpu.VMEM((devices, 2 * LANES), jnp.float32)],
         compiler_params=PARAMS,
     )(order, asked, centers, radii)
     each = tiles // len(slabs)
@@ -208,7 +218,7 @@
         if i:
             slab, _ = lax.optimization_barrier((slab, partials[0]))
         got = pl.pallas_call(
-            functools.partial(first_pass, i * each, LANES // slots),
+            functools.partial(first_pass, i * each, group),
             in_specs=[VMEM] * 3,
             out_specs=[VMEM] * 2,
             out_shape=(f32(each, 4, BLOCK, LANES), f32(each, ROWS, LANES)),
@@ -218,12 +228,12 @@
         partials.append(got[1])
     centers, radii, profile = pl.pallas_call(
         functools.partial(finish, len(slabs)),
-        in_specs=[VMEM] * (3 + 2 * len(slabs)),
+        in_specs=[VMEM] * (4 + 2 * len(slabs)),
         out_specs=[VMEM] * 3,
         out_shape=(f32(3, halos), f32(1, halos), f32(SHELLS, halos)),
         scratch_shapes=[pltpu.VMEM((tiles, 8, LANES), jnp.float32), pltpu.VMEM((tiles, ROWS, LANES), jnp.float32)],
         compiler_params=PARAMS,
-    )(one_hot, centers, radii, *points, *partials)
+    )(one_hot, halo_hot, centers, radii, *points, *partials)
     return (centers, radii[0], profile)
 
 

time: 78.4 us -> 75 us (0.957)
  blocking collectives: 27.5 us -> 0 us
  waiting for transfers between devices: 8.7 us -> 29.2 us
  starting transfers between devices: 17.5 us -> 24.1 us
  Pallas kernels: 17.4 us -> 14.6 us
  local copies, waits for them, and re-layouts: 4.3 us -> 3.3 us
    all_to_all x1 -> x0, blocking collectives: 27.5 us -> none  [body(): asked = lax.all_to_all(pairs, AXES, split_axis=0, concat_axis=0, tiled=True)]
    ppermute x13, waiting for transfers between devices: 8.7 us -> 24.4 us  [shifted(): lax.ppermute(value, axis, [(i, (i + k) % size) for i in range(size)])]
    all_to_all x0 -> x1, starting transfers between devices: none -> 8.03 us  [body(): asked = lax.all_to_all(pairs, AXES, split_axis=0, concat_axis=0, tiled=True)]
    all_to_all x0 -> x1, waiting for transfers between devices: none -> 4.78 us  [body(): asked = lax.all_to_all(pairs, AXES, split_axis=0, concat_axis=0, tiled=True)]
    pallas_call x1, Pallas kernels: 9.66 us -> 6.2 us  [body(): pl.pallas_call(functools.partial(finish, len(slabs)), in_specs=[VMEM] * (...]
    reshape x4 -> x0, local copies, waits for them, and re-layouts: 1.67 us -> none  [the longest x2 0.85 us: body(): pair_halo.reshape(devices, slots)]
    ppermute x13, starting transfers between devices: 17.5 us -> 16.1 us  [shifted(): lax.ppermute(value, axis, [(i, (i + k) % size) for i in range(size)])]
    unnamed x14 -> x13, local copies, waits for them, and re-layouts: 2.22 us -> 2.22 us
  transfers between devices with their start and end apart: 13 -> 14, of which waited for: 2 -> 5; matrix products, arithmetic and copies ran while one was open for 3% -> 3% of each run, Pallas kernels for 8% -> 10%
where the time goes in v4:
time: 75 us; the launch traced here: 74.5 us
  waiting for transfers between devices  29.2 us (39%)
  starting transfers between devices  24.1 us (32%)
  Pallas kernels  14.6 us (19%)
  local copies, waits for them, and re-layouts  3.3 us (4%)
  other arithmetic  2.41 us (3%)
  between operations  0.87 us (1%)
    ppermute x13, waiting for transfers between devices, shifted(): lax.ppermute(value, axis, [(i, (i + k) % size) for i in range(size)])  24.4 us
    ppermute x13, starting transfers between devices, shifted(): lax.ppermute(value, axis, [(i, (i + k) % size) for i in range(size)])  16.1 us
    all_to_all x1, starting transfers between devices, body(): asked = lax.all_to_all(pairs, AXES, split_axis=0, concat_axis=0, tiled=True)  8.03 us
    pallas_call x1, Pallas kernels, body(): pl.pallas_call(functools.partial(finish, len(slabs)), in_specs=[VMEM] * (...  6.2 us
    pallas_call x4, Pallas kernels, body(): pl.pallas_call(functools.partial(first_pass, i * each, group), in_specs=[...  5.3 us
    all_to_all x1, waiting for transfers between devices, body(): asked = lax.all_to_all(pairs, AXES, split_axis=0, concat_axis=0, tiled=True)  4.78 us
    pallas_call x1, Pallas kernels, body(): pl.pallas_call(functools.partial(prepare, blocks, slots), in_specs=[pl.Bl...  3.13 us
    unnamed x13, local copies, waits for them, and re-layouts  2.22 us
  transfers between devices with their start and end apart: 14, of which 5 were waited for; matrix products, arithmetic and copies ran while one was open for 3% of the time, Pallas kernels for 10%

profile of v4, /device:TPU:1, one launch (start us, length us, event | category | flops | bytes accessed | tf_op | source)
XLA Modules:
  0.0 74.5 jit_solution(13049332840276749472)
XLA Ops:
  0.6 0.0 copy-start.1
  0.6 0.8 %copy.14 = f32[1,3,16,128]{3,2,1,0:T(8,128)S(1)} copy(f32[1,3,16,128]{3,1,2,0:T(4,128)} %bitcast.19) | data formatting | bytes 49152
  1.4 0.7 pad_maximum_fusion.1
  2.1 4.4 %collective-permute-start.1 = (f32[1,4,16,128]{3,2,1,0:T(8,128)S(1)}, f32[1,4,16,128]{3,2,1,0:T(8,128)S(1)}, u32[]{:S(2)}, u32[]{:S(2)}) collective-permute-start(f32[1,4,16,128]{3,2,1,0:T(8,128)S(1)} %get-tuple-element.43), channel_id=1, source_target_pairs={{0,2},{1,3},{2,0},{3,1},{4,6},{5,7},{6,4},{7,5},{8,10},{9,11},{10,... | collective-permute-start | bytes 98312 | tf_op jit(solution)/shard_map/ppermute | solution.py:174
  6.5 0.7 collective-permute-start
  7.3 1.9 %collective-permute-start.2 = (f32[1,4,16,128]{3,2,1,0:T(8,128)S(1)}, f32[1,4,16,128]{3,2,1,0:T(8,128)S(1)}, u32[]{:S(2)}, u32[]{:S(2)}) collective-permute-start(f32[1,4,16,128]{3,2,1,0:T(8,128)S(1)} %get-tuple-element.43), channel_id=1, source_target_pairs={{0,3},{1,0},{2,1},{3,2},{4,7},{5,4},{6,5},{7,6},{8,11},{9,8},{10,9... | collective-permute-start | bytes 98312 | tf_op jit(solution)/shard_map/ppermute | solution.py:174
  9.2 0.7 pad_add_fusion
  9.9 0.8 %all_to_all.8 = s32[128,1,256]{2,1,0:T(1,128)} reshape(s32[16,8,256]{2,1,0:T(8,128)S(1)} %broadcast_in_dim.6) | data formatting | bytes 262144 | tf_op jit(solution)/shard_map/all_to_all | solution.py:195
  10.7 8.0 %all-to-all-start = ((s32[128,1,256]{2,1,0:T(1,128)}), s32[128,1,256]{2,1,0:T(1,128)S(1)}, u32[]{:S(2)}, u32[]{:S(2)}) async-start(s32[128,1,256]{2,1,0:T(1,128)} %all_to_all.8), calls=%async_computation | async-start | bytes 262144 | tf_op jit(solution)/shard_map/all_to_all | solution.py:195
  18.9 0.1 broadcast_add_fusion.2
  18.9 0.1 add.113
  19.0 0.1 broadcast_add_fusion.1
  19.1 0.1 add.118
  19.2 0.1 broadcast_add_fusion
  19.2 0.1 add.123
  19.4 0.0 collective-permute-done.1
  19.4 0.0 collective-permute-done
  19.4 0.0 collective-permute-done.2
  19.4 0.7 pad_maximum_fusion
  20.1 2.7 %collective-permute-start.5 = (f32[4,4,16,128]{3,2,1,0:T(8,128)S(1)}, f32[4,4,16,128]{3,2,1,0:T(8,128)S(1)}, u32[]{:S(2)}, u32[]{:S(2)}) collective-permute-start(f32[4,4,16,128]{3,2,1,0:T(8,128)S(1)} %pad_maximum_fusion), channel_id=1, source_target_pairs={{0,12},{4,0},{8,4},{12,8},{1,13},{5,1},{9,5},{13,9},{2,14},{6,2},{... | collective-permute-start | bytes 393224 | tf_op jit(solution)/shard_map/ppermute | solution.py:174
  22.8 0.5 collective-permute-start.4
  23.4 0.6 collective-permute-start.3
  24.0 4.8 %all-to-all-done = s32[128,1,256]{2,1,0:T(1,128)S(1)} async-done(((s32[128,1,256]{2,1,0:T(1,128)}), s32[128,1,256]{2,1,0:T(1,128)S(1)}, u32[]{:S(2)}, u32[]{:S(2)}) %all-to-all-start) | async-done | bytes 131104 | tf_op jit(solution)/shard_map/all_to_all | solution.py:195
  28.8 3.8 %collective-permute-done.3 = f32[4,4,16,128]{3,2,1,0:T(8,128)S(1)} collective-permute-done((f32[4,4,16,128]{3,2,1,0:T(8,128)S(1)}, f32[4,4,16,128]{3,2,1,0:T(8,128)S(1)}, u32[]{:S(2)}, u32[]{:S(2)}) %collective-permute-start.3) | collective-permute-done | bytes 131104 | tf_op jit(solution)/shard_map/ppermute | solution.py:174
  32.6 0.0 collective-permute-done.4
  32.6 0.0 collective-permute-done.5
  32.7 0.6 collective-permute-start.6
  33.2 2.5 %collective-permute-start.11 = (f32[16,4,16,128]{3,2,1,0:T(8,128)S(1)}, f32[16,4,16,128]{3,2,1,0:T(8,128)S(1)}, u32[]{:S(2)}, u32[]{:S(2)}) collective-permute-start(f32[16,4,16,128]{3,2,1,0:T(8,128)S(1)} %constant_dynamic-update-slice_fusion.refs_0_), channel_id=1, source_target_pairs={{0,96},{32,0},{64,32},{96,64},{1,97},{33,1},{65,33},{97,65},{2,98}... | collective-permute-start | bytes 1572872 | tf_op jit(solution)/shard_map/ppermute | solution.py:174
  35.7 0.5 collective-permute-start.9
  36.2 0.6 collective-permute-start.7
  36.8 0.0 copy-start
  36.8 0.7 copy-done
  37.5 0.0 copy-start.2
  37.5 0.7 copy-done.2
  38.2 3.1 %shard_map.85 = (bf16[1024,2048]{1,0:T(8,128)(2,1)S(1)}, bf16[2048,1024]{1,0:T(8,128)(2,1)S(1)}, f32[16,8,128]{2,1,0:T(8,128)S(1)}) custom-call(s32[129]{0:T(256)S(1)} %pad_add_fusion.1.order, s32[128,256]{1,0:T(8,128)S(1)} %bitcast.14, f32[3,1024]{1,0:T(4,128)S(1)} %copy-done, f32[1,1024]{1,0:T(1,128)S(1)} %bitcast.15), custom_call_target="tpu_custom_call" | custom-call | tf_op jit(solution)/shard_map/pallas_call | solution.py:203
  41.4 0.0 collective-permute-done.6.refs_1_
  41.4 1.3 %shard_map.86 = (f32[4,4,128,128]{3,2,1,0:T(8,128)S(1)}, f32[4,24,128]{2,1,0:T(8,128)S(1)}) custom-call(f32[16,8,128]{2,1,0:T(8,128)S(1)} %get-tuple-element.27.slot_state, f32[16,4,16,128]{3,2,1,0:T(8,128)S(1)} %constant_dynamic-update-slice_fusion.refs_0_, f32[16,4,16,128]{3,2,1,0:T(8,128)S(1)} %collective-permute-done.6.refs_1_), custom_call_target="tpu_custom_call" | custom-call | tf_op jit(solution)/shard_map/pallas_call | solution.py:220
  42.7 15.3 %collective-permute-done.11.refs_0_ = f32[16,4,16,128]{3,2,1,0:T(8,128)S(1)} collective-permute-done((f32[16,4,16,128]{3,2,1,0:T(8,128)S(1)}, f32[16,4,16,128]{3,2,1,0:T(8,128)S(1)}, u32[]{:S(2)}, u32[]{:S(2)}) %collective-permute-start.11) | collective-permute-done | bytes 524320 | tf_op jit(solution)/shard_map/ppermute | solution.py:174
  58.1 0.0 collective-permute-done.9.refs_0_
  58.1 4.2 %collective-permute-done.7.refs_0_ = f32[16,4,16,128]{3,2,1,0:T(8,128)S(1)} collective-permute-done((f32[16,4,16,128]{3,2,1,0:T(8,128)S(1)}, f32[16,4,16,128]{3,2,1,0:T(8,128)S(1)}, u32[]{:S(2)}, u32[]{:S(2)}) %collective-permute-start.7) | collective-permute-done | bytes 524320 | tf_op jit(solution)/shard_map/ppermute | solution.py:174
  62.3 0.5 collective-permute-start.8
  62.8 0.0 collective-permute-start.10
  62.8 0.5 collective-permute-start.12
  63.3 1.0 %collective-permute-done.8.refs_1_ = f32[16,4,16,128]{3,2,1,0:T(8,128)S(1)} collective-permute-done((f32[16,4,16,128]{3,2,1,0:T(8,128)S(1)}, f32[16,4,16,128]{3,2,1,0:T(8,128)S(1)}, u32[]{:S(2)}, u32[]{:S(2)}) %collective-permute-start.8) | collective-permute-done | bytes 524320 | tf_op jit(solution)/shard_map/ppermute | solution.py:174
  64.3 1.3 %shard_map.87 = (f32[4,4,128,128]{3,2,1,0:T(8,128)S(1)}, f32[4,24,128]{2,1,0:T(8,128)S(1)}) custom-call(f32[16,8,128]{2,1,0:T(8,128)S(1)} %get-tuple-element.27.slot_state, f32[16,4,16,128]{3,2,1,0:T(8,128)S(1)} %collective-permute-done.7.refs_0_, f32[16,4,16,128]{3,2,1,0:T(8,128)S(1)} %collective-permute-done.8.refs_1_), custom_call_target="tpu_custom_call" | custom-call | tf_op jit(solution)/shard_map/pallas_call | solution.py:220
  65.6 0.0 collective-permute-done.10.refs_1_
  65.6 1.3 %shard_map.88 = (f32[4,4,128,128]{3,2,1,0:T(8,128)S(1)}, f32[4,24,128]{2,1,0:T(8,128)S(1)}) custom-call(f32[16,8,128]{2,1,0:T(8,128)S(1)} %get-tuple-element.27.slot_state, f32[16,4,16,128]{3,2,1,0:T(8,128)S(1)} %collective-permute-done.9.refs_0_, f32[16,4,16,128]{3,2,1,0:T(8,128)S(1)} %collective-permute-done.10.refs_1_), custom_call_target="tpu_custom_call" | custom-call | tf_op jit(solution)/shard_map/pallas_call | solution.py:220
  67.0 0.0 collective-permute-done.12.refs_1_
  67.0 1.3 %shard_map.89 = (f32[4,4,128,128]{3,2,1,0:T(8,128)S(1)}, f32[4,24,128]{2,1,0:T(8,128)S(1)}) custom-call(f32[16,8,128]{2,1,0:T(8,128)S(1)} %get-tuple-element.27.slot_state, f32[16,4,16,128]{3,2,1,0:T(8,128)S(1)} %collective-permute-done.11.refs_0_, f32[16,4,16,128]{3,2,1,0:T(8,128)S(1)} %collective-permute-done.12.refs_1_), custom_call_target="tpu_custom_call" | custom-call | tf_op jit(solution)/shard_map/pallas_call | solution.py:220
  68.3 0.0 copy-done.1
  68.3 6.2 %shard_map.90 = (f32[3,1024]{1,0:T(4,128)}, f32[1,1024]{1,0:T(1,128)}, f32[16,1024]{1,0:T(8,128)}) custom-call(bf16[1024,2048]{1,0:T(8,128)(2,1)S(1)} %get-tuple-element.25.one_hot, bf16[2048,1024]{1,0:T(8,128)(2,1)S(1)} %get-tuple-element.26.halo_hot, f32[3,1024]{1,0:T(4,128)S(1)} %copy-done.1, f32[1,1024]{1,0:T(1,128)S(1)} %bitcast.16, ...), custom_call_target="tpu_custom_call" | custom-call | tf_op jit(solution)/shard_map/pallas_call | solution.py:229
  (13 shorter events, 0.1 us)
Async XLA Ops:
  0.6 67.7 %copy-start.1 = (f32[3,1024]{1,0:T(4,128)S(1)}, f32[3,1024]{1,0:T(4,128)}, u32[]{:S(2)}) copy-start(f32[3,1024]{1,0:T(4,128)} %centers.3) | copy-start | bytes 36868
  2.1 17.3 %collective-permute-start.1 = (f32[1,4,16,128]{3,2,1,0:T(8,128)S(1)}, f32[1,4,16,128]{3,2,1,0:T(8,128)S(1)}, u32[]{:S(2)}, u32[]{:S(2)}) collective-permute-start(f32[1,4,16,128]{3,2,1,0:T(8,128)S(1)} %get-tuple-element.43), channel_id=1, source_target_pairs={{0,2},{1,3},{2,0},{3,1},{4,6},{5,7},{6,4},{7,5},{8,10},{9,11},{10,... | collective-permute-start | bytes 98312 | tf_op jit(solution)/shard_map/ppermute | solution.py:174
  6.5 12.9 %collective-permute-start = (f32[1,4,16,128]{3,2,1,0:T(8,128)S(1)}, f32[1,4,16,128]{3,2,1,0:T(8,128)S(1)}, u32[]{:S(2)}, u32[]{:S(2)}) collective-permute-start(f32[1,4,16,128]{3,2,1,0:T(8,128)S(1)} %get-tuple-element.43), channel_id=1, source_target_pairs={{0,1},{1,2},{2,3},{3,0},{4,5},{5,6},{6,7},{7,4},{8,9},{9,10},{10,1... | collective-permute-start | bytes 98312 | tf_op jit(solution)/shard_map/ppermute | solution.py:174
  7.3 12.1 %collective-permute-start.2 = (f32[1,4,16,128]{3,2,1,0:T(8,128)S(1)}, f32[1,4,16,128]{3,2,1,0:T(8,128)S(1)}, u32[]{:S(2)}, u32[]{:S(2)}) collective-permute-start(f32[1,4,16,128]{3,2,1,0:T(8,128)S(1)} %get-tuple-element.43), channel_id=1, source_target_pairs={{0,3},{1,0},{2,1},{3,2},{4,7},{5,4},{6,5},{7,6},{8,11},{9,8},{10,9... | collective-permute-start | bytes 98312 | tf_op jit(solution)/shard_map/ppermute | solution.py:174
  10.7 18.0 %all-to-all-start = ((s32[128,1,256]{2,1,0:T(1,128)}), s32[128,1,256]{2,1,0:T(1,128)S(1)}, u32[]{:S(2)}, u32[]{:S(2)}) async-start(s32[128,1,256]{2,1,0:T(1,128)} %all_to_all.8), calls=%async_computation | async-start | bytes 262144 | tf_op jit(solution)/shard_map/all_to_all | solution.py:195
  20.1 12.5 %collective-permute-start.5 = (f32[4,4,16,128]{3,2,1,0:T(8,128)S(1)}, f32[4,4,16,128]{3,2,1,0:T(8,128)S(1)}, u32[]{:S(2)}, u32[]{:S(2)}) collective-permute-start(f32[4,4,16,128]{3,2,1,0:T(8,128)S(1)} %pad_maximum_fusion), channel_id=1, source_target_pairs={{0,12},{4,0},{8,4},{12,8},{1,13},{5,1},{9,5},{13,9},{2,14},{6,2},{... | collective-permute-start | bytes 393224 | tf_op jit(solution)/shard_map/ppermute | solution.py:174
  22.8 9.7 %collective-permute-start.4 = (f32[4,4,16,128]{3,2,1,0:T(8,128)S(1)}, f32[4,4,16,128]{3,2,1,0:T(8,128)S(1)}, u32[]{:S(2)}, u32[]{:S(2)}) collective-permute-start(f32[4,4,16,128]{3,2,1,0:T(8,128)S(1)} %pad_maximum_fusion), channel_id=1, source_target_pairs={{0,8},{4,12},{8,0},{12,4},{1,9},{5,13},{9,1},{13,5},{2,10},{6,14},... | collective-permute-start | bytes 393224 | tf_op jit(solution)/shard_map/ppermute | solution.py:174
  23.4 9.2 %collective-permute-start.3 = (f32[4,4,16,128]{3,2,1,0:T(8,128)S(1)}, f32[4,4,16,128]{3,2,1,0:T(8,128)S(1)}, u32[]{:S(2)}, u32[]{:S(2)}) collective-permute-start(f32[4,4,16,128]{3,2,1,0:T(8,128)S(1)} %pad_maximum_fusion), channel_id=1, source_target_pairs={{0,4},{4,8},{8,12},{12,0},{1,5},{5,9},{9,13},{13,1},{2,6},{6,10},{... | collective-permute-start | bytes 393224 | tf_op jit(solution)/shard_map/ppermute | solution.py:174
  32.7 8.7 %collective-permute-start.6 = (f32[16,4,16,128]{3,2,1,0:T(8,128)S(1)}, f32[16,4,16,128]{3,2,1,0:T(8,128)S(1)}, u32[]{:S(2)}, u32[]{:S(2)}) collective-permute-start(f32[16,4,16,128]{3,2,1,0:T(8,128)S(1)} %constant_dynamic-update-slice_fusion.refs_0_), channel_id=1, source_target_pairs={{0,16},{16,0},{1,17},{17,1},{2,18},{18,2},{3,19},{19,3},{4,20},{20... | collective-permute-start | bytes 1572872 | tf_op jit(solution)/shard_map/ppermute | solution.py:174
  33.2 24.8 %collective-permute-start.11 = (f32[16,4,16,128]{3,2,1,0:T(8,128)S(1)}, f32[16,4,16,128]{3,2,1,0:T(8,128)S(1)}, u32[]{:S(2)}, u32[]{:S(2)}) collective-permute-start(f32[16,4,16,128]{3,2,1,0:T(8,128)S(1)} %constant_dynamic-update-slice_fusion.refs_0_), channel_id=1, source_target_pairs={{0,96},{32,0},{64,32},{96,64},{1,97},{33,1},{65,33},{97,65},{2,98}... | collective-permute-start | bytes 1572872 | tf_op jit(solution)/shard_map/ppermute | solution.py:174
  35.7 22.4 %collective-permute-start.9 = (f32[16,4,16,128]{3,2,1,0:T(8,128)S(1)}, f32[16,4,16,128]{3,2,1,0:T(8,128)S(1)}, u32[]{:S(2)}, u32[]{:S(2)}) collective-permute-start(f32[16,4,16,128]{3,2,1,0:T(8,128)S(1)} %constant_dynamic-update-slice_fusion.refs_0_), channel_id=1, source_target_pairs={{0,64},{32,96},{64,0},{96,32},{1,65},{33,97},{65,1},{97,33},{2,66}... | collective-permute-start | bytes 1572872 | tf_op jit(solution)/shard_map/ppermute | solution.py:174
  36.2 26.0 %collective-permute-start.7 = (f32[16,4,16,128]{3,2,1,0:T(8,128)S(1)}, f32[16,4,16,128]{3,2,1,0:T(8,128)S(1)}, u32[]{:S(2)}, u32[]{:S(2)}) collective-permute-start(f32[16,4,16,128]{3,2,1,0:T(8,128)S(1)} %constant_dynamic-update-slice_fusion.refs_0_), channel_id=1, source_target_pairs={{0,32},{32,64},{64,96},{96,0},{1,33},{33,65},{65,97},{97,1},{2,34}... | collective-permute-start | bytes 1572872 | tf_op jit(solution)/shard_map/ppermute | solution.py:174
  36.8 0.7 copy-start
  37.5 0.7 copy-start.2
  62.3 2.0 %collective-permute-start.8 = (f32[16,4,16,128]{3,2,1,0:T(8,128)S(1)}, f32[16,4,16,128]{3,2,1,0:T(8,128)S(1)}, u32[]{:S(2)}, u32[]{:S(2)}) collective-permute-start(f32[16,4,16,128]{3,2,1,0:T(8,128)S(1)} %collective-permute-done.7.refs_0_), channel_id=1, source_target_pairs={{0,16},{16,0},{1,17},{17,1},{2,18},{18,2},{3,19},{19,3},{4,20},{20... | collective-permute-start | bytes 1572872 | tf_op jit(solution)/shard_map/ppermute | solution.py:174
  62.8 2.9 %collective-permute-start.10 = (f32[16,4,16,128]{3,2,1,0:T(8,128)S(1)}, f32[16,4,16,128]{3,2,1,0:T(8,128)S(1)}, u32[]{:S(2)}, u32[]{:S(2)}) collective-permute-start(f32[16,4,16,128]{3,2,1,0:T(8,128)S(1)} %collective-permute-done.9.refs_0_), channel_id=1, source_target_pairs={{0,16},{16,0},{1,17},{17,1},{2,18},{18,2},{3,19},{19,3},{4,20},{20... | collective-permute-start | bytes 1572872 | tf_op jit(solution)/shard_map/ppermute | solution.py:174
  62.8 4.2 %collective-permute-start.12 = (f32[16,4,16,128]{3,2,1,0:T(8,128)S(1)}, f32[16,4,16,128]{3,2,1,0:T(8,128)S(1)}, u32[]{:S(2)}, u32[]{:S(2)}) collective-permute-start(f32[16,4,16,128]{3,2,1,0:T(8,128)S(1)} %collective-permute-done.11.refs_0_), channel_id=1, source_target_pairs={{0,16},{16,0},{1,17},{17,1},{2,18},{18,2},{3,19},{19,3},{4,20},{20... | collective-permute-start | bytes 1572872 | tf_op jit(solution)/shard_map/ppermute | solution.py:174

commit v5 on v4

--- a/solution.py
+++ b/solution.py
@@ -36,25 +36,73 @@
     return got[0:4] + got[4:8] + got[8:12]
 
 
-def prepare(blocks, slots, order, asked, centers, radii, one_hot, halo_hot, slot_state, wide):
+def spread(rows, keep, own, slots):
+    rows = jnp.where(keep, rows, 0.0)
+    shift = slots
+    while shift < LANES:
+        rows = rows + pltpu.roll(rows, shift, 1)
+        shift *= 2
+    return jnp.sum(jnp.where(own, rows, 0.0), axis=0, keepdims=True)
+
+
+def pack(positions, masses, halo, block, out):
+    blocks = masses.shape[0]
+    for c in range(3):
+        for b in range(blocks):
+            out[c * blocks + b : c * blocks + b + 1] = positions[c : c + 1, b * BLOCK : (b + 1) * BLOCK]
+    at = 3 * blocks
+    for part in (masses, halo, block):
+        out[at : at + part.shape[0]] = part[...].astype(jnp.float32)
+        at += part.shape[0]
+
+
+def merge_z(slots, width, place, *refs):
+    size = len(refs) // 2
+    parts, outs = refs[:size], refs[size:]
+    index_rows = (parts[0].shape[0] - width) // 2
+    row = lax.broadcasted_iota(jnp.int32, (index_rows, LANES), 0)
+    group = lax.broadcasted_iota(jnp.int32, (index_rows, LANES), 1) // slots
+    for k in range(size):
+        for i in range(size):
+            outs[k][i * width : (i + 1) * width] = parts[i][:width]
+        y = (place[2] + k) % size
+        keep = (group == y % 2 * size + place[3]) & (row % 2 == y // 2)
+        for which in range(2):
+            for i in range(size):
+                at = width + which * index_rows
+                to = size * width + which * size + i
+                outs[k][to : to + 1] = spread(parts[i][at : at + index_rows], keep, group == row // 2, slots)
+
+
+def merge_y(*refs):
+    size = len(refs) - 3
+    parts, (low, high, index) = refs[:size], refs[size:]
+    rows = parts[0].shape[0] - 2 * size
+    for i in range(size):
+        half = (low, high)[i // 2]
+        half[i % 2 * rows : (i % 2 + 1) * rows] = parts[i][:rows]
+        for which in range(2):
+            to = which * size * size + i * size
+            at = rows + which * size
+            index[to : to + size] = parts[i][at : at + size]
+
+
+def prepare(slots, blocks, place, mine, other, centers, radii, one_hot, halo_hot, slot_state):
     halos = radii.shape[1]
-    domains = wide.shape[0]
     tiles = slot_state.shape[0]
-    group = LANES // slots
-    for d in range(domains):
-        wide[d : d + 1] = asked[pl.ds(order[d], 1)].astype(jnp.float32)
-    lane = lax.broadcasted_iota(jnp.int32, (group, LANES), 1)
-    own = lane // slots == lax.broadcasted_iota(jnp.int32, (group, LANES), 0)
-    here = lax.broadcasted_iota(jnp.int32, (domains, LANES), 1) // slots == order[domains]
-    rows = []
-    for which in range(2):
-        row = jnp.where(here, wide[:, which * LANES : (which + 1) * LANES], 0.0)
-        shift = slots
-        while shift < LANES:
-            row = row + pltpu.roll(row, shift, 1)
-            shift *= 2
-        rows.append([jnp.sum(jnp.where(own, row[t * group : (t + 1) * group], 0.0), axis=0, keepdims=True) for t in range(tiles)])
-    halo_rows, block_rows = rows
+    each = tiles // 4
+    lane_group = lax.broadcasted_iota(jnp.int32, (8, LANES), 1) // slots
+    own = lane_group == lax.broadcasted_iota(jnp.int32, (8, LANES), 0)
+    keep = lane_group == place[0] * 2 + place[1]
+
+    def slot_rows(which):
+        rows = []
+        for t in range(tiles):
+            at = t // each * 32 + which * 16 + t % 2 * 8
+            rows.append(spread((mine, other)[t % each // 2][at : at + 8], keep, own, slots))
+        return rows
+
+    halo_rows, block_rows = slot_rows(0), slot_rows(1)
     halo_index = lax.broadcasted_iota(jnp.int32, (halos, LANES), 0).astype(jnp.float32)
     first = (lax.broadcasted_iota(jnp.int32, (1, LANES), 1) // slots * blocks).astype(jnp.float32)
     for t in range(tiles):
@@ -106,19 +154,19 @@
         out[o, SHELLS + k : SHELLS + k + 1] = jnp.sum(inner[k], axis=0, keepdims=True)
 
 
-def first_pass(offset, group, slot_state, *refs):
+def first_pass(offset, blocks, slot_state, *refs):
     chunks, (points, partial) = refs[:-2], refs[-2:]
-    chunk, _, blocks, _ = chunks[0].shape
-    count = group * blocks
-    tiles = chunk // group
+    tiles = len(chunks)
+    domain = 4 * blocks
+    count = chunks[0].shape[0] // 4
     block_index = lax.broadcasted_iota(jnp.int32, (count, LANES), 0).astype(jnp.float32)
     partial[...] = jnp.zeros_like(partial)
-    for t in range(tiles * len(chunks)):
+    for t in range(tiles):
         hit = block_index == slot_state[offset + t, 4:5]
         pick = jnp.where(hit, 1.0, 0.0).astype(jnp.bfloat16)
-        at = t % tiles * group
         for c in range(4):
-            chosen = chunks[t // tiles][at : at + group, c].reshape(count, BLOCK).T
+            rows = [chunks[t][a + c * blocks : a + (c + 1) * blocks] for a in range(0, chunks[t].shape[0], domain)]
+            chosen = jnp.concatenate(rows, axis=0).T
             high, low = split(chosen, 2)
             points[t, c] = jnp.dot(high, pick, preferred_element_type=jnp.float32) + jnp.dot(
                 low, pick, preferred_element_type=jnp.float32
@@ -128,7 +176,7 @@
         tile_sums(slot_state[offset + t], points, t, partial, t)
         return carry
 
-    lax.fori_loop(0, tiles * len(chunks), one_tile, 0)
+    lax.fori_loop(0, tiles, one_tile, 0)
 
 
 def finish(slabs, one_hot, halo_hot, centers, radii, *refs):
@@ -169,18 +217,15 @@
     profile_out[...] = profile
 
 
-def shifted(value, axis):
+def step(value, axis, by):
     size = lax.axis_size(axis)
-    return [value] + [lax.ppermute(value, axis, [(i, (i + k) % size) for i in range(size)]) for k in range(1, size)]
-
-
-def sources():
-    index = jnp.zeros((1,), jnp.int32)
-    for axis, stride in (("x", 32), ("core", 16), ("y", 4), ("z", 1)):
-        size = lax.axis_size(axis)
-        here = (lax.axis_index(axis) - jnp.arange(size, dtype=jnp.int32)) % size * stride
-        index = (index[:, None] + here[None, :]).reshape(-1)
-    return index
+    return lax.ppermute(value, axis, [(i, (i + by) % size) for i in range(size)])
+
+
+def call(fn, outs, *args):
+    specs = [pl.BlockSpec(memory_space=pltpu.SMEM) if a.ndim == 1 else VMEM for a in args]
+    out_specs = [VMEM] * len(outs)
+    return pl.pallas_call(fn, in_specs=specs, out_specs=out_specs, out_shape=outs, compiler_params=PARAMS)(*args)
 
 
 def body(positions, masses, centers, radii, pair_block, pair_halo):
@@ -189,43 +234,47 @@
     blocks = masses.shape[0] // BLOCK
     slots = pair_halo.shape[0] // devices
     tiles = devices * slots // LANES
-    group = LANES // slots
-    pairs = jnp.concatenate([pair_halo.reshape(tiles, LANES), pair_block.reshape(tiles, LANES)], axis=1)
-    pairs = jnp.broadcast_to(pairs[:, None], (tiles, group, 2 * LANES)).reshape(devices, 2 * LANES)
-    asked = lax.all_to_all(pairs, AXES, split_axis=0, concat_axis=0, tiled=True)
-    plane = jnp.concatenate([positions, masses[None]], axis=0).reshape(1, 4, blocks, BLOCK)
-    order = jnp.concatenate([sources(), lax.axis_index(AXES)[None] % group])
-    for axis in ("z", "y"):
-        plane = jnp.concatenate(shifted(plane, axis), axis=0)
-    plane, asked, order = lax.optimization_barrier((plane, asked, order))
-    slabs = shifted(plane, "x")
+    domain = 4 * blocks
     radii = radii[None]
-    one_hot, halo_hot, slot_state = pl.pallas_call(
-        functools.partial(prepare, blocks, slots),
-        in_specs=[pl.BlockSpec(memory_space=pltpu.SMEM), VMEM, VMEM, VMEM],
-        out_specs=[VMEM] * 3,
-        out_shape=(
+    place = jnp.stack([lax.axis_index(axis) for axis in AXES]).astype(jnp.int32)
+    row = lambda a: a.reshape(-1, LANES)
+    (payload,) = call(pack, [f32(domain + 2 * tiles, LANES)], positions, row(masses), row(pair_halo), row(pair_block))
+    along_z = [payload] + [step(payload, "z", k) for k in range(1, 4)]
+    to_y = call(functools.partial(merge_z, slots, domain), [f32(4 * domain + 8, LANES)] * 4, place, *along_z)
+    along_y = [step(to_y[k], "y", k) if k else to_y[k] for k in range(4)]
+    low, high, index = call(merge_y, [f32(8 * domain, LANES)] * 2 + [f32(32, LANES)], *along_y)
+    indices = jnp.concatenate([index, step(index, "x", 1), step(index, "x", 2), step(index, "x", 3)], axis=0)
+    below_low, above_high = step(low, "x", 1), step(high, "x", -1)
+    below_high, above_low = step(high, "x", 1), step(low, "x", -1)
+    far_low, far_high = step(below_low, "x", 1), step(above_high, "x", -1)
+    slabs = [(low, high), (below_low, below_high), (far_low, far_high), (above_low, above_high)]
+    one_hot, halo_hot, slot_state = call(
+        functools.partial(prepare, slots, blocks),
+        [
             jax.ShapeDtypeStruct((halos, devices * slots), jnp.bfloat16),
             jax.ShapeDtypeStruct((devices * slots, halos), jnp.bfloat16),
             f32(tiles, 8, LANES),
-        ),
-        scratch_shapes=[pltpu.VMEM((devices, 2 * LANES), jnp.float32)],
-        compiler_params=PARAMS,
-    )(order, asked, centers, radii)
+        ],
+        place,
+        indices,
+        step(indices, "core", 1),
+        centers,
+        radii,
+    )
     each = tiles // len(slabs)
-    points, partials = [], []
-    for i, slab in enumerate(slabs):
+    got = {}
+    for i in (0, 1, 3, 2):
+        slab = slabs[i]
         if i:
-            slab, _ = lax.optimization_barrier((slab, partials[0]))
-        got = pl.pallas_call(
-            functools.partial(first_pass, i * each, group),
-            in_specs=[VMEM] * 3,
-            out_specs=[VMEM] * 2,
-            out_shape=(f32(each, 4, BLOCK, LANES), f32(each, ROWS, LANES)),
-            compiler_params=PARAMS,
-        )(slot_state, *shifted(slab, "core"))
-        points.append(got[0])
-        partials.append(got[1])
+            slab, _ = lax.optimization_barrier((slab, got[0][1]))
+        got[i] = call(
+            functools.partial(first_pass, i * each, blocks),
+            [f32(each, 4, BLOCK, LANES), f32(each, ROWS, LANES)],
+            slot_state,
+            *slab,
+            *[step(half, "core", 1) for half in slab],
+        )
+    points, partials = zip(*[got[i] for i in range(len(slabs))])
     centers, radii, profile = pl.pallas_call(
         functools.partial(finish, len(slabs)),
         in_specs=[VMEM] * (4 + 2 * len(slabs)),

time: 75 us -> 69.9 us (0.932)
  waiting for transfers between devices: 29.2 us -> 17.8 us
  starting transfers between devices: 24.1 us -> 30.1 us
  other arithmetic: 2.41 us -> 0.08 us
  Pallas kernels: 14.6 us -> 16.5 us
  local copies, waits for them, and re-layouts: 3.3 us -> 4.27 us
    ppermute x13 -> x24, starting transfers between devices: 16.1 us -> 30.1 us  [step(): lax.ppermute(value, axis, [(i, (i + by) % size) for i in range(size)])]
    all_to_all x1 -> x0, starting transfers between devices: 8.03 us -> none  [body(): asked = lax.all_to_all(pairs, AXES, split_axis=0, concat_axis=0, tiled=True)]
    ppermute x13 -> x24, waiting for transfers between devices: 24.4 us -> 17.8 us  [step(): lax.ppermute(value, axis, [(i, (i + by) % size) for i in range(size)])]
    all_to_all x1 -> x0, waiting for transfers between devices: 4.78 us -> none  [body(): asked = lax.all_to_all(pairs, AXES, split_axis=0, concat_axis=0, tiled=True)]
    concatenate x4 -> x0, other arithmetic: 2.14 us -> none  [the longest x1 0.72 us: body(): jnp.concatenate([pair_halo.reshape(tiles, LANES), pair_block.reshape(tile...]
    unnamed x13 -> x19, local copies, waits for them, and re-layouts: 2.22 us -> 4.27 us
    pallas_call x5 -> x8, Pallas kernels: 8.43 us -> 10.3 us  [call(): pl.pallas_call(fn, in_specs=specs, out_specs=out_specs, out_shape=outs, c...]
    all_to_all x1 -> x0, local copies, waits for them, and re-layouts: 0.78 us -> none  [body(): asked = lax.all_to_all(pairs, AXES, split_axis=0, concat_axis=0, tiled=True)]
  transfers between devices with their start and end apart: 14 -> 24, of which waited for: 5 -> 9; matrix products, arithmetic and copies ran while one was open for 3% -> 0% of each run, Pallas kernels for 10% -> 12%
where the time goes in v5:
time: 69.9 us; the launch traced here: 69.5 us
  starting transfers between devices  30.1 us (43%)
  waiting for transfers between devices  17.8 us (25%)
  Pallas kernels  16.5 us (24%)
  local copies, waits for them, and re-layouts  4.27 us (6%)
  between operations  0.81 us (1%)
    ppermute x24, starting transfers between devices, step(): lax.ppermute(value, axis, [(i, (i + by) % size) for i in range(size)])  30.1 us
    ppermute x24, waiting for transfers between devices, step(): lax.ppermute(value, axis, [(i, (i + by) % size) for i in range(size)])  17.8 us
    pallas_call x8, Pallas kernels, call(): pl.pallas_call(fn, in_specs=specs, out_specs=out_specs, out_shape=outs, c...  10.3 us
    pallas_call x1, Pallas kernels, body(): pl.pallas_call(functools.partial(finish, len(slabs)), in_specs=[VMEM] * (...  6.2 us
    unnamed x19, local copies, waits for them, and re-layouts  4.27 us
  transfers between devices with their start and end apart: 24, of which 9 were waited for; matrix products, arithmetic and copies ran while one was open for 0% of the time, Pallas kernels for 12%

profile of v5, /device:TPU:1, one launch (start us, length us, event | category | flops | bytes accessed | tf_op | source)
XLA Modules:
  0.0 69.5 jit_solution(8588352152964051128)
XLA Ops:
  0.6 0.0 copy-start.1
  0.7 0.8 %copy-done.2 = f32[3,2048]{1,0:T(4,128)S(1)} copy-done((f32[3,2048]{1,0:T(4,128)S(1)}, f32[3,2048]{1,0:T(4,128)}, u32[]{:S(2)}) %copy-start.2) | copy-done | bytes 24600
  1.4 0.7 copy-done.5
  2.1 0.7 copy-done.6
  2.8 0.7 copy-done.7
  3.5 4.7 %collective-permute-start.2 = (f32[96,128]{1,0:T(8,128)S(1)}, f32[96,128]{1,0:T(8,128)S(1)}, u32[]{:S(2)}, u32[]{:S(2)}) collective-permute-start(f32[96,128]{1,0:T(8,128)S(1)} %shard_map.85.refs_0_), channel_id=1, source_target_pairs={{0,3},{1,0},{2,1},{3,2},{4,7},{5,4},{6,5},{7,6},{8,11},{9,8},{10,9... | collective-permute-start | bytes 147464 | tf_op jit(solution)/shard_map/ppermute | solution.py:222
  8.2 0.0 collective-permute-start.1
  8.2 0.7 %collective-permute-start = (f32[96,128]{1,0:T(8,128)S(1)}, f32[96,128]{1,0:T(8,128)S(1)}, u32[]{:S(2)}, u32[]{:S(2)}) collective-permute-start(f32[96,128]{1,0:T(8,128)S(1)} %shard_map.85.refs_0_), channel_id=1, source_target_pairs={{0,1},{1,2},{2,3},{3,0},{4,5},{5,6},{6,7},{7,4},{8,9},{9,10},{10,1... | collective-permute-start | bytes 147464 | tf_op jit(solution)/shard_map/ppermute | solution.py:222
  8.9 0.1 pad_add_fusion.place
  9.0 0.4 collective-permute-done.2.refs_3_
  9.4 3.4 %collective-permute-done.1.refs_2_ = f32[96,128]{1,0:T(8,128)S(1)} collective-permute-done((f32[96,128]{1,0:T(8,128)S(1)}, f32[96,128]{1,0:T(8,128)S(1)}, u32[]{:S(2)}, u32[]{:S(2)}) %collective-permute-start.1) | collective-permute-done | bytes 49184 | tf_op jit(solution)/shard_map/ppermute | solution.py:222
  12.7 0.1 collective-permute-done.refs_1_
  12.9 0.9 %shard_map.86 = (f32[264,128]{1,0:T(8,128)S(1)}, f32[264,128]{1,0:T(8,128)S(1)}, f32[264,128]{1,0:T(8,128)S(1)}, f32[264,128]{1,0:T(8,128)S(1)}) custom-call(s32[4]{0:T(128)S(1)} %pad_add_fusion.place, f32[96,128]{1,0:T(8,128)S(1)} %shard_map.85.refs_0_, f32[96,128]{1,0:T(8,128)S(1)} %collective-permute-done.refs_1_, ...), custom_call_target="tpu_custom_call" | custom-call | tf_op jit(solution)/shard_map/pallas_call | solution.py:228
  13.8 1.4 %collective-permute-start.3 = (f32[264,128]{1,0:T(8,128)S(1)}, f32[264,128]{1,0:T(8,128)S(1)}, u32[]{:S(2)}, u32[]{:S(2)}) collective-permute-start(f32[264,128]{1,0:T(8,128)S(1)} %get-tuple-element.31), channel_id=1, source_target_pairs={{0,4},{4,8},{8,12},{12,0},{1,5},{5,9},{9,13},{13,1},{2,6},{6,10},{... | collective-permute-start | bytes 405512 | tf_op jit(solution)/shard_map/ppermute | solution.py:222
  15.1 2.6 %collective-permute-start.4 = (f32[264,128]{1,0:T(8,128)S(1)}, f32[264,128]{1,0:T(8,128)S(1)}, u32[]{:S(2)}, u32[]{:S(2)}) collective-permute-start(f32[264,128]{1,0:T(8,128)S(1)} %get-tuple-element.32), channel_id=1, source_target_pairs={{0,8},{4,12},{8,0},{12,4},{1,9},{5,13},{9,1},{13,5},{2,10},{6,14},... | collective-permute-start | bytes 405512 | tf_op jit(solution)/shard_map/ppermute | solution.py:222
  17.8 1.1 %collective-permute-start.5 = (f32[264,128]{1,0:T(8,128)S(1)}, f32[264,128]{1,0:T(8,128)S(1)}, u32[]{:S(2)}, u32[]{:S(2)}) collective-permute-start(f32[264,128]{1,0:T(8,128)S(1)} %get-tuple-element.33), channel_id=1, source_target_pairs={{0,12},{4,0},{8,4},{12,8},{1,13},{5,1},{9,5},{13,9},{2,14},{6,2},{... | collective-permute-start | bytes 405512 | tf_op jit(solution)/shard_map/ppermute | solution.py:222
  18.8 0.1 collective-permute-done.3.refs_1_
  19.0 3.0 %collective-permute-done.4.refs_2_ = f32[264,128]{1,0:T(8,128)S(1)} collective-permute-done((f32[264,128]{1,0:T(8,128)S(1)}, f32[264,128]{1,0:T(8,128)S(1)}, u32[]{:S(2)}, u32[]{:S(2)}) %collective-permute-start.4) | collective-permute-done | bytes 135200 | tf_op jit(solution)/shard_map/ppermute | solution.py:222
  22.0 0.7 %collective-permute-done.5.refs_3_ = f32[264,128]{1,0:T(8,128)S(1)} collective-permute-done((f32[264,128]{1,0:T(8,128)S(1)}, f32[264,128]{1,0:T(8,128)S(1)}, u32[]{:S(2)}, u32[]{:S(2)}) %collective-permute-start.5) | collective-permute-done | bytes 135200 | tf_op jit(solution)/shard_map/ppermute | solution.py:222
  22.7 2.5 %collective-permute-start.8 = (f32[32,128]{1,0:T(8,128)S(1)}, f32[32,128]{1,0:T(8,128)S(1)}, u32[]{:S(2)}, u32[]{:S(2)}) collective-permute-start(f32[32,128]{1,0:T(8,128)S(1)} %get-tuple-element.34), channel_id=1, source_target_pairs={{0,96},{32,0},{64,32},{96,64},{1,97},{33,1},{65,33},{97,65},{2,98}... | collective-permute-start | bytes 49160 | tf_op jit(solution)/shard_map/ppermute | solution.py:222
  25.3 0.5 collective-permute-start.7
  25.8 0.6 collective-permute-start.6
  26.4 3.2 %collective-permute-done.6 = f32[32,128]{1,0:T(8,128)S(1)} collective-permute-done((f32[32,128]{1,0:T(8,128)S(1)}, f32[32,128]{1,0:T(8,128)S(1)}, u32[]{:S(2)}, u32[]{:S(2)}) %collective-permute-start.6) | collective-permute-done | bytes 16416 | tf_op jit(solution)/shard_map/ppermute | solution.py:222
  29.6 0.0 collective-permute-done.7
  29.6 0.0 collective-permute-done.8
  29.6 4.5 %collective-permute-start.9 = (f32[128,128]{1,0:T(8,128)S(1)}, f32[128,128]{1,0:T(8,128)S(1)}, u32[]{:S(2)}, u32[]{:S(2)}) collective-permute-start(f32[128,128]{1,0:T(8,128)S(1)} %constant_dynamic-update-slice_fusion.mine), channel_id=1, source_target_pairs={{0,16},{16,0},{1,17},{17,1},{2,18},{18,2},{3,19},{19,3},{4,20},{20... | collective-permute-start | bytes 196616 | tf_op jit(solution)/shard_map/ppermute | solution.py:222
  34.2 0.0 collective-permute-start.12
  34.2 0.2 collective-permute-start.10
  34.3 2.9 %collective-permute-start.17 = (f32[512,128]{1,0:T(8,128)S(1)}, f32[512,128]{1,0:T(8,128)S(1)}, u32[]{:S(2)}, u32[]{:S(2)}) collective-permute-start(f32[512,128]{1,0:T(8,128)S(1)} %get-tuple-element.39.refs_1_), channel_id=1, source_target_pairs={{0,96},{32,0},{64,32},{96,64},{1,97},{33,1},{65,33},{97,65},{2,98}... | collective-permute-start | bytes 786440 | tf_op jit(solution)/shard_map/ppermute | solution.py:222
  37.2 0.4 collective-permute-start.11
  37.6 0.0 collective-permute-done.9.other
  37.7 0.0 collective-permute-start.13
  37.7 5.6 %collective-permute-done.12.refs_0_ = f32[512,128]{1,0:T(8,128)S(1)} collective-permute-done((f32[512,128]{1,0:T(8,128)S(1)}, f32[512,128]{1,0:T(8,128)S(1)}, u32[]{:S(2)}, u32[]{:S(2)}) %collective-permute-start.12) | collective-permute-done | bytes 262176 | tf_op jit(solution)/shard_map/ppermute | solution.py:222
  43.3 0.0 collective-permute-start.21
  43.3 0.7 %copy-done = f32[3,1024]{1,0:T(4,128)S(1)} copy-done((f32[3,1024]{1,0:T(4,128)S(1)}, f32[3,1024]{1,0:T(4,128)}, u32[]{:S(2)}) %copy-start) | copy-done | bytes 12312
  44.0 0.7 copy-done.3
  44.7 4.1 %shard_map.88 = (bf16[1024,2048]{1,0:T(8,128)(2,1)S(1)}, bf16[2048,1024]{1,0:T(8,128)(2,1)S(1)}, f32[16,8,128]{2,1,0:T(8,128)S(1)}) custom-call(s32[4]{0:T(128)S(1)} %pad_add_fusion.place, f32[128,128]{1,0:T(8,128)S(1)} %constant_dynamic-update-slice_fusion.mine, f32[128,128]{1,0:T(8,128)S(1)} %collective-permute-done.9.other, f32[3,1024]{1,0:T(4,128)S(1)} %copy-done, ...), custom_call_target="tpu_custom_call" | custom-call | tf_op jit(solution)/shard_map/pallas_call | solution.py:228
  48.7 0.0 collective-permute-done.10.refs_2_
  48.8 1.5 %collective-permute-start.16 = (f32[512,128]{1,0:T(8,128)S(1)}, f32[512,128]{1,0:T(8,128)S(1)}, u32[]{:S(2)}, u32[]{:S(2)}) collective-permute-start(f32[512,128]{1,0:T(8,128)S(1)} %collective-permute-done.12.refs_0_), channel_id=1, source_target_pairs={{0,32},{32,64},{64,96},{96,0},{1,33},{33,65},{65,97},{97,1},{2,34}... | collective-permute-start | bytes 786440 | tf_op jit(solution)/shard_map/ppermute | solution.py:222
  50.3 0.0 collective-permute-done.17.refs_1_
  50.3 1.2 %collective-permute-start.18 = (f32[512,128]{1,0:T(8,128)S(1)}, f32[512,128]{1,0:T(8,128)S(1)}, u32[]{:S(2)}, u32[]{:S(2)}) collective-permute-start(f32[512,128]{1,0:T(8,128)S(1)} %collective-permute-done.17.refs_1_), channel_id=1, source_target_pairs={{0,96},{32,0},{64,32},{96,64},{1,97},{33,1},{65,33},{97,65},{2,98}... | collective-permute-start | bytes 786440 | tf_op jit(solution)/shard_map/ppermute | solution.py:222
  51.5 0.0 collective-permute-done.11.refs_3_
  51.5 1.3 %shard_map.89 = (f32[4,4,128,128]{3,2,1,0:T(8,128)S(1)}, f32[4,24,128]{2,1,0:T(8,128)S(1)}) custom-call(f32[16,8,128]{2,1,0:T(8,128)S(1)} %get-tuple-element.37.slot_state, f32[512,128]{1,0:T(8,128)S(1)} %get-tuple-element.38.refs_0_, f32[512,128]{1,0:T(8,128)S(1)} %get-tuple-element.39.refs_1_, f32[512,128]{1,0:T(8,128)S(1)} %collective-permute-done.10.refs_2_, ...), custom_call_target="tpu_custom_call" | custom-call | tf_op jit(solution)/shard_map/pallas_call | solution.py:228
  52.8 0.0 collective-permute-done.13.refs_1_
  52.8 2.0 %collective-permute-start.14 = (f32[512,128]{1,0:T(8,128)S(1)}, f32[512,128]{1,0:T(8,128)S(1)}, u32[]{:S(2)}, u32[]{:S(2)}) collective-permute-start(f32[512,128]{1,0:T(8,128)S(1)} %collective-permute-done.12.refs_0_), channel_id=1, source_target_pairs={{0,16},{16,0},{1,17},{17,1},{2,18},{18,2},{3,19},{19,3},{4,20},{20... | collective-permute-start | bytes 786440 | tf_op jit(solution)/shard_map/ppermute | solution.py:222
  54.8 0.0 collective-permute-done.21.refs_0_
  54.8 0.1 collective-permute-start.15
  54.9 0.4 collective-permute-start.22
  55.3 1.2 %collective-permute-done.16.refs_0_ = f32[512,128]{1,0:T(8,128)S(1)} collective-permute-done((f32[512,128]{1,0:T(8,128)S(1)}, f32[512,128]{1,0:T(8,128)S(1)}, u32[]{:S(2)}, u32[]{:S(2)}) %collective-permute-start.16) | collective-permute-done | bytes 262176 | tf_op jit(solution)/shard_map/ppermute | solution.py:222
  56.5 2.2 %collective-permute-start.23 = (f32[512,128]{1,0:T(8,128)S(1)}, f32[512,128]{1,0:T(8,128)S(1)}, u32[]{:S(2)}, u32[]{:S(2)}) collective-permute-start(f32[512,128]{1,0:T(8,128)S(1)} %collective-permute-done.17.refs_1_), channel_id=1, source_target_pairs={{0,16},{16,0},{1,17},{17,1},{2,18},{18,2},{3,19},{19,3},{4,20},{20... | collective-permute-start | bytes 786440 | tf_op jit(solution)/shard_map/ppermute | solution.py:222
  58.8 0.0 collective-permute-done.18.refs_1_
  58.8 0.3 collective-permute-start.19
  59.0 0.0 collective-permute-done.14.refs_2_
  59.0 0.3 collective-permute-start.20
  59.3 0.0 collective-permute-done.15.refs_3_
  59.3 1.3 %shard_map.90 = (f32[4,4,128,128]{3,2,1,0:T(8,128)S(1)}, f32[4,24,128]{2,1,0:T(8,128)S(1)}) custom-call(f32[16,8,128]{2,1,0:T(8,128)S(1)} %get-tuple-element.37.slot_state, f32[512,128]{1,0:T(8,128)S(1)} %collective-permute-done.12.refs_0_, f32[512,128]{1,0:T(8,128)S(1)} %collective-permute-done.13.refs_1_, f32[512,128]{1,0:T(8,128)S(1)} %collective-permute-done.14.refs_2_, ...), custom_call_target="tpu_custom_call" | custom-call | tf_op jit(solution)/shard_map/pallas_call | solution.py:228
  60.6 0.0 collective-permute-done.22.refs_2_
  60.6 0.0 collective-permute-done.23.refs_3_
  60.6 1.3 %shard_map.92 = (f32[4,4,128,128]{3,2,1,0:T(8,128)S(1)}, f32[4,24,128]{2,1,0:T(8,128)S(1)}) custom-call(f32[16,8,128]{2,1,0:T(8,128)S(1)} %get-tuple-element.37.slot_state, f32[512,128]{1,0:T(8,128)S(1)} %collective-permute-done.21.refs_0_, f32[512,128]{1,0:T(8,128)S(1)} %collective-permute-done.17.refs_1_, f32[512,128]{1,0:T(8,128)S(1)} %collective-permute-done.22.refs_2_, ...), custom_call_target="tpu_custom_call" | custom-call | tf_op jit(solution)/shard_map/pallas_call | solution.py:228
  62.0 0.0 collective-permute-done.19.refs_2_
  62.0 0.0 collective-permute-done.20.refs_3_
  62.0 1.3 %shard_map.91 = (f32[4,4,128,128]{3,2,1,0:T(8,128)S(1)}, f32[4,24,128]{2,1,0:T(8,128)S(1)}) custom-call(f32[16,8,128]{2,1,0:T(8,128)S(1)} %get-tuple-element.37.slot_state, f32[512,128]{1,0:T(8,128)S(1)} %collective-permute-done.16.refs_0_, f32[512,128]{1,0:T(8,128)S(1)} %collective-permute-done.18.refs_1_, f32[512,128]{1,0:T(8,128)S(1)} %collective-permute-done.19.refs_2_, ...), custom_call_target="tpu_custom_call" | custom-call | tf_op jit(solution)/shard_map/pallas_call | solution.py:228
  63.3 0.0 copy-done.1
  63.3 6.2 %shard_map.93 = (f32[3,1024]{1,0:T(4,128)}, f32[1,1024]{1,0:T(1,128)}, f32[16,1024]{1,0:T(8,128)}) custom-call(bf16[1024,2048]{1,0:T(8,128)(2,1)S(1)} %get-tuple-element.35.one_hot, bf16[2048,1024]{1,0:T(8,128)(2,1)S(1)} %get-tuple-element.36.halo_hot, f32[3,1024]{1,0:T(4,128)S(1)} %copy-done.1, f32[1,1024]{1,0:T(1,128)S(1)} %bitcast.10, ...), custom_call_target="tpu_custom_call" | custom-call | tf_op jit(solution)/shard_map/pallas_call | solution.py:278
  (14 shorter events, 0.1 us)
Async XLA Ops:
  0.6 62.7 %copy-start.1 = (f32[3,1024]{1,0:T(4,128)S(1)}, f32[3,1024]{1,0:T(4,128)}, u32[]{:S(2)}) copy-start(f32[3,1024]{1,0:T(4,128)} %centers.3) | copy-start | bytes 36868
  0.6 0.8 %copy-start.2 = (f32[3,2048]{1,0:T(4,128)S(1)}, f32[3,2048]{1,0:T(4,128)}, u32[]{:S(2)}) copy-start(f32[3,2048]{1,0:T(4,128)} %positions.1) | copy-start | bytes 73732
  1.4 0.7 %copy-start.5 = (f32[2048]{0:T(1024)S(1)}, f32[2048]{0:T(1024)}, u32[]{:S(2)}) copy-start(f32[2048]{0:T(1024)} %param.7) | copy-start | bytes 24580
  2.1 0.7 %copy-start.6 = (s32[2048]{0:T(1024)S(1)}, s32[2048]{0:T(1024)}, u32[]{:S(2)}) copy-start(s32[2048]{0:T(1024)} %param.11) | copy-start | bytes 24580
  2.8 0.7 %copy-start.7 = (s32[2048]{0:T(1024)S(1)}, s32[2048]{0:T(1024)}, u32[]{:S(2)}) copy-start(s32[2048]{0:T(1024)} %param.10) | copy-start | bytes 24580
  3.5 59.8 %copy-start.4 = (f32[1024]{0:T(1024)S(1)}, f32[1024]{0:T(1024)}, u32[]{:S(2)}) copy-start(f32[1024]{0:T(1024)} %param.9) | copy-start | bytes 12292
  3.5 5.8 %collective-permute-start.2 = (f32[96,128]{1,0:T(8,128)S(1)}, f32[96,128]{1,0:T(8,128)S(1)}, u32[]{:S(2)}, u32[]{:S(2)}) collective-permute-start(f32[96,128]{1,0:T(8,128)S(1)} %shard_map.85.refs_0_), channel_id=1, source_target_pairs={{0,3},{1,0},{2,1},{3,2},{4,7},{5,4},{6,5},{7,6},{8,11},{9,8},{10,9... | collective-permute-start | bytes 147464 | tf_op jit(solution)/shard_map/ppermute | solution.py:222
  8.2 4.5 %collective-permute-start.1 = (f32[96,128]{1,0:T(8,128)S(1)}, f32[96,128]{1,0:T(8,128)S(1)}, u32[]{:S(2)}, u32[]{:S(2)}) collective-permute-start(f32[96,128]{1,0:T(8,128)S(1)} %shard_map.85.refs_0_), channel_id=1, source_target_pairs={{0,2},{1,3},{2,0},{3,1},{4,6},{5,7},{6,4},{7,5},{8,10},{9,11},{10,... | collective-permute-start | bytes 147464 | tf_op jit(solution)/shard_map/ppermute | solution.py:222
  8.2 4.7 %collective-permute-start = (f32[96,128]{1,0:T(8,128)S(1)}, f32[96,128]{1,0:T(8,128)S(1)}, u32[]{:S(2)}, u32[]{:S(2)}) collective-permute-start(f32[96,128]{1,0:T(8,128)S(1)} %shard_map.85.refs_0_), channel_id=1, source_target_pairs={{0,1},{1,2},{2,3},{3,0},{4,5},{5,6},{6,7},{7,4},{8,9},{9,10},{10,1... | collective-permute-start | bytes 147464 | tf_op jit(solution)/shard_map/ppermute | solution.py:222
  13.8 5.2 %collective-permute-start.3 = (f32[264,128]{1,0:T(8,128)S(1)}, f32[264,128]{1,0:T(8,128)S(1)}, u32[]{:S(2)}, u32[]{:S(2)}) collective-permute-start(f32[264,128]{1,0:T(8,128)S(1)} %get-tuple-element.31), channel_id=1, source_target_pairs={{0,4},{4,8},{8,12},{12,0},{1,5},{5,9},{9,13},{13,1},{2,6},{6,10},{... | collective-permute-start | bytes 405512 | tf_op jit(solution)/shard_map/ppermute | solution.py:222
  15.1 6.8 %collective-permute-start.4 = (f32[264,128]{1,0:T(8,128)S(1)}, f32[264,128]{1,0:T(8,128)S(1)}, u32[]{:S(2)}, u32[]{:S(2)}) collective-permute-start(f32[264,128]{1,0:T(8,128)S(1)} %get-tuple-element.32), channel_id=1, source_target_pairs={{0,8},{4,12},{8,0},{12,4},{1,9},{5,13},{9,1},{13,5},{2,10},{6,14},... | collective-permute-start | bytes 405512 | tf_op jit(solution)/shard_map/ppermute | solution.py:222
  17.8 4.9 %collective-permute-start.5 = (f32[264,128]{1,0:T(8,128)S(1)}, f32[264,128]{1,0:T(8,128)S(1)}, u32[]{:S(2)}, u32[]{:S(2)}) collective-permute-start(f32[264,128]{1,0:T(8,128)S(1)} %get-tuple-element.33), channel_id=1, source_target_pairs={{0,12},{4,0},{8,4},{12,8},{1,13},{5,1},{9,5},{13,9},{2,14},{6,2},{... | collective-permute-start | bytes 405512 | tf_op jit(solution)/shard_map/ppermute | solution.py:222
  22.7 6.9 %collective-permute-start.8 = (f32[32,128]{1,0:T(8,128)S(1)}, f32[32,128]{1,0:T(8,128)S(1)}, u32[]{:S(2)}, u32[]{:S(2)}) collective-permute-start(f32[32,128]{1,0:T(8,128)S(1)} %get-tuple-element.34), channel_id=1, source_target_pairs={{0,96},{32,0},{64,32},{96,64},{1,97},{33,1},{65,33},{97,65},{2,98}... | collective-permute-start | bytes 49160 | tf_op jit(solution)/shard_map/ppermute | solution.py:222
  25.3 4.3 %collective-permute-start.7 = (f32[32,128]{1,0:T(8,128)S(1)}, f32[32,128]{1,0:T(8,128)S(1)}, u32[]{:S(2)}, u32[]{:S(2)}) collective-permute-start(f32[32,128]{1,0:T(8,128)S(1)} %get-tuple-element.34), channel_id=1, source_target_pairs={{0,64},{32,96},{64,0},{96,32},{1,65},{33,97},{65,1},{97,33},{2,66}... | collective-permute-start | bytes 49160 | tf_op jit(solution)/shard_map/ppermute | solution.py:222
  25.8 3.8 %collective-permute-start.6 = (f32[32,128]{1,0:T(8,128)S(1)}, f32[32,128]{1,0:T(8,128)S(1)}, u32[]{:S(2)}, u32[]{:S(2)}) collective-permute-start(f32[32,128]{1,0:T(8,128)S(1)} %get-tuple-element.34), channel_id=1, source_target_pairs={{0,32},{32,64},{64,96},{96,0},{1,33},{33,65},{65,97},{97,1},{2,34}... | collective-permute-start | bytes 49160 | tf_op jit(solution)/shard_map/ppermute | solution.py:222
  29.6 8.0 %collective-permute-start.9 = (f32[128,128]{1,0:T(8,128)S(1)}, f32[128,128]{1,0:T(8,128)S(1)}, u32[]{:S(2)}, u32[]{:S(2)}) collective-permute-start(f32[128,128]{1,0:T(8,128)S(1)} %constant_dynamic-update-slice_fusion.mine), channel_id=1, source_target_pairs={{0,16},{16,0},{1,17},{17,1},{2,18},{18,2},{3,19},{19,3},{4,20},{20... | collective-permute-start | bytes 196616 | tf_op jit(solution)/shard_map/ppermute | solution.py:222
  34.2 9.1 %collective-permute-start.12 = (f32[512,128]{1,0:T(8,128)S(1)}, f32[512,128]{1,0:T(8,128)S(1)}, u32[]{:S(2)}, u32[]{:S(2)}) collective-permute-start(f32[512,128]{1,0:T(8,128)S(1)} %get-tuple-element.38.refs_0_), channel_id=1, source_target_pairs={{0,32},{32,64},{64,96},{96,0},{1,33},{33,65},{65,97},{97,1},{2,34}... | collective-permute-start | bytes 786440 | tf_op jit(solution)/shard_map/ppermute | solution.py:222
  34.2 14.6 %collective-permute-start.10 = (f32[512,128]{1,0:T(8,128)S(1)}, f32[512,128]{1,0:T(8,128)S(1)}, u32[]{:S(2)}, u32[]{:S(2)}) collective-permute-start(f32[512,128]{1,0:T(8,128)S(1)} %get-tuple-element.38.refs_0_), channel_id=1, source_target_pairs={{0,16},{16,0},{1,17},{17,1},{2,18},{18,2},{3,19},{19,3},{4,20},{20... | collective-permute-start | bytes 786440 | tf_op jit(solution)/shard_map/ppermute | solution.py:222
  34.3 15.9 %collective-permute-start.17 = (f32[512,128]{1,0:T(8,128)S(1)}, f32[512,128]{1,0:T(8,128)S(1)}, u32[]{:S(2)}, u32[]{:S(2)}) collective-permute-start(f32[512,128]{1,0:T(8,128)S(1)} %get-tuple-element.39.refs_1_), channel_id=1, source_target_pairs={{0,96},{32,0},{64,32},{96,64},{1,97},{33,1},{65,33},{97,65},{2,98}... | collective-permute-start | bytes 786440 | tf_op jit(solution)/shard_map/ppermute | solution.py:222
  37.2 14.3 %collective-permute-start.11 = (f32[512,128]{1,0:T(8,128)S(1)}, f32[512,128]{1,0:T(8,128)S(1)}, u32[]{:S(2)}, u32[]{:S(2)}) collective-permute-start(f32[512,128]{1,0:T(8,128)S(1)} %get-tuple-element.39.refs_1_), channel_id=1, source_target_pairs={{0,16},{16,0},{1,17},{17,1},{2,18},{18,2},{3,19},{19,3},{4,20},{20... | collective-permute-start | bytes 786440 | tf_op jit(solution)/shard_map/ppermute | solution.py:222
  37.7 15.2 %collective-permute-start.13 = (f32[512,128]{1,0:T(8,128)S(1)}, f32[512,128]{1,0:T(8,128)S(1)}, u32[]{:S(2)}, u32[]{:S(2)}) collective-permute-start(f32[512,128]{1,0:T(8,128)S(1)} %get-tuple-element.39.refs_1_), channel_id=1, source_target_pairs={{0,32},{32,64},{64,96},{96,0},{1,33},{33,65},{65,97},{97,1},{2,34}... | collective-permute-start | bytes 786440 | tf_op jit(solution)/shard_map/ppermute | solution.py:222
  43.3 11.6 %collective-permute-start.21 = (f32[512,128]{1,0:T(8,128)S(1)}, f32[512,128]{1,0:T(8,128)S(1)}, u32[]{:S(2)}, u32[]{:S(2)}) collective-permute-start(f32[512,128]{1,0:T(8,128)S(1)} %get-tuple-element.38.refs_0_), channel_id=1, source_target_pairs={{0,96},{32,0},{64,32},{96,64},{1,97},{33,1},{65,33},{97,65},{2,98}... | collective-permute-start | bytes 786440 | tf_op jit(solution)/shard_map/ppermute | solution.py:222
  43.3 0.7 %copy-start = (f32[3,1024]{1,0:T(4,128)S(1)}, f32[3,1024]{1,0:T(4,128)}, u32[]{:S(2)}) copy-start(f32[3,1024]{1,0:T(4,128)} %centers.3) | copy-start | bytes 36868
  44.0 0.7 copy-start.3
  48.8 7.8 %collective-permute-start.16 = (f32[512,128]{1,0:T(8,128)S(1)}, f32[512,128]{1,0:T(8,128)S(1)}, u32[]{:S(2)}, u32[]{:S(2)}) collective-permute-start(f32[512,128]{1,0:T(8,128)S(1)} %collective-permute-done.12.refs_0_), channel_id=1, source_target_pairs={{0,32},{32,64},{64,96},{96,0},{1,33},{33,65},{65,97},{97,1},{2,34}... | collective-permute-start | bytes 786440 | tf_op jit(solution)/shard_map/ppermute | solution.py:222
  50.3 8.5 %collective-permute-start.18 = (f32[512,128]{1,0:T(8,128)S(1)}, f32[512,128]{1,0:T(8,128)S(1)}, u32[]{:S(2)}, u32[]{:S(2)}) collective-permute-start(f32[512,128]{1,0:T(8,128)S(1)} %collective-permute-done.17.refs_1_), channel_id=1, source_target_pairs={{0,96},{32,0},{64,32},{96,64},{1,97},{33,1},{65,33},{97,65},{2,98}... | collective-permute-start | bytes 786440 | tf_op jit(solution)/shard_map/ppermute | solution.py:222
  52.8 6.2 %collective-permute-start.14 = (f32[512,128]{1,0:T(8,128)S(1)}, f32[512,128]{1,0:T(8,128)S(1)}, u32[]{:S(2)}, u32[]{:S(2)}) collective-permute-start(f32[512,128]{1,0:T(8,128)S(1)} %collective-permute-done.12.refs_0_), channel_id=1, source_target_pairs={{0,16},{16,0},{1,17},{17,1},{2,18},{18,2},{3,19},{19,3},{4,20},{20... | collective-permute-start | bytes 786440 | tf_op jit(solution)/shard_map/ppermute | solution.py:222
  54.8 4.5 %collective-permute-start.15 = (f32[512,128]{1,0:T(8,128)S(1)}, f32[512,128]{1,0:T(8,128)S(1)}, u32[]{:S(2)}, u32[]{:S(2)}) collective-permute-start(f32[512,128]{1,0:T(8,128)S(1)} %collective-permute-done.13.refs_1_), channel_id=1, source_target_pairs={{0,16},{16,0},{1,17},{17,1},{2,18},{18,2},{3,19},{19,3},{4,20},{20... | collective-permute-start | bytes 786440 | tf_op jit(solution)/shard_map/ppermute | solution.py:222
  54.9 5.7 %collective-permute-start.22 = (f32[512,128]{1,0:T(8,128)S(1)}, f32[512,128]{1,0:T(8,128)S(1)}, u32[]{:S(2)}, u32[]{:S(2)}) collective-permute-start(f32[512,128]{1,0:T(8,128)S(1)} %collective-permute-done.21.refs_0_), channel_id=1, source_target_pairs={{0,16},{16,0},{1,17},{17,1},{2,18},{18,2},{3,19},{19,3},{4,20},{20... | collective-permute-start | bytes 786440 | tf_op jit(solution)/shard_map/ppermute | solution.py:222
  56.5 4.1 %collective-permute-start.23 = (f32[512,128]{1,0:T(8,128)S(1)}, f32[512,128]{1,0:T(8,128)S(1)}, u32[]{:S(2)}, u32[]{:S(2)}) collective-permute-start(f32[512,128]{1,0:T(8,128)S(1)} %collective-permute-done.17.refs_1_), channel_id=1, source_target_pairs={{0,16},{16,0},{1,17},{17,1},{2,18},{18,2},{3,19},{19,3},{4,20},{20... | collective-permute-start | bytes 786440 | tf_op jit(solution)/shard_map/ppermute | solution.py:222
  58.8 3.2 %collective-permute-start.19 = (f32[512,128]{1,0:T(8,128)S(1)}, f32[512,128]{1,0:T(8,128)S(1)}, u32[]{:S(2)}, u32[]{:S(2)}) collective-permute-start(f32[512,128]{1,0:T(8,128)S(1)} %collective-permute-done.16.refs_0_), channel_id=1, source_target_pairs={{0,16},{16,0},{1,17},{17,1},{2,18},{18,2},{3,19},{19,3},{4,20},{20... | collective-permute-start | bytes 786440 | tf_op jit(solution)/shard_map/ppermute | solution.py:222
  59.0 3.0 %collective-permute-start.20 = (f32[512,128]{1,0:T(8,128)S(1)}, f32[512,128]{1,0:T(8,128)S(1)}, u32[]{:S(2)}, u32[]{:S(2)}) collective-permute-start(f32[512,128]{1,0:T(8,128)S(1)} %collective-permute-done.18.refs_1_), channel_id=1, source_target_pairs={{0,16},{16,0},{1,17},{17,1},{2,18},{18,2},{3,19},{19,3},{4,20},{20... | collective-permute-start | bytes 786440 | tf_op jit(solution)/shard_map/ppermute | solution.py:222

commit v6 on v5

v6 whole, which is shorter than its diff:
```python
import functools

import jax
import jax.numpy as jnp
from jax import lax
from jax.experimental import pallas as pl
from jax.experimental.pallas import tpu as pltpu
from jax.sharding import Mesh, PartitionSpec as P

SHELLS = 16
BLOCK = 128
LANES = 128
ROWS = 24
AXES = ("x", "core", "y", "z")
VMEM = pl.BlockSpec(memory_space=pltpu.VMEM)
PARAMS = pltpu.CompilerParams(vmem_limit_bytes=16 * 2**20)


def f32(*shape):
    return jax.ShapeDtypeStruct(shape, jnp.float32)


def split(value, terms):
    parts = []
    for _ in range(terms):
        part = value.astype(jnp.bfloat16)
        parts.append(part)
        value = value - part.astype(jnp.float32)
    return parts


def gather_state(state, one_hot):
    stacked = jnp.concatenate([s.astype(jnp.float32) for s in split(state, 3)] + [jnp.zeros_like(state)], axis=0)
    got = jnp.dot(stacked.astype(jnp.bfloat16), one_hot, preferred_element_type=jnp.float32)
    return got[0:4] + got[4:8] + got[8:12]


def spread(rows, keep, own, slots):
    rows = jnp.where(keep, rows, 0.0)
    shift = slots
    while shift < LANES:
        rows = rows + pltpu.roll(rows, shift, 1)
        shift *= 2
    return jnp.sum(jnp.where(own, rows, 0.0), axis=0, keepdims=True)


def pack(positions, masses, halo, block, centers, radii, out, state, *scratch):
    arrays = (positions, masses, halo, block, centers, radii)
    held, sems = scratch[:-1], scratch[-1]
    copies = [pltpu.make_async_copy(a, v, sems.at[n]) for n, (a, v) in enumerate(zip(arrays, held))]
    for copy in copies:
        copy.start()
    for copy in copies:
        copy.wait()
    blocks = masses.shape[0]
    for c in range(3):
        for b in range(blocks):
            out[c * blocks + b : c * blocks + b + 1] = held[0][c : c + 1, b * BLOCK : (b + 1) * BLOCK]
    at = 3 * blocks
    for part in held[1:4]:
        out[at : at + part.shape[0]] = part[...].astype(jnp.float32)
        at += part.shape[0]
    state[0:3] = held[4][...]
    state[3:4] = held[5][...]


def merge_z(slots, width, place, *refs):
    size = len(refs) // 2
    parts, outs = refs[:size], refs[size:]
    index_rows = (parts[0].shape[0] - width) // 2
    row = lax.broadcasted_iota(jnp.int32, (index_rows, LANES), 0)
    group = lax.broadcasted_iota(jnp.int32, (index_rows, LANES), 1) // slots
    for k in range(size):
        for i in range(size):
            outs[k][i * width : (i + 1) * width] = parts[i][:width]
        y = (place[2] + k) % size
        keep = (group == y % 2 * size + place[3]) & (row % 2 == y // 2)
        for which in range(2):
            for i in range(size):
                at = width + which * index_rows
                to = size * width + which * size + i
                outs[k][to : to + 1] = spread(parts[i][at : at + index_rows], keep, group == row // 2, slots)


def merge_y(*refs):
    size = len(refs) - 3
    parts, halves, both = refs[:size], refs[size : size + 2], refs[-1]
    rows = parts[0].shape[0] - 2 * size
    for i in range(size):
        at = i % 2
        for half, start in ((halves[i // 2], 0), (both, i // 2 * halves[0].shape[0])):
            half[start + at * rows : start + (at + 1) * rows] = parts[i][:rows]
            for which in range(2):
                to = start + 2 * rows + which * 2 * size + at * size
                half[to : to + size] = parts[i][rows + which * size : rows + (which + 1) * size]


def tile_sums(mine, points, t, out, o):
    cx, cy, cz, rad = mine[0:1], mine[1:2], mine[2:3], mine[3:4]
    scale = (SHELLS / 2.0) / jnp.where(rad > 0.0, rad, 1.0)
    ramps = [None] * (SHELLS + 1)
    inner = [None] * 4

    def add(sums, k, value):
        sums[k] = value if sums[k] is None else sums[k] + value

    for p in range(0, BLOCK, 8):
        x = points[t, 0, p : p + 8] - cx
        y = points[t, 1, p : p + 8] - cy
        z = points[t, 2, p : p + 8] - cz
        mass = points[t, 3, p : p + 8]
        scaled = jnp.sqrt(x * x + y * y + z * z) * scale
        half = mass * 0.5
        reach = half - mass * scaled
        for k in range(SHELLS + 1):
            add(ramps, k, jnp.maximum(reach, 0.0))
            if k == SHELLS // 2 - 1:
                weight = jnp.maximum(jnp.minimum(reach + half, mass), 0.0)
            reach = reach + mass
        add(inner, 0, weight)
        add(inner, 1, weight * x)
        add(inner, 2, weight * y)
        add(inner, 3, weight * z)
    for k in range(SHELLS):
        cumulative = ramps[k + 1] - ramps[k] - ramps[0]
        out[o, k : k + 1] = jnp.sum(cumulative, axis=0, keepdims=True)
    for k in range(4):
        out[o, SHELLS + k : SHELLS + k + 1] = jnp.sum(inner[k], axis=0, keepdims=True)


def halo_sums(terms, halo_hot):
    high, low = [part.astype(jnp.float32) for part in split(terms, 2)]
    both = jnp.concatenate([high, low], axis=0).astype(jnp.bfloat16)
    sums = jnp.dot(both, halo_hot, preferred_element_type=jnp.float32)
    return sums[:ROWS] + sums[ROWS:]


def first_pass(slots, blocks, place, state, *refs):
    whole, (one_hot, halo_hot, points, sums, slot_state, partial) = refs[:-6], refs[-6:]
    halos = state.shape[1]
    domain = 4 * blocks
    rows = 8 * domain + 16
    chunks = [ref.at[pl.ds(at, rows)] for ref in whole for at in range(0, ref.shape[0], rows)]
    tiles = len(chunks)
    count = 8 * blocks
    lane_group = lax.broadcasted_iota(jnp.int32, (8, LANES), 1) // slots
    own = lane_group == lax.broadcasted_iota(jnp.int32, (8, LANES), 0)
    keep = lane_group == place[0] * 2 + place[1]
    halo_index = lax.broadcasted_iota(jnp.int32, (halos, LANES), 0).astype(jnp.float32)
    across = lax.broadcasted_iota(jnp.int32, (LANES, halos), 1).astype(jnp.float32)
    block_index = lax.broadcasted_iota(jnp.int32, (count, LANES), 0).astype(jnp.float32)
    first = (lax.broadcasted_iota(jnp.int32, (1, LANES), 1) // slots * blocks).astype(jnp.float32)
    for t in range(tiles):
        at = 8 * domain
        halo_row = spread(chunks[t][at : at + 8], keep, own, slots)
        hit = halo_index == halo_row
        one_hot[:, t * LANES : (t + 1) * LANES] = jnp.where(hit, 1.0, 0.0).astype(jnp.bfloat16)
        column = jnp.broadcast_to(halo_row, (LANES, LANES)).T
        for h in range(0, halos, LANES):
            hit = across[:, h : h + LANES] == column
            halo_hot[t * LANES : (t + 1) * LANES, h : h + LANES] = jnp.where(hit, 1.0, 0.0).astype(jnp.bfloat16)
        hit = block_index == spread(chunks[t][at + 8 : at + 16], keep, own, slots) + first
        pick = jnp.where(hit, 1.0, 0.0).astype(jnp.bfloat16)
        for c in range(4):
            parts = [chunks[t][a + c * blocks : a + (c + 1) * blocks] for a in range(0, 8 * domain, domain)]
            chosen = jnp.concatenate(parts, axis=0).T
            high, low = split(chosen, 2)
            points[t, c] = jnp.dot(high, pick, preferred_element_type=jnp.float32) + jnp.dot(
                low, pick, preferred_element_type=jnp.float32
            )
    slab_sums(state[...], one_hot, halo_hot, points, sums, slot_state, partial)


def slab_sums(state, one_hot, halo_hot, points, sums, slot_state, partial):
    tiles = points.shape[0]
    got = gather_state(state, one_hot[...])
    for t in range(tiles):
        slot_state[t, 0:4] = got[:, t * LANES : (t + 1) * LANES]
    partial[...] = jnp.zeros_like(partial)

    def one_tile(t, carry):
        tile_sums(slot_state[t], points, t, partial, t)
        return carry

    lax.fori_loop(0, tiles, one_tile, 0)
    sums[...] = halo_sums(jnp.concatenate([partial[t] for t in range(tiles)], axis=1), halo_hot[...])


def finish(slabs, state, *refs):
    inputs, (centers_out, radii_out, profile_out, held, slot_state, partial) = refs[: 4 * slabs], refs[4 * slabs :]
    parts = [inputs[4 * i : 4 * i + 4] for i in range(slabs)]

    def advance(center, radius, sums):
        profile = sums[:SHELLS]
        enclosed = profile[SHELLS // 2 - 1 : SHELLS // 2]
        ratio = (1.0 + enclosed) / (1.0 + radius * radius * radius)
        radius = radius * jnp.exp(jnp.log(ratio) * (1.0 / 3.0))
        center = center + sums[SHELLS + 1 : SHELLS + 4] / jnp.maximum(sums[SHELLS : SHELLS + 1], 1.0)
        return center, radius, profile

    sums = sum(part[3][...] for part in parts)
    center, radius, _ = advance(state[0:3], state[3:4], sums)
    both = jnp.concatenate([center, radius], axis=0)
    for i, (one_hot, halo_hot, points, _) in enumerate(parts):
        slab_sums(both, one_hot, halo_hot, points, held.at[i], slot_state, partial)
    center, radius, profile = advance(center, radius, sum(held[i] for i in range(slabs)))
    centers_out[...] = center
    radii_out[...] = radius
    profile_out[...] = profile


def step(value, axis, by):
    size = lax.axis_size(axis)
    return lax.ppermute(value, axis, [(i, (i + by) % size) for i in range(size)])


def call(fn, outs, *args, scratch=(), near=True):
    place = VMEM if near else pl.BlockSpec(memory_space=pltpu.HBM)
    specs = [pl.BlockSpec(memory_space=pltpu.SMEM) if a.ndim == 1 else place for a in args]
    out_specs = [VMEM] * len(outs)
    return pl.pallas_call(
        fn, in_specs=specs, out_specs=out_specs, out_shape=outs, scratch_shapes=scratch, compiler_params=PARAMS
    )(*args)


def body(positions, masses, centers, radii, pair_block, pair_halo):
    devices = lax.axis_size(AXES)
    halos = radii.shape[0]
    blocks = masses.shape[0] // BLOCK
    slots = pair_halo.shape[0] // devices
    domain = 4 * blocks
    half = 8 * domain + 16
    place = jnp.stack([lax.axis_index(axis) for axis in AXES]).astype(jnp.int32)
    row = lambda a: a.reshape(-1, LANES)
    inputs = (positions, row(masses), row(pair_halo), row(pair_block), centers, radii[None])
    payload, state = call(
        pack,
        [f32(domain + 2 * row(pair_halo).shape[0], LANES), f32(4, halos)],
        *inputs,
        scratch=[pltpu.VMEM(a.shape, a.dtype) for a in inputs] + [pltpu.SemaphoreType.DMA((len(inputs),))],
        near=False,
    )
    along_z = [payload] + [step(payload, "z", k) for k in range(1, 4)]
    to_y = call(functools.partial(merge_z, slots, domain), [f32(4 * domain + 8, LANES)] * 4, place, *along_z)
    along_y = [step(to_y[k], "y", k) if k else to_y[k] for k in range(4)]
    low, high, both = call(merge_y, [f32(rows, LANES) for rows in (half, half, 2 * half)], *along_y)
    below_low, above_high = step(low, "x", 1), step(high, "x", -1)
    below_high, above_low = step(high, "x", 1), step(low, "x", -1)
    far_low, far_high = step(below_low, "x", 1), step(above_high, "x", -1)
    slabs = [(both,), (below_low, below_high), (far_low, far_high), (above_low, above_high)]
    each = devices * slots // LANES // len(slabs)
    held = [pltpu.VMEM((each, 8, LANES), jnp.float32), pltpu.VMEM((each, ROWS, LANES), jnp.float32)]
    outs = [
        jax.ShapeDtypeStruct((halos, each * LANES), jnp.bfloat16),
        jax.ShapeDtypeStruct((each * LANES, halos), jnp.bfloat16),
        f32(each, 4, BLOCK, LANES),
        f32(ROWS, halos),
    ]
    got = {}
    for i in (0, 1, 3, 2):
        slab = slabs[i]
        if i == 2:
            slab = lax.optimization_barrier((*slab, *[got[k][3] for k in got]))[: len(slab)]
        others = [step(part, "core", 1) for part in slab]
        got[i] = call(functools.partial(first_pass, slots, blocks), outs, place, state, *slab, *others, scratch=held)
    centers, radii, profile = call(
        functools.partial(finish, len(slabs)),
        [f32(3, halos), f32(1, halos), f32(SHELLS, halos)],
        state,
        *[array for i in got for array in got[i]],
        scratch=[pltpu.VMEM((len(slabs), ROWS, halos), jnp.float32), *held],
    )
    return (centers, radii[0], profile)


def solution(mesh):
    chips = Mesh(mesh.devices.reshape(4, 2, 4, 4), AXES)
    in_specs = (
        P(None, AXES),
        P(AXES),
        P(None, AXES),
        P(AXES),
        P(AXES),
        P(AXES),
    )
    out_specs = (P(None, AXES), P(AXES), P(None, AXES))
    return jax.shard_map(body, mesh=chips, in_specs=in_specs, out_specs=out_specs, check_vma=False)
```

time: 69.9 us -> 64.6 us (0.924)
  waiting for transfers between devices: 17.8 us -> 14.6 us
  starting transfers between devices: 30.1 us -> 27.5 us
    ppermute x24 -> x19, waiting for transfers between devices: 17.8 us -> 14.6 us  [step(): lax.ppermute(value, axis, [(i, (i + by) % size) for i in range(size)])]
    ppermute x24 -> x19, starting transfers between devices: 30.1 us -> 27.5 us  [step(): lax.ppermute(value, axis, [(i, (i + by) % size) for i in range(size)])]
    pallas_call x9 -> x8, Pallas kernels: 16.5 us -> 17 us  [call(): pl.pallas_call(fn, in_specs=specs, out_specs=out_specs, out_shape=outs, s...]
    unnamed x19 -> x12, local copies, waits for them, and re-layouts: 4.27 us -> 4.24 us
  transfers between devices with their start and end apart: 24 -> 19, of which waited for: 9 -> 11; matrix products, arithmetic and copies ran while one was open for 0% -> 0% of each run, Pallas kernels for 12% -> 12%
where the time goes in v6:
time: 64.6 us; the launch traced here: 64.2 us
  starting transfers between devices  27.5 us (43%)
  Pallas kernels  17 us (26%)
  waiting for transfers between devices  14.6 us (23%)
  local copies, waits for them, and re-layouts  4.24 us (7%)
  between operations  0.75 us (1%)
    ppermute x19, starting transfers between devices, step(): lax.ppermute(value, axis, [(i, (i + by) % size) for i in range(size)])  27.5 us
    pallas_call x8, Pallas kernels, call(): pl.pallas_call(fn, in_specs=specs, out_specs=out_specs, out_shape=outs, s...  17 us
    ppermute x19, waiting for transfers between devices, step(): lax.ppermute(value, axis, [(i, (i + by) % size) for i in range(size)])  14.6 us
    unnamed x12, local copies, waits for them, and re-layouts  4.24 us
  transfers between devices with their start and end apart: 19, of which 11 were waited for; matrix products, arithmetic and copies ran while one was open for 0% of the time, Pallas kernels for 12%

profile of v6, /device:TPU:1, one launch (start us, length us, event | category | flops | bytes accessed | tf_op | source)
XLA Modules:
  0.0 64.2 jit_solution(12504846147865902878)
XLA Ops:
  0.6 0.0 copy-start.5
  0.6 0.7 %copy-done.5 = f32[1024]{0:T(1024)S(1)} copy-done((f32[1024]{0:T(1024)S(1)}, f32[1024]{0:T(1024)}, u32[]{:S(2)}) %copy-start.5) | copy-done | bytes 4120
  1.3 0.0 copy-start
  1.3 0.8 %copy-done = f32[3,2048]{1,0:T(4,128)S(1)} copy-done((f32[3,2048]{1,0:T(4,128)S(1)}, f32[3,2048]{1,0:T(4,128)}, u32[]{:S(2)}) %copy-start) | copy-done | bytes 24600
  2.1 0.0 copy-start.1
  2.1 0.7 %copy-done.1 = f32[3,1024]{1,0:T(4,128)S(1)} copy-done((f32[3,1024]{1,0:T(4,128)S(1)}, f32[3,1024]{1,0:T(4,128)}, u32[]{:S(2)}) %copy-start.1) | copy-done | bytes 12312
  2.8 0.0 copy-start.2
  2.8 0.7 %copy-done.2 = f32[2048]{0:T(1024)S(1)} copy-done((f32[2048]{0:T(1024)S(1)}, f32[2048]{0:T(1024)}, u32[]{:S(2)}) %copy-start.2) | copy-done | bytes 8216
  3.5 0.0 copy-start.3
  3.5 0.7 %copy-done.3 = s32[2048]{0:T(1024)S(1)} copy-done((s32[2048]{0:T(1024)S(1)}, s32[2048]{0:T(1024)}, u32[]{:S(2)}) %copy-start.3) | copy-done | bytes 8216
  4.2 0.0 copy-start.4
  4.2 0.7 %copy-done.4 = s32[2048]{0:T(1024)S(1)} copy-done((s32[2048]{0:T(1024)S(1)}, s32[2048]{0:T(1024)}, u32[]{:S(2)}) %copy-start.4) | copy-done | bytes 8216
  4.9 0.1 shard_map.85
  5.0 4.7 %collective-permute-start.2 = (f32[96,128]{1,0:T(8,128)S(1)}, f32[96,128]{1,0:T(8,128)S(1)}, u32[]{:S(2)}, u32[]{:S(2)}) collective-permute-start(f32[96,128]{1,0:T(8,128)S(1)} %get-tuple-element.34.refs_0_), channel_id=1, source_target_pairs={{0,3},{1,0},{2,1},{3,2},{4,7},{5,4},{6,5},{7,6},{8,11},{9,8},{10,9... | collective-permute-start | bytes 147464 | tf_op jit(solution)/shard_map/ppermute | solution.py:214
  9.7 0.0 collective-permute-start.1
  9.7 0.7 %collective-permute-start = (f32[96,128]{1,0:T(8,128)S(1)}, f32[96,128]{1,0:T(8,128)S(1)}, u32[]{:S(2)}, u32[]{:S(2)}) collective-permute-start(f32[96,128]{1,0:T(8,128)S(1)} %get-tuple-element.34.refs_0_), channel_id=1, source_target_pairs={{0,1},{1,2},{2,3},{3,0},{4,5},{5,6},{6,7},{7,4},{8,9},{9,10},{10,1... | collective-permute-start | bytes 147464 | tf_op jit(solution)/shard_map/ppermute | solution.py:214
  10.4 0.1 pad_add_fusion.place
  10.5 0.4 collective-permute-done.2.refs_3_
  10.9 3.4 %collective-permute-done.1.refs_2_ = f32[96,128]{1,0:T(8,128)S(1)} collective-permute-done((f32[96,128]{1,0:T(8,128)S(1)}, f32[96,128]{1,0:T(8,128)S(1)}, u32[]{:S(2)}, u32[]{:S(2)}) %collective-permute-start.1) | collective-permute-done | bytes 49184 | tf_op jit(solution)/shard_map/ppermute | solution.py:214
  14.2 0.1 collective-permute-done.refs_1_
  14.4 0.9 %shard_map.86 = (f32[264,128]{1,0:T(8,128)S(1)}, f32[264,128]{1,0:T(8,128)S(1)}, f32[264,128]{1,0:T(8,128)S(1)}, f32[264,128]{1,0:T(8,128)S(1)}) custom-call(s32[4]{0:T(128)S(1)} %pad_add_fusion.place, f32[96,128]{1,0:T(8,128)S(1)} %get-tuple-element.34.refs_0_, f32[96,128]{1,0:T(8,128)S(1)} %collective-permute-done.refs_1_, ...), custom_call_target="tpu_custom_call" | custom-call | tf_op jit(solution)/shard_map/pallas_call | solution.py:221
  15.3 1.4 %collective-permute-start.3 = (f32[264,128]{1,0:T(8,128)S(1)}, f32[264,128]{1,0:T(8,128)S(1)}, u32[]{:S(2)}, u32[]{:S(2)}) collective-permute-start(f32[264,128]{1,0:T(8,128)S(1)} %get-tuple-element.36), channel_id=1, source_target_pairs={{0,4},{4,8},{8,12},{12,0},{1,5},{5,9},{9,13},{13,1},{2,6},{6,10},{... | collective-permute-start | bytes 405512 | tf_op jit(solution)/shard_map/ppermute | solution.py:214
  16.7 2.6 %collective-permute-start.4 = (f32[264,128]{1,0:T(8,128)S(1)}, f32[264,128]{1,0:T(8,128)S(1)}, u32[]{:S(2)}, u32[]{:S(2)}) collective-permute-start(f32[264,128]{1,0:T(8,128)S(1)} %get-tuple-element.37), channel_id=1, source_target_pairs={{0,8},{4,12},{8,0},{12,4},{1,9},{5,13},{9,1},{13,5},{2,10},{6,14},... | collective-permute-start | bytes 405512 | tf_op jit(solution)/shard_map/ppermute | solution.py:214
  19.3 1.1 %collective-permute-start.5 = (f32[264,128]{1,0:T(8,128)S(1)}, f32[264,128]{1,0:T(8,128)S(1)}, u32[]{:S(2)}, u32[]{:S(2)}) collective-permute-start(f32[264,128]{1,0:T(8,128)S(1)} %get-tuple-element.38), channel_id=1, source_target_pairs={{0,12},{4,0},{8,4},{12,8},{1,13},{5,1},{9,5},{13,9},{2,14},{6,2},{... | collective-permute-start | bytes 405512 | tf_op jit(solution)/shard_map/ppermute | solution.py:214
  20.3 0.1 collective-permute-done.3.refs_1_
  20.5 3.0 %collective-permute-done.4.refs_2_ = f32[264,128]{1,0:T(8,128)S(1)} collective-permute-done((f32[264,128]{1,0:T(8,128)S(1)}, f32[264,128]{1,0:T(8,128)S(1)}, u32[]{:S(2)}, u32[]{:S(2)}) %collective-permute-start.4) | collective-permute-done | bytes 135200 | tf_op jit(solution)/shard_map/ppermute | solution.py:214
  23.5 0.7 %collective-permute-done.5.refs_3_ = f32[264,128]{1,0:T(8,128)S(1)} collective-permute-done((f32[264,128]{1,0:T(8,128)S(1)}, f32[264,128]{1,0:T(8,128)S(1)}, u32[]{:S(2)}, u32[]{:S(2)}) %collective-permute-start.5) | collective-permute-done | bytes 135200 | tf_op jit(solution)/shard_map/ppermute | solution.py:214
  24.2 0.1 shard_map.87
  24.3 1.3 %collective-permute-start.7 = (f32[528,128]{1,0:T(8,128)S(1)}, f32[528,128]{1,0:T(8,128)S(1)}, u32[]{:S(2)}, u32[]{:S(2)}) collective-permute-start(f32[528,128]{1,0:T(8,128)S(1)} %get-tuple-element.44), channel_id=1, source_target_pairs={{0,32},{32,64},{64,96},{96,0},{1,33},{33,65},{65,97},{97,1},{2,34}... | collective-permute-start | bytes 811016 | tf_op jit(solution)/shard_map/ppermute | solution.py:214
  25.6 3.0 %collective-permute-start.6 = (f32[1056,128]{1,0:T(8,128)S(1)}, f32[1056,128]{1,0:T(8,128)S(1)}, u32[]{:S(2)}, u32[]{:S(2)}) collective-permute-start(f32[1056,128]{1,0:T(8,128)S(1)} %get-tuple-element.39.refs_0_), channel_id=1, source_target_pairs={{0,16},{16,0},{1,17},{17,1},{2,18},{18,2},{3,19},{19,3},{4,20},{20... | collective-permute-start | bytes 1622024 | tf_op jit(solution)/shard_map/ppermute | solution.py:214
  28.6 1.5 %collective-permute-start.11 = (f32[528,128]{1,0:T(8,128)S(1)}, f32[528,128]{1,0:T(8,128)S(1)}, u32[]{:S(2)}, u32[]{:S(2)}) collective-permute-start(f32[528,128]{1,0:T(8,128)S(1)} %get-tuple-element.44), channel_id=1, source_target_pairs={{0,96},{32,0},{64,32},{96,64},{1,97},{33,1},{65,33},{97,65},{2,98}... | collective-permute-start | bytes 811016 | tf_op jit(solution)/shard_map/ppermute | solution.py:214
  30.1 0.0 collective-permute-start.8
  30.1 2.7 %collective-permute-start.12 = (f32[528,128]{1,0:T(8,128)S(1)}, f32[528,128]{1,0:T(8,128)S(1)}, u32[]{:S(2)}, u32[]{:S(2)}) collective-permute-start(f32[528,128]{1,0:T(8,128)S(1)} %get-tuple-element.45), channel_id=1, source_target_pairs={{0,96},{32,0},{64,32},{96,64},{1,97},{33,1},{65,33},{97,65},{2,98}... | collective-permute-start | bytes 811016 | tf_op jit(solution)/shard_map/ppermute | solution.py:214
  32.7 0.0 collective-permute-done.7.refs_0_
  32.7 2.4 %collective-permute-start.9 = (f32[528,128]{1,0:T(8,128)S(1)}, f32[528,128]{1,0:T(8,128)S(1)}, u32[]{:S(2)}, u32[]{:S(2)}) collective-permute-start(f32[528,128]{1,0:T(8,128)S(1)} %collective-permute-done.7.refs_0_), channel_id=1, source_target_pairs={{0,16},{16,0},{1,17},{17,1},{2,18},{18,2},{3,19},{19,3},{4,20},{20... | collective-permute-start | bytes 811016 | tf_op jit(solution)/shard_map/ppermute | solution.py:214
  35.1 1.6 %collective-permute-done.11.refs_0_ = f32[528,128]{1,0:T(8,128)S(1)} collective-permute-done((f32[528,128]{1,0:T(8,128)S(1)}, f32[528,128]{1,0:T(8,128)S(1)}, u32[]{:S(2)}, u32[]{:S(2)}) %collective-permute-start.11) | collective-permute-done | bytes 270368 | tf_op jit(solution)/shard_map/ppermute | solution.py:214
  36.7 1.2 %collective-permute-start.13 = (f32[528,128]{1,0:T(8,128)S(1)}, f32[528,128]{1,0:T(8,128)S(1)}, u32[]{:S(2)}, u32[]{:S(2)}) collective-permute-start(f32[528,128]{1,0:T(8,128)S(1)} %collective-permute-done.11.refs_0_), channel_id=1, source_target_pairs={{0,16},{16,0},{1,17},{17,1},{2,18},{18,2},{3,19},{19,3},{4,20},{20... | collective-permute-start | bytes 811016 | tf_op jit(solution)/shard_map/ppermute | solution.py:214
  37.9 1.9 %collective-permute-done.8.refs_1_ = f32[528,128]{1,0:T(8,128)S(1)} collective-permute-done((f32[528,128]{1,0:T(8,128)S(1)}, f32[528,128]{1,0:T(8,128)S(1)}, u32[]{:S(2)}, u32[]{:S(2)}) %collective-permute-start.8) | collective-permute-done | bytes 270368 | tf_op jit(solution)/shard_map/ppermute | solution.py:214
  39.8 0.7 %collective-permute-start.10 = (f32[528,128]{1,0:T(8,128)S(1)}, f32[528,128]{1,0:T(8,128)S(1)}, u32[]{:S(2)}, u32[]{:S(2)}) collective-permute-start(f32[528,128]{1,0:T(8,128)S(1)} %collective-permute-done.8.refs_1_), channel_id=1, source_target_pairs={{0,16},{16,0},{1,17},{17,1},{2,18},{18,2},{3,19},{19,3},{4,20},{20... | collective-permute-start | bytes 811016 | tf_op jit(solution)/shard_map/ppermute | solution.py:214
  40.6 1.9 %collective-permute-done.12.refs_1_ = f32[528,128]{1,0:T(8,128)S(1)} collective-permute-done((f32[528,128]{1,0:T(8,128)S(1)}, f32[528,128]{1,0:T(8,128)S(1)}, u32[]{:S(2)}, u32[]{:S(2)}) %collective-permute-start.12) | collective-permute-done | bytes 270368 | tf_op jit(solution)/shard_map/ppermute | solution.py:214
  42.5 0.8 %collective-permute-start.14 = (f32[528,128]{1,0:T(8,128)S(1)}, f32[528,128]{1,0:T(8,128)S(1)}, u32[]{:S(2)}, u32[]{:S(2)}) collective-permute-start(f32[528,128]{1,0:T(8,128)S(1)} %collective-permute-done.12.refs_1_), channel_id=1, source_target_pairs={{0,16},{16,0},{1,17},{17,1},{2,18},{18,2},{3,19},{19,3},{4,20},{20... | collective-permute-start | bytes 811016 | tf_op jit(solution)/shard_map/ppermute | solution.py:214
  43.3 0.0 collective-permute-done.9.refs_2_
  43.3 1.2 %collective-permute-start.15 = (f32[528,128]{1,0:T(8,128)S(1)}, f32[528,128]{1,0:T(8,128)S(1)}, u32[]{:S(2)}, u32[]{:S(2)}) collective-permute-start(f32[528,128]{1,0:T(8,128)S(1)} %collective-permute-done.7.refs_0_), channel_id=1, source_target_pairs={{0,32},{32,64},{64,96},{96,0},{1,33},{33,65},{65,97},{97,1},{2,34}... | collective-permute-start | bytes 811016 | tf_op jit(solution)/shard_map/ppermute | solution.py:214
  44.5 0.0 collective-permute-done.6.refs_1_
  44.5 1.5 %collective-permute-start.16 = (f32[528,128]{1,0:T(8,128)S(1)}, f32[528,128]{1,0:T(8,128)S(1)}, u32[]{:S(2)}, u32[]{:S(2)}) collective-permute-start(f32[528,128]{1,0:T(8,128)S(1)} %collective-permute-done.12.refs_1_), channel_id=1, source_target_pairs={{0,96},{32,0},{64,32},{96,64},{1,97},{33,1},{65,33},{97,65},{2,98}... | collective-permute-start | bytes 811016 | tf_op jit(solution)/shard_map/ppermute | solution.py:214
  46.0 2.5 %shard_map.88 = (bf16[1024,512]{1,0:T(8,128)(2,1)S(1)}, bf16[512,1024]{1,0:T(8,128)(2,1)S(1)}, f32[4,4,128,128]{3,2,1,0:T(8,128)S(1)}, f32[24,1024]{1,0:T(8,128)S(1)}) custom-call(s32[4]{0:T(128)S(1)} %pad_add_fusion.place, f32[4,1024]{1,0:T(4,128)S(1)} %get-tuple-element.33.state, f32[1056,128]{1,0:T(8,128)S(1)} %get-tuple-element.39.refs_0_, ...), custom_call_target="tpu_custom_call" | custom-call | tf_op jit(solution)/shard_map/pallas_call | solution.py:221
  48.6 0.0 collective-permute-done.10.refs_3_
  48.6 2.5 %shard_map.89 = (bf16[1024,512]{1,0:T(8,128)(2,1)S(1)}, bf16[512,1024]{1,0:T(8,128)(2,1)S(1)}, f32[4,4,128,128]{3,2,1,0:T(8,128)S(1)}, f32[24,1024]{1,0:T(8,128)S(1)}) custom-call(s32[4]{0:T(128)S(1)} %pad_add_fusion.place, f32[4,1024]{1,0:T(4,128)S(1)} %get-tuple-element.33.state, f32[528,128]{1,0:T(8,128)S(1)} %collective-permute-done.7.refs_0_, ...), custom_call_target="tpu_custom_call" | custom-call | tf_op jit(solution)/shard_map/pallas_call | solution.py:221
  51.2 0.0 collective-permute-done.13.refs_2_
  51.2 0.0 collective-permute-done.14.refs_3_
  51.2 2.5 %shard_map.90 = (bf16[1024,512]{1,0:T(8,128)(2,1)S(1)}, bf16[512,1024]{1,0:T(8,128)(2,1)S(1)}, f32[4,4,128,128]{3,2,1,0:T(8,128)S(1)}, f32[24,1024]{1,0:T(8,128)S(1)}) custom-call(s32[4]{0:T(128)S(1)} %pad_add_fusion.place, f32[4,1024]{1,0:T(4,128)S(1)} %get-tuple-element.33.state, f32[528,128]{1,0:T(8,128)S(1)} %collective-permute-done.11.refs_0_, ...), custom_call_target="tpu_custom_call" | custom-call | tf_op jit(solution)/shard_map/pallas_call | solution.py:221
  53.7 0.0 collective-permute-done.15.refs_0_
  53.7 0.0 collective-permute-done.16.refs_1_
  53.7 0.6 collective-permute-start.17
  54.3 0.3 collective-permute-start.18
  54.6 0.9 %collective-permute-done.17.refs_2_ = f32[528,128]{1,0:T(8,128)S(1)} collective-permute-done((f32[528,128]{1,0:T(8,128)S(1)}, f32[528,128]{1,0:T(8,128)S(1)}, u32[]{:S(2)}, u32[]{:S(2)}) %collective-permute-start.17) | collective-permute-done | bytes 270368 | tf_op jit(solution)/shard_map/ppermute | solution.py:214
  55.5 0.4 collective-permute-done.18.refs_3_
  55.9 2.5 %shard_map.91 = (bf16[1024,512]{1,0:T(8,128)(2,1)S(1)}, bf16[512,1024]{1,0:T(8,128)(2,1)S(1)}, f32[4,4,128,128]{3,2,1,0:T(8,128)S(1)}, f32[24,1024]{1,0:T(8,128)S(1)}) custom-call(s32[4]{0:T(128)S(1)} %pad_add_fusion.place, f32[4,1024]{1,0:T(4,128)S(1)} %get-tuple-element.33.state, f32[528,128]{1,0:T(8,128)S(1)} %collective-permute-done.15.refs_0_, ...), custom_call_target="tpu_custom_call" | custom-call | tf_op jit(solution)/shard_map/pallas_call | solution.py:221
  58.4 5.7 %shard_map.92 = (f32[3,1024]{1,0:T(4,128)}, f32[1,1024]{1,0:T(1,128)}, f32[16,1024]{1,0:T(8,128)}) custom-call(f32[4,1024]{1,0:T(4,128)S(1)} %get-tuple-element.33.state, bf16[1024,512]{1,0:T(8,128)(2,1)S(1)} %get-tuple-element.40.refs_0_, bf16[512,1024]{1,0:T(8,128)(2,1)S(1)} %get-tuple-element.41.refs_1_, ...), custom_call_target="tpu_custom_call" | custom-call | tf_op jit(solution)/shard_map/pallas_call | solution.py:221
Async XLA Ops:
  0.6 0.7 %copy-start.5 = (f32[1024]{0:T(1024)S(1)}, f32[1024]{0:T(1024)}, u32[]{:S(2)}) copy-start(f32[1024]{0:T(1024)} %param.9) | copy-start | bytes 12292
  1.3 0.8 %copy-start = (f32[3,2048]{1,0:T(4,128)S(1)}, f32[3,2048]{1,0:T(4,128)}, u32[]{:S(2)}) copy-start(f32[3,2048]{1,0:T(4,128)} %positions.1) | copy-start | bytes 73732
  2.1 0.7 %copy-start.1 = (f32[3,1024]{1,0:T(4,128)S(1)}, f32[3,1024]{1,0:T(4,128)}, u32[]{:S(2)}) copy-start(f32[3,1024]{1,0:T(4,128)} %centers.1) | copy-start | bytes 36868
  2.8 0.7 %copy-start.2 = (f32[2048]{0:T(1024)S(1)}, f32[2048]{0:T(1024)}, u32[]{:S(2)}) copy-start(f32[2048]{0:T(1024)} %param.7) | copy-start | bytes 24580
  3.5 0.7 %copy-start.3 = (s32[2048]{0:T(1024)S(1)}, s32[2048]{0:T(1024)}, u32[]{:S(2)}) copy-start(s32[2048]{0:T(1024)} %param.11) | copy-start | bytes 24580
  4.2 0.7 %copy-start.4 = (s32[2048]{0:T(1024)S(1)}, s32[2048]{0:T(1024)}, u32[]{:S(2)}) copy-start(s32[2048]{0:T(1024)} %param.10) | copy-start | bytes 24580
  5.0 5.8 %collective-permute-start.2 = (f32[96,128]{1,0:T(8,128)S(1)}, f32[96,128]{1,0:T(8,128)S(1)}, u32[]{:S(2)}, u32[]{:S(2)}) collective-permute-start(f32[96,128]{1,0:T(8,128)S(1)} %get-tuple-element.34.refs_0_), channel_id=1, source_target_pairs={{0,3},{1,0},{2,1},{3,2},{4,7},{5,4},{6,5},{7,6},{8,11},{9,8},{10,9... | collective-permute-start | bytes 147464 | tf_op jit(solution)/shard_map/ppermute | solution.py:214
  9.7 4.5 %collective-permute-start.1 = (f32[96,128]{1,0:T(8,128)S(1)}, f32[96,128]{1,0:T(8,128)S(1)}, u32[]{:S(2)}, u32[]{:S(2)}) collective-permute-start(f32[96,128]{1,0:T(8,128)S(1)} %get-tuple-element.34.refs_0_), channel_id=1, source_target_pairs={{0,2},{1,3},{2,0},{3,1},{4,6},{5,7},{6,4},{7,5},{8,10},{9,11},{10,... | collective-permute-start | bytes 147464 | tf_op jit(solution)/shard_map/ppermute | solution.py:214
  9.7 4.7 %collective-permute-start = (f32[96,128]{1,0:T(8,128)S(1)}, f32[96,128]{1,0:T(8,128)S(1)}, u32[]{:S(2)}, u32[]{:S(2)}) collective-permute-start(f32[96,128]{1,0:T(8,128)S(1)} %get-tuple-element.34.refs_0_), channel_id=1, source_target_pairs={{0,1},{1,2},{2,3},{3,0},{4,5},{5,6},{6,7},{7,4},{8,9},{9,10},{10,1... | collective-permute-start | bytes 147464 | tf_op jit(solution)/shard_map/ppermute | solution.py:214
  15.3 5.2 %collective-permute-start.3 = (f32[264,128]{1,0:T(8,128)S(1)}, f32[264,128]{1,0:T(8,128)S(1)}, u32[]{:S(2)}, u32[]{:S(2)}) collective-permute-start(f32[264,128]{1,0:T(8,128)S(1)} %get-tuple-element.36), channel_id=1, source_target_pairs={{0,4},{4,8},{8,12},{12,0},{1,5},{5,9},{9,13},{13,1},{2,6},{6,10},{... | collective-permute-start | bytes 405512 | tf_op jit(solution)/shard_map/ppermute | solution.py:214
  16.7 6.8 %collective-permute-start.4 = (f32[264,128]{1,0:T(8,128)S(1)}, f32[264,128]{1,0:T(8,128)S(1)}, u32[]{:S(2)}, u32[]{:S(2)}) collective-permute-start(f32[264,128]{1,0:T(8,128)S(1)} %get-tuple-element.37), channel_id=1, source_target_pairs={{0,8},{4,12},{8,0},{12,4},{1,9},{5,13},{9,1},{13,5},{2,10},{6,14},... | collective-permute-start | bytes 405512 | tf_op jit(solution)/shard_map/ppermute | solution.py:214
  19.3 4.9 %collective-permute-start.5 = (f32[264,128]{1,0:T(8,128)S(1)}, f32[264,128]{1,0:T(8,128)S(1)}, u32[]{:S(2)}, u32[]{:S(2)}) collective-permute-start(f32[264,128]{1,0:T(8,128)S(1)} %get-tuple-element.38), channel_id=1, source_target_pairs={{0,12},{4,0},{8,4},{12,8},{1,13},{5,1},{9,5},{13,9},{2,14},{6,2},{... | collective-permute-start | bytes 405512 | tf_op jit(solution)/shard_map/ppermute | solution.py:214
  24.3 8.5 %collective-permute-start.7 = (f32[528,128]{1,0:T(8,128)S(1)}, f32[528,128]{1,0:T(8,128)S(1)}, u32[]{:S(2)}, u32[]{:S(2)}) collective-permute-start(f32[528,128]{1,0:T(8,128)S(1)} %get-tuple-element.44), channel_id=1, source_target_pairs={{0,32},{32,64},{64,96},{96,0},{1,33},{33,65},{65,97},{97,1},{2,34}... | collective-permute-start | bytes 811016 | tf_op jit(solution)/shard_map/ppermute | solution.py:214
  25.6 18.9 %collective-permute-start.6 = (f32[1056,128]{1,0:T(8,128)S(1)}, f32[1056,128]{1,0:T(8,128)S(1)}, u32[]{:S(2)}, u32[]{:S(2)}) collective-permute-start(f32[1056,128]{1,0:T(8,128)S(1)} %get-tuple-element.39.refs_0_), channel_id=1, source_target_pairs={{0,16},{16,0},{1,17},{17,1},{2,18},{18,2},{3,19},{19,3},{4,20},{20... | collective-permute-start | bytes 1622024 | tf_op jit(solution)/shard_map/ppermute | solution.py:214
  28.6 8.1 %collective-permute-start.11 = (f32[528,128]{1,0:T(8,128)S(1)}, f32[528,128]{1,0:T(8,128)S(1)}, u32[]{:S(2)}, u32[]{:S(2)}) collective-permute-start(f32[528,128]{1,0:T(8,128)S(1)} %get-tuple-element.44), channel_id=1, source_target_pairs={{0,96},{32,0},{64,32},{96,64},{1,97},{33,1},{65,33},{97,65},{2,98}... | collective-permute-start | bytes 811016 | tf_op jit(solution)/shard_map/ppermute | solution.py:214
  30.1 9.8 %collective-permute-start.8 = (f32[528,128]{1,0:T(8,128)S(1)}, f32[528,128]{1,0:T(8,128)S(1)}, u32[]{:S(2)}, u32[]{:S(2)}) collective-permute-start(f32[528,128]{1,0:T(8,128)S(1)} %get-tuple-element.45), channel_id=1, source_target_pairs={{0,32},{32,64},{64,96},{96,0},{1,33},{33,65},{65,97},{97,1},{2,34}... | collective-permute-start | bytes 811016 | tf_op jit(solution)/shard_map/ppermute | solution.py:214
  30.1 12.4 %collective-permute-start.12 = (f32[528,128]{1,0:T(8,128)S(1)}, f32[528,128]{1,0:T(8,128)S(1)}, u32[]{:S(2)}, u32[]{:S(2)}) collective-permute-start(f32[528,128]{1,0:T(8,128)S(1)} %get-tuple-element.45), channel_id=1, source_target_pairs={{0,96},{32,0},{64,32},{96,64},{1,97},{33,1},{65,33},{97,65},{2,98}... | collective-permute-start | bytes 811016 | tf_op jit(solution)/shard_map/ppermute | solution.py:214
  32.7 10.5 %collective-permute-start.9 = (f32[528,128]{1,0:T(8,128)S(1)}, f32[528,128]{1,0:T(8,128)S(1)}, u32[]{:S(2)}, u32[]{:S(2)}) collective-permute-start(f32[528,128]{1,0:T(8,128)S(1)} %collective-permute-done.7.refs_0_), channel_id=1, source_target_pairs={{0,16},{16,0},{1,17},{17,1},{2,18},{18,2},{3,19},{19,3},{4,20},{20... | collective-permute-start | bytes 811016 | tf_op jit(solution)/shard_map/ppermute | solution.py:214
  36.7 14.5 %collective-permute-start.13 = (f32[528,128]{1,0:T(8,128)S(1)}, f32[528,128]{1,0:T(8,128)S(1)}, u32[]{:S(2)}, u32[]{:S(2)}) collective-permute-start(f32[528,128]{1,0:T(8,128)S(1)} %collective-permute-done.11.refs_0_), channel_id=1, source_target_pairs={{0,16},{16,0},{1,17},{17,1},{2,18},{18,2},{3,19},{19,3},{4,20},{20... | collective-permute-start | bytes 811016 | tf_op jit(solution)/shard_map/ppermute | solution.py:214
  39.8 8.8 %collective-permute-start.10 = (f32[528,128]{1,0:T(8,128)S(1)}, f32[528,128]{1,0:T(8,128)S(1)}, u32[]{:S(2)}, u32[]{:S(2)}) collective-permute-start(f32[528,128]{1,0:T(8,128)S(1)} %collective-permute-done.8.refs_1_), channel_id=1, source_target_pairs={{0,16},{16,0},{1,17},{17,1},{2,18},{18,2},{3,19},{19,3},{4,20},{20... | collective-permute-start | bytes 811016 | tf_op jit(solution)/shard_map/ppermute | solution.py:214
  42.5 8.7 %collective-permute-start.14 = (f32[528,128]{1,0:T(8,128)S(1)}, f32[528,128]{1,0:T(8,128)S(1)}, u32[]{:S(2)}, u32[]{:S(2)}) collective-permute-start(f32[528,128]{1,0:T(8,128)S(1)} %collective-permute-done.12.refs_1_), channel_id=1, source_target_pairs={{0,16},{16,0},{1,17},{17,1},{2,18},{18,2},{3,19},{19,3},{4,20},{20... | collective-permute-start | bytes 811016 | tf_op jit(solution)/shard_map/ppermute | solution.py:214
  43.3 10.4 %collective-permute-start.15 = (f32[528,128]{1,0:T(8,128)S(1)}, f32[528,128]{1,0:T(8,128)S(1)}, u32[]{:S(2)}, u32[]{:S(2)}) collective-permute-start(f32[528,128]{1,0:T(8,128)S(1)} %collective-permute-done.7.refs_0_), channel_id=1, source_target_pairs={{0,32},{32,64},{64,96},{96,0},{1,33},{33,65},{65,97},{97,1},{2,34}... | collective-permute-start | bytes 811016 | tf_op jit(solution)/shard_map/ppermute | solution.py:214
  44.5 9.2 %collective-permute-start.16 = (f32[528,128]{1,0:T(8,128)S(1)}, f32[528,128]{1,0:T(8,128)S(1)}, u32[]{:S(2)}, u32[]{:S(2)}) collective-permute-start(f32[528,128]{1,0:T(8,128)S(1)} %collective-permute-done.12.refs_1_), channel_id=1, source_target_pairs={{0,96},{32,0},{64,32},{96,64},{1,97},{33,1},{65,33},{97,65},{2,98}... | collective-permute-start | bytes 811016 | tf_op jit(solution)/shard_map/ppermute | solution.py:214
  53.7 1.7 %collective-permute-start.17 = (f32[528,128]{1,0:T(8,128)S(1)}, f32[528,128]{1,0:T(8,128)S(1)}, u32[]{:S(2)}, u32[]{:S(2)}) collective-permute-start(f32[528,128]{1,0:T(8,128)S(1)} %collective-permute-done.15.refs_0_), channel_id=1, source_target_pairs={{0,16},{16,0},{1,17},{17,1},{2,18},{18,2},{3,19},{19,3},{4,20},{20... | collective-permute-start | bytes 811016 | tf_op jit(solution)/shard_map/ppermute | solution.py:214
  54.3 1.6 %collective-permute-start.18 = (f32[528,128]{1,0:T(8,128)S(1)}, f32[528,128]{1,0:T(8,128)S(1)}, u32[]{:S(2)}, u32[]{:S(2)}) collective-permute-start(f32[528,128]{1,0:T(8,128)S(1)} %collective-permute-done.16.refs_1_), channel_id=1, source_target_pairs={{0,16},{16,0},{1,17},{17,1},{2,18},{18,2},{3,19},{19,3},{4,20},{20... | collective-permute-start | bytes 811016 | tf_op jit(solution)/shard_map/ppermute | solution.py:214

commit v7 on v6

--- a/solution.py
+++ b/solution.py
@@ -83,16 +83,15 @@
 
 
 def merge_y(*refs):
-    size = len(refs) - 3
-    parts, halves, both = refs[:size], refs[size : size + 2], refs[-1]
+    size = len(refs) - 2
+    parts, halves = refs[:size], refs[size:]
     rows = parts[0].shape[0] - 2 * size
     for i in range(size):
-        at = i % 2
-        for half, start in ((halves[i // 2], 0), (both, i // 2 * halves[0].shape[0])):
-            half[start + at * rows : start + (at + 1) * rows] = parts[i][:rows]
-            for which in range(2):
-                to = start + 2 * rows + which * 2 * size + at * size
-                half[to : to + size] = parts[i][rows + which * size : rows + (which + 1) * size]
+        half, at = halves[i // 2], i % 2
+        half[at * rows : (at + 1) * rows] = parts[i][:rows]
+        for which in range(2):
+            to = 2 * rows + which * 2 * size + at * size
+            half[to : to + size] = parts[i][rows + which * size : rows + (which + 1) * size]
 
 
 def tile_sums(mine, points, t, out, o):
@@ -135,47 +134,56 @@
     return sums[:ROWS] + sums[ROWS:]
 
 
-def first_pass(slots, blocks, place, state, *refs):
-    whole, (one_hot, halo_hot, points, sums, slot_state, partial) = refs[:-6], refs[-6:]
-    halos = state.shape[1]
+def first_pass(slots, blocks, place, *refs):
+    inputs, (one_hot, halo_hot, points, sums, slot_state, partial) = refs[:-6], refs[-6:]
+    states, before, halves = inputs[:2], inputs[2:-2], inputs[-2:]
+    halos = states[0].shape[1]
     domain = 4 * blocks
-    rows = 8 * domain + 16
-    chunks = [ref.at[pl.ds(at, rows)] for ref in whole for at in range(0, ref.shape[0], rows)]
-    tiles = len(chunks)
     count = 8 * blocks
     lane_group = lax.broadcasted_iota(jnp.int32, (8, LANES), 1) // slots
     own = lane_group == lax.broadcasted_iota(jnp.int32, (8, LANES), 0)
-    keep = lane_group == place[0] * 2 + place[1]
     halo_index = lax.broadcasted_iota(jnp.int32, (halos, LANES), 0).astype(jnp.float32)
     across = lax.broadcasted_iota(jnp.int32, (LANES, halos), 1).astype(jnp.float32)
     block_index = lax.broadcasted_iota(jnp.int32, (count, LANES), 0).astype(jnp.float32)
     first = (lax.broadcasted_iota(jnp.int32, (1, LANES), 1) // slots * blocks).astype(jnp.float32)
-    for t in range(tiles):
-        at = 8 * domain
-        halo_row = spread(chunks[t][at : at + 8], keep, own, slots)
-        hit = halo_index == halo_row
-        one_hot[:, t * LANES : (t + 1) * LANES] = jnp.where(hit, 1.0, 0.0).astype(jnp.bfloat16)
-        column = jnp.broadcast_to(halo_row, (LANES, LANES)).T
-        for h in range(0, halos, LANES):
-            hit = across[:, h : h + LANES] == column
-            halo_hot[t * LANES : (t + 1) * LANES, h : h + LANES] = jnp.where(hit, 1.0, 0.0).astype(jnp.bfloat16)
-        hit = block_index == spread(chunks[t][at + 8 : at + 16], keep, own, slots) + first
-        pick = jnp.where(hit, 1.0, 0.0).astype(jnp.bfloat16)
+    for h, half in enumerate(halves):
+        picks = []
+        for o in range(2):
+            t = o * 2 + h
+            at = 8 * domain
+            keep = lane_group == place[0] * 2 + (place[1] if o == 0 else 1 - place[1])
+            halo_row = spread(half[at : at + 8], keep, own, slots)
+            hit = halo_index == halo_row
+            one_hot[:, t * LANES : (t + 1) * LANES] = jnp.where(hit, 1.0, 0.0).astype(jnp.bfloat16)
+            column = jnp.broadcast_to(halo_row, (LANES, LANES)).T
+            for a in range(0, halos, LANES):
+                hit = across[:, a : a + LANES] == column
+                halo_hot[t * LANES : (t + 1) * LANES, a : a + LANES] = jnp.where(hit, 1.0, 0.0).astype(jnp.bfloat16)
+            hit = block_index == spread(half[at + 8 : at + 16], keep, own, slots) + first
+            picks.append(jnp.where(hit, 1.0, 0.0).astype(jnp.bfloat16))
+        pick = jnp.concatenate(picks, axis=1)
         for c in range(4):
-            parts = [chunks[t][a + c * blocks : a + (c + 1) * blocks] for a in range(0, 8 * domain, domain)]
-            chosen = jnp.concatenate(parts, axis=0).T
-            high, low = split(chosen, 2)
-            points[t, c] = jnp.dot(high, pick, preferred_element_type=jnp.float32) + jnp.dot(
+            parts = [half[a + c * blocks : a + (c + 1) * blocks] for a in range(0, 8 * domain, domain)]
+            high, low = split(jnp.concatenate(parts, axis=0).T, 2)
+            chosen = jnp.dot(high, pick, preferred_element_type=jnp.float32) + jnp.dot(
                 low, pick, preferred_element_type=jnp.float32
             )
-    slab_sums(state[...], one_hot, halo_hot, points, sums, slot_state, partial)
-
-
-def slab_sums(state, one_hot, halo_hot, points, sums, slot_state, partial):
+            for o in range(2):
+                points[o * 2 + h, c] = chosen[:, o * LANES : (o + 1) * LANES]
+    value = slab_sums([state[...] for state in states], one_hot, halo_hot, points, slot_state, partial)
+    for ref in before:
+        value = value + ref[...]
+    sums[...] = value
+
+
+def slab_sums(states, one_hot, halo_hot, points, slot_state, partial):
     tiles = points.shape[0]
-    got = gather_state(state, one_hot[...])
-    for t in range(tiles):
-        slot_state[t, 0:4] = got[:, t * LANES : (t + 1) * LANES]
+    each = tiles // 2
+    width = each * LANES
+    for o in range(2):
+        got = gather_state(states[o], one_hot[:, o * width : (o + 1) * width])
+        for t in range(each):
+            slot_state[o * each + t, 0:4] = got[:, t * LANES : (t + 1) * LANES]
     partial[...] = jnp.zeros_like(partial)
 
     def one_tile(t, carry):
@@ -183,30 +191,38 @@
         return carry
 
     lax.fori_loop(0, tiles, one_tile, 0)
-    sums[...] = halo_sums(jnp.concatenate([partial[t] for t in range(tiles)], axis=1), halo_hot[...])
-
-
-def finish(slabs, state, *refs):
-    inputs, (centers_out, radii_out, profile_out, held, slot_state, partial) = refs[: 4 * slabs], refs[4 * slabs :]
-    parts = [inputs[4 * i : 4 * i + 4] for i in range(slabs)]
-
-    def advance(center, radius, sums):
-        profile = sums[:SHELLS]
-        enclosed = profile[SHELLS // 2 - 1 : SHELLS // 2]
-        ratio = (1.0 + enclosed) / (1.0 + radius * radius * radius)
-        radius = radius * jnp.exp(jnp.log(ratio) * (1.0 / 3.0))
-        center = center + sums[SHELLS + 1 : SHELLS + 4] / jnp.maximum(sums[SHELLS : SHELLS + 1], 1.0)
-        return center, radius, profile
-
-    sums = sum(part[3][...] for part in parts)
-    center, radius, _ = advance(state[0:3], state[3:4], sums)
-    both = jnp.concatenate([center, radius], axis=0)
-    for i, (one_hot, halo_hot, points, _) in enumerate(parts):
-        slab_sums(both, one_hot, halo_hot, points, held.at[i], slot_state, partial)
-    center, radius, profile = advance(center, radius, sum(held[i] for i in range(slabs)))
-    centers_out[...] = center
-    radii_out[...] = radius
-    profile_out[...] = profile
+    sums = []
+    for o in range(2):
+        terms = jnp.concatenate([partial[o * each + t] for t in range(each)], axis=1)
+        sums.append(halo_sums(terms, halo_hot[o * width : (o + 1) * width]))
+    return jnp.concatenate(sums, axis=0)
+
+
+def advance(state, sums):
+    center, radius = state[0:3], state[3:4]
+    profile = sums[:SHELLS]
+    enclosed = profile[SHELLS // 2 - 1 : SHELLS // 2]
+    ratio = (1.0 + enclosed) / (1.0 + radius * radius * radius)
+    radius = radius * jnp.exp(jnp.log(ratio) * (1.0 / 3.0))
+    center = center + sums[SHELLS + 1 : SHELLS + 4] / jnp.maximum(sums[SHELLS : SHELLS + 1], 1.0)
+    return center, radius, profile
+
+
+def second_pass(mine, other, sums, received, *refs):
+    inputs, (state, own, partner, slot_state, partial) = refs[:-5], refs[-5:]
+    totals = (sums[:ROWS] + received[ROWS:], sums[ROWS:] + received[:ROWS])
+    states = [jnp.concatenate(advance(s[...], t)[:2], axis=0) for s, t in zip((mine, other), totals)]
+    state[...] = states[0]
+    value = None
+    for i in range(0, len(inputs), 3):
+        part = slab_sums(states, *inputs[i : i + 3], slot_state, partial)
+        value = part if value is None else value + part
+    own[...] = value[:ROWS]
+    partner[...] = value[ROWS:]
+
+
+def finish(state, own, received, centers_out, radii_out, profile_out):
+    centers_out[...], radii_out[...], profile_out[...] = advance(state[...], own[...] + received[...])
 
 
 def step(value, axis, by):
@@ -229,10 +245,10 @@
     blocks = masses.shape[0] // BLOCK
     slots = pair_halo.shape[0] // devices
     domain = 4 * blocks
-    half = 8 * domain + 16
     place = jnp.stack([lax.axis_index(axis) for axis in AXES]).astype(jnp.int32)
     row = lambda a: a.reshape(-1, LANES)
     inputs = (positions, row(masses), row(pair_halo), row(pair_block), centers, radii[None])
+    inputs = [pltpu.with_memory_space_constraint(a, pltpu.HBM) for a in inputs]
     payload, state = call(
         pack,
         [f32(domain + 2 * row(pair_halo).shape[0], LANES), f32(4, halos)],
@@ -240,36 +256,40 @@
         scratch=[pltpu.VMEM(a.shape, a.dtype) for a in inputs] + [pltpu.SemaphoreType.DMA((len(inputs),))],
         near=False,
     )
+    other = step(state, "core", 1)
     along_z = [payload] + [step(payload, "z", k) for k in range(1, 4)]
     to_y = call(functools.partial(merge_z, slots, domain), [f32(4 * domain + 8, LANES)] * 4, place, *along_z)
     along_y = [step(to_y[k], "y", k) if k else to_y[k] for k in range(4)]
-    low, high, both = call(merge_y, [f32(rows, LANES) for rows in (half, half, 2 * half)], *along_y)
+    low, high = call(merge_y, [f32(8 * domain + 16, LANES)] * 2, *along_y)
     below_low, above_high = step(low, "x", 1), step(high, "x", -1)
     below_high, above_low = step(high, "x", 1), step(low, "x", -1)
     far_low, far_high = step(below_low, "x", 1), step(above_high, "x", -1)
-    slabs = [(both,), (below_low, below_high), (far_low, far_high), (above_low, above_high)]
+    slabs = [(low, high), (below_low, below_high), (above_low, above_high), (far_low, far_high)]
     each = devices * slots // LANES // len(slabs)
     held = [pltpu.VMEM((each, 8, LANES), jnp.float32), pltpu.VMEM((each, ROWS, LANES), jnp.float32)]
     outs = [
         jax.ShapeDtypeStruct((halos, each * LANES), jnp.bfloat16),
         jax.ShapeDtypeStruct((each * LANES, halos), jnp.bfloat16),
         f32(each, 4, BLOCK, LANES),
-        f32(ROWS, halos),
+        f32(2 * ROWS, halos),
     ]
-    got = {}
-    for i in (0, 1, 3, 2):
-        slab = slabs[i]
-        if i == 2:
-            slab = lax.optimization_barrier((*slab, *[got[k][3] for k in got]))[: len(slab)]
-        others = [step(part, "core", 1) for part in slab]
-        got[i] = call(functools.partial(first_pass, slots, blocks), outs, place, state, *slab, *others, scratch=held)
-    centers, radii, profile = call(
-        functools.partial(finish, len(slabs)),
-        [f32(3, halos), f32(1, halos), f32(SHELLS, halos)],
+    kept, sums = [], []
+    for slab in slabs:
+        *arrays, total = call(functools.partial(first_pass, slots, blocks), outs, place, state, other, *sums, *slab, scratch=held)
+        kept.extend(arrays)
+        sums = [total]
+    state, own, partner = call(
+        second_pass,
+        [f32(4, halos), f32(ROWS, halos), f32(ROWS, halos)],
         state,
-        *[array for i in got for array in got[i]],
-        scratch=[pltpu.VMEM((len(slabs), ROWS, halos), jnp.float32), *held],
+        other,
+        sums[0],
+        step(sums[0], "core", 1),
+        *kept,
+        scratch=held,
     )
+    outs = [f32(3, halos), f32(1, halos), f32(SHELLS, halos)]
+    centers, radii, profile = call(finish, outs, state, own, step(partner, "core", 1))
     return (centers, radii[0], profile)
 
 

time: 64.6 us -> 58.8 us (0.910)
  local copies, waits for them, and re-layouts: 4.24 us -> 0 us
  waiting for transfers between devices: 14.6 us -> 11.8 us
  Pallas kernels: 17 us -> 19.2 us
  starting transfers between devices: 27.5 us -> 26.8 us
    unnamed x12 -> x0, local copies, waits for them, and re-layouts: 4.24 us -> none
    ppermute x19 -> x15, waiting for transfers between devices: 14.6 us -> 11.8 us  [step(): lax.ppermute(value, axis, [(i, (i + by) % size) for i in range(size)])]
    pallas_call x8 -> x9, Pallas kernels: 17 us -> 19.2 us  [call(): pl.pallas_call(fn, in_specs=specs, out_specs=out_specs, out_shape=outs, s...]
    ppermute x19 -> x15, starting transfers between devices: 27.5 us -> 26.8 us  [step(): lax.ppermute(value, axis, [(i, (i + by) % size) for i in range(size)])]
  transfers between devices with their start and end apart: 19 -> 15, of which waited for: 11 -> 10; matrix products, arithmetic and copies ran while one was open for 0% -> 0% of each run, Pallas kernels for 12% -> 15%
where the time goes in v7:
time: 58.8 us; the launch traced here: 58.6 us
  starting transfers between devices  26.8 us (46%)
  Pallas kernels  19.2 us (33%)
  waiting for transfers between devices  11.8 us (20%)
  between operations  0.73 us (1%)
    ppermute x15, starting transfers between devices, step(): lax.ppermute(value, axis, [(i, (i + by) % size) for i in range(size)])  26.8 us
    pallas_call x9, Pallas kernels, call(): pl.pallas_call(fn, in_specs=specs, out_specs=out_specs, out_shape=outs, s...  19.2 us
    ppermute x15, waiting for transfers between devices, step(): lax.ppermute(value, axis, [(i, (i + by) % size) for i in range(size)])  11.8 us
  transfers between devices with their start and end apart: 15, of which 10 were waited for; matrix products, arithmetic and copies ran while one was open for 0% of the time, Pallas kernels for 15%

profile of v7, /device:TPU:1, one launch (start us, length us, event | category | flops | bytes accessed | tf_op | source)
XLA Modules:
  0.0 58.6 jit_solution(18339567238964134499)
XLA Ops:
  0.6 0.9 %shard_map.85 = (f32[96,128]{1,0:T(8,128)S(1)}, f32[4,1024]{1,0:T(4,128)S(1)}) custom-call(f32[3,2048]{1,0:T(4,128)} %positions.1, f32[16,128]{1,0:T(8,128)} %bitcast.9, s32[16,128]{1,0:T(8,128)} %bitcast.10, s32[16,128]{1,0:T(8,128)} %bitcast.11, f32[3,1024]{1,0:T(4,128)} %centers.1, f32[1,1024]{1,0:T(1,128)} %bitcast.12), custom_call_target="tpu_custom_call" | custom-call | tf_op jit(solution)/shard_map/pallas_call | solution.py:237
  1.5 4.7 %collective-permute-start.3 = (f32[96,128]{1,0:T(8,128)S(1)}, f32[96,128]{1,0:T(8,128)S(1)}, u32[]{:S(2)}, u32[]{:S(2)}) collective-permute-start(f32[96,128]{1,0:T(8,128)S(1)} %get-tuple-element.34.refs_0_), channel_id=1, source_target_pairs={{0,3},{1,0},{2,1},{3,2},{4,7},{5,4},{6,5},{7,6},{8,11},{9,8},{10,9... | collective-permute-start | bytes 147464 | tf_op jit(solution)/shard_map/ppermute | solution.py:230
  6.2 0.0 collective-permute-start.2
  6.2 0.7 %collective-permute-start.1 = (f32[96,128]{1,0:T(8,128)S(1)}, f32[96,128]{1,0:T(8,128)S(1)}, u32[]{:S(2)}, u32[]{:S(2)}) collective-permute-start(f32[96,128]{1,0:T(8,128)S(1)} %get-tuple-element.34.refs_0_), channel_id=1, source_target_pairs={{0,1},{1,2},{2,3},{3,0},{4,5},{5,6},{6,7},{7,4},{8,9},{9,10},{10,1... | collective-permute-start | bytes 147464 | tf_op jit(solution)/shard_map/ppermute | solution.py:230
  6.9 0.1 pad_add_fusion.place
  6.9 0.4 collective-permute-done.3.refs_3_
  7.3 3.4 %collective-permute-done.2.refs_2_ = f32[96,128]{1,0:T(8,128)S(1)} collective-permute-done((f32[96,128]{1,0:T(8,128)S(1)}, f32[96,128]{1,0:T(8,128)S(1)}, u32[]{:S(2)}, u32[]{:S(2)}) %collective-permute-start.2) | collective-permute-done | bytes 49184 | tf_op jit(solution)/shard_map/ppermute | solution.py:230
  10.7 0.1 collective-permute-done.1.refs_1_
  10.8 0.9 %shard_map.86 = (f32[264,128]{1,0:T(8,128)S(1)}, f32[264,128]{1,0:T(8,128)S(1)}, f32[264,128]{1,0:T(8,128)S(1)}, f32[264,128]{1,0:T(8,128)S(1)}) custom-call(s32[4]{0:T(128)S(1)} %pad_add_fusion.place, f32[96,128]{1,0:T(8,128)S(1)} %get-tuple-element.34.refs_0_, f32[96,128]{1,0:T(8,128)S(1)} %collective-permute-done.1.refs_1_, ...), custom_call_target="tpu_custom_call" | custom-call | tf_op jit(solution)/shard_map/pallas_call | solution.py:237
  11.7 1.4 %collective-permute-start.4 = (f32[264,128]{1,0:T(8,128)S(1)}, f32[264,128]{1,0:T(8,128)S(1)}, u32[]{:S(2)}, u32[]{:S(2)}) collective-permute-start(f32[264,128]{1,0:T(8,128)S(1)} %get-tuple-element.36), channel_id=1, source_target_pairs={{0,4},{4,8},{8,12},{12,0},{1,5},{5,9},{9,13},{13,1},{2,6},{6,10},{... | collective-permute-start | bytes 405512 | tf_op jit(solution)/shard_map/ppermute | solution.py:230
  13.1 2.6 %collective-permute-start.5 = (f32[264,128]{1,0:T(8,128)S(1)}, f32[264,128]{1,0:T(8,128)S(1)}, u32[]{:S(2)}, u32[]{:S(2)}) collective-permute-start(f32[264,128]{1,0:T(8,128)S(1)} %get-tuple-element.37), channel_id=1, source_target_pairs={{0,8},{4,12},{8,0},{12,4},{1,9},{5,13},{9,1},{13,5},{2,10},{6,14},... | collective-permute-start | bytes 405512 | tf_op jit(solution)/shard_map/ppermute | solution.py:230
  15.7 1.1 %collective-permute-start.6 = (f32[264,128]{1,0:T(8,128)S(1)}, f32[264,128]{1,0:T(8,128)S(1)}, u32[]{:S(2)}, u32[]{:S(2)}) collective-permute-start(f32[264,128]{1,0:T(8,128)S(1)} %get-tuple-element.38), channel_id=1, source_target_pairs={{0,12},{4,0},{8,4},{12,8},{1,13},{5,1},{9,5},{13,9},{2,14},{6,2},{... | collective-permute-start | bytes 405512 | tf_op jit(solution)/shard_map/ppermute | solution.py:230
  16.8 0.1 collective-permute-done.4.refs_1_
  16.9 3.0 %collective-permute-done.5.refs_2_ = f32[264,128]{1,0:T(8,128)S(1)} collective-permute-done((f32[264,128]{1,0:T(8,128)S(1)}, f32[264,128]{1,0:T(8,128)S(1)}, u32[]{:S(2)}, u32[]{:S(2)}) %collective-permute-start.5) | collective-permute-done | bytes 135200 | tf_op jit(solution)/shard_map/ppermute | solution.py:230
  19.9 0.7 %collective-permute-done.6.refs_3_ = f32[264,128]{1,0:T(8,128)S(1)} collective-permute-done((f32[264,128]{1,0:T(8,128)S(1)}, f32[264,128]{1,0:T(8,128)S(1)}, u32[]{:S(2)}, u32[]{:S(2)}) %collective-permute-start.6) | collective-permute-done | bytes 135200 | tf_op jit(solution)/shard_map/ppermute | solution.py:230
  20.7 1.3 %collective-permute-start.7 = (f32[528,128]{1,0:T(8,128)S(1)}, f32[528,128]{1,0:T(8,128)S(1)}, u32[]{:S(2)}, u32[]{:S(2)}) collective-permute-start(f32[528,128]{1,0:T(8,128)S(1)} %get-tuple-element.39.refs_2_), channel_id=1, source_target_pairs={{0,32},{32,64},{64,96},{96,0},{1,33},{33,65},{65,97},{97,1},{2,34}... | collective-permute-start | bytes 811016 | tf_op jit(solution)/shard_map/ppermute | solution.py:230
  22.0 1.5 %collective-permute-start.10 = (f32[528,128]{1,0:T(8,128)S(1)}, f32[528,128]{1,0:T(8,128)S(1)}, u32[]{:S(2)}, u32[]{:S(2)}) collective-permute-start(f32[528,128]{1,0:T(8,128)S(1)} %get-tuple-element.40.refs_3_), channel_id=1, source_target_pairs={{0,96},{32,0},{64,32},{96,64},{1,97},{33,1},{65,33},{97,65},{2,98}... | collective-permute-start | bytes 811016 | tf_op jit(solution)/shard_map/ppermute | solution.py:230
  23.4 0.0 collective-permute-start.8
  23.5 2.7 %collective-permute-start.9 = (f32[528,128]{1,0:T(8,128)S(1)}, f32[528,128]{1,0:T(8,128)S(1)}, u32[]{:S(2)}, u32[]{:S(2)}) collective-permute-start(f32[528,128]{1,0:T(8,128)S(1)} %get-tuple-element.39.refs_2_), channel_id=1, source_target_pairs={{0,96},{32,0},{64,32},{96,64},{1,97},{33,1},{65,33},{97,65},{2,98}... | collective-permute-start | bytes 811016 | tf_op jit(solution)/shard_map/ppermute | solution.py:230
  26.1 1.2 %collective-permute-done.7.refs_3_ = f32[528,128]{1,0:T(8,128)S(1)} collective-permute-done((f32[528,128]{1,0:T(8,128)S(1)}, f32[528,128]{1,0:T(8,128)S(1)}, u32[]{:S(2)}, u32[]{:S(2)}) %collective-permute-start.7) | collective-permute-done | bytes 270368 | tf_op jit(solution)/shard_map/ppermute | solution.py:230
  27.3 0.0 collective-permute-start.11
  27.3 0.0 collective-permute-done.10.refs_4_
  27.3 2.7 %collective-permute-start.12 = (f32[528,128]{1,0:T(8,128)S(1)}, f32[528,128]{1,0:T(8,128)S(1)}, u32[]{:S(2)}, u32[]{:S(2)}) collective-permute-start(f32[528,128]{1,0:T(8,128)S(1)} %collective-permute-done.10.refs_4_), channel_id=1, source_target_pairs={{0,96},{32,0},{64,32},{96,64},{1,97},{33,1},{65,33},{97,65},{2,98}... | collective-permute-start | bytes 811016 | tf_op jit(solution)/shard_map/ppermute | solution.py:230
  30.0 7.4 %collective-permute-start = (f32[4,1024]{1,0:T(4,128)S(1)}, f32[4,1024]{1,0:T(4,128)S(1)}, u32[]{:S(2)}, u32[]{:S(2)}) collective-permute-start(f32[4,1024]{1,0:T(4,128)S(1)} %get-tuple-element.33.refs_0_.mine), channel_id=1, source_target_pairs={{0,16},{16,0},{1,17},{17,1},{2,18},{18,2},{3,19},{19,3},{4,20},{20... | collective-permute-start | bytes 49160 | tf_op jit(solution)/shard_map/ppermute | solution.py:230
  37.4 0.8 %collective-permute-done.refs_1_.other = f32[4,1024]{1,0:T(4,128)S(1)} collective-permute-done((f32[4,1024]{1,0:T(4,128)S(1)}, f32[4,1024]{1,0:T(4,128)S(1)}, u32[]{:S(2)}, u32[]{:S(2)}) %collective-permute-start) | collective-permute-done | bytes 16416 | tf_op jit(solution)/shard_map/ppermute | solution.py:230
  38.2 2.9 %shard_map.88 = (bf16[1024,512]{1,0:T(8,128)(2,1)S(1)}, bf16[512,1024]{1,0:T(8,128)(2,1)S(1)}, f32[4,4,128,128]{3,2,1,0:T(8,128)S(1)}, f32[48,1024]{1,0:T(8,128)S(1)}) custom-call(s32[4]{0:T(128)S(1)} %pad_add_fusion.place, f32[4,1024]{1,0:T(4,128)S(1)} %get-tuple-element.33.refs_0_.mine, f32[4,1024]{1,0:T(4,128)S(1)} %collective-permute-done.refs_1_.other, ...), custom_call_target="tpu_custom_call" | custom-call | tf_op jit(solution)/shard_map/pallas_call | solution.py:237
  41.1 0.0 collective-permute-done.8.refs_4_
  41.1 2.9 %shard_map.89 = (bf16[1024,512]{1,0:T(8,128)(2,1)S(1)}, bf16[512,1024]{1,0:T(8,128)(2,1)S(1)}, f32[4,4,128,128]{3,2,1,0:T(8,128)S(1)}, f32[48,1024]{1,0:T(8,128)S(1)}) custom-call(s32[4]{0:T(128)S(1)} %pad_add_fusion.place, f32[4,1024]{1,0:T(4,128)S(1)} %get-tuple-element.33.refs_0_.mine, f32[4,1024]{1,0:T(4,128)S(1)} %collective-permute-done.refs_1_.other, ...), custom_call_target="tpu_custom_call" | custom-call | tf_op jit(solution)/shard_map/pallas_call | solution.py:237
  44.0 0.0 collective-permute-done.9.refs_3_
  44.1 2.9 %shard_map.90 = (bf16[1024,512]{1,0:T(8,128)(2,1)S(1)}, bf16[512,1024]{1,0:T(8,128)(2,1)S(1)}, f32[4,4,128,128]{3,2,1,0:T(8,128)S(1)}, f32[48,1024]{1,0:T(8,128)S(1)}) custom-call(s32[4]{0:T(128)S(1)} %pad_add_fusion.place, f32[4,1024]{1,0:T(4,128)S(1)} %get-tuple-element.33.refs_0_.mine, f32[4,1024]{1,0:T(4,128)S(1)} %collective-permute-done.refs_1_.other, ...), custom_call_target="tpu_custom_call" | custom-call | tf_op jit(solution)/shard_map/pallas_call | solution.py:237
  47.0 0.0 collective-permute-done.11.refs_3_
  47.0 0.0 collective-permute-done.12.refs_4_
  47.0 2.9 %shard_map.91 = (bf16[1024,512]{1,0:T(8,128)(2,1)S(1)}, bf16[512,1024]{1,0:T(8,128)(2,1)S(1)}, f32[4,4,128,128]{3,2,1,0:T(8,128)S(1)}, f32[48,1024]{1,0:T(8,128)S(1)}) custom-call(s32[4]{0:T(128)S(1)} %pad_add_fusion.place, f32[4,1024]{1,0:T(4,128)S(1)} %get-tuple-element.33.refs_0_.mine, f32[4,1024]{1,0:T(4,128)S(1)} %collective-permute-done.refs_1_.other, ...), custom_call_target="tpu_custom_call" | custom-call | tf_op jit(solution)/shard_map/pallas_call | solution.py:237
  49.9 0.4 collective-permute-start.13
  50.3 1.1 %collective-permute-done.13.received = f32[48,1024]{1,0:T(8,128)S(1)} collective-permute-done((f32[48,1024]{1,0:T(8,128)S(1)}, f32[48,1024]{1,0:T(8,128)S(1)}, u32[]{:S(2)}, u32[]{:S(2)}) %collective-permute-start.13) | collective-permute-done | bytes 196640 | tf_op jit(solution)/shard_map/ppermute | solution.py:230
  51.4 5.1 %shard_map.92 = (f32[4,1024]{1,0:T(4,128)S(1)}, f32[24,1024]{1,0:T(8,128)S(1)}, f32[24,1024]{1,0:T(8,128)S(1)}) custom-call(f32[4,1024]{1,0:T(4,128)S(1)} %get-tuple-element.33.refs_0_.mine, f32[4,1024]{1,0:T(4,128)S(1)} %collective-permute-done.refs_1_.other, f32[48,1024]{1,0:T(8,128)S(1)} %get-tuple-element.44.sums, ...), custom_call_target="tpu_custom_call" | custom-call | tf_op jit(solution)/shard_map/pallas_call | solution.py:237
  56.5 0.4 collective-permute-start.14
  56.9 1.0 %collective-permute-done.14.received = f32[24,1024]{1,0:T(8,128)S(1)} collective-permute-done((f32[24,1024]{1,0:T(8,128)S(1)}, f32[24,1024]{1,0:T(8,128)S(1)}, u32[]{:S(2)}, u32[]{:S(2)}) %collective-permute-start.14) | collective-permute-done | bytes 98336 | tf_op jit(solution)/shard_map/ppermute | solution.py:230
  57.9 0.7 %shard_map.93 = (f32[3,1024]{1,0:T(4,128)}, f32[1,1024]{1,0:T(1,128)}, f32[16,1024]{1,0:T(8,128)}) custom-call(f32[4,1024]{1,0:T(4,128)S(1)} %get-tuple-element.57.state, f32[24,1024]{1,0:T(8,128)S(1)} %get-tuple-element.58.own, f32[24,1024]{1,0:T(8,128)S(1)} %collective-permute-done.14.received), custom_call_target="tpu_custom_call" | custom-call | tf_op jit(solution)/shard_map/pallas_call | solution.py:237
  (1 shorter events, 0.0 us)
Async XLA Ops:
  1.5 5.8 %collective-permute-start.3 = (f32[96,128]{1,0:T(8,128)S(1)}, f32[96,128]{1,0:T(8,128)S(1)}, u32[]{:S(2)}, u32[]{:S(2)}) collective-permute-start(f32[96,128]{1,0:T(8,128)S(1)} %get-tuple-element.34.refs_0_), channel_id=1, source_target_pairs={{0,3},{1,0},{2,1},{3,2},{4,7},{5,4},{6,5},{7,6},{8,11},{9,8},{10,9... | collective-permute-start | bytes 147464 | tf_op jit(solution)/shard_map/ppermute | solution.py:230
  6.2 4.5 %collective-permute-start.2 = (f32[96,128]{1,0:T(8,128)S(1)}, f32[96,128]{1,0:T(8,128)S(1)}, u32[]{:S(2)}, u32[]{:S(2)}) collective-permute-start(f32[96,128]{1,0:T(8,128)S(1)} %get-tuple-element.34.refs_0_), channel_id=1, source_target_pairs={{0,2},{1,3},{2,0},{3,1},{4,6},{5,7},{6,4},{7,5},{8,10},{9,11},{10,... | collective-permute-start | bytes 147464 | tf_op jit(solution)/shard_map/ppermute | solution.py:230
  6.2 4.7 %collective-permute-start.1 = (f32[96,128]{1,0:T(8,128)S(1)}, f32[96,128]{1,0:T(8,128)S(1)}, u32[]{:S(2)}, u32[]{:S(2)}) collective-permute-start(f32[96,128]{1,0:T(8,128)S(1)} %get-tuple-element.34.refs_0_), channel_id=1, source_target_pairs={{0,1},{1,2},{2,3},{3,0},{4,5},{5,6},{6,7},{7,4},{8,9},{9,10},{10,1... | collective-permute-start | bytes 147464 | tf_op jit(solution)/shard_map/ppermute | solution.py:230
  11.7 5.2 %collective-permute-start.4 = (f32[264,128]{1,0:T(8,128)S(1)}, f32[264,128]{1,0:T(8,128)S(1)}, u32[]{:S(2)}, u32[]{:S(2)}) collective-permute-start(f32[264,128]{1,0:T(8,128)S(1)} %get-tuple-element.36), channel_id=1, source_target_pairs={{0,4},{4,8},{8,12},{12,0},{1,5},{5,9},{9,13},{13,1},{2,6},{6,10},{... | collective-permute-start | bytes 405512 | tf_op jit(solution)/shard_map/ppermute | solution.py:230
  13.1 6.8 %collective-permute-start.5 = (f32[264,128]{1,0:T(8,128)S(1)}, f32[264,128]{1,0:T(8,128)S(1)}, u32[]{:S(2)}, u32[]{:S(2)}) collective-permute-start(f32[264,128]{1,0:T(8,128)S(1)} %get-tuple-element.37), channel_id=1, source_target_pairs={{0,8},{4,12},{8,0},{12,4},{1,9},{5,13},{9,1},{13,5},{2,10},{6,14},... | collective-permute-start | bytes 405512 | tf_op jit(solution)/shard_map/ppermute | solution.py:230
  15.7 4.9 %collective-permute-start.6 = (f32[264,128]{1,0:T(8,128)S(1)}, f32[264,128]{1,0:T(8,128)S(1)}, u32[]{:S(2)}, u32[]{:S(2)}) collective-permute-start(f32[264,128]{1,0:T(8,128)S(1)} %get-tuple-element.38), channel_id=1, source_target_pairs={{0,12},{4,0},{8,4},{12,8},{1,13},{5,1},{9,5},{13,9},{2,14},{6,2},{... | collective-permute-start | bytes 405512 | tf_op jit(solution)/shard_map/ppermute | solution.py:230
  20.7 6.6 %collective-permute-start.7 = (f32[528,128]{1,0:T(8,128)S(1)}, f32[528,128]{1,0:T(8,128)S(1)}, u32[]{:S(2)}, u32[]{:S(2)}) collective-permute-start(f32[528,128]{1,0:T(8,128)S(1)} %get-tuple-element.39.refs_2_), channel_id=1, source_target_pairs={{0,32},{32,64},{64,96},{96,0},{1,33},{33,65},{65,97},{97,1},{2,34}... | collective-permute-start | bytes 811016 | tf_op jit(solution)/shard_map/ppermute | solution.py:230
  22.0 5.3 %collective-permute-start.10 = (f32[528,128]{1,0:T(8,128)S(1)}, f32[528,128]{1,0:T(8,128)S(1)}, u32[]{:S(2)}, u32[]{:S(2)}) collective-permute-start(f32[528,128]{1,0:T(8,128)S(1)} %get-tuple-element.40.refs_3_), channel_id=1, source_target_pairs={{0,96},{32,0},{64,32},{96,64},{1,97},{33,1},{65,33},{97,65},{2,98}... | collective-permute-start | bytes 811016 | tf_op jit(solution)/shard_map/ppermute | solution.py:230
  23.4 17.7 %collective-permute-start.8 = (f32[528,128]{1,0:T(8,128)S(1)}, f32[528,128]{1,0:T(8,128)S(1)}, u32[]{:S(2)}, u32[]{:S(2)}) collective-permute-start(f32[528,128]{1,0:T(8,128)S(1)} %get-tuple-element.40.refs_3_), channel_id=1, source_target_pairs={{0,32},{32,64},{64,96},{96,0},{1,33},{33,65},{65,97},{97,1},{2,34}... | collective-permute-start | bytes 811016 | tf_op jit(solution)/shard_map/ppermute | solution.py:230
  23.5 20.6 %collective-permute-start.9 = (f32[528,128]{1,0:T(8,128)S(1)}, f32[528,128]{1,0:T(8,128)S(1)}, u32[]{:S(2)}, u32[]{:S(2)}) collective-permute-start(f32[528,128]{1,0:T(8,128)S(1)} %get-tuple-element.39.refs_2_), channel_id=1, source_target_pairs={{0,96},{32,0},{64,32},{96,64},{1,97},{33,1},{65,33},{97,65},{2,98}... | collective-permute-start | bytes 811016 | tf_op jit(solution)/shard_map/ppermute | solution.py:230
  27.3 19.7 %collective-permute-start.11 = (f32[528,128]{1,0:T(8,128)S(1)}, f32[528,128]{1,0:T(8,128)S(1)}, u32[]{:S(2)}, u32[]{:S(2)}) collective-permute-start(f32[528,128]{1,0:T(8,128)S(1)} %collective-permute-done.7.refs_3_), channel_id=1, source_target_pairs={{0,32},{32,64},{64,96},{96,0},{1,33},{33,65},{65,97},{97,1},{2,34}... | collective-permute-start | bytes 811016 | tf_op jit(solution)/shard_map/ppermute | solution.py:230
  27.3 19.7 %collective-permute-start.12 = (f32[528,128]{1,0:T(8,128)S(1)}, f32[528,128]{1,0:T(8,128)S(1)}, u32[]{:S(2)}, u32[]{:S(2)}) collective-permute-start(f32[528,128]{1,0:T(8,128)S(1)} %collective-permute-done.10.refs_4_), channel_id=1, source_target_pairs={{0,96},{32,0},{64,32},{96,64},{1,97},{33,1},{65,33},{97,65},{2,98}... | collective-permute-start | bytes 811016 | tf_op jit(solution)/shard_map/ppermute | solution.py:230
  30.0 8.3 %collective-permute-start = (f32[4,1024]{1,0:T(4,128)S(1)}, f32[4,1024]{1,0:T(4,128)S(1)}, u32[]{:S(2)}, u32[]{:S(2)}) collective-permute-start(f32[4,1024]{1,0:T(4,128)S(1)} %get-tuple-element.33.refs_0_.mine), channel_id=1, source_target_pairs={{0,16},{16,0},{1,17},{17,1},{2,18},{18,2},{3,19},{19,3},{4,20},{20... | collective-permute-start | bytes 49160 | tf_op jit(solution)/shard_map/ppermute | solution.py:230
  49.9 1.5 %collective-permute-start.13 = (f32[48,1024]{1,0:T(8,128)S(1)}, f32[48,1024]{1,0:T(8,128)S(1)}, u32[]{:S(2)}, u32[]{:S(2)}) collective-permute-start(f32[48,1024]{1,0:T(8,128)S(1)} %get-tuple-element.44.sums), channel_id=1, source_target_pairs={{0,16},{16,0},{1,17},{17,1},{2,18},{18,2},{3,19},{19,3},{4,20},{20... | collective-permute-start | bytes 589832 | tf_op jit(solution)/shard_map/ppermute | solution.py:230
  56.5 1.4 %collective-permute-start.14 = (f32[24,1024]{1,0:T(8,128)S(1)}, f32[24,1024]{1,0:T(8,128)S(1)}, u32[]{:S(2)}, u32[]{:S(2)}) collective-permute-start(f32[24,1024]{1,0:T(8,128)S(1)} %get-tuple-element.59), channel_id=1, source_target_pairs={{0,16},{16,0},{1,17},{17,1},{2,18},{18,2},{3,19},{19,3},{4,20},{20... | collective-permute-start | bytes 294920 | tf_op jit(solution)/shard_map/ppermute | solution.py:230

commit v8 on v7

--- a/solution.py
+++ b/solution.py
@@ -258,6 +258,7 @@
     )
     other = step(state, "core", 1)
     along_z = [payload] + [step(payload, "z", k) for k in range(1, 4)]
+    *along_z, other = lax.optimization_barrier((*along_z, other))
     to_y = call(functools.partial(merge_z, slots, domain), [f32(4 * domain + 8, LANES)] * 4, place, *along_z)
     along_y = [step(to_y[k], "y", k) if k else to_y[k] for k in range(4)]
     low, high = call(merge_y, [f32(8 * domain + 16, LANES)] * 2, *along_y)

time: 58.8 us -> 57.6 us (0.980)
  waiting for transfers between devices: 11.8 us -> 9.57 us
  starting transfers between devices: 26.8 us -> 27.8 us
    ppermute x15, waiting for transfers between devices: 11.8 us -> 9.57 us  [step(): lax.ppermute(value, axis, [(i, (i + by) % size) for i in range(size)])]
    ppermute x15, starting transfers between devices: 26.8 us -> 27.8 us  [step(): lax.ppermute(value, axis, [(i, (i + by) % size) for i in range(size)])]
where the time goes in v8:
time: 57.6 us; the launch traced here: 57.4 us
  starting transfers between devices  27.8 us (48%)
  Pallas kernels  19.2 us (33%)
  waiting for transfers between devices  9.57 us (17%)
  between operations  0.73 us (1%)
    ppermute x15, starting transfers between devices, step(): lax.ppermute(value, axis, [(i, (i + by) % size) for i in range(size)])  27.8 us
    pallas_call x9, Pallas kernels, call(): pl.pallas_call(fn, in_specs=specs, out_specs=out_specs, out_shape=outs, s...  19.2 us
    ppermute x15, waiting for transfers between devices, step(): lax.ppermute(value, axis, [(i, (i + by) % size) for i in range(size)])  9.57 us
  transfers between devices with their start and end apart: 15, of which 10 were waited for; matrix products, arithmetic and copies ran while one was open for 0% of the time, Pallas kernels for 15%

profile of v8, /device:TPU:1, one launch (start us, length us, event | category | flops | bytes accessed | tf_op | source)
XLA Modules:
  0.0 57.4 jit_solution(7793224980035677617)
XLA Ops:
  0.6 0.9 %shard_map.85 = (f32[96,128]{1,0:T(8,128)S(1)}, f32[4,1024]{1,0:T(4,128)S(1)}) custom-call(f32[3,2048]{1,0:T(4,128)} %positions.1, f32[16,128]{1,0:T(8,128)} %bitcast.9, s32[16,128]{1,0:T(8,128)} %bitcast.10, s32[16,128]{1,0:T(8,128)} %bitcast.11, f32[3,1024]{1,0:T(4,128)} %centers.1, f32[1,1024]{1,0:T(1,128)} %bitcast.12), custom_call_target="tpu_custom_call" | custom-call | tf_op jit(solution)/shard_map/pallas_call | solution.py:237
  1.5 4.7 %collective-permute-start.2 = (f32[96,128]{1,0:T(8,128)S(1)}, f32[96,128]{1,0:T(8,128)S(1)}, u32[]{:S(2)}, u32[]{:S(2)}) collective-permute-start(f32[96,128]{1,0:T(8,128)S(1)} %get-tuple-element.41.refs_0_), channel_id=1, source_target_pairs={{0,3},{1,0},{2,1},{3,2},{4,7},{5,4},{6,5},{7,6},{8,11},{9,8},{10,9... | collective-permute-start | bytes 147464 | tf_op jit(solution)/shard_map/ppermute | solution.py:230
  6.2 0.0 collective-permute-start.1
  6.2 0.7 %collective-permute-start = (f32[96,128]{1,0:T(8,128)S(1)}, f32[96,128]{1,0:T(8,128)S(1)}, u32[]{:S(2)}, u32[]{:S(2)}) collective-permute-start(f32[96,128]{1,0:T(8,128)S(1)} %get-tuple-element.41.refs_0_), channel_id=1, source_target_pairs={{0,1},{1,2},{2,3},{3,0},{4,5},{5,6},{6,7},{7,4},{8,9},{9,10},{10,1... | collective-permute-start | bytes 147464 | tf_op jit(solution)/shard_map/ppermute | solution.py:230
  6.9 1.5 %collective-permute-start.3 = (f32[4,1024]{1,0:T(4,128)S(1)}, f32[4,1024]{1,0:T(4,128)S(1)}, u32[]{:S(2)}, u32[]{:S(2)}) collective-permute-start(f32[4,1024]{1,0:T(4,128)S(1)} %get-tuple-element.38.refs_0_.mine), channel_id=1, source_target_pairs={{0,16},{16,0},{1,17},{17,1},{2,18},{18,2},{3,19},{19,3},{4,20},{20... | collective-permute-start | bytes 49160 | tf_op jit(solution)/shard_map/ppermute | solution.py:230
  8.4 0.1 pad_add_fusion.place
  8.4 0.8 %collective-permute-done.3.refs_1_.other = f32[4,1024]{1,0:T(4,128)S(1)} collective-permute-done((f32[4,1024]{1,0:T(4,128)S(1)}, f32[4,1024]{1,0:T(4,128)S(1)}, u32[]{:S(2)}, u32[]{:S(2)}) %collective-permute-start.3) | collective-permute-done | bytes 16416 | tf_op jit(solution)/shard_map/ppermute | solution.py:230
  9.2 0.0 collective-permute-done.2.refs_3_
  9.2 1.5 %collective-permute-done.1.refs_2_ = f32[96,128]{1,0:T(8,128)S(1)} collective-permute-done((f32[96,128]{1,0:T(8,128)S(1)}, f32[96,128]{1,0:T(8,128)S(1)}, u32[]{:S(2)}, u32[]{:S(2)}) %collective-permute-start.1) | collective-permute-done | bytes 49184 | tf_op jit(solution)/shard_map/ppermute | solution.py:230
  10.7 0.1 collective-permute-done.refs_1_
  10.8 0.9 %shard_map.86 = (f32[264,128]{1,0:T(8,128)S(1)}, f32[264,128]{1,0:T(8,128)S(1)}, f32[264,128]{1,0:T(8,128)S(1)}, f32[264,128]{1,0:T(8,128)S(1)}) custom-call(s32[4]{0:T(128)S(1)} %pad_add_fusion.place, f32[96,128]{1,0:T(8,128)S(1)} %get-tuple-element.41.refs_0_, f32[96,128]{1,0:T(8,128)S(1)} %collective-permute-done.refs_1_, ...), custom_call_target="tpu_custom_call" | custom-call | tf_op jit(solution)/shard_map/pallas_call | solution.py:237
  11.7 1.4 %collective-permute-start.4 = (f32[264,128]{1,0:T(8,128)S(1)}, f32[264,128]{1,0:T(8,128)S(1)}, u32[]{:S(2)}, u32[]{:S(2)}) collective-permute-start(f32[264,128]{1,0:T(8,128)S(1)} %get-tuple-element.46), channel_id=1, source_target_pairs={{0,4},{4,8},{8,12},{12,0},{1,5},{5,9},{9,13},{13,1},{2,6},{6,10},{... | collective-permute-start | bytes 405512 | tf_op jit(solution)/shard_map/ppermute | solution.py:230
  13.1 2.6 %collective-permute-start.5 = (f32[264,128]{1,0:T(8,128)S(1)}, f32[264,128]{1,0:T(8,128)S(1)}, u32[]{:S(2)}, u32[]{:S(2)}) collective-permute-start(f32[264,128]{1,0:T(8,128)S(1)} %get-tuple-element.47), channel_id=1, source_target_pairs={{0,8},{4,12},{8,0},{12,4},{1,9},{5,13},{9,1},{13,5},{2,10},{6,14},... | collective-permute-start | bytes 405512 | tf_op jit(solution)/shard_map/ppermute | solution.py:230
  15.7 1.1 %collective-permute-start.6 = (f32[264,128]{1,0:T(8,128)S(1)}, f32[264,128]{1,0:T(8,128)S(1)}, u32[]{:S(2)}, u32[]{:S(2)}) collective-permute-start(f32[264,128]{1,0:T(8,128)S(1)} %get-tuple-element.48), channel_id=1, source_target_pairs={{0,12},{4,0},{8,4},{12,8},{1,13},{5,1},{9,5},{13,9},{2,14},{6,2},{... | collective-permute-start | bytes 405512 | tf_op jit(solution)/shard_map/ppermute | solution.py:230
  16.8 0.1 collective-permute-done.4.refs_1_
  16.9 3.0 %collective-permute-done.5.refs_2_ = f32[264,128]{1,0:T(8,128)S(1)} collective-permute-done((f32[264,128]{1,0:T(8,128)S(1)}, f32[264,128]{1,0:T(8,128)S(1)}, u32[]{:S(2)}, u32[]{:S(2)}) %collective-permute-start.5) | collective-permute-done | bytes 135200 | tf_op jit(solution)/shard_map/ppermute | solution.py:230
  19.9 0.7 %collective-permute-done.6.refs_3_ = f32[264,128]{1,0:T(8,128)S(1)} collective-permute-done((f32[264,128]{1,0:T(8,128)S(1)}, f32[264,128]{1,0:T(8,128)S(1)}, u32[]{:S(2)}, u32[]{:S(2)}) %collective-permute-start.6) | collective-permute-done | bytes 135200 | tf_op jit(solution)/shard_map/ppermute | solution.py:230
  20.7 1.3 %collective-permute-start.7 = (f32[528,128]{1,0:T(8,128)S(1)}, f32[528,128]{1,0:T(8,128)S(1)}, u32[]{:S(2)}, u32[]{:S(2)}) collective-permute-start(f32[528,128]{1,0:T(8,128)S(1)} %get-tuple-element.49.refs_2_), channel_id=1, source_target_pairs={{0,32},{32,64},{64,96},{96,0},{1,33},{33,65},{65,97},{97,1},{2,34}... | collective-permute-start | bytes 811016 | tf_op jit(solution)/shard_map/ppermute | solution.py:230
  22.0 1.5 %collective-permute-start.10 = (f32[528,128]{1,0:T(8,128)S(1)}, f32[528,128]{1,0:T(8,128)S(1)}, u32[]{:S(2)}, u32[]{:S(2)}) collective-permute-start(f32[528,128]{1,0:T(8,128)S(1)} %get-tuple-element.50.refs_3_), channel_id=1, source_target_pairs={{0,96},{32,0},{64,32},{96,64},{1,97},{33,1},{65,33},{97,65},{2,98}... | collective-permute-start | bytes 811016 | tf_op jit(solution)/shard_map/ppermute | solution.py:230
  23.4 0.0 collective-permute-start.8
  23.5 2.7 %collective-permute-start.9 = (f32[528,128]{1,0:T(8,128)S(1)}, f32[528,128]{1,0:T(8,128)S(1)}, u32[]{:S(2)}, u32[]{:S(2)}) collective-permute-start(f32[528,128]{1,0:T(8,128)S(1)} %get-tuple-element.49.refs_2_), channel_id=1, source_target_pairs={{0,96},{32,0},{64,32},{96,64},{1,97},{33,1},{65,33},{97,65},{2,98}... | collective-permute-start | bytes 811016 | tf_op jit(solution)/shard_map/ppermute | solution.py:230
  26.1 1.2 %collective-permute-done.7.refs_3_ = f32[528,128]{1,0:T(8,128)S(1)} collective-permute-done((f32[528,128]{1,0:T(8,128)S(1)}, f32[528,128]{1,0:T(8,128)S(1)}, u32[]{:S(2)}, u32[]{:S(2)}) %collective-permute-start.7) | collective-permute-done | bytes 270368 | tf_op jit(solution)/shard_map/ppermute | solution.py:230
  27.3 0.0 collective-permute-start.11
  27.3 0.0 collective-permute-done.10.refs_4_
  27.3 2.7 %collective-permute-start.12 = (f32[528,128]{1,0:T(8,128)S(1)}, f32[528,128]{1,0:T(8,128)S(1)}, u32[]{:S(2)}, u32[]{:S(2)}) collective-permute-start(f32[528,128]{1,0:T(8,128)S(1)} %collective-permute-done.10.refs_4_), channel_id=1, source_target_pairs={{0,96},{32,0},{64,32},{96,64},{1,97},{33,1},{65,33},{97,65},{2,98}... | collective-permute-start | bytes 811016 | tf_op jit(solution)/shard_map/ppermute | solution.py:230
  30.0 2.9 %shard_map.88 = (bf16[1024,512]{1,0:T(8,128)(2,1)S(1)}, bf16[512,1024]{1,0:T(8,128)(2,1)S(1)}, f32[4,4,128,128]{3,2,1,0:T(8,128)S(1)}, f32[48,1024]{1,0:T(8,128)S(1)}) custom-call(s32[4]{0:T(128)S(1)} %pad_add_fusion.place, f32[4,1024]{1,0:T(4,128)S(1)} %get-tuple-element.38.refs_0_.mine, f32[4,1024]{1,0:T(4,128)S(1)} %collective-permute-done.3.refs_1_.other, ...), custom_call_target="tpu_custom_call" | custom-call | tf_op jit(solution)/shard_map/pallas_call | solution.py:237
  32.9 0.1 collective-permute-done.8.refs_4_
  33.0 2.9 %shard_map.89 = (bf16[1024,512]{1,0:T(8,128)(2,1)S(1)}, bf16[512,1024]{1,0:T(8,128)(2,1)S(1)}, f32[4,4,128,128]{3,2,1,0:T(8,128)S(1)}, f32[48,1024]{1,0:T(8,128)S(1)}) custom-call(s32[4]{0:T(128)S(1)} %pad_add_fusion.place, f32[4,1024]{1,0:T(4,128)S(1)} %get-tuple-element.38.refs_0_.mine, f32[4,1024]{1,0:T(4,128)S(1)} %collective-permute-done.3.refs_1_.other, ...), custom_call_target="tpu_custom_call" | custom-call | tf_op jit(solution)/shard_map/pallas_call | solution.py:237
  35.9 0.0 collective-permute-done.9.refs_3_
  35.9 2.9 %shard_map.90 = (bf16[1024,512]{1,0:T(8,128)(2,1)S(1)}, bf16[512,1024]{1,0:T(8,128)(2,1)S(1)}, f32[4,4,128,128]{3,2,1,0:T(8,128)S(1)}, f32[48,1024]{1,0:T(8,128)S(1)}) custom-call(s32[4]{0:T(128)S(1)} %pad_add_fusion.place, f32[4,1024]{1,0:T(4,128)S(1)} %get-tuple-element.38.refs_0_.mine, f32[4,1024]{1,0:T(4,128)S(1)} %collective-permute-done.3.refs_1_.other, ...), custom_call_target="tpu_custom_call" | custom-call | tf_op jit(solution)/shard_map/pallas_call | solution.py:237
  38.8 0.0 collective-permute-done.11.refs_3_
  38.8 0.0 collective-permute-done.12.refs_4_
  38.8 2.9 %shard_map.91 = (bf16[1024,512]{1,0:T(8,128)(2,1)S(1)}, bf16[512,1024]{1,0:T(8,128)(2,1)S(1)}, f32[4,4,128,128]{3,2,1,0:T(8,128)S(1)}, f32[48,1024]{1,0:T(8,128)S(1)}) custom-call(s32[4]{0:T(128)S(1)} %pad_add_fusion.place, f32[4,1024]{1,0:T(4,128)S(1)} %get-tuple-element.38.refs_0_.mine, f32[4,1024]{1,0:T(4,128)S(1)} %collective-permute-done.3.refs_1_.other, ...), custom_call_target="tpu_custom_call" | custom-call | tf_op jit(solution)/shard_map/pallas_call | solution.py:237
  41.8 7.4 %collective-permute-start.13 = (f32[48,1024]{1,0:T(8,128)S(1)}, f32[48,1024]{1,0:T(8,128)S(1)}, u32[]{:S(2)}, u32[]{:S(2)}) collective-permute-start(f32[48,1024]{1,0:T(8,128)S(1)} %get-tuple-element.54.sums), channel_id=1, source_target_pairs={{0,16},{16,0},{1,17},{17,1},{2,18},{18,2},{3,19},{19,3},{4,20},{20... | collective-permute-start | bytes 589832 | tf_op jit(solution)/shard_map/ppermute | solution.py:230
  49.1 1.1 %collective-permute-done.13.received = f32[48,1024]{1,0:T(8,128)S(1)} collective-permute-done((f32[48,1024]{1,0:T(8,128)S(1)}, f32[48,1024]{1,0:T(8,128)S(1)}, u32[]{:S(2)}, u32[]{:S(2)}) %collective-permute-start.13) | collective-permute-done | bytes 196640 | tf_op jit(solution)/shard_map/ppermute | solution.py:230
  50.2 5.1 %shard_map.92 = (f32[4,1024]{1,0:T(4,128)S(1)}, f32[24,1024]{1,0:T(8,128)S(1)}, f32[24,1024]{1,0:T(8,128)S(1)}) custom-call(f32[4,1024]{1,0:T(4,128)S(1)} %get-tuple-element.38.refs_0_.mine, f32[4,1024]{1,0:T(4,128)S(1)} %collective-permute-done.3.refs_1_.other, f32[48,1024]{1,0:T(8,128)S(1)} %get-tuple-element.54.sums, ...), custom_call_target="tpu_custom_call" | custom-call | tf_op jit(solution)/shard_map/pallas_call | solution.py:237
  55.3 0.5 collective-permute-start.14
  55.8 0.9 %collective-permute-done.14.received = f32[24,1024]{1,0:T(8,128)S(1)} collective-permute-done((f32[24,1024]{1,0:T(8,128)S(1)}, f32[24,1024]{1,0:T(8,128)S(1)}, u32[]{:S(2)}, u32[]{:S(2)}) %collective-permute-start.14) | collective-permute-done | bytes 98336 | tf_op jit(solution)/shard_map/ppermute | solution.py:230
  56.7 0.7 %shard_map.93 = (f32[3,1024]{1,0:T(4,128)}, f32[1,1024]{1,0:T(1,128)}, f32[16,1024]{1,0:T(8,128)}) custom-call(f32[4,1024]{1,0:T(4,128)S(1)} %get-tuple-element.67.state, f32[24,1024]{1,0:T(8,128)S(1)} %get-tuple-element.68.own, f32[24,1024]{1,0:T(8,128)S(1)} %collective-permute-done.14.received), custom_call_target="tpu_custom_call" | custom-call | tf_op jit(solution)/shard_map/pallas_call | solution.py:237
  (1 shorter events, 0.0 us)
Async XLA Ops:
  1.5 7.7 %collective-permute-start.2 = (f32[96,128]{1,0:T(8,128)S(1)}, f32[96,128]{1,0:T(8,128)S(1)}, u32[]{:S(2)}, u32[]{:S(2)}) collective-permute-start(f32[96,128]{1,0:T(8,128)S(1)} %get-tuple-element.41.refs_0_), channel_id=1, source_target_pairs={{0,3},{1,0},{2,1},{3,2},{4,7},{5,4},{6,5},{7,6},{8,11},{9,8},{10,9... | collective-permute-start | bytes 147464 | tf_op jit(solution)/shard_map/ppermute | solution.py:230
  6.2 4.5 %collective-permute-start.1 = (f32[96,128]{1,0:T(8,128)S(1)}, f32[96,128]{1,0:T(8,128)S(1)}, u32[]{:S(2)}, u32[]{:S(2)}) collective-permute-start(f32[96,128]{1,0:T(8,128)S(1)} %get-tuple-element.41.refs_0_), channel_id=1, source_target_pairs={{0,2},{1,3},{2,0},{3,1},{4,6},{5,7},{6,4},{7,5},{8,10},{9,11},{10,... | collective-permute-start | bytes 147464 | tf_op jit(solution)/shard_map/ppermute | solution.py:230
  6.2 4.7 %collective-permute-start = (f32[96,128]{1,0:T(8,128)S(1)}, f32[96,128]{1,0:T(8,128)S(1)}, u32[]{:S(2)}, u32[]{:S(2)}) collective-permute-start(f32[96,128]{1,0:T(8,128)S(1)} %get-tuple-element.41.refs_0_), channel_id=1, source_target_pairs={{0,1},{1,2},{2,3},{3,0},{4,5},{5,6},{6,7},{7,4},{8,9},{9,10},{10,1... | collective-permute-start | bytes 147464 | tf_op jit(solution)/shard_map/ppermute | solution.py:230
  6.9 2.4 %collective-permute-start.3 = (f32[4,1024]{1,0:T(4,128)S(1)}, f32[4,1024]{1,0:T(4,128)S(1)}, u32[]{:S(2)}, u32[]{:S(2)}) collective-permute-start(f32[4,1024]{1,0:T(4,128)S(1)} %get-tuple-element.38.refs_0_.mine), channel_id=1, source_target_pairs={{0,16},{16,0},{1,17},{17,1},{2,18},{18,2},{3,19},{19,3},{4,20},{20... | collective-permute-start | bytes 49160 | tf_op jit(solution)/shard_map/ppermute | solution.py:230
  11.7 5.2 %collective-permute-start.4 = (f32[264,128]{1,0:T(8,128)S(1)}, f32[264,128]{1,0:T(8,128)S(1)}, u32[]{:S(2)}, u32[]{:S(2)}) collective-permute-start(f32[264,128]{1,0:T(8,128)S(1)} %get-tuple-element.46), channel_id=1, source_target_pairs={{0,4},{4,8},{8,12},{12,0},{1,5},{5,9},{9,13},{13,1},{2,6},{6,10},{... | collective-permute-start | bytes 405512 | tf_op jit(solution)/shard_map/ppermute | solution.py:230
  13.1 6.8 %collective-permute-start.5 = (f32[264,128]{1,0:T(8,128)S(1)}, f32[264,128]{1,0:T(8,128)S(1)}, u32[]{:S(2)}, u32[]{:S(2)}) collective-permute-start(f32[264,128]{1,0:T(8,128)S(1)} %get-tuple-element.47), channel_id=1, source_target_pairs={{0,8},{4,12},{8,0},{12,4},{1,9},{5,13},{9,1},{13,5},{2,10},{6,14},... | collective-permute-start | bytes 405512 | tf_op jit(solution)/shard_map/ppermute | solution.py:230
  15.7 4.9 %collective-permute-start.6 = (f32[264,128]{1,0:T(8,128)S(1)}, f32[264,128]{1,0:T(8,128)S(1)}, u32[]{:S(2)}, u32[]{:S(2)}) collective-permute-start(f32[264,128]{1,0:T(8,128)S(1)} %get-tuple-element.48), channel_id=1, source_target_pairs={{0,12},{4,0},{8,4},{12,8},{1,13},{5,1},{9,5},{13,9},{2,14},{6,2},{... | collective-permute-start | bytes 405512 | tf_op jit(solution)/shard_map/ppermute | solution.py:230
  20.7 6.6 %collective-permute-start.7 = (f32[528,128]{1,0:T(8,128)S(1)}, f32[528,128]{1,0:T(8,128)S(1)}, u32[]{:S(2)}, u32[]{:S(2)}) collective-permute-start(f32[528,128]{1,0:T(8,128)S(1)} %get-tuple-element.49.refs_2_), channel_id=1, source_target_pairs={{0,32},{32,64},{64,96},{96,0},{1,33},{33,65},{65,97},{97,1},{2,34}... | collective-permute-start | bytes 811016 | tf_op jit(solution)/shard_map/ppermute | solution.py:230
  22.0 5.3 %collective-permute-start.10 = (f32[528,128]{1,0:T(8,128)S(1)}, f32[528,128]{1,0:T(8,128)S(1)}, u32[]{:S(2)}, u32[]{:S(2)}) collective-permute-start(f32[528,128]{1,0:T(8,128)S(1)} %get-tuple-element.50.refs_3_), channel_id=1, source_target_pairs={{0,96},{32,0},{64,32},{96,64},{1,97},{33,1},{65,33},{97,65},{2,98}... | collective-permute-start | bytes 811016 | tf_op jit(solution)/shard_map/ppermute | solution.py:230
  23.4 9.6 %collective-permute-start.8 = (f32[528,128]{1,0:T(8,128)S(1)}, f32[528,128]{1,0:T(8,128)S(1)}, u32[]{:S(2)}, u32[]{:S(2)}) collective-permute-start(f32[528,128]{1,0:T(8,128)S(1)} %get-tuple-element.50.refs_3_), channel_id=1, source_target_pairs={{0,32},{32,64},{64,96},{96,0},{1,33},{33,65},{65,97},{97,1},{2,34}... | collective-permute-start | bytes 811016 | tf_op jit(solution)/shard_map/ppermute | solution.py:230
  23.5 12.5 %collective-permute-start.9 = (f32[528,128]{1,0:T(8,128)S(1)}, f32[528,128]{1,0:T(8,128)S(1)}, u32[]{:S(2)}, u32[]{:S(2)}) collective-permute-start(f32[528,128]{1,0:T(8,128)S(1)} %get-tuple-element.49.refs_2_), channel_id=1, source_target_pairs={{0,96},{32,0},{64,32},{96,64},{1,97},{33,1},{65,33},{97,65},{2,98}... | collective-permute-start | bytes 811016 | tf_op jit(solution)/shard_map/ppermute | solution.py:230
  27.3 11.5 %collective-permute-start.11 = (f32[528,128]{1,0:T(8,128)S(1)}, f32[528,128]{1,0:T(8,128)S(1)}, u32[]{:S(2)}, u32[]{:S(2)}) collective-permute-start(f32[528,128]{1,0:T(8,128)S(1)} %collective-permute-done.7.refs_3_), channel_id=1, source_target_pairs={{0,32},{32,64},{64,96},{96,0},{1,33},{33,65},{65,97},{97,1},{2,34}... | collective-permute-start | bytes 811016 | tf_op jit(solution)/shard_map/ppermute | solution.py:230
  27.3 11.5 %collective-permute-start.12 = (f32[528,128]{1,0:T(8,128)S(1)}, f32[528,128]{1,0:T(8,128)S(1)}, u32[]{:S(2)}, u32[]{:S(2)}) collective-permute-start(f32[528,128]{1,0:T(8,128)S(1)} %collective-permute-done.10.refs_4_), channel_id=1, source_target_pairs={{0,96},{32,0},{64,32},{96,64},{1,97},{33,1},{65,33},{97,65},{2,98}... | collective-permute-start | bytes 811016 | tf_op jit(solution)/shard_map/ppermute | solution.py:230
  41.8 8.4 %collective-permute-start.13 = (f32[48,1024]{1,0:T(8,128)S(1)}, f32[48,1024]{1,0:T(8,128)S(1)}, u32[]{:S(2)}, u32[]{:S(2)}) collective-permute-start(f32[48,1024]{1,0:T(8,128)S(1)} %get-tuple-element.54.sums), channel_id=1, source_target_pairs={{0,16},{16,0},{1,17},{17,1},{2,18},{18,2},{3,19},{19,3},{4,20},{20... | collective-permute-start | bytes 589832 | tf_op jit(solution)/shard_map/ppermute | solution.py:230
  55.3 1.4 %collective-permute-start.14 = (f32[24,1024]{1,0:T(8,128)S(1)}, f32[24,1024]{1,0:T(8,128)S(1)}, u32[]{:S(2)}, u32[]{:S(2)}) collective-permute-start(f32[24,1024]{1,0:T(8,128)S(1)} %get-tuple-element.69), channel_id=1, source_target_pairs={{0,16},{16,0},{1,17},{17,1},{2,18},{18,2},{3,19},{19,3},{4,20},{20... | collective-permute-start | bytes 294920 | tf_op jit(solution)/shard_map/ppermute | solution.py:230

commit v9 on v7

--- a/solution.py
+++ b/solution.py
@@ -65,21 +65,22 @@
 
 
 def merge_z(slots, width, place, *refs):
-    size = len(refs) // 2
-    parts, outs = refs[:size], refs[size:]
+    parts, outs = refs[:-3], refs[-3:]
+    size = len(parts)
     index_rows = (parts[0].shape[0] - width) // 2
     row = lax.broadcasted_iota(jnp.int32, (index_rows, LANES), 0)
     group = lax.broadcasted_iota(jnp.int32, (index_rows, LANES), 1) // slots
-    for k in range(size):
+    for out, steps in zip(outs, ((0,), (1, 2), (size - 1,))):
         for i in range(size):
-            outs[k][i * width : (i + 1) * width] = parts[i][:width]
-        y = (place[2] + k) % size
-        keep = (group == y % 2 * size + place[3]) & (row % 2 == y // 2)
-        for which in range(2):
-            for i in range(size):
-                at = width + which * index_rows
-                to = size * width + which * size + i
-                outs[k][to : to + 1] = spread(parts[i][at : at + index_rows], keep, group == row // 2, slots)
+            out[i * width : (i + 1) * width] = parts[i][:width]
+        for n, k in enumerate(steps):
+            y = (place[2] + k) % size
+            keep = (group == y % 2 * size + place[3]) & (row % 2 == y // 2)
+            for which in range(2):
+                for i in range(size):
+                    at = width + which * index_rows
+                    to = size * width + (2 * n + which) * size + i
+                    out[to : to + 1] = spread(parts[i][at : at + index_rows], keep, group == row // 2, slots)
 
 
 def merge_y(*refs):
@@ -88,10 +89,11 @@
     rows = parts[0].shape[0] - 2 * size
     for i in range(size):
         half, at = halves[i // 2], i % 2
+        start = rows + (2 * size if i == 2 else 0)
         half[at * rows : (at + 1) * rows] = parts[i][:rows]
         for which in range(2):
             to = 2 * rows + which * 2 * size + at * size
-            half[to : to + size] = parts[i][rows + which * size : rows + (which + 1) * size]
+            half[to : to + size] = parts[i][start + which * size : start + (which + 1) * size]
 
 
 def tile_sums(mine, points, t, out, o):
@@ -257,15 +259,19 @@
         near=False,
     )
     other = step(state, "core", 1)
-    along_z = [payload] + [step(payload, "z", k) for k in range(1, 4)]
-    to_y = call(functools.partial(merge_z, slots, domain), [f32(4 * domain + 8, LANES)] * 4, place, *along_z)
-    along_y = [step(to_y[k], "y", k) if k else to_y[k] for k in range(4)]
-    low, high = call(merge_y, [f32(8 * domain + 16, LANES)] * 2, *along_y)
+    up, down = step(payload, "z", 1), step(payload, "z", -1)
+    along_z = lax.optimization_barrier((payload, up, step(up, "z", 1), down, other))
+    *along_z, other = along_z
+    here, above, below = call(
+        functools.partial(merge_z, slots, domain), [f32(4 * domain + rows, LANES) for rows in (8, 16, 8)], place, *along_z
+    )
+    up, down = step(above, "y", 1), step(below, "y", -1)
+    up, down = lax.optimization_barrier((up, down))
+    low, high = call(merge_y, [f32(8 * domain + 16, LANES)] * 2, here, up, step(up, "y", 1), down)
     below_low, above_high = step(low, "x", 1), step(high, "x", -1)
     below_high, above_low = step(high, "x", 1), step(low, "x", -1)
-    far_low, far_high = step(below_low, "x", 1), step(above_high, "x", -1)
-    slabs = [(low, high), (below_low, below_high), (above_low, above_high), (far_low, far_high)]
-    each = devices * slots // LANES // len(slabs)
+    slabs = [(low, high), (below_low, below_high), (above_low, above_high)]
+    each = devices * slots // LANES // 4
     held = [pltpu.VMEM((each, 8, LANES), jnp.float32), pltpu.VMEM((each, ROWS, LANES), jnp.float32)]
     outs = [
         jax.ShapeDtypeStruct((halos, each * LANES), jnp.bfloat16),
@@ -277,6 +283,9 @@
     for slab in slabs:
         *arrays, total = call(functools.partial(first_pass, slots, blocks), outs, place, state, other, *sums, *slab, scratch=held)
         kept.extend(arrays)
+        if not sums:
+            first, second, _ = lax.optimization_barrier((below_low, above_high, total))
+            slabs.append((step(first, "x", 1), step(second, "x", -1)))
         sums = [total]
     state, own, partner = call(
         second_pass,

time: 58.8 us -> 60.3 us (1.026)
  waiting for transfers between devices: 11.8 us -> 14.8 us
  starting transfers between devices: 26.8 us -> 25.3 us
    ppermute x15, waiting for transfers between devices: 11.8 us -> 14.8 us  [step(): lax.ppermute(value, axis, [(i, (i + by) % size) for i in range(size)])]
    ppermute x15, starting transfers between devices: 26.8 us -> 25.3 us  [step(): lax.ppermute(value, axis, [(i, (i + by) % size) for i in range(size)])]
  transfers between devices with their start and end apart: 15 -> 15, of which waited for: 10 -> 8; matrix products, arithmetic and copies ran while one was open for 0% -> 0% of each run, Pallas kernels for 15% -> 14%
where the time goes in v9:
time: 60.3 us; the launch traced here: 60.1 us
  starting transfers between devices  25.3 us (42%)
  Pallas kernels  19.1 us (32%)
  waiting for transfers between devices  14.8 us (25%)
  between operations  0.74 us (1%)
    ppermute x15, starting transfers between devices, step(): lax.ppermute(value, axis, [(i, (i + by) % size) for i in range(size)])  25.3 us
    pallas_call x9, Pallas kernels, call(): pl.pallas_call(fn, in_specs=specs, out_specs=out_specs, out_shape=outs, s...  19.1 us
    ppermute x15, waiting for transfers between devices, step(): lax.ppermute(value, axis, [(i, (i + by) % size) for i in range(size)])  14.8 us
  transfers between devices with their start and end apart: 15, of which 8 were waited for; matrix products, arithmetic and copies ran while one was open for 0% of the time, Pallas kernels for 14%

profile of v9, /device:TPU:1, one launch (start us, length us, event | category | flops | bytes accessed | tf_op | source)
XLA Modules:
  0.0 60.1 jit_solution(14002223910328311387)
XLA Ops:
  0.6 0.9 %shard_map.85 = (f32[96,128]{1,0:T(8,128)S(1)}, f32[4,1024]{1,0:T(4,128)S(1)}) custom-call(f32[3,2048]{1,0:T(4,128)} %positions.1, f32[16,128]{1,0:T(8,128)} %bitcast.9, s32[16,128]{1,0:T(8,128)} %bitcast.10, s32[16,128]{1,0:T(8,128)} %bitcast.11, f32[3,1024]{1,0:T(4,128)} %centers.1, f32[1,1024]{1,0:T(1,128)} %bitcast.12), custom_call_target="tpu_custom_call" | custom-call | tf_op jit(solution)/shard_map/pallas_call | solution.py:239
  1.5 2.5 %collective-permute-start = (f32[96,128]{1,0:T(8,128)S(1)}, f32[96,128]{1,0:T(8,128)S(1)}, u32[]{:S(2)}, u32[]{:S(2)}) collective-permute-start(f32[96,128]{1,0:T(8,128)S(1)} %get-tuple-element.44.refs_0_), channel_id=1, source_target_pairs={{0,1},{1,2},{2,3},{3,0},{4,5},{5,6},{6,7},{7,4},{8,9},{9,10},{10,1... | collective-permute-start | bytes 147464 | tf_op jit(solution)/shard_map/ppermute | solution.py:232
  4.0 2.2 %collective-permute-start.2 = (f32[96,128]{1,0:T(8,128)S(1)}, f32[96,128]{1,0:T(8,128)S(1)}, u32[]{:S(2)}, u32[]{:S(2)}) collective-permute-start(f32[96,128]{1,0:T(8,128)S(1)} %get-tuple-element.44.refs_0_), channel_id=1, source_target_pairs={{0,3},{1,0},{2,1},{3,2},{4,7},{5,4},{6,5},{7,6},{8,11},{9,8},{10,9... | collective-permute-start | bytes 147464 | tf_op jit(solution)/shard_map/ppermute | solution.py:232
  6.2 1.0 %collective-permute-start.3 = (f32[4,1024]{1,0:T(4,128)S(1)}, f32[4,1024]{1,0:T(4,128)S(1)}, u32[]{:S(2)}, u32[]{:S(2)}) collective-permute-start(f32[4,1024]{1,0:T(4,128)S(1)} %get-tuple-element.41.refs_0_.mine), channel_id=1, source_target_pairs={{0,16},{16,0},{1,17},{17,1},{2,18},{18,2},{3,19},{19,3},{4,20},{20... | collective-permute-start | bytes 49160 | tf_op jit(solution)/shard_map/ppermute | solution.py:232
  7.2 0.4 collective-permute-done.refs_1_
  7.6 0.0 collective-permute-start.1
  7.6 0.1 pad_add_fusion.place
  7.7 0.3 collective-permute-done.3.refs_1_.other
  8.0 0.0 collective-permute-done.2.refs_3_
  8.0 3.8 %collective-permute-done.1.refs_2_ = f32[96,128]{1,0:T(8,128)S(1)} collective-permute-done((f32[96,128]{1,0:T(8,128)S(1)}, f32[96,128]{1,0:T(8,128)S(1)}, u32[]{:S(2)}, u32[]{:S(2)}) %collective-permute-start.1) | collective-permute-done | bytes 49184 | tf_op jit(solution)/shard_map/ppermute | solution.py:232
  11.8 0.9 %shard_map.86 = (f32[264,128]{1,0:T(8,128)S(1)}, f32[272,128]{1,0:T(8,128)S(1)}, f32[264,128]{1,0:T(8,128)S(1)}) custom-call(s32[4]{0:T(128)S(1)} %pad_add_fusion.place, f32[96,128]{1,0:T(8,128)S(1)} %get-tuple-element.44.refs_0_, f32[96,128]{1,0:T(8,128)S(1)} %collective-permute-done.refs_1_, f32[96,128]{1,0:T(8,128)S(1)} %collective-permute-done.1.refs_2_, ...), custom_call_target="tpu_custom_call" | custom-call | tf_op jit(solution)/shard_map/pallas_call | solution.py:239
  12.7 1.4 %collective-permute-start.4 = (f32[272,128]{1,0:T(8,128)S(1)}, f32[272,128]{1,0:T(8,128)S(1)}, u32[]{:S(2)}, u32[]{:S(2)}) collective-permute-start(f32[272,128]{1,0:T(8,128)S(1)} %get-tuple-element.49), channel_id=1, source_target_pairs={{0,4},{4,8},{8,12},{12,0},{1,5},{5,9},{9,13},{13,1},{2,6},{6,10},{... | collective-permute-start | bytes 417800 | tf_op jit(solution)/shard_map/ppermute | solution.py:232
  14.1 1.5 %collective-permute-start.5 = (f32[264,128]{1,0:T(8,128)S(1)}, f32[264,128]{1,0:T(8,128)S(1)}, u32[]{:S(2)}, u32[]{:S(2)}) collective-permute-start(f32[264,128]{1,0:T(8,128)S(1)} %get-tuple-element.50), channel_id=1, source_target_pairs={{0,12},{4,0},{8,4},{12,8},{1,13},{5,1},{9,5},{13,9},{2,14},{6,2},{... | collective-permute-start | bytes 405512 | tf_op jit(solution)/shard_map/ppermute | solution.py:232
  15.6 2.3 %collective-permute-done.5.refs_3_ = f32[264,128]{1,0:T(8,128)S(1)} collective-permute-done((f32[264,128]{1,0:T(8,128)S(1)}, f32[264,128]{1,0:T(8,128)S(1)}, u32[]{:S(2)}, u32[]{:S(2)}) %collective-permute-start.5) | collective-permute-done | bytes 135200 | tf_op jit(solution)/shard_map/ppermute | solution.py:232
  17.9 0.0 collective-permute-done.4.refs_1_
  17.9 1.3 %collective-permute-start.6 = (f32[272,128]{1,0:T(8,128)S(1)}, f32[272,128]{1,0:T(8,128)S(1)}, u32[]{:S(2)}, u32[]{:S(2)}) collective-permute-start(f32[272,128]{1,0:T(8,128)S(1)} %collective-permute-done.4.refs_1_), channel_id=1, source_target_pairs={{0,4},{4,8},{8,12},{12,0},{1,5},{5,9},{9,13},{13,1},{2,6},{6,10},{... | collective-permute-start | bytes 417800 | tf_op jit(solution)/shard_map/ppermute | solution.py:232
  19.2 3.9 %collective-permute-done.6.refs_2_ = f32[272,128]{1,0:T(8,128)S(1)} collective-permute-done((f32[272,128]{1,0:T(8,128)S(1)}, f32[272,128]{1,0:T(8,128)S(1)}, u32[]{:S(2)}, u32[]{:S(2)}) %collective-permute-start.6) | collective-permute-done | bytes 139296 | tf_op jit(solution)/shard_map/ppermute | solution.py:232
  23.1 1.3 %collective-permute-start.7 = (f32[528,128]{1,0:T(8,128)S(1)}, f32[528,128]{1,0:T(8,128)S(1)}, u32[]{:S(2)}, u32[]{:S(2)}) collective-permute-start(f32[528,128]{1,0:T(8,128)S(1)} %get-tuple-element.53.refs_2_), channel_id=1, source_target_pairs={{0,32},{32,64},{64,96},{96,0},{1,33},{33,65},{65,97},{97,1},{2,34}... | collective-permute-start | bytes 811016 | tf_op jit(solution)/shard_map/ppermute | solution.py:232
  24.4 1.5 %collective-permute-start.10 = (f32[528,128]{1,0:T(8,128)S(1)}, f32[528,128]{1,0:T(8,128)S(1)}, u32[]{:S(2)}, u32[]{:S(2)}) collective-permute-start(f32[528,128]{1,0:T(8,128)S(1)} %get-tuple-element.54.refs_3_), channel_id=1, source_target_pairs={{0,96},{32,0},{64,32},{96,64},{1,97},{33,1},{65,33},{97,65},{2,98}... | collective-permute-start | bytes 811016 | tf_op jit(solution)/shard_map/ppermute | solution.py:232
  25.9 1.3 %collective-permute-start.9 = (f32[528,128]{1,0:T(8,128)S(1)}, f32[528,128]{1,0:T(8,128)S(1)}, u32[]{:S(2)}, u32[]{:S(2)}) collective-permute-start(f32[528,128]{1,0:T(8,128)S(1)} %get-tuple-element.53.refs_2_), channel_id=1, source_target_pairs={{0,96},{32,0},{64,32},{96,64},{1,97},{33,1},{65,33},{97,65},{2,98}... | collective-permute-start | bytes 811016 | tf_op jit(solution)/shard_map/ppermute | solution.py:232
  27.2 0.2 collective-permute-start.8
  27.4 2.9 %shard_map.88 = (bf16[1024,512]{1,0:T(8,128)(2,1)S(1)}, bf16[512,1024]{1,0:T(8,128)(2,1)S(1)}, f32[4,4,128,128]{3,2,1,0:T(8,128)S(1)}, f32[48,1024]{1,0:T(8,128)S(1)}) custom-call(s32[4]{0:T(128)S(1)} %pad_add_fusion.place, f32[4,1024]{1,0:T(4,128)S(1)} %get-tuple-element.41.refs_0_.mine, f32[4,1024]{1,0:T(4,128)S(1)} %collective-permute-done.3.refs_1_.other, ...), custom_call_target="tpu_custom_call" | custom-call | tf_op jit(solution)/shard_map/pallas_call | solution.py:239
  30.2 0.0 collective-permute-done.7.refs_3_
  30.2 0.0 collective-permute-done.10.refs_4_
  30.3 0.7 %collective-permute-start.11 = (f32[528,128]{1,0:T(8,128)S(1)}, f32[528,128]{1,0:T(8,128)S(1)}, u32[]{:S(2)}, u32[]{:S(2)}) collective-permute-start(f32[528,128]{1,0:T(8,128)S(1)} %collective-permute-done.7.refs_3_), channel_id=1, source_target_pairs={{0,32},{32,64},{64,96},{96,0},{1,33},{33,65},{65,97},{97,1},{2,34}... | collective-permute-start | bytes 811016 | tf_op jit(solution)/shard_map/ppermute | solution.py:232
  30.9 2.1 %collective-permute-start.12 = (f32[528,128]{1,0:T(8,128)S(1)}, f32[528,128]{1,0:T(8,128)S(1)}, u32[]{:S(2)}, u32[]{:S(2)}) collective-permute-start(f32[528,128]{1,0:T(8,128)S(1)} %collective-permute-done.10.refs_4_), channel_id=1, source_target_pairs={{0,96},{32,0},{64,32},{96,64},{1,97},{33,1},{65,33},{97,65},{2,98}... | collective-permute-start | bytes 811016 | tf_op jit(solution)/shard_map/ppermute | solution.py:232
  33.0 2.1 %collective-permute-done.8.refs_4_ = f32[528,128]{1,0:T(8,128)S(1)} collective-permute-done((f32[528,128]{1,0:T(8,128)S(1)}, f32[528,128]{1,0:T(8,128)S(1)}, u32[]{:S(2)}, u32[]{:S(2)}) %collective-permute-start.8) | collective-permute-done | bytes 270368 | tf_op jit(solution)/shard_map/ppermute | solution.py:232
  35.1 2.9 %shard_map.89 = (bf16[1024,512]{1,0:T(8,128)(2,1)S(1)}, bf16[512,1024]{1,0:T(8,128)(2,1)S(1)}, f32[4,4,128,128]{3,2,1,0:T(8,128)S(1)}, f32[48,1024]{1,0:T(8,128)S(1)}) custom-call(s32[4]{0:T(128)S(1)} %pad_add_fusion.place, f32[4,1024]{1,0:T(4,128)S(1)} %get-tuple-element.41.refs_0_.mine, f32[4,1024]{1,0:T(4,128)S(1)} %collective-permute-done.3.refs_1_.other, ...), custom_call_target="tpu_custom_call" | custom-call | tf_op jit(solution)/shard_map/pallas_call | solution.py:239
  38.0 0.0 collective-permute-done.9.refs_3_
  38.0 2.9 %shard_map.90 = (bf16[1024,512]{1,0:T(8,128)(2,1)S(1)}, bf16[512,1024]{1,0:T(8,128)(2,1)S(1)}, f32[4,4,128,128]{3,2,1,0:T(8,128)S(1)}, f32[48,1024]{1,0:T(8,128)S(1)}) custom-call(s32[4]{0:T(128)S(1)} %pad_add_fusion.place, f32[4,1024]{1,0:T(4,128)S(1)} %get-tuple-element.41.refs_0_.mine, f32[4,1024]{1,0:T(4,128)S(1)} %collective-permute-done.3.refs_1_.other, ...), custom_call_target="tpu_custom_call" | custom-call | tf_op jit(solution)/shard_map/pallas_call | solution.py:239
  40.9 0.0 collective-permute-done.11.refs_3_
  40.9 0.0 collective-permute-done.12.refs_4_
  40.9 2.9 %shard_map.91 = (bf16[1024,512]{1,0:T(8,128)(2,1)S(1)}, bf16[512,1024]{1,0:T(8,128)(2,1)S(1)}, f32[4,4,128,128]{3,2,1,0:T(8,128)S(1)}, f32[48,1024]{1,0:T(8,128)S(1)}) custom-call(s32[4]{0:T(128)S(1)} %pad_add_fusion.place, f32[4,1024]{1,0:T(4,128)S(1)} %get-tuple-element.41.refs_0_.mine, f32[4,1024]{1,0:T(4,128)S(1)} %collective-permute-done.3.refs_1_.other, ...), custom_call_target="tpu_custom_call" | custom-call | tf_op jit(solution)/shard_map/pallas_call | solution.py:239
  43.8 8.1 %collective-permute-start.13 = (f32[48,1024]{1,0:T(8,128)S(1)}, f32[48,1024]{1,0:T(8,128)S(1)}, u32[]{:S(2)}, u32[]{:S(2)}) collective-permute-start(f32[48,1024]{1,0:T(8,128)S(1)} %get-tuple-element.60.sums), channel_id=1, source_target_pairs={{0,16},{16,0},{1,17},{17,1},{2,18},{18,2},{3,19},{19,3},{4,20},{20... | collective-permute-start | bytes 589832 | tf_op jit(solution)/shard_map/ppermute | solution.py:232
  51.9 1.1 %collective-permute-done.13.received = f32[48,1024]{1,0:T(8,128)S(1)} collective-permute-done((f32[48,1024]{1,0:T(8,128)S(1)}, f32[48,1024]{1,0:T(8,128)S(1)}, u32[]{:S(2)}, u32[]{:S(2)}) %collective-permute-start.13) | collective-permute-done | bytes 196640 | tf_op jit(solution)/shard_map/ppermute | solution.py:232
  53.0 5.1 %shard_map.92 = (f32[4,1024]{1,0:T(4,128)S(1)}, f32[24,1024]{1,0:T(8,128)S(1)}, f32[24,1024]{1,0:T(8,128)S(1)}) custom-call(f32[4,1024]{1,0:T(4,128)S(1)} %get-tuple-element.41.refs_0_.mine, f32[4,1024]{1,0:T(4,128)S(1)} %collective-permute-done.3.refs_1_.other, f32[48,1024]{1,0:T(8,128)S(1)} %get-tuple-element.60.sums, ...), custom_call_target="tpu_custom_call" | custom-call | tf_op jit(solution)/shard_map/pallas_call | solution.py:239
  58.1 0.5 collective-permute-start.14
  58.5 0.9 %collective-permute-done.14.received = f32[24,1024]{1,0:T(8,128)S(1)} collective-permute-done((f32[24,1024]{1,0:T(8,128)S(1)}, f32[24,1024]{1,0:T(8,128)S(1)}, u32[]{:S(2)}, u32[]{:S(2)}) %collective-permute-start.14) | collective-permute-done | bytes 98336 | tf_op jit(solution)/shard_map/ppermute | solution.py:232
  59.5 0.7 %shard_map.93 = (f32[3,1024]{1,0:T(4,128)}, f32[1,1024]{1,0:T(1,128)}, f32[16,1024]{1,0:T(8,128)}) custom-call(f32[4,1024]{1,0:T(4,128)S(1)} %get-tuple-element.73.state, f32[24,1024]{1,0:T(8,128)S(1)} %get-tuple-element.74.own, f32[24,1024]{1,0:T(8,128)S(1)} %collective-permute-done.14.received), custom_call_target="tpu_custom_call" | custom-call | tf_op jit(solution)/shard_map/pallas_call | solution.py:239
  (1 shorter events, 0.0 us)
Async XLA Ops:
  1.5 6.1 %collective-permute-start = (f32[96,128]{1,0:T(8,128)S(1)}, f32[96,128]{1,0:T(8,128)S(1)}, u32[]{:S(2)}, u32[]{:S(2)}) collective-permute-start(f32[96,128]{1,0:T(8,128)S(1)} %get-tuple-element.44.refs_0_), channel_id=1, source_target_pairs={{0,1},{1,2},{2,3},{3,0},{4,5},{5,6},{6,7},{7,4},{8,9},{9,10},{10,1... | collective-permute-start | bytes 147464 | tf_op jit(solution)/shard_map/ppermute | solution.py:232
  4.0 4.0 %collective-permute-start.2 = (f32[96,128]{1,0:T(8,128)S(1)}, f32[96,128]{1,0:T(8,128)S(1)}, u32[]{:S(2)}, u32[]{:S(2)}) collective-permute-start(f32[96,128]{1,0:T(8,128)S(1)} %get-tuple-element.44.refs_0_), channel_id=1, source_target_pairs={{0,3},{1,0},{2,1},{3,2},{4,7},{5,4},{6,5},{7,6},{8,11},{9,8},{10,9... | collective-permute-start | bytes 147464 | tf_op jit(solution)/shard_map/ppermute | solution.py:232
  6.2 1.8 %collective-permute-start.3 = (f32[4,1024]{1,0:T(4,128)S(1)}, f32[4,1024]{1,0:T(4,128)S(1)}, u32[]{:S(2)}, u32[]{:S(2)}) collective-permute-start(f32[4,1024]{1,0:T(4,128)S(1)} %get-tuple-element.41.refs_0_.mine), channel_id=1, source_target_pairs={{0,16},{16,0},{1,17},{17,1},{2,18},{18,2},{3,19},{19,3},{4,20},{20... | collective-permute-start | bytes 49160 | tf_op jit(solution)/shard_map/ppermute | solution.py:232
  7.6 4.2 %collective-permute-start.1 = (f32[96,128]{1,0:T(8,128)S(1)}, f32[96,128]{1,0:T(8,128)S(1)}, u32[]{:S(2)}, u32[]{:S(2)}) collective-permute-start(f32[96,128]{1,0:T(8,128)S(1)} %collective-permute-done.refs_1_), channel_id=1, source_target_pairs={{0,1},{1,2},{2,3},{3,0},{4,5},{5,6},{6,7},{7,4},{8,9},{9,10},{10,1... | collective-permute-start | bytes 147464 | tf_op jit(solution)/shard_map/ppermute | solution.py:232
  12.7 5.2 %collective-permute-start.4 = (f32[272,128]{1,0:T(8,128)S(1)}, f32[272,128]{1,0:T(8,128)S(1)}, u32[]{:S(2)}, u32[]{:S(2)}) collective-permute-start(f32[272,128]{1,0:T(8,128)S(1)} %get-tuple-element.49), channel_id=1, source_target_pairs={{0,4},{4,8},{8,12},{12,0},{1,5},{5,9},{9,13},{13,1},{2,6},{6,10},{... | collective-permute-start | bytes 417800 | tf_op jit(solution)/shard_map/ppermute | solution.py:232
  14.1 3.9 %collective-permute-start.5 = (f32[264,128]{1,0:T(8,128)S(1)}, f32[264,128]{1,0:T(8,128)S(1)}, u32[]{:S(2)}, u32[]{:S(2)}) collective-permute-start(f32[264,128]{1,0:T(8,128)S(1)} %get-tuple-element.50), channel_id=1, source_target_pairs={{0,12},{4,0},{8,4},{12,8},{1,13},{5,1},{9,5},{13,9},{2,14},{6,2},{... | collective-permute-start | bytes 405512 | tf_op jit(solution)/shard_map/ppermute | solution.py:232
  17.9 5.2 %collective-permute-start.6 = (f32[272,128]{1,0:T(8,128)S(1)}, f32[272,128]{1,0:T(8,128)S(1)}, u32[]{:S(2)}, u32[]{:S(2)}) collective-permute-start(f32[272,128]{1,0:T(8,128)S(1)} %collective-permute-done.4.refs_1_), channel_id=1, source_target_pairs={{0,4},{4,8},{8,12},{12,0},{1,5},{5,9},{9,13},{13,1},{2,6},{6,10},{... | collective-permute-start | bytes 417800 | tf_op jit(solution)/shard_map/ppermute | solution.py:232
  23.1 7.1 %collective-permute-start.7 = (f32[528,128]{1,0:T(8,128)S(1)}, f32[528,128]{1,0:T(8,128)S(1)}, u32[]{:S(2)}, u32[]{:S(2)}) collective-permute-start(f32[528,128]{1,0:T(8,128)S(1)} %get-tuple-element.53.refs_2_), channel_id=1, source_target_pairs={{0,32},{32,64},{64,96},{96,0},{1,33},{33,65},{65,97},{97,1},{2,34}... | collective-permute-start | bytes 811016 | tf_op jit(solution)/shard_map/ppermute | solution.py:232
  24.4 5.8 %collective-permute-start.10 = (f32[528,128]{1,0:T(8,128)S(1)}, f32[528,128]{1,0:T(8,128)S(1)}, u32[]{:S(2)}, u32[]{:S(2)}) collective-permute-start(f32[528,128]{1,0:T(8,128)S(1)} %get-tuple-element.54.refs_3_), channel_id=1, source_target_pairs={{0,96},{32,0},{64,32},{96,64},{1,97},{33,1},{65,33},{97,65},{2,98}... | collective-permute-start | bytes 811016 | tf_op jit(solution)/shard_map/ppermute | solution.py:232
  25.9 12.1 %collective-permute-start.9 = (f32[528,128]{1,0:T(8,128)S(1)}, f32[528,128]{1,0:T(8,128)S(1)}, u32[]{:S(2)}, u32[]{:S(2)}) collective-permute-start(f32[528,128]{1,0:T(8,128)S(1)} %get-tuple-element.53.refs_2_), channel_id=1, source_target_pairs={{0,96},{32,0},{64,32},{96,64},{1,97},{33,1},{65,33},{97,65},{2,98}... | collective-permute-start | bytes 811016 | tf_op jit(solution)/shard_map/ppermute | solution.py:232
  27.2 7.9 %collective-permute-start.8 = (f32[528,128]{1,0:T(8,128)S(1)}, f32[528,128]{1,0:T(8,128)S(1)}, u32[]{:S(2)}, u32[]{:S(2)}) collective-permute-start(f32[528,128]{1,0:T(8,128)S(1)} %get-tuple-element.54.refs_3_), channel_id=1, source_target_pairs={{0,32},{32,64},{64,96},{96,0},{1,33},{33,65},{65,97},{97,1},{2,34}... | collective-permute-start | bytes 811016 | tf_op jit(solution)/shard_map/ppermute | solution.py:232
  30.3 10.6 %collective-permute-start.11 = (f32[528,128]{1,0:T(8,128)S(1)}, f32[528,128]{1,0:T(8,128)S(1)}, u32[]{:S(2)}, u32[]{:S(2)}) collective-permute-start(f32[528,128]{1,0:T(8,128)S(1)} %collective-permute-done.7.refs_3_), channel_id=1, source_target_pairs={{0,32},{32,64},{64,96},{96,0},{1,33},{33,65},{65,97},{97,1},{2,34}... | collective-permute-start | bytes 811016 | tf_op jit(solution)/shard_map/ppermute | solution.py:232
  30.9 10.0 %collective-permute-start.12 = (f32[528,128]{1,0:T(8,128)S(1)}, f32[528,128]{1,0:T(8,128)S(1)}, u32[]{:S(2)}, u32[]{:S(2)}) collective-permute-start(f32[528,128]{1,0:T(8,128)S(1)} %collective-permute-done.10.refs_4_), channel_id=1, source_target_pairs={{0,96},{32,0},{64,32},{96,64},{1,97},{33,1},{65,33},{97,65},{2,98}... | collective-permute-start | bytes 811016 | tf_op jit(solution)/shard_map/ppermute | solution.py:232
  43.8 9.1 %collective-permute-start.13 = (f32[48,1024]{1,0:T(8,128)S(1)}, f32[48,1024]{1,0:T(8,128)S(1)}, u32[]{:S(2)}, u32[]{:S(2)}) collective-permute-start(f32[48,1024]{1,0:T(8,128)S(1)} %get-tuple-element.60.sums), channel_id=1, source_target_pairs={{0,16},{16,0},{1,17},{17,1},{2,18},{18,2},{3,19},{19,3},{4,20},{20... | collective-permute-start | bytes 589832 | tf_op jit(solution)/shard_map/ppermute | solution.py:232
  58.1 1.4 %collective-permute-start.14 = (f32[24,1024]{1,0:T(8,128)S(1)}, f32[24,1024]{1,0:T(8,128)S(1)}, u32[]{:S(2)}, u32[]{:S(2)}) collective-permute-start(f32[24,1024]{1,0:T(8,128)S(1)} %get-tuple-element.75), channel_id=1, source_target_pairs={{0,16},{16,0},{1,17},{17,1},{2,18},{18,2},{3,19},{19,3},{4,20},{20... | collective-permute-start | bytes 294920 | tf_op jit(solution)/shard_map/ppermute | solution.py:232

commit v10 on v8

--- a/solution.py
+++ b/solution.py
@@ -264,9 +264,8 @@
     low, high = call(merge_y, [f32(8 * domain + 16, LANES)] * 2, *along_y)
     below_low, above_high = step(low, "x", 1), step(high, "x", -1)
     below_high, above_low = step(high, "x", 1), step(low, "x", -1)
-    far_low, far_high = step(below_low, "x", 1), step(above_high, "x", -1)
-    slabs = [(low, high), (below_low, below_high), (above_low, above_high), (far_low, far_high)]
-    each = devices * slots // LANES // len(slabs)
+    slabs = [(low, high), (below_low, below_high), (above_low, above_high)]
+    each = devices * slots // LANES // 4
     held = [pltpu.VMEM((each, 8, LANES), jnp.float32), pltpu.VMEM((each, ROWS, LANES), jnp.float32)]
     outs = [
         jax.ShapeDtypeStruct((halos, each * LANES), jnp.bfloat16),
@@ -278,6 +277,9 @@
     for slab in slabs:
         *arrays, total = call(functools.partial(first_pass, slots, blocks), outs, place, state, other, *sums, *slab, scratch=held)
         kept.extend(arrays)
+        if not sums:
+            first, second, _ = lax.optimization_barrier((below_low, above_high, total))
+            slabs.append((step(first, "x", 1), step(second, "x", -1)))
         sums = [total]
     state, own, partner = call(
         second_pass,

time: 57.6 us -> 56.4 us (0.979)
  starting transfers between devices: 27.8 us -> 24.2 us
  waiting for transfers between devices: 9.57 us -> 12.1 us
    ppermute x15, starting transfers between devices: 27.8 us -> 24.2 us  [step(): lax.ppermute(value, axis, [(i, (i + by) % size) for i in range(size)])]
    ppermute x15, waiting for transfers between devices: 9.57 us -> 12.1 us  [step(): lax.ppermute(value, axis, [(i, (i + by) % size) for i in range(size)])]
  transfers between devices with their start and end apart: 15 -> 15, of which waited for: 10 -> 9; matrix products, arithmetic and copies ran while one was open for 0% -> 0% of each run, Pallas kernels for 15% -> 15%
where the time goes in v10:
time: 56.4 us; the launch traced here: 56.3 us
  starting transfers between devices  24.2 us (43%)
  Pallas kernels  19.1 us (34%)
  waiting for transfers between devices  12.1 us (21%)
  between operations  0.74 us (1%)
    ppermute x15, starting transfers between devices, step(): lax.ppermute(value, axis, [(i, (i + by) % size) for i in range(size)])  24.2 us
    pallas_call x9, Pallas kernels, call(): pl.pallas_call(fn, in_specs=specs, out_specs=out_specs, out_shape=outs, s...  19.1 us
    ppermute x15, waiting for transfers between devices, step(): lax.ppermute(value, axis, [(i, (i + by) % size) for i in range(size)])  12.1 us
  transfers between devices with their start and end apart: 15, of which 9 were waited for; matrix products, arithmetic and copies ran while one was open for 0% of the time, Pallas kernels for 15%

profile of v10, /device:TPU:1, one launch (start us, length us, event | category | flops | bytes accessed | tf_op | source)
XLA Modules:
  0.0 56.3 jit_solution(5571994032375865837)
XLA Ops:
  0.6 0.9 %shard_map.85 = (f32[96,128]{1,0:T(8,128)S(1)}, f32[4,1024]{1,0:T(4,128)S(1)}) custom-call(f32[3,2048]{1,0:T(4,128)} %positions.1, f32[16,128]{1,0:T(8,128)} %bitcast.9, s32[16,128]{1,0:T(8,128)} %bitcast.10, s32[16,128]{1,0:T(8,128)} %bitcast.11, f32[3,1024]{1,0:T(4,128)} %centers.1, f32[1,1024]{1,0:T(1,128)} %bitcast.12), custom_call_target="tpu_custom_call" | custom-call | tf_op jit(solution)/shard_map/pallas_call | solution.py:237
  1.5 4.7 %collective-permute-start.2 = (f32[96,128]{1,0:T(8,128)S(1)}, f32[96,128]{1,0:T(8,128)S(1)}, u32[]{:S(2)}, u32[]{:S(2)}) collective-permute-start(f32[96,128]{1,0:T(8,128)S(1)} %get-tuple-element.43.refs_0_), channel_id=1, source_target_pairs={{0,3},{1,0},{2,1},{3,2},{4,7},{5,4},{6,5},{7,6},{8,11},{9,8},{10,9... | collective-permute-start | bytes 147464 | tf_op jit(solution)/shard_map/ppermute | solution.py:230
  6.2 0.0 collective-permute-start.1
  6.2 0.7 %collective-permute-start = (f32[96,128]{1,0:T(8,128)S(1)}, f32[96,128]{1,0:T(8,128)S(1)}, u32[]{:S(2)}, u32[]{:S(2)}) collective-permute-start(f32[96,128]{1,0:T(8,128)S(1)} %get-tuple-element.43.refs_0_), channel_id=1, source_target_pairs={{0,1},{1,2},{2,3},{3,0},{4,5},{5,6},{6,7},{7,4},{8,9},{9,10},{10,1... | collective-permute-start | bytes 147464 | tf_op jit(solution)/shard_map/ppermute | solution.py:230
  6.9 1.5 %collective-permute-start.3 = (f32[4,1024]{1,0:T(4,128)S(1)}, f32[4,1024]{1,0:T(4,128)S(1)}, u32[]{:S(2)}, u32[]{:S(2)}) collective-permute-start(f32[4,1024]{1,0:T(4,128)S(1)} %get-tuple-element.40.refs_0_.mine), channel_id=1, source_target_pairs={{0,16},{16,0},{1,17},{17,1},{2,18},{18,2},{3,19},{19,3},{4,20},{20... | collective-permute-start | bytes 49160 | tf_op jit(solution)/shard_map/ppermute | solution.py:230
  8.4 0.1 pad_add_fusion.place
  8.4 0.8 %collective-permute-done.3.refs_1_.other = f32[4,1024]{1,0:T(4,128)S(1)} collective-permute-done((f32[4,1024]{1,0:T(4,128)S(1)}, f32[4,1024]{1,0:T(4,128)S(1)}, u32[]{:S(2)}, u32[]{:S(2)}) %collective-permute-start.3) | collective-permute-done | bytes 16416 | tf_op jit(solution)/shard_map/ppermute | solution.py:230
  9.2 0.0 collective-permute-done.2.refs_3_
  9.2 1.5 %collective-permute-done.1.refs_2_ = f32[96,128]{1,0:T(8,128)S(1)} collective-permute-done((f32[96,128]{1,0:T(8,128)S(1)}, f32[96,128]{1,0:T(8,128)S(1)}, u32[]{:S(2)}, u32[]{:S(2)}) %collective-permute-start.1) | collective-permute-done | bytes 49184 | tf_op jit(solution)/shard_map/ppermute | solution.py:230
  10.7 0.1 collective-permute-done.refs_1_
  10.8 0.9 %shard_map.86 = (f32[264,128]{1,0:T(8,128)S(1)}, f32[264,128]{1,0:T(8,128)S(1)}, f32[264,128]{1,0:T(8,128)S(1)}, f32[264,128]{1,0:T(8,128)S(1)}) custom-call(s32[4]{0:T(128)S(1)} %pad_add_fusion.place, f32[96,128]{1,0:T(8,128)S(1)} %get-tuple-element.43.refs_0_, f32[96,128]{1,0:T(8,128)S(1)} %collective-permute-done.refs_1_, ...), custom_call_target="tpu_custom_call" | custom-call | tf_op jit(solution)/shard_map/pallas_call | solution.py:237
  11.7 1.4 %collective-permute-start.4 = (f32[264,128]{1,0:T(8,128)S(1)}, f32[264,128]{1,0:T(8,128)S(1)}, u32[]{:S(2)}, u32[]{:S(2)}) collective-permute-start(f32[264,128]{1,0:T(8,128)S(1)} %get-tuple-element.48), channel_id=1, source_target_pairs={{0,4},{4,8},{8,12},{12,0},{1,5},{5,9},{9,13},{13,1},{2,6},{6,10},{... | collective-permute-start | bytes 405512 | tf_op jit(solution)/shard_map/ppermute | solution.py:230
  13.1 2.6 %collective-permute-start.5 = (f32[264,128]{1,0:T(8,128)S(1)}, f32[264,128]{1,0:T(8,128)S(1)}, u32[]{:S(2)}, u32[]{:S(2)}) collective-permute-start(f32[264,128]{1,0:T(8,128)S(1)} %get-tuple-element.49), channel_id=1, source_target_pairs={{0,8},{4,12},{8,0},{12,4},{1,9},{5,13},{9,1},{13,5},{2,10},{6,14},... | collective-permute-start | bytes 405512 | tf_op jit(solution)/shard_map/ppermute | solution.py:230
  15.7 1.1 %collective-permute-start.6 = (f32[264,128]{1,0:T(8,128)S(1)}, f32[264,128]{1,0:T(8,128)S(1)}, u32[]{:S(2)}, u32[]{:S(2)}) collective-permute-start(f32[264,128]{1,0:T(8,128)S(1)} %get-tuple-element.50), channel_id=1, source_target_pairs={{0,12},{4,0},{8,4},{12,8},{1,13},{5,1},{9,5},{13,9},{2,14},{6,2},{... | collective-permute-start | bytes 405512 | tf_op jit(solution)/shard_map/ppermute | solution.py:230
  16.8 0.1 collective-permute-done.4.refs_1_
  16.9 3.0 %collective-permute-done.5.refs_2_ = f32[264,128]{1,0:T(8,128)S(1)} collective-permute-done((f32[264,128]{1,0:T(8,128)S(1)}, f32[264,128]{1,0:T(8,128)S(1)}, u32[]{:S(2)}, u32[]{:S(2)}) %collective-permute-start.5) | collective-permute-done | bytes 135200 | tf_op jit(solution)/shard_map/ppermute | solution.py:230
  19.9 0.7 %collective-permute-done.6.refs_3_ = f32[264,128]{1,0:T(8,128)S(1)} collective-permute-done((f32[264,128]{1,0:T(8,128)S(1)}, f32[264,128]{1,0:T(8,128)S(1)}, u32[]{:S(2)}, u32[]{:S(2)}) %collective-permute-start.6) | collective-permute-done | bytes 135200 | tf_op jit(solution)/shard_map/ppermute | solution.py:230
  20.7 1.3 %collective-permute-start.7 = (f32[528,128]{1,0:T(8,128)S(1)}, f32[528,128]{1,0:T(8,128)S(1)}, u32[]{:S(2)}, u32[]{:S(2)}) collective-permute-start(f32[528,128]{1,0:T(8,128)S(1)} %get-tuple-element.51.refs_2_), channel_id=1, source_target_pairs={{0,32},{32,64},{64,96},{96,0},{1,33},{33,65},{65,97},{97,1},{2,34}... | collective-permute-start | bytes 811016 | tf_op jit(solution)/shard_map/ppermute | solution.py:230
  22.0 1.5 %collective-permute-start.10 = (f32[528,128]{1,0:T(8,128)S(1)}, f32[528,128]{1,0:T(8,128)S(1)}, u32[]{:S(2)}, u32[]{:S(2)}) collective-permute-start(f32[528,128]{1,0:T(8,128)S(1)} %get-tuple-element.52.refs_3_), channel_id=1, source_target_pairs={{0,96},{32,0},{64,32},{96,64},{1,97},{33,1},{65,33},{97,65},{2,98}... | collective-permute-start | bytes 811016 | tf_op jit(solution)/shard_map/ppermute | solution.py:230
  23.4 1.3 %collective-permute-start.9 = (f32[528,128]{1,0:T(8,128)S(1)}, f32[528,128]{1,0:T(8,128)S(1)}, u32[]{:S(2)}, u32[]{:S(2)}) collective-permute-start(f32[528,128]{1,0:T(8,128)S(1)} %get-tuple-element.51.refs_2_), channel_id=1, source_target_pairs={{0,96},{32,0},{64,32},{96,64},{1,97},{33,1},{65,33},{97,65},{2,98}... | collective-permute-start | bytes 811016 | tf_op jit(solution)/shard_map/ppermute | solution.py:230
  24.7 0.2 collective-permute-start.8
  24.9 2.9 %shard_map.88 = (bf16[1024,512]{1,0:T(8,128)(2,1)S(1)}, bf16[512,1024]{1,0:T(8,128)(2,1)S(1)}, f32[4,4,128,128]{3,2,1,0:T(8,128)S(1)}, f32[48,1024]{1,0:T(8,128)S(1)}) custom-call(s32[4]{0:T(128)S(1)} %pad_add_fusion.place, f32[4,1024]{1,0:T(4,128)S(1)} %get-tuple-element.40.refs_0_.mine, f32[4,1024]{1,0:T(4,128)S(1)} %collective-permute-done.3.refs_1_.other, ...), custom_call_target="tpu_custom_call" | custom-call | tf_op jit(solution)/shard_map/pallas_call | solution.py:237
  27.8 0.0 collective-permute-done.7.refs_3_
  27.8 0.0 collective-permute-done.10.refs_4_
  27.8 1.0 %collective-permute-start.11 = (f32[528,128]{1,0:T(8,128)S(1)}, f32[528,128]{1,0:T(8,128)S(1)}, u32[]{:S(2)}, u32[]{:S(2)}) collective-permute-start(f32[528,128]{1,0:T(8,128)S(1)} %collective-permute-done.7.refs_3_), channel_id=1, source_target_pairs={{0,32},{32,64},{64,96},{96,0},{1,33},{33,65},{65,97},{97,1},{2,34}... | collective-permute-start | bytes 811016 | tf_op jit(solution)/shard_map/ppermute | solution.py:230
  28.8 1.8 %collective-permute-start.12 = (f32[528,128]{1,0:T(8,128)S(1)}, f32[528,128]{1,0:T(8,128)S(1)}, u32[]{:S(2)}, u32[]{:S(2)}) collective-permute-start(f32[528,128]{1,0:T(8,128)S(1)} %collective-permute-done.10.refs_4_), channel_id=1, source_target_pairs={{0,96},{32,0},{64,32},{96,64},{1,97},{33,1},{65,33},{97,65},{2,98}... | collective-permute-start | bytes 811016 | tf_op jit(solution)/shard_map/ppermute | solution.py:230
  30.6 3.8 %collective-permute-done.8.refs_4_ = f32[528,128]{1,0:T(8,128)S(1)} collective-permute-done((f32[528,128]{1,0:T(8,128)S(1)}, f32[528,128]{1,0:T(8,128)S(1)}, u32[]{:S(2)}, u32[]{:S(2)}) %collective-permute-start.8) | collective-permute-done | bytes 270368 | tf_op jit(solution)/shard_map/ppermute | solution.py:230
  34.4 2.9 %shard_map.89 = (bf16[1024,512]{1,0:T(8,128)(2,1)S(1)}, bf16[512,1024]{1,0:T(8,128)(2,1)S(1)}, f32[4,4,128,128]{3,2,1,0:T(8,128)S(1)}, f32[48,1024]{1,0:T(8,128)S(1)}) custom-call(s32[4]{0:T(128)S(1)} %pad_add_fusion.place, f32[4,1024]{1,0:T(4,128)S(1)} %get-tuple-element.40.refs_0_.mine, f32[4,1024]{1,0:T(4,128)S(1)} %collective-permute-done.3.refs_1_.other, ...), custom_call_target="tpu_custom_call" | custom-call | tf_op jit(solution)/shard_map/pallas_call | solution.py:237
  37.3 0.0 collective-permute-done.9.refs_3_
  37.3 2.9 %shard_map.90 = (bf16[1024,512]{1,0:T(8,128)(2,1)S(1)}, bf16[512,1024]{1,0:T(8,128)(2,1)S(1)}, f32[4,4,128,128]{3,2,1,0:T(8,128)S(1)}, f32[48,1024]{1,0:T(8,128)S(1)}) custom-call(s32[4]{0:T(128)S(1)} %pad_add_fusion.place, f32[4,1024]{1,0:T(4,128)S(1)} %get-tuple-element.40.refs_0_.mine, f32[4,1024]{1,0:T(4,128)S(1)} %collective-permute-done.3.refs_1_.other, ...), custom_call_target="tpu_custom_call" | custom-call | tf_op jit(solution)/shard_map/pallas_call | solution.py:237
  40.2 0.0 collective-permute-done.11.refs_3_
  40.2 0.0 collective-permute-done.12.refs_4_
  40.2 2.9 %shard_map.91 = (bf16[1024,512]{1,0:T(8,128)(2,1)S(1)}, bf16[512,1024]{1,0:T(8,128)(2,1)S(1)}, f32[4,4,128,128]{3,2,1,0:T(8,128)S(1)}, f32[48,1024]{1,0:T(8,128)S(1)}) custom-call(s32[4]{0:T(128)S(1)} %pad_add_fusion.place, f32[4,1024]{1,0:T(4,128)S(1)} %get-tuple-element.40.refs_0_.mine, f32[4,1024]{1,0:T(4,128)S(1)} %collective-permute-done.3.refs_1_.other, ...), custom_call_target="tpu_custom_call" | custom-call | tf_op jit(solution)/shard_map/pallas_call | solution.py:237
  43.1 4.9 %collective-permute-start.13 = (f32[48,1024]{1,0:T(8,128)S(1)}, f32[48,1024]{1,0:T(8,128)S(1)}, u32[]{:S(2)}, u32[]{:S(2)}) collective-permute-start(f32[48,1024]{1,0:T(8,128)S(1)} %get-tuple-element.58.sums), channel_id=1, source_target_pairs={{0,16},{16,0},{1,17},{17,1},{2,18},{18,2},{3,19},{19,3},{4,20},{20... | collective-permute-start | bytes 589832 | tf_op jit(solution)/shard_map/ppermute | solution.py:230
  48.0 1.1 %collective-permute-done.13.received = f32[48,1024]{1,0:T(8,128)S(1)} collective-permute-done((f32[48,1024]{1,0:T(8,128)S(1)}, f32[48,1024]{1,0:T(8,128)S(1)}, u32[]{:S(2)}, u32[]{:S(2)}) %collective-permute-start.13) | collective-permute-done | bytes 196640 | tf_op jit(solution)/shard_map/ppermute | solution.py:230
  49.1 5.1 %shard_map.92 = (f32[4,1024]{1,0:T(4,128)S(1)}, f32[24,1024]{1,0:T(8,128)S(1)}, f32[24,1024]{1,0:T(8,128)S(1)}) custom-call(f32[4,1024]{1,0:T(4,128)S(1)} %get-tuple-element.40.refs_0_.mine, f32[4,1024]{1,0:T(4,128)S(1)} %collective-permute-done.3.refs_1_.other, f32[48,1024]{1,0:T(8,128)S(1)} %get-tuple-element.58.sums, ...), custom_call_target="tpu_custom_call" | custom-call | tf_op jit(solution)/shard_map/pallas_call | solution.py:237
  54.2 0.5 collective-permute-start.14
  54.6 0.9 %collective-permute-done.14.received = f32[24,1024]{1,0:T(8,128)S(1)} collective-permute-done((f32[24,1024]{1,0:T(8,128)S(1)}, f32[24,1024]{1,0:T(8,128)S(1)}, u32[]{:S(2)}, u32[]{:S(2)}) %collective-permute-start.14) | collective-permute-done | bytes 98336 | tf_op jit(solution)/shard_map/ppermute | solution.py:230
  55.6 0.7 %shard_map.93 = (f32[3,1024]{1,0:T(4,128)}, f32[1,1024]{1,0:T(1,128)}, f32[16,1024]{1,0:T(8,128)}) custom-call(f32[4,1024]{1,0:T(4,128)S(1)} %get-tuple-element.71.state, f32[24,1024]{1,0:T(8,128)S(1)} %get-tuple-element.72.own, f32[24,1024]{1,0:T(8,128)S(1)} %collective-permute-done.14.received), custom_call_target="tpu_custom_call" | custom-call | tf_op jit(solution)/shard_map/pallas_call | solution.py:237
  (1 shorter events, 0.0 us)
Async XLA Ops:
  1.5 7.7 %collective-permute-start.2 = (f32[96,128]{1,0:T(8,128)S(1)}, f32[96,128]{1,0:T(8,128)S(1)}, u32[]{:S(2)}, u32[]{:S(2)}) collective-permute-start(f32[96,128]{1,0:T(8,128)S(1)} %get-tuple-element.43.refs_0_), channel_id=1, source_target_pairs={{0,3},{1,0},{2,1},{3,2},{4,7},{5,4},{6,5},{7,6},{8,11},{9,8},{10,9... | collective-permute-start | bytes 147464 | tf_op jit(solution)/shard_map/ppermute | solution.py:230
  6.2 4.5 %collective-permute-start.1 = (f32[96,128]{1,0:T(8,128)S(1)}, f32[96,128]{1,0:T(8,128)S(1)}, u32[]{:S(2)}, u32[]{:S(2)}) collective-permute-start(f32[96,128]{1,0:T(8,128)S(1)} %get-tuple-element.43.refs_0_), channel_id=1, source_target_pairs={{0,2},{1,3},{2,0},{3,1},{4,6},{5,7},{6,4},{7,5},{8,10},{9,11},{10,... | collective-permute-start | bytes 147464 | tf_op jit(solution)/shard_map/ppermute | solution.py:230
  6.2 4.7 %collective-permute-start = (f32[96,128]{1,0:T(8,128)S(1)}, f32[96,128]{1,0:T(8,128)S(1)}, u32[]{:S(2)}, u32[]{:S(2)}) collective-permute-start(f32[96,128]{1,0:T(8,128)S(1)} %get-tuple-element.43.refs_0_), channel_id=1, source_target_pairs={{0,1},{1,2},{2,3},{3,0},{4,5},{5,6},{6,7},{7,4},{8,9},{9,10},{10,1... | collective-permute-start | bytes 147464 | tf_op jit(solution)/shard_map/ppermute | solution.py:230
  6.9 2.4 %collective-permute-start.3 = (f32[4,1024]{1,0:T(4,128)S(1)}, f32[4,1024]{1,0:T(4,128)S(1)}, u32[]{:S(2)}, u32[]{:S(2)}) collective-permute-start(f32[4,1024]{1,0:T(4,128)S(1)} %get-tuple-element.40.refs_0_.mine), channel_id=1, source_target_pairs={{0,16},{16,0},{1,17},{17,1},{2,18},{18,2},{3,19},{19,3},{4,20},{20... | collective-permute-start | bytes 49160 | tf_op jit(solution)/shard_map/ppermute | solution.py:230
  11.7 5.2 %collective-permute-start.4 = (f32[264,128]{1,0:T(8,128)S(1)}, f32[264,128]{1,0:T(8,128)S(1)}, u32[]{:S(2)}, u32[]{:S(2)}) collective-permute-start(f32[264,128]{1,0:T(8,128)S(1)} %get-tuple-element.48), channel_id=1, source_target_pairs={{0,4},{4,8},{8,12},{12,0},{1,5},{5,9},{9,13},{13,1},{2,6},{6,10},{... | collective-permute-start | bytes 405512 | tf_op jit(solution)/shard_map/ppermute | solution.py:230
  13.1 6.8 %collective-permute-start.5 = (f32[264,128]{1,0:T(8,128)S(1)}, f32[264,128]{1,0:T(8,128)S(1)}, u32[]{:S(2)}, u32[]{:S(2)}) collective-permute-start(f32[264,128]{1,0:T(8,128)S(1)} %get-tuple-element.49), channel_id=1, source_target_pairs={{0,8},{4,12},{8,0},{12,4},{1,9},{5,13},{9,1},{13,5},{2,10},{6,14},... | collective-permute-start | bytes 405512 | tf_op jit(solution)/shard_map/ppermute | solution.py:230
  15.7 4.9 %collective-permute-start.6 = (f32[264,128]{1,0:T(8,128)S(1)}, f32[264,128]{1,0:T(8,128)S(1)}, u32[]{:S(2)}, u32[]{:S(2)}) collective-permute-start(f32[264,128]{1,0:T(8,128)S(1)} %get-tuple-element.50), channel_id=1, source_target_pairs={{0,12},{4,0},{8,4},{12,8},{1,13},{5,1},{9,5},{13,9},{2,14},{6,2},{... | collective-permute-start | bytes 405512 | tf_op jit(solution)/shard_map/ppermute | solution.py:230
  20.7 7.1 %collective-permute-start.7 = (f32[528,128]{1,0:T(8,128)S(1)}, f32[528,128]{1,0:T(8,128)S(1)}, u32[]{:S(2)}, u32[]{:S(2)}) collective-permute-start(f32[528,128]{1,0:T(8,128)S(1)} %get-tuple-element.51.refs_2_), channel_id=1, source_target_pairs={{0,32},{32,64},{64,96},{96,0},{1,33},{33,65},{65,97},{97,1},{2,34}... | collective-permute-start | bytes 811016 | tf_op jit(solution)/shard_map/ppermute | solution.py:230
  22.0 5.8 %collective-permute-start.10 = (f32[528,128]{1,0:T(8,128)S(1)}, f32[528,128]{1,0:T(8,128)S(1)}, u32[]{:S(2)}, u32[]{:S(2)}) collective-permute-start(f32[528,128]{1,0:T(8,128)S(1)} %get-tuple-element.52.refs_3_), channel_id=1, source_target_pairs={{0,96},{32,0},{64,32},{96,64},{1,97},{33,1},{65,33},{97,65},{2,98}... | collective-permute-start | bytes 811016 | tf_op jit(solution)/shard_map/ppermute | solution.py:230
  23.4 13.8 %collective-permute-start.9 = (f32[528,128]{1,0:T(8,128)S(1)}, f32[528,128]{1,0:T(8,128)S(1)}, u32[]{:S(2)}, u32[]{:S(2)}) collective-permute-start(f32[528,128]{1,0:T(8,128)S(1)} %get-tuple-element.51.refs_2_), channel_id=1, source_target_pairs={{0,96},{32,0},{64,32},{96,64},{1,97},{33,1},{65,33},{97,65},{2,98}... | collective-permute-start | bytes 811016 | tf_op jit(solution)/shard_map/ppermute | solution.py:230
  24.7 9.7 %collective-permute-start.8 = (f32[528,128]{1,0:T(8,128)S(1)}, f32[528,128]{1,0:T(8,128)S(1)}, u32[]{:S(2)}, u32[]{:S(2)}) collective-permute-start(f32[528,128]{1,0:T(8,128)S(1)} %get-tuple-element.52.refs_3_), channel_id=1, source_target_pairs={{0,32},{32,64},{64,96},{96,0},{1,33},{33,65},{65,97},{97,1},{2,34}... | collective-permute-start | bytes 811016 | tf_op jit(solution)/shard_map/ppermute | solution.py:230
  27.8 12.4 %collective-permute-start.11 = (f32[528,128]{1,0:T(8,128)S(1)}, f32[528,128]{1,0:T(8,128)S(1)}, u32[]{:S(2)}, u32[]{:S(2)}) collective-permute-start(f32[528,128]{1,0:T(8,128)S(1)} %collective-permute-done.7.refs_3_), channel_id=1, source_target_pairs={{0,32},{32,64},{64,96},{96,0},{1,33},{33,65},{65,97},{97,1},{2,34}... | collective-permute-start | bytes 811016 | tf_op jit(solution)/shard_map/ppermute | solution.py:230
  28.8 11.4 %collective-permute-start.12 = (f32[528,128]{1,0:T(8,128)S(1)}, f32[528,128]{1,0:T(8,128)S(1)}, u32[]{:S(2)}, u32[]{:S(2)}) collective-permute-start(f32[528,128]{1,0:T(8,128)S(1)} %collective-permute-done.10.refs_4_), channel_id=1, source_target_pairs={{0,96},{32,0},{64,32},{96,64},{1,97},{33,1},{65,33},{97,65},{2,98}... | collective-permute-start | bytes 811016 | tf_op jit(solution)/shard_map/ppermute | solution.py:230
  43.1 6.0 %collective-permute-start.13 = (f32[48,1024]{1,0:T(8,128)S(1)}, f32[48,1024]{1,0:T(8,128)S(1)}, u32[]{:S(2)}, u32[]{:S(2)}) collective-permute-start(f32[48,1024]{1,0:T(8,128)S(1)} %get-tuple-element.58.sums), channel_id=1, source_target_pairs={{0,16},{16,0},{1,17},{17,1},{2,18},{18,2},{3,19},{19,3},{4,20},{20... | collective-permute-start | bytes 589832 | tf_op jit(solution)/shard_map/ppermute | solution.py:230
  54.2 1.4 %collective-permute-start.14 = (f32[24,1024]{1,0:T(8,128)S(1)}, f32[24,1024]{1,0:T(8,128)S(1)}, u32[]{:S(2)}, u32[]{:S(2)}) collective-permute-start(f32[24,1024]{1,0:T(8,128)S(1)} %get-tuple-element.73), channel_id=1, source_target_pairs={{0,16},{16,0},{1,17},{17,1},{2,18},{18,2},{3,19},{19,3},{4,20},{20... | collective-permute-start | bytes 294920 | tf_op jit(solution)/shard_map/ppermute | solution.py:230

commit v11 on v10

--- a/solution.py
+++ b/solution.py
@@ -120,11 +120,10 @@
         add(inner, 1, weight * x)
         add(inner, 2, weight * y)
         add(inner, 3, weight * z)
-    for k in range(SHELLS):
-        cumulative = ramps[k + 1] - ramps[k] - ramps[0]
-        out[o, k : k + 1] = jnp.sum(cumulative, axis=0, keepdims=True)
-    for k in range(4):
-        out[o, SHELLS + k : SHELLS + k + 1] = jnp.sum(inner[k], axis=0, keepdims=True)
+    rows = [jnp.sum(ramps[k + 1] - ramps[k] - ramps[0], axis=0, keepdims=True) for k in range(SHELLS)]
+    rows += [jnp.sum(value, axis=0, keepdims=True) for value in inner]
+    rows += [jnp.zeros_like(rows[0])] * (ROWS - len(rows))
+    out[o] = jnp.concatenate(rows, axis=0)
 
 
 def halo_sums(terms, halo_hot):
@@ -162,35 +161,43 @@
             hit = block_index == spread(half[at + 8 : at + 16], keep, own, slots) + first
             picks.append(jnp.where(hit, 1.0, 0.0).astype(jnp.bfloat16))
         pick = jnp.concatenate(picks, axis=1)
+        pick = jnp.concatenate([pick, pick], axis=0)
+        stacked = []
         for c in range(4):
             parts = [half[a + c * blocks : a + (c + 1) * blocks] for a in range(0, 8 * domain, domain)]
-            high, low = split(jnp.concatenate(parts, axis=0).T, 2)
-            chosen = jnp.dot(high, pick, preferred_element_type=jnp.float32) + jnp.dot(
-                low, pick, preferred_element_type=jnp.float32
-            )
+            stacked.append(jnp.concatenate(split(jnp.concatenate(parts, axis=0), 2), axis=0))
+        chosen = lax.dot_general(
+            jnp.concatenate(stacked, axis=1), pick, (((0,), (0,)), ((), ())), preferred_element_type=jnp.float32
+        )
+        for c in range(4):
             for o in range(2):
-                points[o * 2 + h, c] = chosen[:, o * LANES : (o + 1) * LANES]
-    value = slab_sums([state[...] for state in states], one_hot, halo_hot, points, slot_state, partial)
+                points[o * 2 + h, c] = chosen[c * BLOCK : (c + 1) * BLOCK, o * LANES : (o + 1) * LANES]
+    slot_states([state[...] for state in states], one_hot, slot_state)
+    slab_terms(points, slot_state, partial)
+    value = slab_sums(halo_hot, partial)
     for ref in before:
         value = value + ref[...]
     sums[...] = value
 
 
-def slab_sums(states, one_hot, halo_hot, points, slot_state, partial):
-    tiles = points.shape[0]
+def slot_states(states, one_hot, slot_state):
+    tiles = slot_state.shape[0]
     each = tiles // 2
     width = each * LANES
     for o in range(2):
         got = gather_state(states[o], one_hot[:, o * width : (o + 1) * width])
         for t in range(each):
             slot_state[o * each + t, 0:4] = got[:, t * LANES : (t + 1) * LANES]
-    partial[...] = jnp.zeros_like(partial)
-
-    def one_tile(t, carry):
+
+
+def slab_terms(points, slot_state, partial):
+    for t in range(points.shape[0]):
         tile_sums(slot_state[t], points, t, partial, t)
-        return carry
-
-    lax.fori_loop(0, tiles, one_tile, 0)
+
+
+def slab_sums(halo_hot, partial):
+    each = partial.shape[0] // 2
+    width = each * LANES
     sums = []
     for o in range(2):
         terms = jnp.concatenate([partial[o * each + t] for t in range(each)], axis=1)
@@ -213,10 +220,20 @@
     totals = (sums[:ROWS] + received[ROWS:], sums[ROWS:] + received[:ROWS])
     states = [jnp.concatenate(advance(s[...], t)[:2], axis=0) for s, t in zip((mine, other), totals)]
     state[...] = states[0]
+    one_hots, halo_hots, points = inputs[0::3], inputs[1::3], inputs[2::3]
+    slabs = len(points)
+    each = points[0].shape[0]
+    at = [pl.ds(i * each, each) for i in range(slabs)]
     value = None
-    for i in range(0, len(inputs), 3):
-        part = slab_sums(states, *inputs[i : i + 3], slot_state, partial)
-        value = part if value is None else value + part
+    slot_states(states, one_hots[0], slot_state.at[at[0]])
+    for i in range(slabs):
+        if i + 1 < slabs:
+            slot_states(states, one_hots[i + 1], slot_state.at[at[i + 1]])
+        if i:
+            part = slab_sums(halo_hots[i - 1], partial.at[at[i - 1]])
+            value = part if value is None else value + part
+        slab_terms(points[i], slot_state.at[at[i]], partial.at[at[i]])
+    value = value + slab_sums(halo_hots[-1], partial.at[at[-1]])
     own[...] = value[:ROWS]
     partner[...] = value[ROWS:]
 
@@ -266,7 +283,9 @@
     below_high, above_low = step(high, "x", 1), step(low, "x", -1)
     slabs = [(low, high), (below_low, below_high), (above_low, above_high)]
     each = devices * slots // LANES // 4
-    held = [pltpu.VMEM((each, 8, LANES), jnp.float32), pltpu.VMEM((each, ROWS, LANES), jnp.float32)]
+    held, all_held = (
+        [pltpu.VMEM((n, 8, LANES), jnp.float32), pltpu.VMEM((n, ROWS, LANES), jnp.float32)] for n in (each, 4 * each)
+    )
     outs = [
         jax.ShapeDtypeStruct((halos, each * LANES), jnp.bfloat16),
         jax.ShapeDtypeStruct((each * LANES, halos), jnp.bfloat16),
@@ -289,7 +308,7 @@
         sums[0],
         step(sums[0], "core", 1),
         *kept,
-        scratch=held,
+        scratch=all_held,
     )
     outs = [f32(3, halos), f32(1, halos), f32(SHELLS, halos)]
     centers, radii, profile = call(finish, outs, state, own, step(partner, "core", 1))

time: 56.4 us -> 54.2 us (0.961)
  Pallas kernels: 19.1 us -> 16.3 us
  waiting for transfers between devices: 12.1 us -> 13.3 us
  starting transfers between devices: 24.2 us -> 23.6 us
    pallas_call x9, Pallas kernels: 19.1 us -> 16.3 us  [call(): pl.pallas_call(fn, in_specs=specs, out_specs=out_specs, out_shape=outs, s...]
    ppermute x15, waiting for transfers between devices: 12.1 us -> 13.3 us  [step(): lax.ppermute(value, axis, [(i, (i + by) % size) for i in range(size)])]
    ppermute x15, starting transfers between devices: 24.2 us -> 23.6 us  [step(): lax.ppermute(value, axis, [(i, (i + by) % size) for i in range(size)])]
  transfers between devices with their start and end apart: 15 -> 15, of which waited for: 9 -> 10; matrix products, arithmetic and copies ran while one was open for 0% -> 0% of each run, Pallas kernels for 15% -> 14%
where the time goes in v11:
time: 54.2 us; the launch traced here: 54 us
  starting transfers between devices  23.6 us (44%)
  Pallas kernels  16.3 us (30%)
  waiting for transfers between devices  13.3 us (25%)
  between operations  0.73 us (1%)
    ppermute x15, starting transfers between devices, step(): lax.ppermute(value, axis, [(i, (i + by) % size) for i in range(size)])  23.6 us
    pallas_call x9, Pallas kernels, call(): pl.pallas_call(fn, in_specs=specs, out_specs=out_specs, out_shape=outs, s...  16.3 us
    ppermute x15, waiting for transfers between devices, step(): lax.ppermute(value, axis, [(i, (i + by) % size) for i in range(size)])  13.3 us
  transfers between devices with their start and end apart: 15, of which 10 were waited for; matrix products, arithmetic and copies ran while one was open for 0% of the time, Pallas kernels for 14%

profile of v11, /device:TPU:1, one launch (start us, length us, event | category | flops | bytes accessed | tf_op | source)
XLA Modules:
  0.0 54.0 jit_solution(8856653073367132474)
XLA Ops:
  0.6 0.9 %shard_map.85 = (f32[96,128]{1,0:T(8,128)S(1)}, f32[4,1024]{1,0:T(4,128)S(1)}) custom-call(f32[3,2048]{1,0:T(4,128)} %positions.1, f32[16,128]{1,0:T(8,128)} %bitcast.9, s32[16,128]{1,0:T(8,128)} %bitcast.10, s32[16,128]{1,0:T(8,128)} %bitcast.11, f32[3,1024]{1,0:T(4,128)} %centers.1, f32[1,1024]{1,0:T(1,128)} %bitcast.12), custom_call_target="tpu_custom_call" | custom-call | tf_op jit(solution)/shard_map/pallas_call | solution.py:254
  1.5 4.7 %collective-permute-start.2 = (f32[96,128]{1,0:T(8,128)S(1)}, f32[96,128]{1,0:T(8,128)S(1)}, u32[]{:S(2)}, u32[]{:S(2)}) collective-permute-start(f32[96,128]{1,0:T(8,128)S(1)} %get-tuple-element.43.refs_0_), channel_id=1, source_target_pairs={{0,3},{1,0},{2,1},{3,2},{4,7},{5,4},{6,5},{7,6},{8,11},{9,8},{10,9... | collective-permute-start | bytes 147464 | tf_op jit(solution)/shard_map/ppermute | solution.py:247
  6.2 0.0 collective-permute-start.1
  6.2 0.7 %collective-permute-start = (f32[96,128]{1,0:T(8,128)S(1)}, f32[96,128]{1,0:T(8,128)S(1)}, u32[]{:S(2)}, u32[]{:S(2)}) collective-permute-start(f32[96,128]{1,0:T(8,128)S(1)} %get-tuple-element.43.refs_0_), channel_id=1, source_target_pairs={{0,1},{1,2},{2,3},{3,0},{4,5},{5,6},{6,7},{7,4},{8,9},{9,10},{10,1... | collective-permute-start | bytes 147464 | tf_op jit(solution)/shard_map/ppermute | solution.py:247
  6.9 1.5 %collective-permute-start.3 = (f32[4,1024]{1,0:T(4,128)S(1)}, f32[4,1024]{1,0:T(4,128)S(1)}, u32[]{:S(2)}, u32[]{:S(2)}) collective-permute-start(f32[4,1024]{1,0:T(4,128)S(1)} %get-tuple-element.40.refs_0_.mine), channel_id=1, source_target_pairs={{0,16},{16,0},{1,17},{17,1},{2,18},{18,2},{3,19},{19,3},{4,20},{20... | collective-permute-start | bytes 49160 | tf_op jit(solution)/shard_map/ppermute | solution.py:247
  8.4 0.1 pad_add_fusion.place
  8.4 0.8 %collective-permute-done.3.refs_1_.other = f32[4,1024]{1,0:T(4,128)S(1)} collective-permute-done((f32[4,1024]{1,0:T(4,128)S(1)}, f32[4,1024]{1,0:T(4,128)S(1)}, u32[]{:S(2)}, u32[]{:S(2)}) %collective-permute-start.3) | collective-permute-done | bytes 16416 | tf_op jit(solution)/shard_map/ppermute | solution.py:247
  9.2 0.0 collective-permute-done.2.refs_3_
  9.2 1.5 %collective-permute-done.1.refs_2_ = f32[96,128]{1,0:T(8,128)S(1)} collective-permute-done((f32[96,128]{1,0:T(8,128)S(1)}, f32[96,128]{1,0:T(8,128)S(1)}, u32[]{:S(2)}, u32[]{:S(2)}) %collective-permute-start.1) | collective-permute-done | bytes 49184 | tf_op jit(solution)/shard_map/ppermute | solution.py:247
  10.7 0.1 collective-permute-done.refs_1_
  10.8 0.9 %shard_map.86 = (f32[264,128]{1,0:T(8,128)S(1)}, f32[264,128]{1,0:T(8,128)S(1)}, f32[264,128]{1,0:T(8,128)S(1)}, f32[264,128]{1,0:T(8,128)S(1)}) custom-call(s32[4]{0:T(128)S(1)} %pad_add_fusion.place, f32[96,128]{1,0:T(8,128)S(1)} %get-tuple-element.43.refs_0_, f32[96,128]{1,0:T(8,128)S(1)} %collective-permute-done.refs_1_, ...), custom_call_target="tpu_custom_call" | custom-call | tf_op jit(solution)/shard_map/pallas_call | solution.py:254
  11.7 1.4 %collective-permute-start.4 = (f32[264,128]{1,0:T(8,128)S(1)}, f32[264,128]{1,0:T(8,128)S(1)}, u32[]{:S(2)}, u32[]{:S(2)}) collective-permute-start(f32[264,128]{1,0:T(8,128)S(1)} %get-tuple-element.48), channel_id=1, source_target_pairs={{0,4},{4,8},{8,12},{12,0},{1,5},{5,9},{9,13},{13,1},{2,6},{6,10},{... | collective-permute-start | bytes 405512 | tf_op jit(solution)/shard_map/ppermute | solution.py:247
  13.1 2.6 %collective-permute-start.5 = (f32[264,128]{1,0:T(8,128)S(1)}, f32[264,128]{1,0:T(8,128)S(1)}, u32[]{:S(2)}, u32[]{:S(2)}) collective-permute-start(f32[264,128]{1,0:T(8,128)S(1)} %get-tuple-element.49), channel_id=1, source_target_pairs={{0,8},{4,12},{8,0},{12,4},{1,9},{5,13},{9,1},{13,5},{2,10},{6,14},... | collective-permute-start | bytes 405512 | tf_op jit(solution)/shard_map/ppermute | solution.py:247
  15.7 1.1 %collective-permute-start.6 = (f32[264,128]{1,0:T(8,128)S(1)}, f32[264,128]{1,0:T(8,128)S(1)}, u32[]{:S(2)}, u32[]{:S(2)}) collective-permute-start(f32[264,128]{1,0:T(8,128)S(1)} %get-tuple-element.50), channel_id=1, source_target_pairs={{0,12},{4,0},{8,4},{12,8},{1,13},{5,1},{9,5},{13,9},{2,14},{6,2},{... | collective-permute-start | bytes 405512 | tf_op jit(solution)/shard_map/ppermute | solution.py:247
  16.8 0.1 collective-permute-done.4.refs_1_
  16.9 3.0 %collective-permute-done.5.refs_2_ = f32[264,128]{1,0:T(8,128)S(1)} collective-permute-done((f32[264,128]{1,0:T(8,128)S(1)}, f32[264,128]{1,0:T(8,128)S(1)}, u32[]{:S(2)}, u32[]{:S(2)}) %collective-permute-start.5) | collective-permute-done | bytes 135200 | tf_op jit(solution)/shard_map/ppermute | solution.py:247
  19.9 0.7 %collective-permute-done.6.refs_3_ = f32[264,128]{1,0:T(8,128)S(1)} collective-permute-done((f32[264,128]{1,0:T(8,128)S(1)}, f32[264,128]{1,0:T(8,128)S(1)}, u32[]{:S(2)}, u32[]{:S(2)}) %collective-permute-start.6) | collective-permute-done | bytes 135200 | tf_op jit(solution)/shard_map/ppermute | solution.py:247
  20.7 1.3 %collective-permute-start.7 = (f32[528,128]{1,0:T(8,128)S(1)}, f32[528,128]{1,0:T(8,128)S(1)}, u32[]{:S(2)}, u32[]{:S(2)}) collective-permute-start(f32[528,128]{1,0:T(8,128)S(1)} %get-tuple-element.51.refs_2_), channel_id=1, source_target_pairs={{0,32},{32,64},{64,96},{96,0},{1,33},{33,65},{65,97},{97,1},{2,34}... | collective-permute-start | bytes 811016 | tf_op jit(solution)/shard_map/ppermute | solution.py:247
  22.0 1.5 %collective-permute-start.10 = (f32[528,128]{1,0:T(8,128)S(1)}, f32[528,128]{1,0:T(8,128)S(1)}, u32[]{:S(2)}, u32[]{:S(2)}) collective-permute-start(f32[528,128]{1,0:T(8,128)S(1)} %get-tuple-element.52.refs_3_), channel_id=1, source_target_pairs={{0,96},{32,0},{64,32},{96,64},{1,97},{33,1},{65,33},{97,65},{2,98}... | collective-permute-start | bytes 811016 | tf_op jit(solution)/shard_map/ppermute | solution.py:247
  23.4 1.3 %collective-permute-start.9 = (f32[528,128]{1,0:T(8,128)S(1)}, f32[528,128]{1,0:T(8,128)S(1)}, u32[]{:S(2)}, u32[]{:S(2)}) collective-permute-start(f32[528,128]{1,0:T(8,128)S(1)} %get-tuple-element.51.refs_2_), channel_id=1, source_target_pairs={{0,96},{32,0},{64,32},{96,64},{1,97},{33,1},{65,33},{97,65},{2,98}... | collective-permute-start | bytes 811016 | tf_op jit(solution)/shard_map/ppermute | solution.py:247
  24.7 0.2 collective-permute-start.8
  24.9 2.4 %shard_map.88 = (bf16[1024,512]{1,0:T(8,128)(2,1)S(1)}, bf16[512,1024]{1,0:T(8,128)(2,1)S(1)}, f32[4,4,128,128]{3,2,1,0:T(8,128)S(1)}, f32[48,1024]{1,0:T(8,128)S(1)}) custom-call(s32[4]{0:T(128)S(1)} %pad_add_fusion.place, f32[4,1024]{1,0:T(4,128)S(1)} %get-tuple-element.40.refs_0_.mine, f32[4,1024]{1,0:T(4,128)S(1)} %collective-permute-done.3.refs_1_.other, ...), custom_call_target="tpu_custom_call" | custom-call | tf_op jit(solution)/shard_map/pallas_call | solution.py:254
  27.3 0.0 collective-permute-done.7.refs_3_
  27.3 0.0 collective-permute-done.10.refs_4_
  27.4 1.4 %collective-permute-start.11 = (f32[528,128]{1,0:T(8,128)S(1)}, f32[528,128]{1,0:T(8,128)S(1)}, u32[]{:S(2)}, u32[]{:S(2)}) collective-permute-start(f32[528,128]{1,0:T(8,128)S(1)} %collective-permute-done.7.refs_3_), channel_id=1, source_target_pairs={{0,32},{32,64},{64,96},{96,0},{1,33},{33,65},{65,97},{97,1},{2,34}... | collective-permute-start | bytes 811016 | tf_op jit(solution)/shard_map/ppermute | solution.py:247
  28.8 1.3 %collective-permute-start.12 = (f32[528,128]{1,0:T(8,128)S(1)}, f32[528,128]{1,0:T(8,128)S(1)}, u32[]{:S(2)}, u32[]{:S(2)}) collective-permute-start(f32[528,128]{1,0:T(8,128)S(1)} %collective-permute-done.10.refs_4_), channel_id=1, source_target_pairs={{0,96},{32,0},{64,32},{96,64},{1,97},{33,1},{65,33},{97,65},{2,98}... | collective-permute-start | bytes 811016 | tf_op jit(solution)/shard_map/ppermute | solution.py:247
  30.1 4.3 %collective-permute-done.8.refs_4_ = f32[528,128]{1,0:T(8,128)S(1)} collective-permute-done((f32[528,128]{1,0:T(8,128)S(1)}, f32[528,128]{1,0:T(8,128)S(1)}, u32[]{:S(2)}, u32[]{:S(2)}) %collective-permute-start.8) | collective-permute-done | bytes 270368 | tf_op jit(solution)/shard_map/ppermute | solution.py:247
  34.4 2.4 %shard_map.89 = (bf16[1024,512]{1,0:T(8,128)(2,1)S(1)}, bf16[512,1024]{1,0:T(8,128)(2,1)S(1)}, f32[4,4,128,128]{3,2,1,0:T(8,128)S(1)}, f32[48,1024]{1,0:T(8,128)S(1)}) custom-call(s32[4]{0:T(128)S(1)} %pad_add_fusion.place, f32[4,1024]{1,0:T(4,128)S(1)} %get-tuple-element.40.refs_0_.mine, f32[4,1024]{1,0:T(4,128)S(1)} %collective-permute-done.3.refs_1_.other, ...), custom_call_target="tpu_custom_call" | custom-call | tf_op jit(solution)/shard_map/pallas_call | solution.py:254
  36.8 0.0 collective-permute-done.9.refs_3_
  36.8 2.5 %shard_map.90 = (bf16[1024,512]{1,0:T(8,128)(2,1)S(1)}, bf16[512,1024]{1,0:T(8,128)(2,1)S(1)}, f32[4,4,128,128]{3,2,1,0:T(8,128)S(1)}, f32[48,1024]{1,0:T(8,128)S(1)}) custom-call(s32[4]{0:T(128)S(1)} %pad_add_fusion.place, f32[4,1024]{1,0:T(4,128)S(1)} %get-tuple-element.40.refs_0_.mine, f32[4,1024]{1,0:T(4,128)S(1)} %collective-permute-done.3.refs_1_.other, ...), custom_call_target="tpu_custom_call" | custom-call | tf_op jit(solution)/shard_map/pallas_call | solution.py:254
  39.3 0.8 %collective-permute-done.11.refs_3_ = f32[528,128]{1,0:T(8,128)S(1)} collective-permute-done((f32[528,128]{1,0:T(8,128)S(1)}, f32[528,128]{1,0:T(8,128)S(1)}, u32[]{:S(2)}, u32[]{:S(2)}) %collective-permute-start.11) | collective-permute-done | bytes 270368 | tf_op jit(solution)/shard_map/ppermute | solution.py:247
  40.1 0.0 collective-permute-done.12.refs_4_
  40.1 2.5 %shard_map.91 = (bf16[1024,512]{1,0:T(8,128)(2,1)S(1)}, bf16[512,1024]{1,0:T(8,128)(2,1)S(1)}, f32[4,4,128,128]{3,2,1,0:T(8,128)S(1)}, f32[48,1024]{1,0:T(8,128)S(1)}) custom-call(s32[4]{0:T(128)S(1)} %pad_add_fusion.place, f32[4,1024]{1,0:T(4,128)S(1)} %get-tuple-element.40.refs_0_.mine, f32[4,1024]{1,0:T(4,128)S(1)} %collective-permute-done.3.refs_1_.other, ...), custom_call_target="tpu_custom_call" | custom-call | tf_op jit(solution)/shard_map/pallas_call | solution.py:254
  42.6 4.3 %collective-permute-start.13 = (f32[48,1024]{1,0:T(8,128)S(1)}, f32[48,1024]{1,0:T(8,128)S(1)}, u32[]{:S(2)}, u32[]{:S(2)}) collective-permute-start(f32[48,1024]{1,0:T(8,128)S(1)} %get-tuple-element.58.sums), channel_id=1, source_target_pairs={{0,16},{16,0},{1,17},{17,1},{2,18},{18,2},{3,19},{19,3},{4,20},{20... | collective-permute-start | bytes 589832 | tf_op jit(solution)/shard_map/ppermute | solution.py:247
  46.8 1.1 %collective-permute-done.13.received = f32[48,1024]{1,0:T(8,128)S(1)} collective-permute-done((f32[48,1024]{1,0:T(8,128)S(1)}, f32[48,1024]{1,0:T(8,128)S(1)}, u32[]{:S(2)}, u32[]{:S(2)}) %collective-permute-start.13) | collective-permute-done | bytes 196640 | tf_op jit(solution)/shard_map/ppermute | solution.py:247
  47.9 4.0 %shard_map.92 = (f32[4,1024]{1,0:T(4,128)S(1)}, f32[24,1024]{1,0:T(8,128)S(1)}, f32[24,1024]{1,0:T(8,128)S(1)}) custom-call(f32[4,1024]{1,0:T(4,128)S(1)} %get-tuple-element.40.refs_0_.mine, f32[4,1024]{1,0:T(4,128)S(1)} %collective-permute-done.3.refs_1_.other, f32[48,1024]{1,0:T(8,128)S(1)} %get-tuple-element.58.sums, ...), custom_call_target="tpu_custom_call" | custom-call | tf_op jit(solution)/shard_map/pallas_call | solution.py:254
  51.9 0.5 collective-permute-start.14
  52.4 0.9 %collective-permute-done.14.received = f32[24,1024]{1,0:T(8,128)S(1)} collective-permute-done((f32[24,1024]{1,0:T(8,128)S(1)}, f32[24,1024]{1,0:T(8,128)S(1)}, u32[]{:S(2)}, u32[]{:S(2)}) %collective-permute-start.14) | collective-permute-done | bytes 98336 | tf_op jit(solution)/shard_map/ppermute | solution.py:247
  53.3 0.7 %shard_map.93 = (f32[3,1024]{1,0:T(4,128)}, f32[1,1024]{1,0:T(1,128)}, f32[16,1024]{1,0:T(8,128)}) custom-call(f32[4,1024]{1,0:T(4,128)S(1)} %get-tuple-element.71.state, f32[24,1024]{1,0:T(8,128)S(1)} %get-tuple-element.72.own, f32[24,1024]{1,0:T(8,128)S(1)} %collective-permute-done.14.received), custom_call_target="tpu_custom_call" | custom-call | tf_op jit(solution)/shard_map/pallas_call | solution.py:254
  (1 shorter events, 0.0 us)
Async XLA Ops:
  1.5 7.7 %collective-permute-start.2 = (f32[96,128]{1,0:T(8,128)S(1)}, f32[96,128]{1,0:T(8,128)S(1)}, u32[]{:S(2)}, u32[]{:S(2)}) collective-permute-start(f32[96,128]{1,0:T(8,128)S(1)} %get-tuple-element.43.refs_0_), channel_id=1, source_target_pairs={{0,3},{1,0},{2,1},{3,2},{4,7},{5,4},{6,5},{7,6},{8,11},{9,8},{10,9... | collective-permute-start | bytes 147464 | tf_op jit(solution)/shard_map/ppermute | solution.py:247
  6.2 4.5 %collective-permute-start.1 = (f32[96,128]{1,0:T(8,128)S(1)}, f32[96,128]{1,0:T(8,128)S(1)}, u32[]{:S(2)}, u32[]{:S(2)}) collective-permute-start(f32[96,128]{1,0:T(8,128)S(1)} %get-tuple-element.43.refs_0_), channel_id=1, source_target_pairs={{0,2},{1,3},{2,0},{3,1},{4,6},{5,7},{6,4},{7,5},{8,10},{9,11},{10,... | collective-permute-start | bytes 147464 | tf_op jit(solution)/shard_map/ppermute | solution.py:247
  6.2 4.7 %collective-permute-start = (f32[96,128]{1,0:T(8,128)S(1)}, f32[96,128]{1,0:T(8,128)S(1)}, u32[]{:S(2)}, u32[]{:S(2)}) collective-permute-start(f32[96,128]{1,0:T(8,128)S(1)} %get-tuple-element.43.refs_0_), channel_id=1, source_target_pairs={{0,1},{1,2},{2,3},{3,0},{4,5},{5,6},{6,7},{7,4},{8,9},{9,10},{10,1... | collective-permute-start | bytes 147464 | tf_op jit(solution)/shard_map/ppermute | solution.py:247
  6.9 2.4 %collective-permute-start.3 = (f32[4,1024]{1,0:T(4,128)S(1)}, f32[4,1024]{1,0:T(4,128)S(1)}, u32[]{:S(2)}, u32[]{:S(2)}) collective-permute-start(f32[4,1024]{1,0:T(4,128)S(1)} %get-tuple-element.40.refs_0_.mine), channel_id=1, source_target_pairs={{0,16},{16,0},{1,17},{17,1},{2,18},{18,2},{3,19},{19,3},{4,20},{20... | collective-permute-start | bytes 49160 | tf_op jit(solution)/shard_map/ppermute | solution.py:247
  11.7 5.2 %collective-permute-start.4 = (f32[264,128]{1,0:T(8,128)S(1)}, f32[264,128]{1,0:T(8,128)S(1)}, u32[]{:S(2)}, u32[]{:S(2)}) collective-permute-start(f32[264,128]{1,0:T(8,128)S(1)} %get-tuple-element.48), channel_id=1, source_target_pairs={{0,4},{4,8},{8,12},{12,0},{1,5},{5,9},{9,13},{13,1},{2,6},{6,10},{... | collective-permute-start | bytes 405512 | tf_op jit(solution)/shard_map/ppermute | solution.py:247
  13.1 6.8 %collective-permute-start.5 = (f32[264,128]{1,0:T(8,128)S(1)}, f32[264,128]{1,0:T(8,128)S(1)}, u32[]{:S(2)}, u32[]{:S(2)}) collective-permute-start(f32[264,128]{1,0:T(8,128)S(1)} %get-tuple-element.49), channel_id=1, source_target_pairs={{0,8},{4,12},{8,0},{12,4},{1,9},{5,13},{9,1},{13,5},{2,10},{6,14},... | collective-permute-start | bytes 405512 | tf_op jit(solution)/shard_map/ppermute | solution.py:247
  15.7 4.9 %collective-permute-start.6 = (f32[264,128]{1,0:T(8,128)S(1)}, f32[264,128]{1,0:T(8,128)S(1)}, u32[]{:S(2)}, u32[]{:S(2)}) collective-permute-start(f32[264,128]{1,0:T(8,128)S(1)} %get-tuple-element.50), channel_id=1, source_target_pairs={{0,12},{4,0},{8,4},{12,8},{1,13},{5,1},{9,5},{13,9},{2,14},{6,2},{... | collective-permute-start | bytes 405512 | tf_op jit(solution)/shard_map/ppermute | solution.py:247
  20.7 6.6 %collective-permute-start.7 = (f32[528,128]{1,0:T(8,128)S(1)}, f32[528,128]{1,0:T(8,128)S(1)}, u32[]{:S(2)}, u32[]{:S(2)}) collective-permute-start(f32[528,128]{1,0:T(8,128)S(1)} %get-tuple-element.51.refs_2_), channel_id=1, source_target_pairs={{0,32},{32,64},{64,96},{96,0},{1,33},{33,65},{65,97},{97,1},{2,34}... | collective-permute-start | bytes 811016 | tf_op jit(solution)/shard_map/ppermute | solution.py:247
  22.0 5.4 %collective-permute-start.10 = (f32[528,128]{1,0:T(8,128)S(1)}, f32[528,128]{1,0:T(8,128)S(1)}, u32[]{:S(2)}, u32[]{:S(2)}) collective-permute-start(f32[528,128]{1,0:T(8,128)S(1)} %get-tuple-element.52.refs_3_), channel_id=1, source_target_pairs={{0,96},{32,0},{64,32},{96,64},{1,97},{33,1},{65,33},{97,65},{2,98}... | collective-permute-start | bytes 811016 | tf_op jit(solution)/shard_map/ppermute | solution.py:247
  23.4 13.4 %collective-permute-start.9 = (f32[528,128]{1,0:T(8,128)S(1)}, f32[528,128]{1,0:T(8,128)S(1)}, u32[]{:S(2)}, u32[]{:S(2)}) collective-permute-start(f32[528,128]{1,0:T(8,128)S(1)} %get-tuple-element.51.refs_2_), channel_id=1, source_target_pairs={{0,96},{32,0},{64,32},{96,64},{1,97},{33,1},{65,33},{97,65},{2,98}... | collective-permute-start | bytes 811016 | tf_op jit(solution)/shard_map/ppermute | solution.py:247
  24.7 9.7 %collective-permute-start.8 = (f32[528,128]{1,0:T(8,128)S(1)}, f32[528,128]{1,0:T(8,128)S(1)}, u32[]{:S(2)}, u32[]{:S(2)}) collective-permute-start(f32[528,128]{1,0:T(8,128)S(1)} %get-tuple-element.52.refs_3_), channel_id=1, source_target_pairs={{0,32},{32,64},{64,96},{96,0},{1,33},{33,65},{65,97},{97,1},{2,34}... | collective-permute-start | bytes 811016 | tf_op jit(solution)/shard_map/ppermute | solution.py:247
  27.4 12.7 %collective-permute-start.11 = (f32[528,128]{1,0:T(8,128)S(1)}, f32[528,128]{1,0:T(8,128)S(1)}, u32[]{:S(2)}, u32[]{:S(2)}) collective-permute-start(f32[528,128]{1,0:T(8,128)S(1)} %collective-permute-done.7.refs_3_), channel_id=1, source_target_pairs={{0,32},{32,64},{64,96},{96,0},{1,33},{33,65},{65,97},{97,1},{2,34}... | collective-permute-start | bytes 811016 | tf_op jit(solution)/shard_map/ppermute | solution.py:247
  28.8 11.3 %collective-permute-start.12 = (f32[528,128]{1,0:T(8,128)S(1)}, f32[528,128]{1,0:T(8,128)S(1)}, u32[]{:S(2)}, u32[]{:S(2)}) collective-permute-start(f32[528,128]{1,0:T(8,128)S(1)} %collective-permute-done.10.refs_4_), channel_id=1, source_target_pairs={{0,96},{32,0},{64,32},{96,64},{1,97},{33,1},{65,33},{97,65},{2,98}... | collective-permute-start | bytes 811016 | tf_op jit(solution)/shard_map/ppermute | solution.py:247
  42.6 5.4 %collective-permute-start.13 = (f32[48,1024]{1,0:T(8,128)S(1)}, f32[48,1024]{1,0:T(8,128)S(1)}, u32[]{:S(2)}, u32[]{:S(2)}) collective-permute-start(f32[48,1024]{1,0:T(8,128)S(1)} %get-tuple-element.58.sums), channel_id=1, source_target_pairs={{0,16},{16,0},{1,17},{17,1},{2,18},{18,2},{3,19},{19,3},{4,20},{20... | collective-permute-start | bytes 589832 | tf_op jit(solution)/shard_map/ppermute | solution.py:247
  51.9 1.4 %collective-permute-start.14 = (f32[24,1024]{1,0:T(8,128)S(1)}, f32[24,1024]{1,0:T(8,128)S(1)}, u32[]{:S(2)}, u32[]{:S(2)}) collective-permute-start(f32[24,1024]{1,0:T(8,128)S(1)} %get-tuple-element.73), channel_id=1, source_target_pairs={{0,16},{16,0},{1,17},{17,1},{2,18},{18,2},{3,19},{19,3},{4,20},{20... | collective-permute-start | bytes 294920 | tf_op jit(solution)/shard_map/ppermute | solution.py:247

commit v12 on v11

--- a/solution.py
+++ b/solution.py
@@ -29,10 +29,11 @@
     return parts
 
 
-def gather_state(state, one_hot):
-    stacked = jnp.concatenate([s.astype(jnp.float32) for s in split(state, 3)] + [jnp.zeros_like(state)], axis=0)
-    got = jnp.dot(stacked.astype(jnp.bfloat16), one_hot, preferred_element_type=jnp.float32)
-    return got[0:4] + got[4:8] + got[8:12]
+def state_rows(states):
+    rows = []
+    for state in states:
+        rows += [part.astype(jnp.float32) for part in split(state, 3)] + [jnp.zeros_like(state)]
+    return jnp.concatenate(rows, axis=0).astype(jnp.bfloat16)
 
 
 def spread(rows, keep, own, slots):
@@ -126,16 +127,9 @@
     out[o] = jnp.concatenate(rows, axis=0)
 
 
-def halo_sums(terms, halo_hot):
-    high, low = [part.astype(jnp.float32) for part in split(terms, 2)]
-    both = jnp.concatenate([high, low], axis=0).astype(jnp.bfloat16)
-    sums = jnp.dot(both, halo_hot, preferred_element_type=jnp.float32)
-    return sums[:ROWS] + sums[ROWS:]
-
-
 def first_pass(slots, blocks, place, *refs):
     inputs, (one_hot, halo_hot, points, sums, slot_state, partial) = refs[:-6], refs[-6:]
-    states, before, halves = inputs[:2], inputs[2:-2], inputs[-2:]
+    states, before, half = inputs[:2], inputs[2:-1], inputs[-1]
     halos = states[0].shape[1]
     domain = 4 * blocks
     count = 8 * blocks
@@ -145,34 +139,33 @@
     across = lax.broadcasted_iota(jnp.int32, (LANES, halos), 1).astype(jnp.float32)
     block_index = lax.broadcasted_iota(jnp.int32, (count, LANES), 0).astype(jnp.float32)
     first = (lax.broadcasted_iota(jnp.int32, (1, LANES), 1) // slots * blocks).astype(jnp.float32)
-    for h, half in enumerate(halves):
-        picks = []
+    picks = []
+    for o in range(2):
+        t = o
+        at = 8 * domain
+        keep = lane_group == place[0] * 2 + (place[1] if o == 0 else 1 - place[1])
+        halo_row = spread(half[at : at + 8], keep, own, slots)
+        hit = halo_index == halo_row
+        one_hot[:, t * LANES : (t + 1) * LANES] = jnp.where(hit, 1.0, 0.0).astype(jnp.bfloat16)
+        column = jnp.broadcast_to(halo_row, (LANES, LANES)).T
+        for a in range(0, halos, LANES):
+            hit = across[:, a : a + LANES] == column
+            halo_hot[t * LANES : (t + 1) * LANES, a : a + LANES] = jnp.where(hit, 1.0, 0.0).astype(jnp.bfloat16)
+        hit = block_index == spread(half[at + 8 : at + 16], keep, own, slots) + first
+        picks.append(jnp.where(hit, 1.0, 0.0).astype(jnp.bfloat16))
+    pick = jnp.concatenate(picks, axis=1)
+    pick = jnp.concatenate([pick, pick], axis=0)
+    stacked = []
+    for c in range(4):
+        parts = [half[a + c * blocks : a + (c + 1) * blocks] for a in range(0, 8 * domain, domain)]
+        stacked.append(jnp.concatenate(split(jnp.concatenate(parts, axis=0), 2), axis=0))
+    chosen = lax.dot_general(
+        jnp.concatenate(stacked, axis=1), pick, (((0,), (0,)), ((), ())), preferred_element_type=jnp.float32
+    )
+    for c in range(4):
         for o in range(2):
-            t = o * 2 + h
-            at = 8 * domain
-            keep = lane_group == place[0] * 2 + (place[1] if o == 0 else 1 - place[1])
-            halo_row = spread(half[at : at + 8], keep, own, slots)
-            hit = halo_index == halo_row
-            one_hot[:, t * LANES : (t + 1) * LANES] = jnp.where(hit, 1.0, 0.0).astype(jnp.bfloat16)
-            column = jnp.broadcast_to(halo_row, (LANES, LANES)).T
-            for a in range(0, halos, LANES):
-                hit = across[:, a : a + LANES] == column
-                halo_hot[t * LANES : (t + 1) * LANES, a : a + LANES] = jnp.where(hit, 1.0, 0.0).astype(jnp.bfloat16)
-            hit = block_index == spread(half[at + 8 : at + 16], keep, own, slots) + first
-            picks.append(jnp.where(hit, 1.0, 0.0).astype(jnp.bfloat16))
-        pick = jnp.concatenate(picks, axis=1)
-        pick = jnp.concatenate([pick, pick], axis=0)
-        stacked = []
-        for c in range(4):
-            parts = [half[a + c * blocks : a + (c + 1) * blocks] for a in range(0, 8 * domain, domain)]
-            stacked.append(jnp.concatenate(split(jnp.concatenate(parts, axis=0), 2), axis=0))
-        chosen = lax.dot_general(
-            jnp.concatenate(stacked, axis=1), pick, (((0,), (0,)), ((), ())), preferred_element_type=jnp.float32
-        )
-        for c in range(4):
-            for o in range(2):
-                points[o * 2 + h, c] = chosen[c * BLOCK : (c + 1) * BLOCK, o * LANES : (o + 1) * LANES]
-    slot_states([state[...] for state in states], one_hot, slot_state)
+            points[o, c] = chosen[c * BLOCK : (c + 1) * BLOCK, o * LANES : (o + 1) * LANES]
+    slot_states(state_rows([state[...] for state in states]), one_hot, slot_state)
     slab_terms(points, slot_state, partial)
     value = slab_sums(halo_hot, partial)
     for ref in before:
@@ -180,14 +173,11 @@
     sums[...] = value
 
 
-def slot_states(states, one_hot, slot_state):
-    tiles = slot_state.shape[0]
-    each = tiles // 2
-    width = each * LANES
+def slot_states(rows, one_hot, slot_state):
+    got = jnp.dot(rows, one_hot[...], preferred_element_type=jnp.float32)
     for o in range(2):
-        got = gather_state(states[o], one_hot[:, o * width : (o + 1) * width])
-        for t in range(each):
-            slot_state[o * each + t, 0:4] = got[:, t * LANES : (t + 1) * LANES]
+        part = got[o * 16 : (o + 1) * 16, o * LANES : (o + 1) * LANES]
+        slot_state[o, 0:4] = part[0:4] + part[4:8] + part[8:12]
 
 
 def slab_terms(points, slot_state, partial):
@@ -196,13 +186,14 @@
 
 
 def slab_sums(halo_hot, partial):
-    each = partial.shape[0] // 2
-    width = each * LANES
-    sums = []
+    rows = []
     for o in range(2):
-        terms = jnp.concatenate([partial[o * each + t] for t in range(each)], axis=1)
-        sums.append(halo_sums(terms, halo_hot[o * width : (o + 1) * width]))
-    return jnp.concatenate(sums, axis=0)
+        for part in split(partial[o], 2):
+            value = part.astype(jnp.float32)
+            zero = jnp.zeros_like(value)
+            rows.append(jnp.concatenate([value, zero] if o == 0 else [zero, value], axis=1))
+    sums = jnp.dot(jnp.concatenate(rows, axis=0).astype(jnp.bfloat16), halo_hot[...], preferred_element_type=jnp.float32)
+    return jnp.concatenate([sums[:ROWS] + sums[ROWS : 2 * ROWS], sums[2 * ROWS : 3 * ROWS] + sums[3 * ROWS :]], axis=0)
 
 
 def advance(state, sums):
@@ -225,10 +216,11 @@
     each = points[0].shape[0]
     at = [pl.ds(i * each, each) for i in range(slabs)]
     value = None
-    slot_states(states, one_hots[0], slot_state.at[at[0]])
+    rows = state_rows(states)
+    slot_states(rows, one_hots[0], slot_state.at[at[0]])
     for i in range(slabs):
         if i + 1 < slabs:
-            slot_states(states, one_hots[i + 1], slot_state.at[at[i + 1]])
+            slot_states(rows, one_hots[i + 1], slot_state.at[at[i + 1]])
         if i:
             part = slab_sums(halo_hots[i - 1], partial.at[at[i - 1]])
             value = part if value is None else value + part
@@ -281,10 +273,11 @@
     low, high = call(merge_y, [f32(8 * domain + 16, LANES)] * 2, *along_y)
     below_low, above_high = step(low, "x", 1), step(high, "x", -1)
     below_high, above_low = step(high, "x", 1), step(low, "x", -1)
-    slabs = [(low, high), (below_low, below_high), (above_low, above_high)]
-    each = devices * slots // LANES // 4
+    halves = [low, high, below_low, above_high, below_high, above_low]
+    each = 2
+    units = devices * slots // LANES // each
     held, all_held = (
-        [pltpu.VMEM((n, 8, LANES), jnp.float32), pltpu.VMEM((n, ROWS, LANES), jnp.float32)] for n in (each, 4 * each)
+        [pltpu.VMEM((n, 8, LANES), jnp.float32), pltpu.VMEM((n, ROWS, LANES), jnp.float32)] for n in (each, units * each)
     )
     outs = [
         jax.ShapeDtypeStruct((halos, each * LANES), jnp.bfloat16),
@@ -293,12 +286,12 @@
         f32(2 * ROWS, halos),
     ]
     kept, sums = [], []
-    for slab in slabs:
-        *arrays, total = call(functools.partial(first_pass, slots, blocks), outs, place, state, other, *sums, *slab, scratch=held)
+    for n in range(units):
+        *arrays, total = call(functools.partial(first_pass, slots, blocks), outs, place, state, other, *sums, halves[n], scratch=held)
         kept.extend(arrays)
-        if not sums:
+        if n == 1:
             first, second, _ = lax.optimization_barrier((below_low, above_high, total))
-            slabs.append((step(first, "x", 1), step(second, "x", -1)))
+            halves += [step(first, "x", 1), step(second, "x", -1)]
         sums = [total]
     state, own, partner = call(
         second_pass,

time: 54.2 us -> 55.6 us (1.026)
  Pallas kernels: 16.3 us -> 20.3 us
  waiting for transfers between devices: 13.3 us -> 10.4 us
    pallas_call x9 -> x13, Pallas kernels: 16.3 us -> 20.3 us  [call(): pl.pallas_call(fn, in_specs=specs, out_specs=out_specs, out_shape=outs, s...]
    ppermute x15, waiting for transfers between devices: 13.3 us -> 10.4 us  [step(): lax.ppermute(value, axis, [(i, (i + by) % size) for i in range(size)])]
  transfers between devices with their start and end apart: 15 -> 15, of which waited for: 10 -> 9; matrix products, arithmetic and copies ran while one was open for 0% -> 0% of each run, Pallas kernels for 14% -> 21%
where the time goes in v12:
time: 55.6 us; the launch traced here: 55.5 us
  starting transfers between devices  23.9 us (43%)
  Pallas kernels  20.3 us (37%)
  waiting for transfers between devices  10.4 us (19%)
  between operations  0.76 us (1%)
    ppermute x15, starting transfers between devices, step(): lax.ppermute(value, axis, [(i, (i + by) % size) for i in range(size)])  23.9 us
    pallas_call x13, Pallas kernels, call(): pl.pallas_call(fn, in_specs=specs, out_specs=out_specs, out_shape=outs, s...  20.3 us
    ppermute x15, waiting for transfers between devices, step(): lax.ppermute(value, axis, [(i, (i + by) % size) for i in range(size)])  10.4 us
  transfers between devices with their start and end apart: 15, of which 9 were waited for; matrix products, arithmetic and copies ran while one was open for 0% of the time, Pallas kernels for 21%

profile of v12, /device:TPU:1, one launch (start us, length us, event | category | flops | bytes accessed | tf_op | source)
XLA Modules:
  0.0 55.5 jit_solution(12943524511935808231)
XLA Ops:
  0.6 0.9 %shard_map.85 = (f32[96,128]{1,0:T(8,128)S(1)}, f32[4,1024]{1,0:T(4,128)S(1)}) custom-call(f32[3,2048]{1,0:T(4,128)} %positions.1, f32[16,128]{1,0:T(8,128)} %bitcast.9, s32[16,128]{1,0:T(8,128)} %bitcast.10, s32[16,128]{1,0:T(8,128)} %bitcast.11, f32[3,1024]{1,0:T(4,128)} %centers.1, f32[1,1024]{1,0:T(1,128)} %bitcast.12), custom_call_target="tpu_custom_call" | custom-call | tf_op jit(solution)/shard_map/pallas_call | solution.py:246
  1.5 4.7 %collective-permute-start.2 = (f32[96,128]{1,0:T(8,128)S(1)}, f32[96,128]{1,0:T(8,128)S(1)}, u32[]{:S(2)}, u32[]{:S(2)}) collective-permute-start(f32[96,128]{1,0:T(8,128)S(1)} %get-tuple-element.59.refs_0_), channel_id=1, source_target_pairs={{0,3},{1,0},{2,1},{3,2},{4,7},{5,4},{6,5},{7,6},{8,11},{9,8},{10,9... | collective-permute-start | bytes 147464 | tf_op jit(solution)/shard_map/ppermute | solution.py:239
  6.2 0.0 collective-permute-start.1
  6.2 0.7 %collective-permute-start = (f32[96,128]{1,0:T(8,128)S(1)}, f32[96,128]{1,0:T(8,128)S(1)}, u32[]{:S(2)}, u32[]{:S(2)}) collective-permute-start(f32[96,128]{1,0:T(8,128)S(1)} %get-tuple-element.59.refs_0_), channel_id=1, source_target_pairs={{0,1},{1,2},{2,3},{3,0},{4,5},{5,6},{6,7},{7,4},{8,9},{9,10},{10,1... | collective-permute-start | bytes 147464 | tf_op jit(solution)/shard_map/ppermute | solution.py:239
  6.9 1.5 %collective-permute-start.3 = (f32[4,1024]{1,0:T(4,128)S(1)}, f32[4,1024]{1,0:T(4,128)S(1)}, u32[]{:S(2)}, u32[]{:S(2)}) collective-permute-start(f32[4,1024]{1,0:T(4,128)S(1)} %get-tuple-element.56.refs_0_.mine), channel_id=1, source_target_pairs={{0,16},{16,0},{1,17},{17,1},{2,18},{18,2},{3,19},{19,3},{4,20},{20... | collective-permute-start | bytes 49160 | tf_op jit(solution)/shard_map/ppermute | solution.py:239
  8.4 0.1 pad_add_fusion.place
  8.4 0.8 %collective-permute-done.3.refs_1_.other = f32[4,1024]{1,0:T(4,128)S(1)} collective-permute-done((f32[4,1024]{1,0:T(4,128)S(1)}, f32[4,1024]{1,0:T(4,128)S(1)}, u32[]{:S(2)}, u32[]{:S(2)}) %collective-permute-start.3) | collective-permute-done | bytes 16416 | tf_op jit(solution)/shard_map/ppermute | solution.py:239
  9.2 0.0 collective-permute-done.2.refs_3_
  9.2 1.5 %collective-permute-done.1.refs_2_ = f32[96,128]{1,0:T(8,128)S(1)} collective-permute-done((f32[96,128]{1,0:T(8,128)S(1)}, f32[96,128]{1,0:T(8,128)S(1)}, u32[]{:S(2)}, u32[]{:S(2)}) %collective-permute-start.1) | collective-permute-done | bytes 49184 | tf_op jit(solution)/shard_map/ppermute | solution.py:239
  10.7 0.1 collective-permute-done.refs_1_
  10.8 0.9 %shard_map.86 = (f32[264,128]{1,0:T(8,128)S(1)}, f32[264,128]{1,0:T(8,128)S(1)}, f32[264,128]{1,0:T(8,128)S(1)}, f32[264,128]{1,0:T(8,128)S(1)}) custom-call(s32[4]{0:T(128)S(1)} %pad_add_fusion.place, f32[96,128]{1,0:T(8,128)S(1)} %get-tuple-element.59.refs_0_, f32[96,128]{1,0:T(8,128)S(1)} %collective-permute-done.refs_1_, ...), custom_call_target="tpu_custom_call" | custom-call | tf_op jit(solution)/shard_map/pallas_call | solution.py:246
  11.7 1.4 %collective-permute-start.4 = (f32[264,128]{1,0:T(8,128)S(1)}, f32[264,128]{1,0:T(8,128)S(1)}, u32[]{:S(2)}, u32[]{:S(2)}) collective-permute-start(f32[264,128]{1,0:T(8,128)S(1)} %get-tuple-element.64), channel_id=1, source_target_pairs={{0,4},{4,8},{8,12},{12,0},{1,5},{5,9},{9,13},{13,1},{2,6},{6,10},{... | collective-permute-start | bytes 405512 | tf_op jit(solution)/shard_map/ppermute | solution.py:239
  13.1 2.6 %collective-permute-start.5 = (f32[264,128]{1,0:T(8,128)S(1)}, f32[264,128]{1,0:T(8,128)S(1)}, u32[]{:S(2)}, u32[]{:S(2)}) collective-permute-start(f32[264,128]{1,0:T(8,128)S(1)} %get-tuple-element.65), channel_id=1, source_target_pairs={{0,8},{4,12},{8,0},{12,4},{1,9},{5,13},{9,1},{13,5},{2,10},{6,14},... | collective-permute-start | bytes 405512 | tf_op jit(solution)/shard_map/ppermute | solution.py:239
  15.7 1.1 %collective-permute-start.6 = (f32[264,128]{1,0:T(8,128)S(1)}, f32[264,128]{1,0:T(8,128)S(1)}, u32[]{:S(2)}, u32[]{:S(2)}) collective-permute-start(f32[264,128]{1,0:T(8,128)S(1)} %get-tuple-element.66), channel_id=1, source_target_pairs={{0,12},{4,0},{8,4},{12,8},{1,13},{5,1},{9,5},{13,9},{2,14},{6,2},{... | collective-permute-start | bytes 405512 | tf_op jit(solution)/shard_map/ppermute | solution.py:239
  16.8 0.1 collective-permute-done.4.refs_1_
  16.9 3.0 %collective-permute-done.5.refs_2_ = f32[264,128]{1,0:T(8,128)S(1)} collective-permute-done((f32[264,128]{1,0:T(8,128)S(1)}, f32[264,128]{1,0:T(8,128)S(1)}, u32[]{:S(2)}, u32[]{:S(2)}) %collective-permute-start.5) | collective-permute-done | bytes 135200 | tf_op jit(solution)/shard_map/ppermute | solution.py:239
  19.9 0.7 %collective-permute-done.6.refs_3_ = f32[264,128]{1,0:T(8,128)S(1)} collective-permute-done((f32[264,128]{1,0:T(8,128)S(1)}, f32[264,128]{1,0:T(8,128)S(1)}, u32[]{:S(2)}, u32[]{:S(2)}) %collective-permute-start.6) | collective-permute-done | bytes 135200 | tf_op jit(solution)/shard_map/ppermute | solution.py:239
  20.7 1.3 %collective-permute-start.7 = (f32[528,128]{1,0:T(8,128)S(1)}, f32[528,128]{1,0:T(8,128)S(1)}, u32[]{:S(2)}, u32[]{:S(2)}) collective-permute-start(f32[528,128]{1,0:T(8,128)S(1)} %get-tuple-element.67.refs_2_), channel_id=1, source_target_pairs={{0,32},{32,64},{64,96},{96,0},{1,33},{33,65},{65,97},{97,1},{2,34}... | collective-permute-start | bytes 811016 | tf_op jit(solution)/shard_map/ppermute | solution.py:239
  22.0 1.5 %collective-permute-start.8 = (f32[528,128]{1,0:T(8,128)S(1)}, f32[528,128]{1,0:T(8,128)S(1)}, u32[]{:S(2)}, u32[]{:S(2)}) collective-permute-start(f32[528,128]{1,0:T(8,128)S(1)} %get-tuple-element.69.refs_3_), channel_id=1, source_target_pairs={{0,96},{32,0},{64,32},{96,64},{1,97},{33,1},{65,33},{97,65},{2,98}... | collective-permute-start | bytes 811016 | tf_op jit(solution)/shard_map/ppermute | solution.py:239
  23.4 1.3 %collective-permute-start.10 = (f32[528,128]{1,0:T(8,128)S(1)}, f32[528,128]{1,0:T(8,128)S(1)}, u32[]{:S(2)}, u32[]{:S(2)}) collective-permute-start(f32[528,128]{1,0:T(8,128)S(1)} %get-tuple-element.67.refs_2_), channel_id=1, source_target_pairs={{0,96},{32,0},{64,32},{96,64},{1,97},{33,1},{65,33},{97,65},{2,98}... | collective-permute-start | bytes 811016 | tf_op jit(solution)/shard_map/ppermute | solution.py:239
  24.7 0.2 collective-permute-start.9
  24.9 1.7 %shard_map.88 = (bf16[1024,256]{1,0:T(8,128)(2,1)S(1)}, bf16[256,1024]{1,0:T(8,128)(2,1)S(1)}, f32[2,4,128,128]{3,2,1,0:T(8,128)S(1)}, f32[48,1024]{1,0:T(8,128)S(1)}) custom-call(s32[4]{0:T(128)S(1)} %pad_add_fusion.place, f32[4,1024]{1,0:T(4,128)S(1)} %get-tuple-element.56.refs_0_.mine, f32[4,1024]{1,0:T(4,128)S(1)} %collective-permute-done.3.refs_1_.other, ...), custom_call_target="tpu_custom_call" | custom-call | tf_op jit(solution)/shard_map/pallas_call | solution.py:246
  26.6 1.7 %shard_map.89 = (bf16[1024,256]{1,0:T(8,128)(2,1)S(1)}, bf16[256,1024]{1,0:T(8,128)(2,1)S(1)}, f32[2,4,128,128]{3,2,1,0:T(8,128)S(1)}, f32[48,1024]{1,0:T(8,128)S(1)}) custom-call(s32[4]{0:T(128)S(1)} %pad_add_fusion.place, f32[4,1024]{1,0:T(4,128)S(1)} %get-tuple-element.56.refs_0_.mine, f32[4,1024]{1,0:T(4,128)S(1)} %collective-permute-done.3.refs_1_.other, ...), custom_call_target="tpu_custom_call" | custom-call | tf_op jit(solution)/shard_map/pallas_call | solution.py:246
  28.3 0.0 collective-permute-done.7.refs_3_
  28.3 0.0 collective-permute-done.8.refs_3_
  28.3 0.5 collective-permute-start.11
  28.8 2.3 %collective-permute-start.12 = (f32[528,128]{1,0:T(8,128)S(1)}, f32[528,128]{1,0:T(8,128)S(1)}, u32[]{:S(2)}, u32[]{:S(2)}) collective-permute-start(f32[528,128]{1,0:T(8,128)S(1)} %collective-permute-done.8.refs_3_), channel_id=1, source_target_pairs={{0,96},{32,0},{64,32},{96,64},{1,97},{33,1},{65,33},{97,65},{2,98}... | collective-permute-start | bytes 811016 | tf_op jit(solution)/shard_map/ppermute | solution.py:239
  31.1 1.7 %shard_map.90 = (bf16[1024,256]{1,0:T(8,128)(2,1)S(1)}, bf16[256,1024]{1,0:T(8,128)(2,1)S(1)}, f32[2,4,128,128]{3,2,1,0:T(8,128)S(1)}, f32[48,1024]{1,0:T(8,128)S(1)}) custom-call(s32[4]{0:T(128)S(1)} %pad_add_fusion.place, f32[4,1024]{1,0:T(4,128)S(1)} %get-tuple-element.56.refs_0_.mine, f32[4,1024]{1,0:T(4,128)S(1)} %collective-permute-done.3.refs_1_.other, ...), custom_call_target="tpu_custom_call" | custom-call | tf_op jit(solution)/shard_map/pallas_call | solution.py:246
  32.8 1.7 %shard_map.91 = (bf16[1024,256]{1,0:T(8,128)(2,1)S(1)}, bf16[256,1024]{1,0:T(8,128)(2,1)S(1)}, f32[2,4,128,128]{3,2,1,0:T(8,128)S(1)}, f32[48,1024]{1,0:T(8,128)S(1)}) custom-call(s32[4]{0:T(128)S(1)} %pad_add_fusion.place, f32[4,1024]{1,0:T(4,128)S(1)} %get-tuple-element.56.refs_0_.mine, f32[4,1024]{1,0:T(4,128)S(1)} %collective-permute-done.3.refs_1_.other, ...), custom_call_target="tpu_custom_call" | custom-call | tf_op jit(solution)/shard_map/pallas_call | solution.py:246
  34.5 0.0 collective-permute-done.9.refs_3_
  34.5 1.7 %shard_map.92 = (bf16[1024,256]{1,0:T(8,128)(2,1)S(1)}, bf16[256,1024]{1,0:T(8,128)(2,1)S(1)}, f32[2,4,128,128]{3,2,1,0:T(8,128)S(1)}, f32[48,1024]{1,0:T(8,128)S(1)}) custom-call(s32[4]{0:T(128)S(1)} %pad_add_fusion.place, f32[4,1024]{1,0:T(4,128)S(1)} %get-tuple-element.56.refs_0_.mine, f32[4,1024]{1,0:T(4,128)S(1)} %collective-permute-done.3.refs_1_.other, ...), custom_call_target="tpu_custom_call" | custom-call | tf_op jit(solution)/shard_map/pallas_call | solution.py:246
  36.2 0.0 collective-permute-done.10.refs_3_
  36.2 1.7 %shard_map.93 = (bf16[1024,256]{1,0:T(8,128)(2,1)S(1)}, bf16[256,1024]{1,0:T(8,128)(2,1)S(1)}, f32[2,4,128,128]{3,2,1,0:T(8,128)S(1)}, f32[48,1024]{1,0:T(8,128)S(1)}) custom-call(s32[4]{0:T(128)S(1)} %pad_add_fusion.place, f32[4,1024]{1,0:T(4,128)S(1)} %get-tuple-element.56.refs_0_.mine, f32[4,1024]{1,0:T(4,128)S(1)} %collective-permute-done.3.refs_1_.other, ...), custom_call_target="tpu_custom_call" | custom-call | tf_op jit(solution)/shard_map/pallas_call | solution.py:246
  37.9 2.1 %collective-permute-done.11.refs_3_ = f32[528,128]{1,0:T(8,128)S(1)} collective-permute-done((f32[528,128]{1,0:T(8,128)S(1)}, f32[528,128]{1,0:T(8,128)S(1)}, u32[]{:S(2)}, u32[]{:S(2)}) %collective-permute-start.11) | collective-permute-done | bytes 270368 | tf_op jit(solution)/shard_map/ppermute | solution.py:239
  40.1 1.7 %shard_map.94 = (bf16[1024,256]{1,0:T(8,128)(2,1)S(1)}, bf16[256,1024]{1,0:T(8,128)(2,1)S(1)}, f32[2,4,128,128]{3,2,1,0:T(8,128)S(1)}, f32[48,1024]{1,0:T(8,128)S(1)}) custom-call(s32[4]{0:T(128)S(1)} %pad_add_fusion.place, f32[4,1024]{1,0:T(4,128)S(1)} %get-tuple-element.56.refs_0_.mine, f32[4,1024]{1,0:T(4,128)S(1)} %collective-permute-done.3.refs_1_.other, ...), custom_call_target="tpu_custom_call" | custom-call | tf_op jit(solution)/shard_map/pallas_call | solution.py:246
  41.8 0.0 collective-permute-done.12.refs_3_
  41.8 1.7 %shard_map.95 = (bf16[1024,256]{1,0:T(8,128)(2,1)S(1)}, bf16[256,1024]{1,0:T(8,128)(2,1)S(1)}, f32[2,4,128,128]{3,2,1,0:T(8,128)S(1)}, f32[48,1024]{1,0:T(8,128)S(1)}) custom-call(s32[4]{0:T(128)S(1)} %pad_add_fusion.place, f32[4,1024]{1,0:T(4,128)S(1)} %get-tuple-element.56.refs_0_.mine, f32[4,1024]{1,0:T(4,128)S(1)} %collective-permute-done.3.refs_1_.other, ...), custom_call_target="tpu_custom_call" | custom-call | tf_op jit(solution)/shard_map/pallas_call | solution.py:246
  43.5 4.5 %collective-permute-start.13 = (f32[48,1024]{1,0:T(8,128)S(1)}, f32[48,1024]{1,0:T(8,128)S(1)}, u32[]{:S(2)}, u32[]{:S(2)}) collective-permute-start(f32[48,1024]{1,0:T(8,128)S(1)} %get-tuple-element.78.sums), channel_id=1, source_target_pairs={{0,16},{16,0},{1,17},{17,1},{2,18},{18,2},{3,19},{19,3},{4,20},{20... | collective-permute-start | bytes 589832 | tf_op jit(solution)/shard_map/ppermute | solution.py:239
  48.0 1.1 %collective-permute-done.13.received = f32[48,1024]{1,0:T(8,128)S(1)} collective-permute-done((f32[48,1024]{1,0:T(8,128)S(1)}, f32[48,1024]{1,0:T(8,128)S(1)}, u32[]{:S(2)}, u32[]{:S(2)}) %collective-permute-start.13) | collective-permute-done | bytes 196640 | tf_op jit(solution)/shard_map/ppermute | solution.py:239
  49.1 4.3 %shard_map.96 = (f32[4,1024]{1,0:T(4,128)S(1)}, f32[24,1024]{1,0:T(8,128)S(1)}, f32[24,1024]{1,0:T(8,128)S(1)}) custom-call(f32[4,1024]{1,0:T(4,128)S(1)} %get-tuple-element.56.refs_0_.mine, f32[4,1024]{1,0:T(4,128)S(1)} %collective-permute-done.3.refs_1_.other, f32[48,1024]{1,0:T(8,128)S(1)} %get-tuple-element.78.sums, ...), custom_call_target="tpu_custom_call" | custom-call | tf_op jit(solution)/shard_map/pallas_call | solution.py:246
  53.4 0.4 collective-permute-start.14
  53.8 0.9 %collective-permute-done.14.received = f32[24,1024]{1,0:T(8,128)S(1)} collective-permute-done((f32[24,1024]{1,0:T(8,128)S(1)}, f32[24,1024]{1,0:T(8,128)S(1)}, u32[]{:S(2)}, u32[]{:S(2)}) %collective-permute-start.14) | collective-permute-done | bytes 98336 | tf_op jit(solution)/shard_map/ppermute | solution.py:239
  54.8 0.7 %shard_map.97 = (f32[3,1024]{1,0:T(4,128)}, f32[1,1024]{1,0:T(1,128)}, f32[16,1024]{1,0:T(8,128)}) custom-call(f32[4,1024]{1,0:T(4,128)S(1)} %get-tuple-element.103.state, f32[24,1024]{1,0:T(8,128)S(1)} %get-tuple-element.104.own, f32[24,1024]{1,0:T(8,128)S(1)} %collective-permute-done.14.received), custom_call_target="tpu_custom_call" | custom-call | tf_op jit(solution)/shard_map/pallas_call | solution.py:246
  (1 shorter events, 0.0 us)
Async XLA Ops:
  1.5 7.7 %collective-permute-start.2 = (f32[96,128]{1,0:T(8,128)S(1)}, f32[96,128]{1,0:T(8,128)S(1)}, u32[]{:S(2)}, u32[]{:S(2)}) collective-permute-start(f32[96,128]{1,0:T(8,128)S(1)} %get-tuple-element.59.refs_0_), channel_id=1, source_target_pairs={{0,3},{1,0},{2,1},{3,2},{4,7},{5,4},{6,5},{7,6},{8,11},{9,8},{10,9... | collective-permute-start | bytes 147464 | tf_op jit(solution)/shard_map/ppermute | solution.py:239
  6.2 4.5 %collective-permute-start.1 = (f32[96,128]{1,0:T(8,128)S(1)}, f32[96,128]{1,0:T(8,128)S(1)}, u32[]{:S(2)}, u32[]{:S(2)}) collective-permute-start(f32[96,128]{1,0:T(8,128)S(1)} %get-tuple-element.59.refs_0_), channel_id=1, source_target_pairs={{0,2},{1,3},{2,0},{3,1},{4,6},{5,7},{6,4},{7,5},{8,10},{9,11},{10,... | collective-permute-start | bytes 147464 | tf_op jit(solution)/shard_map/ppermute | solution.py:239
  6.2 4.7 %collective-permute-start = (f32[96,128]{1,0:T(8,128)S(1)}, f32[96,128]{1,0:T(8,128)S(1)}, u32[]{:S(2)}, u32[]{:S(2)}) collective-permute-start(f32[96,128]{1,0:T(8,128)S(1)} %get-tuple-element.59.refs_0_), channel_id=1, source_target_pairs={{0,1},{1,2},{2,3},{3,0},{4,5},{5,6},{6,7},{7,4},{8,9},{9,10},{10,1... | collective-permute-start | bytes 147464 | tf_op jit(solution)/shard_map/ppermute | solution.py:239
  6.9 2.4 %collective-permute-start.3 = (f32[4,1024]{1,0:T(4,128)S(1)}, f32[4,1024]{1,0:T(4,128)S(1)}, u32[]{:S(2)}, u32[]{:S(2)}) collective-permute-start(f32[4,1024]{1,0:T(4,128)S(1)} %get-tuple-element.56.refs_0_.mine), channel_id=1, source_target_pairs={{0,16},{16,0},{1,17},{17,1},{2,18},{18,2},{3,19},{19,3},{4,20},{20... | collective-permute-start | bytes 49160 | tf_op jit(solution)/shard_map/ppermute | solution.py:239
  11.7 5.2 %collective-permute-start.4 = (f32[264,128]{1,0:T(8,128)S(1)}, f32[264,128]{1,0:T(8,128)S(1)}, u32[]{:S(2)}, u32[]{:S(2)}) collective-permute-start(f32[264,128]{1,0:T(8,128)S(1)} %get-tuple-element.64), channel_id=1, source_target_pairs={{0,4},{4,8},{8,12},{12,0},{1,5},{5,9},{9,13},{13,1},{2,6},{6,10},{... | collective-permute-start | bytes 405512 | tf_op jit(solution)/shard_map/ppermute | solution.py:239
  13.1 6.8 %collective-permute-start.5 = (f32[264,128]{1,0:T(8,128)S(1)}, f32[264,128]{1,0:T(8,128)S(1)}, u32[]{:S(2)}, u32[]{:S(2)}) collective-permute-start(f32[264,128]{1,0:T(8,128)S(1)} %get-tuple-element.65), channel_id=1, source_target_pairs={{0,8},{4,12},{8,0},{12,4},{1,9},{5,13},{9,1},{13,5},{2,10},{6,14},... | collective-permute-start | bytes 405512 | tf_op jit(solution)/shard_map/ppermute | solution.py:239
  15.7 4.9 %collective-permute-start.6 = (f32[264,128]{1,0:T(8,128)S(1)}, f32[264,128]{1,0:T(8,128)S(1)}, u32[]{:S(2)}, u32[]{:S(2)}) collective-permute-start(f32[264,128]{1,0:T(8,128)S(1)} %get-tuple-element.66), channel_id=1, source_target_pairs={{0,12},{4,0},{8,4},{12,8},{1,13},{5,1},{9,5},{13,9},{2,14},{6,2},{... | collective-permute-start | bytes 405512 | tf_op jit(solution)/shard_map/ppermute | solution.py:239
  20.7 7.6 %collective-permute-start.7 = (f32[528,128]{1,0:T(8,128)S(1)}, f32[528,128]{1,0:T(8,128)S(1)}, u32[]{:S(2)}, u32[]{:S(2)}) collective-permute-start(f32[528,128]{1,0:T(8,128)S(1)} %get-tuple-element.67.refs_2_), channel_id=1, source_target_pairs={{0,32},{32,64},{64,96},{96,0},{1,33},{33,65},{65,97},{97,1},{2,34}... | collective-permute-start | bytes 811016 | tf_op jit(solution)/shard_map/ppermute | solution.py:239
  22.0 6.3 %collective-permute-start.8 = (f32[528,128]{1,0:T(8,128)S(1)}, f32[528,128]{1,0:T(8,128)S(1)}, u32[]{:S(2)}, u32[]{:S(2)}) collective-permute-start(f32[528,128]{1,0:T(8,128)S(1)} %get-tuple-element.69.refs_3_), channel_id=1, source_target_pairs={{0,96},{32,0},{64,32},{96,64},{1,97},{33,1},{65,33},{97,65},{2,98}... | collective-permute-start | bytes 811016 | tf_op jit(solution)/shard_map/ppermute | solution.py:239
  23.4 12.8 %collective-permute-start.10 = (f32[528,128]{1,0:T(8,128)S(1)}, f32[528,128]{1,0:T(8,128)S(1)}, u32[]{:S(2)}, u32[]{:S(2)}) collective-permute-start(f32[528,128]{1,0:T(8,128)S(1)} %get-tuple-element.67.refs_2_), channel_id=1, source_target_pairs={{0,96},{32,0},{64,32},{96,64},{1,97},{33,1},{65,33},{97,65},{2,98}... | collective-permute-start | bytes 811016 | tf_op jit(solution)/shard_map/ppermute | solution.py:239
  24.7 9.8 %collective-permute-start.9 = (f32[528,128]{1,0:T(8,128)S(1)}, f32[528,128]{1,0:T(8,128)S(1)}, u32[]{:S(2)}, u32[]{:S(2)}) collective-permute-start(f32[528,128]{1,0:T(8,128)S(1)} %get-tuple-element.69.refs_3_), channel_id=1, source_target_pairs={{0,32},{32,64},{64,96},{96,0},{1,33},{33,65},{65,97},{97,1},{2,34}... | collective-permute-start | bytes 811016 | tf_op jit(solution)/shard_map/ppermute | solution.py:239
  28.3 11.8 %collective-permute-start.11 = (f32[528,128]{1,0:T(8,128)S(1)}, f32[528,128]{1,0:T(8,128)S(1)}, u32[]{:S(2)}, u32[]{:S(2)}) collective-permute-start(f32[528,128]{1,0:T(8,128)S(1)} %collective-permute-done.7.refs_3_), channel_id=1, source_target_pairs={{0,32},{32,64},{64,96},{96,0},{1,33},{33,65},{65,97},{97,1},{2,34}... | collective-permute-start | bytes 811016 | tf_op jit(solution)/shard_map/ppermute | solution.py:239
  28.8 13.0 %collective-permute-start.12 = (f32[528,128]{1,0:T(8,128)S(1)}, f32[528,128]{1,0:T(8,128)S(1)}, u32[]{:S(2)}, u32[]{:S(2)}) collective-permute-start(f32[528,128]{1,0:T(8,128)S(1)} %collective-permute-done.8.refs_3_), channel_id=1, source_target_pairs={{0,96},{32,0},{64,32},{96,64},{1,97},{33,1},{65,33},{97,65},{2,98}... | collective-permute-start | bytes 811016 | tf_op jit(solution)/shard_map/ppermute | solution.py:239
  43.5 5.6 %collective-permute-start.13 = (f32[48,1024]{1,0:T(8,128)S(1)}, f32[48,1024]{1,0:T(8,128)S(1)}, u32[]{:S(2)}, u32[]{:S(2)}) collective-permute-start(f32[48,1024]{1,0:T(8,128)S(1)} %get-tuple-element.78.sums), channel_id=1, source_target_pairs={{0,16},{16,0},{1,17},{17,1},{2,18},{18,2},{3,19},{19,3},{4,20},{20... | collective-permute-start | bytes 589832 | tf_op jit(solution)/shard_map/ppermute | solution.py:239
  53.4 1.4 %collective-permute-start.14 = (f32[24,1024]{1,0:T(8,128)S(1)}, f32[24,1024]{1,0:T(8,128)S(1)}, u32[]{:S(2)}, u32[]{:S(2)}) collective-permute-start(f32[24,1024]{1,0:T(8,128)S(1)} %get-tuple-element.105), channel_id=1, source_target_pairs={{0,16},{16,0},{1,17},{17,1},{2,18},{18,2},{3,19},{19,3},{4,20},{20... | collective-permute-start | bytes 294920 | tf_op jit(solution)/shard_map/ppermute | solution.py:239

commit v13 on v11

--- a/solution.py
+++ b/solution.py
@@ -281,7 +281,7 @@
     low, high = call(merge_y, [f32(8 * domain + 16, LANES)] * 2, *along_y)
     below_low, above_high = step(low, "x", 1), step(high, "x", -1)
     below_high, above_low = step(high, "x", 1), step(low, "x", -1)
-    slabs = [(low, high), (below_low, below_high), (above_low, above_high)]
+    slabs = [(low, high), (below_low, above_high), (below_high, above_low)]
     each = devices * slots // LANES // 4
     held, all_held = (
         [pltpu.VMEM((n, 8, LANES), jnp.float32), pltpu.VMEM((n, ROWS, LANES), jnp.float32)] for n in (each, 4 * each)

time: 54.2 us -> 52.9 us (0.976)
  starting transfers between devices: 23.6 us -> 22.3 us
    ppermute x15, starting transfers between devices: 23.6 us -> 22.3 us  [step(): lax.ppermute(value, axis, [(i, (i + by) % size) for i in range(size)])]
  transfers between devices with their start and end apart: 15 -> 15, of which waited for: 10 -> 11; matrix products, arithmetic and copies ran while one was open for 0% -> 0% of each run, Pallas kernels for 14% -> 14%
where the time goes in v13:
time: 52.9 us; the launch traced here: 52.7 us
  starting transfers between devices  22.3 us (42%)
  Pallas kernels  16.3 us (31%)
  waiting for transfers between devices  13.3 us (25%)
  between operations  0.72 us (1%)
    ppermute x15, starting transfers between devices, step(): lax.ppermute(value, axis, [(i, (i + by) % size) for i in range(size)])  22.3 us
    pallas_call x9, Pallas kernels, call(): pl.pallas_call(fn, in_specs=specs, out_specs=out_specs, out_shape=outs, s...  16.3 us
    ppermute x15, waiting for transfers between devices, step(): lax.ppermute(value, axis, [(i, (i + by) % size) for i in range(size)])  13.3 us
  transfers between devices with their start and end apart: 15, of which 11 were waited for; matrix products, arithmetic and copies ran while one was open for 0% of the time, Pallas kernels for 14%

profile of v13, /device:TPU:1, one launch (start us, length us, event | category | flops | bytes accessed | tf_op | source)
XLA Modules:
  0.0 52.7 jit_solution(7767653809999064705)
XLA Ops:
  0.6 0.9 %shard_map.85 = (f32[96,128]{1,0:T(8,128)S(1)}, f32[4,1024]{1,0:T(4,128)S(1)}) custom-call(f32[3,2048]{1,0:T(4,128)} %positions.1, f32[16,128]{1,0:T(8,128)} %bitcast.9, s32[16,128]{1,0:T(8,128)} %bitcast.10, s32[16,128]{1,0:T(8,128)} %bitcast.11, f32[3,1024]{1,0:T(4,128)} %centers.1, f32[1,1024]{1,0:T(1,128)} %bitcast.12), custom_call_target="tpu_custom_call" | custom-call | tf_op jit(solution)/shard_map/pallas_call | solution.py:254
  1.5 4.7 %collective-permute-start.2 = (f32[96,128]{1,0:T(8,128)S(1)}, f32[96,128]{1,0:T(8,128)S(1)}, u32[]{:S(2)}, u32[]{:S(2)}) collective-permute-start(f32[96,128]{1,0:T(8,128)S(1)} %get-tuple-element.43.refs_0_), channel_id=1, source_target_pairs={{0,3},{1,0},{2,1},{3,2},{4,7},{5,4},{6,5},{7,6},{8,11},{9,8},{10,9... | collective-permute-start | bytes 147464 | tf_op jit(solution)/shard_map/ppermute | solution.py:247
  6.2 0.0 collective-permute-start.1
  6.2 0.7 %collective-permute-start = (f32[96,128]{1,0:T(8,128)S(1)}, f32[96,128]{1,0:T(8,128)S(1)}, u32[]{:S(2)}, u32[]{:S(2)}) collective-permute-start(f32[96,128]{1,0:T(8,128)S(1)} %get-tuple-element.43.refs_0_), channel_id=1, source_target_pairs={{0,1},{1,2},{2,3},{3,0},{4,5},{5,6},{6,7},{7,4},{8,9},{9,10},{10,1... | collective-permute-start | bytes 147464 | tf_op jit(solution)/shard_map/ppermute | solution.py:247
  6.9 1.5 %collective-permute-start.3 = (f32[4,1024]{1,0:T(4,128)S(1)}, f32[4,1024]{1,0:T(4,128)S(1)}, u32[]{:S(2)}, u32[]{:S(2)}) collective-permute-start(f32[4,1024]{1,0:T(4,128)S(1)} %get-tuple-element.40.refs_0_.mine), channel_id=1, source_target_pairs={{0,16},{16,0},{1,17},{17,1},{2,18},{18,2},{3,19},{19,3},{4,20},{20... | collective-permute-start | bytes 49160 | tf_op jit(solution)/shard_map/ppermute | solution.py:247
  8.4 0.1 pad_add_fusion.place
  8.4 0.8 %collective-permute-done.3.refs_1_.other = f32[4,1024]{1,0:T(4,128)S(1)} collective-permute-done((f32[4,1024]{1,0:T(4,128)S(1)}, f32[4,1024]{1,0:T(4,128)S(1)}, u32[]{:S(2)}, u32[]{:S(2)}) %collective-permute-start.3) | collective-permute-done | bytes 16416 | tf_op jit(solution)/shard_map/ppermute | solution.py:247
  9.2 0.0 collective-permute-done.2.refs_3_
  9.2 1.5 %collective-permute-done.1.refs_2_ = f32[96,128]{1,0:T(8,128)S(1)} collective-permute-done((f32[96,128]{1,0:T(8,128)S(1)}, f32[96,128]{1,0:T(8,128)S(1)}, u32[]{:S(2)}, u32[]{:S(2)}) %collective-permute-start.1) | collective-permute-done | bytes 49184 | tf_op jit(solution)/shard_map/ppermute | solution.py:247
  10.7 0.1 collective-permute-done.refs_1_
  10.8 0.9 %shard_map.86 = (f32[264,128]{1,0:T(8,128)S(1)}, f32[264,128]{1,0:T(8,128)S(1)}, f32[264,128]{1,0:T(8,128)S(1)}, f32[264,128]{1,0:T(8,128)S(1)}) custom-call(s32[4]{0:T(128)S(1)} %pad_add_fusion.place, f32[96,128]{1,0:T(8,128)S(1)} %get-tuple-element.43.refs_0_, f32[96,128]{1,0:T(8,128)S(1)} %collective-permute-done.refs_1_, ...), custom_call_target="tpu_custom_call" | custom-call | tf_op jit(solution)/shard_map/pallas_call | solution.py:254
  11.7 1.4 %collective-permute-start.4 = (f32[264,128]{1,0:T(8,128)S(1)}, f32[264,128]{1,0:T(8,128)S(1)}, u32[]{:S(2)}, u32[]{:S(2)}) collective-permute-start(f32[264,128]{1,0:T(8,128)S(1)} %get-tuple-element.48), channel_id=1, source_target_pairs={{0,4},{4,8},{8,12},{12,0},{1,5},{5,9},{9,13},{13,1},{2,6},{6,10},{... | collective-permute-start | bytes 405512 | tf_op jit(solution)/shard_map/ppermute | solution.py:247
  13.1 2.6 %collective-permute-start.5 = (f32[264,128]{1,0:T(8,128)S(1)}, f32[264,128]{1,0:T(8,128)S(1)}, u32[]{:S(2)}, u32[]{:S(2)}) collective-permute-start(f32[264,128]{1,0:T(8,128)S(1)} %get-tuple-element.49), channel_id=1, source_target_pairs={{0,8},{4,12},{8,0},{12,4},{1,9},{5,13},{9,1},{13,5},{2,10},{6,14},... | collective-permute-start | bytes 405512 | tf_op jit(solution)/shard_map/ppermute | solution.py:247
  15.7 1.1 %collective-permute-start.6 = (f32[264,128]{1,0:T(8,128)S(1)}, f32[264,128]{1,0:T(8,128)S(1)}, u32[]{:S(2)}, u32[]{:S(2)}) collective-permute-start(f32[264,128]{1,0:T(8,128)S(1)} %get-tuple-element.50), channel_id=1, source_target_pairs={{0,12},{4,0},{8,4},{12,8},{1,13},{5,1},{9,5},{13,9},{2,14},{6,2},{... | collective-permute-start | bytes 405512 | tf_op jit(solution)/shard_map/ppermute | solution.py:247
  16.8 0.1 collective-permute-done.4.refs_1_
  16.9 3.0 %collective-permute-done.5.refs_2_ = f32[264,128]{1,0:T(8,128)S(1)} collective-permute-done((f32[264,128]{1,0:T(8,128)S(1)}, f32[264,128]{1,0:T(8,128)S(1)}, u32[]{:S(2)}, u32[]{:S(2)}) %collective-permute-start.5) | collective-permute-done | bytes 135200 | tf_op jit(solution)/shard_map/ppermute | solution.py:247
  19.9 0.7 %collective-permute-done.6.refs_3_ = f32[264,128]{1,0:T(8,128)S(1)} collective-permute-done((f32[264,128]{1,0:T(8,128)S(1)}, f32[264,128]{1,0:T(8,128)S(1)}, u32[]{:S(2)}, u32[]{:S(2)}) %collective-permute-start.6) | collective-permute-done | bytes 135200 | tf_op jit(solution)/shard_map/ppermute | solution.py:247
  20.7 1.3 %collective-permute-start.7 = (f32[528,128]{1,0:T(8,128)S(1)}, f32[528,128]{1,0:T(8,128)S(1)}, u32[]{:S(2)}, u32[]{:S(2)}) collective-permute-start(f32[528,128]{1,0:T(8,128)S(1)} %get-tuple-element.51.refs_2_), channel_id=1, source_target_pairs={{0,32},{32,64},{64,96},{96,0},{1,33},{33,65},{65,97},{97,1},{2,34}... | collective-permute-start | bytes 811016 | tf_op jit(solution)/shard_map/ppermute | solution.py:247
  22.0 1.5 %collective-permute-start.8 = (f32[528,128]{1,0:T(8,128)S(1)}, f32[528,128]{1,0:T(8,128)S(1)}, u32[]{:S(2)}, u32[]{:S(2)}) collective-permute-start(f32[528,128]{1,0:T(8,128)S(1)} %get-tuple-element.52.refs_3_), channel_id=1, source_target_pairs={{0,96},{32,0},{64,32},{96,64},{1,97},{33,1},{65,33},{97,65},{2,98}... | collective-permute-start | bytes 811016 | tf_op jit(solution)/shard_map/ppermute | solution.py:247
  23.4 1.3 %collective-permute-start.10 = (f32[528,128]{1,0:T(8,128)S(1)}, f32[528,128]{1,0:T(8,128)S(1)}, u32[]{:S(2)}, u32[]{:S(2)}) collective-permute-start(f32[528,128]{1,0:T(8,128)S(1)} %get-tuple-element.51.refs_2_), channel_id=1, source_target_pairs={{0,96},{32,0},{64,32},{96,64},{1,97},{33,1},{65,33},{97,65},{2,98}... | collective-permute-start | bytes 811016 | tf_op jit(solution)/shard_map/ppermute | solution.py:247
  24.7 0.2 collective-permute-start.9
  24.9 2.4 %shard_map.88 = (bf16[1024,512]{1,0:T(8,128)(2,1)S(1)}, bf16[512,1024]{1,0:T(8,128)(2,1)S(1)}, f32[4,4,128,128]{3,2,1,0:T(8,128)S(1)}, f32[48,1024]{1,0:T(8,128)S(1)}) custom-call(s32[4]{0:T(128)S(1)} %pad_add_fusion.place, f32[4,1024]{1,0:T(4,128)S(1)} %get-tuple-element.40.refs_0_.mine, f32[4,1024]{1,0:T(4,128)S(1)} %collective-permute-done.3.refs_1_.other, ...), custom_call_target="tpu_custom_call" | custom-call | tf_op jit(solution)/shard_map/pallas_call | solution.py:254
  27.3 0.0 collective-permute-done.7.refs_3_
  27.3 0.0 collective-permute-done.8.refs_4_
  27.4 1.4 %collective-permute-start.11 = (f32[528,128]{1,0:T(8,128)S(1)}, f32[528,128]{1,0:T(8,128)S(1)}, u32[]{:S(2)}, u32[]{:S(2)}) collective-permute-start(f32[528,128]{1,0:T(8,128)S(1)} %collective-permute-done.7.refs_3_), channel_id=1, source_target_pairs={{0,32},{32,64},{64,96},{96,0},{1,33},{33,65},{65,97},{97,1},{2,34}... | collective-permute-start | bytes 811016 | tf_op jit(solution)/shard_map/ppermute | solution.py:247
  28.8 1.3 %collective-permute-start.12 = (f32[528,128]{1,0:T(8,128)S(1)}, f32[528,128]{1,0:T(8,128)S(1)}, u32[]{:S(2)}, u32[]{:S(2)}) collective-permute-start(f32[528,128]{1,0:T(8,128)S(1)} %collective-permute-done.8.refs_4_), channel_id=1, source_target_pairs={{0,96},{32,0},{64,32},{96,64},{1,97},{33,1},{65,33},{97,65},{2,98}... | collective-permute-start | bytes 811016 | tf_op jit(solution)/shard_map/ppermute | solution.py:247
  30.1 2.4 %shard_map.89 = (bf16[1024,512]{1,0:T(8,128)(2,1)S(1)}, bf16[512,1024]{1,0:T(8,128)(2,1)S(1)}, f32[4,4,128,128]{3,2,1,0:T(8,128)S(1)}, f32[48,1024]{1,0:T(8,128)S(1)}) custom-call(s32[4]{0:T(128)S(1)} %pad_add_fusion.place, f32[4,1024]{1,0:T(4,128)S(1)} %get-tuple-element.40.refs_0_.mine, f32[4,1024]{1,0:T(4,128)S(1)} %collective-permute-done.3.refs_1_.other, ...), custom_call_target="tpu_custom_call" | custom-call | tf_op jit(solution)/shard_map/pallas_call | solution.py:254
  32.5 0.2 collective-permute-done.10.refs_4_
  32.7 1.7 %collective-permute-done.9.refs_3_ = f32[528,128]{1,0:T(8,128)S(1)} collective-permute-done((f32[528,128]{1,0:T(8,128)S(1)}, f32[528,128]{1,0:T(8,128)S(1)}, u32[]{:S(2)}, u32[]{:S(2)}) %collective-permute-start.9) | collective-permute-done | bytes 270368 | tf_op jit(solution)/shard_map/ppermute | solution.py:247
  34.4 2.4 %shard_map.90 = (bf16[1024,512]{1,0:T(8,128)(2,1)S(1)}, bf16[512,1024]{1,0:T(8,128)(2,1)S(1)}, f32[4,4,128,128]{3,2,1,0:T(8,128)S(1)}, f32[48,1024]{1,0:T(8,128)S(1)}) custom-call(s32[4]{0:T(128)S(1)} %pad_add_fusion.place, f32[4,1024]{1,0:T(4,128)S(1)} %get-tuple-element.40.refs_0_.mine, f32[4,1024]{1,0:T(4,128)S(1)} %collective-permute-done.3.refs_1_.other, ...), custom_call_target="tpu_custom_call" | custom-call | tf_op jit(solution)/shard_map/pallas_call | solution.py:254
  36.8 3.2 %collective-permute-done.11.refs_3_ = f32[528,128]{1,0:T(8,128)S(1)} collective-permute-done((f32[528,128]{1,0:T(8,128)S(1)}, f32[528,128]{1,0:T(8,128)S(1)}, u32[]{:S(2)}, u32[]{:S(2)}) %collective-permute-start.11) | collective-permute-done | bytes 270368 | tf_op jit(solution)/shard_map/ppermute | solution.py:247
  40.1 0.0 collective-permute-done.12.refs_4_
  40.1 2.5 %shard_map.91 = (bf16[1024,512]{1,0:T(8,128)(2,1)S(1)}, bf16[512,1024]{1,0:T(8,128)(2,1)S(1)}, f32[4,4,128,128]{3,2,1,0:T(8,128)S(1)}, f32[48,1024]{1,0:T(8,128)S(1)}) custom-call(s32[4]{0:T(128)S(1)} %pad_add_fusion.place, f32[4,1024]{1,0:T(4,128)S(1)} %get-tuple-element.40.refs_0_.mine, f32[4,1024]{1,0:T(4,128)S(1)} %collective-permute-done.3.refs_1_.other, ...), custom_call_target="tpu_custom_call" | custom-call | tf_op jit(solution)/shard_map/pallas_call | solution.py:254
  42.6 2.9 %collective-permute-start.13 = (f32[48,1024]{1,0:T(8,128)S(1)}, f32[48,1024]{1,0:T(8,128)S(1)}, u32[]{:S(2)}, u32[]{:S(2)}) collective-permute-start(f32[48,1024]{1,0:T(8,128)S(1)} %get-tuple-element.58.sums), channel_id=1, source_target_pairs={{0,16},{16,0},{1,17},{17,1},{2,18},{18,2},{3,19},{19,3},{4,20},{20... | collective-permute-start | bytes 589832 | tf_op jit(solution)/shard_map/ppermute | solution.py:247
  45.5 1.1 %collective-permute-done.13.received = f32[48,1024]{1,0:T(8,128)S(1)} collective-permute-done((f32[48,1024]{1,0:T(8,128)S(1)}, f32[48,1024]{1,0:T(8,128)S(1)}, u32[]{:S(2)}, u32[]{:S(2)}) %collective-permute-start.13) | collective-permute-done | bytes 196640 | tf_op jit(solution)/shard_map/ppermute | solution.py:247
  46.6 4.0 %shard_map.92 = (f32[4,1024]{1,0:T(4,128)S(1)}, f32[24,1024]{1,0:T(8,128)S(1)}, f32[24,1024]{1,0:T(8,128)S(1)}) custom-call(f32[4,1024]{1,0:T(4,128)S(1)} %get-tuple-element.40.refs_0_.mine, f32[4,1024]{1,0:T(4,128)S(1)} %collective-permute-done.3.refs_1_.other, f32[48,1024]{1,0:T(8,128)S(1)} %get-tuple-element.58.sums, ...), custom_call_target="tpu_custom_call" | custom-call | tf_op jit(solution)/shard_map/pallas_call | solution.py:254
  50.6 0.5 collective-permute-start.14
  51.1 0.9 %collective-permute-done.14.received = f32[24,1024]{1,0:T(8,128)S(1)} collective-permute-done((f32[24,1024]{1,0:T(8,128)S(1)}, f32[24,1024]{1,0:T(8,128)S(1)}, u32[]{:S(2)}, u32[]{:S(2)}) %collective-permute-start.14) | collective-permute-done | bytes 98336 | tf_op jit(solution)/shard_map/ppermute | solution.py:247
  52.0 0.7 %shard_map.93 = (f32[3,1024]{1,0:T(4,128)}, f32[1,1024]{1,0:T(1,128)}, f32[16,1024]{1,0:T(8,128)}) custom-call(f32[4,1024]{1,0:T(4,128)S(1)} %get-tuple-element.71.state, f32[24,1024]{1,0:T(8,128)S(1)} %get-tuple-element.72.own, f32[24,1024]{1,0:T(8,128)S(1)} %collective-permute-done.14.received), custom_call_target="tpu_custom_call" | custom-call | tf_op jit(solution)/shard_map/pallas_call | solution.py:254
  (1 shorter events, 0.0 us)
Async XLA Ops:
  1.5 7.7 %collective-permute-start.2 = (f32[96,128]{1,0:T(8,128)S(1)}, f32[96,128]{1,0:T(8,128)S(1)}, u32[]{:S(2)}, u32[]{:S(2)}) collective-permute-start(f32[96,128]{1,0:T(8,128)S(1)} %get-tuple-element.43.refs_0_), channel_id=1, source_target_pairs={{0,3},{1,0},{2,1},{3,2},{4,7},{5,4},{6,5},{7,6},{8,11},{9,8},{10,9... | collective-permute-start | bytes 147464 | tf_op jit(solution)/shard_map/ppermute | solution.py:247
  6.2 4.5 %collective-permute-start.1 = (f32[96,128]{1,0:T(8,128)S(1)}, f32[96,128]{1,0:T(8,128)S(1)}, u32[]{:S(2)}, u32[]{:S(2)}) collective-permute-start(f32[96,128]{1,0:T(8,128)S(1)} %get-tuple-element.43.refs_0_), channel_id=1, source_target_pairs={{0,2},{1,3},{2,0},{3,1},{4,6},{5,7},{6,4},{7,5},{8,10},{9,11},{10,... | collective-permute-start | bytes 147464 | tf_op jit(solution)/shard_map/ppermute | solution.py:247
  6.2 4.7 %collective-permute-start = (f32[96,128]{1,0:T(8,128)S(1)}, f32[96,128]{1,0:T(8,128)S(1)}, u32[]{:S(2)}, u32[]{:S(2)}) collective-permute-start(f32[96,128]{1,0:T(8,128)S(1)} %get-tuple-element.43.refs_0_), channel_id=1, source_target_pairs={{0,1},{1,2},{2,3},{3,0},{4,5},{5,6},{6,7},{7,4},{8,9},{9,10},{10,1... | collective-permute-start | bytes 147464 | tf_op jit(solution)/shard_map/ppermute | solution.py:247
  6.9 2.4 %collective-permute-start.3 = (f32[4,1024]{1,0:T(4,128)S(1)}, f32[4,1024]{1,0:T(4,128)S(1)}, u32[]{:S(2)}, u32[]{:S(2)}) collective-permute-start(f32[4,1024]{1,0:T(4,128)S(1)} %get-tuple-element.40.refs_0_.mine), channel_id=1, source_target_pairs={{0,16},{16,0},{1,17},{17,1},{2,18},{18,2},{3,19},{19,3},{4,20},{20... | collective-permute-start | bytes 49160 | tf_op jit(solution)/shard_map/ppermute | solution.py:247
  11.7 5.2 %collective-permute-start.4 = (f32[264,128]{1,0:T(8,128)S(1)}, f32[264,128]{1,0:T(8,128)S(1)}, u32[]{:S(2)}, u32[]{:S(2)}) collective-permute-start(f32[264,128]{1,0:T(8,128)S(1)} %get-tuple-element.48), channel_id=1, source_target_pairs={{0,4},{4,8},{8,12},{12,0},{1,5},{5,9},{9,13},{13,1},{2,6},{6,10},{... | collective-permute-start | bytes 405512 | tf_op jit(solution)/shard_map/ppermute | solution.py:247
  13.1 6.8 %collective-permute-start.5 = (f32[264,128]{1,0:T(8,128)S(1)}, f32[264,128]{1,0:T(8,128)S(1)}, u32[]{:S(2)}, u32[]{:S(2)}) collective-permute-start(f32[264,128]{1,0:T(8,128)S(1)} %get-tuple-element.49), channel_id=1, source_target_pairs={{0,8},{4,12},{8,0},{12,4},{1,9},{5,13},{9,1},{13,5},{2,10},{6,14},... | collective-permute-start | bytes 405512 | tf_op jit(solution)/shard_map/ppermute | solution.py:247
  15.7 4.9 %collective-permute-start.6 = (f32[264,128]{1,0:T(8,128)S(1)}, f32[264,128]{1,0:T(8,128)S(1)}, u32[]{:S(2)}, u32[]{:S(2)}) collective-permute-start(f32[264,128]{1,0:T(8,128)S(1)} %get-tuple-element.50), channel_id=1, source_target_pairs={{0,12},{4,0},{8,4},{12,8},{1,13},{5,1},{9,5},{13,9},{2,14},{6,2},{... | collective-permute-start | bytes 405512 | tf_op jit(solution)/shard_map/ppermute | solution.py:247
  20.7 6.6 %collective-permute-start.7 = (f32[528,128]{1,0:T(8,128)S(1)}, f32[528,128]{1,0:T(8,128)S(1)}, u32[]{:S(2)}, u32[]{:S(2)}) collective-permute-start(f32[528,128]{1,0:T(8,128)S(1)} %get-tuple-element.51.refs_2_), channel_id=1, source_target_pairs={{0,32},{32,64},{64,96},{96,0},{1,33},{33,65},{65,97},{97,1},{2,34}... | collective-permute-start | bytes 811016 | tf_op jit(solution)/shard_map/ppermute | solution.py:247
  22.0 5.4 %collective-permute-start.8 = (f32[528,128]{1,0:T(8,128)S(1)}, f32[528,128]{1,0:T(8,128)S(1)}, u32[]{:S(2)}, u32[]{:S(2)}) collective-permute-start(f32[528,128]{1,0:T(8,128)S(1)} %get-tuple-element.52.refs_3_), channel_id=1, source_target_pairs={{0,96},{32,0},{64,32},{96,64},{1,97},{33,1},{65,33},{97,65},{2,98}... | collective-permute-start | bytes 811016 | tf_op jit(solution)/shard_map/ppermute | solution.py:247
  23.4 9.3 %collective-permute-start.10 = (f32[528,128]{1,0:T(8,128)S(1)}, f32[528,128]{1,0:T(8,128)S(1)}, u32[]{:S(2)}, u32[]{:S(2)}) collective-permute-start(f32[528,128]{1,0:T(8,128)S(1)} %get-tuple-element.51.refs_2_), channel_id=1, source_target_pairs={{0,96},{32,0},{64,32},{96,64},{1,97},{33,1},{65,33},{97,65},{2,98}... | collective-permute-start | bytes 811016 | tf_op jit(solution)/shard_map/ppermute | solution.py:247
  24.7 9.7 %collective-permute-start.9 = (f32[528,128]{1,0:T(8,128)S(1)}, f32[528,128]{1,0:T(8,128)S(1)}, u32[]{:S(2)}, u32[]{:S(2)}) collective-permute-start(f32[528,128]{1,0:T(8,128)S(1)} %get-tuple-element.52.refs_3_), channel_id=1, source_target_pairs={{0,32},{32,64},{64,96},{96,0},{1,33},{33,65},{65,97},{97,1},{2,34}... | collective-permute-start | bytes 811016 | tf_op jit(solution)/shard_map/ppermute | solution.py:247
  27.4 12.7 %collective-permute-start.11 = (f32[528,128]{1,0:T(8,128)S(1)}, f32[528,128]{1,0:T(8,128)S(1)}, u32[]{:S(2)}, u32[]{:S(2)}) collective-permute-start(f32[528,128]{1,0:T(8,128)S(1)} %collective-permute-done.7.refs_3_), channel_id=1, source_target_pairs={{0,32},{32,64},{64,96},{96,0},{1,33},{33,65},{65,97},{97,1},{2,34}... | collective-permute-start | bytes 811016 | tf_op jit(solution)/shard_map/ppermute | solution.py:247
  28.8 11.3 %collective-permute-start.12 = (f32[528,128]{1,0:T(8,128)S(1)}, f32[528,128]{1,0:T(8,128)S(1)}, u32[]{:S(2)}, u32[]{:S(2)}) collective-permute-start(f32[528,128]{1,0:T(8,128)S(1)} %collective-permute-done.8.refs_4_), channel_id=1, source_target_pairs={{0,96},{32,0},{64,32},{96,64},{1,97},{33,1},{65,33},{97,65},{2,98}... | collective-permute-start | bytes 811016 | tf_op jit(solution)/shard_map/ppermute | solution.py:247
  42.6 4.0 %collective-permute-start.13 = (f32[48,1024]{1,0:T(8,128)S(1)}, f32[48,1024]{1,0:T(8,128)S(1)}, u32[]{:S(2)}, u32[]{:S(2)}) collective-permute-start(f32[48,1024]{1,0:T(8,128)S(1)} %get-tuple-element.58.sums), channel_id=1, source_target_pairs={{0,16},{16,0},{1,17},{17,1},{2,18},{18,2},{3,19},{19,3},{4,20},{20... | collective-permute-start | bytes 589832 | tf_op jit(solution)/shard_map/ppermute | solution.py:247
  50.6 1.4 %collective-permute-start.14 = (f32[24,1024]{1,0:T(8,128)S(1)}, f32[24,1024]{1,0:T(8,128)S(1)}, u32[]{:S(2)}, u32[]{:S(2)}) collective-permute-start(f32[24,1024]{1,0:T(8,128)S(1)} %get-tuple-element.73), channel_id=1, source_target_pairs={{0,16},{16,0},{1,17},{17,1},{2,18},{18,2},{3,19},{19,3},{4,20},{20... | collective-permute-start | bytes 294920 | tf_op jit(solution)/shard_map/ppermute | solution.py:247

commit v14 on v13

--- a/solution.py
+++ b/solution.py
@@ -280,8 +280,7 @@
     along_y = [step(to_y[k], "y", k) if k else to_y[k] for k in range(4)]
     low, high = call(merge_y, [f32(8 * domain + 16, LANES)] * 2, *along_y)
     below_low, above_high = step(low, "x", 1), step(high, "x", -1)
-    below_high, above_low = step(high, "x", 1), step(low, "x", -1)
-    slabs = [(low, high), (below_low, above_high), (below_high, above_low)]
+    slabs = [[low, high], [below_low, above_high]]
     each = devices * slots // LANES // 4
     held, all_held = (
         [pltpu.VMEM((n, 8, LANES), jnp.float32), pltpu.VMEM((n, ROWS, LANES), jnp.float32)] for n in (each, 4 * each)
@@ -293,12 +292,13 @@
         f32(2 * ROWS, halos),
     ]
     kept, sums = [], []
-    for slab in slabs:
-        *arrays, total = call(functools.partial(first_pass, slots, blocks), outs, place, state, other, *sums, *slab, scratch=held)
+    for n in range(4):
+        *arrays, total = call(functools.partial(first_pass, slots, blocks), outs, place, state, other, *sums, *slabs[n], scratch=held)
         kept.extend(arrays)
         if not sums:
-            first, second, _ = lax.optimization_barrier((below_low, above_high, total))
-            slabs.append((step(first, "x", 1), step(second, "x", -1)))
+            *slabs[1], low, high, _ = lax.optimization_barrier((*slabs[1], low, high, total))
+            far = (step(slabs[1][0], "x", 1), step(slabs[1][1], "x", -1))
+            slabs += [(step(high, "x", 1), step(low, "x", -1)), far]
         sums = [total]
     state, own, partner = call(
         second_pass,

time: 52.9 us -> 53.6 us (1.013)
  starting transfers between devices: 22.3 us -> 25.8 us
  waiting for transfers between devices: 13.3 us -> 10.5 us
    ppermute x15, starting transfers between devices: 22.3 us -> 25.8 us  [step(): lax.ppermute(value, axis, [(i, (i + by) % size) for i in range(size)])]
    ppermute x15, waiting for transfers between devices: 13.3 us -> 10.5 us  [step(): lax.ppermute(value, axis, [(i, (i + by) % size) for i in range(size)])]
where the time goes in v14:
time: 53.6 us; the launch traced here: 53.4 us
  starting transfers between devices  25.8 us (48%)
  Pallas kernels  16.3 us (30%)
  waiting for transfers between devices  10.5 us (20%)
  between operations  0.72 us (1%)
    ppermute x15, starting transfers between devices, step(): lax.ppermute(value, axis, [(i, (i + by) % size) for i in range(size)])  25.8 us
    pallas_call x9, Pallas kernels, call(): pl.pallas_call(fn, in_specs=specs, out_specs=out_specs, out_shape=outs, s...  16.3 us
    ppermute x15, waiting for transfers between devices, step(): lax.ppermute(value, axis, [(i, (i + by) % size) for i in range(size)])  10.5 us
  transfers between devices with their start and end apart: 15, of which 11 were waited for; matrix products, arithmetic and copies ran while one was open for 0% of the time, Pallas kernels for 14%

profile of v14, /device:TPU:1, one launch (start us, length us, event | category | flops | bytes accessed | tf_op | source)
XLA Modules:
  0.0 53.4 jit_solution(2957335377173821792)
XLA Ops:
  0.6 0.9 %shard_map.85 = (f32[96,128]{1,0:T(8,128)S(1)}, f32[4,1024]{1,0:T(4,128)S(1)}) custom-call(f32[3,2048]{1,0:T(4,128)} %positions.1, f32[16,128]{1,0:T(8,128)} %bitcast.9, s32[16,128]{1,0:T(8,128)} %bitcast.10, s32[16,128]{1,0:T(8,128)} %bitcast.11, f32[3,1024]{1,0:T(4,128)} %centers.1, f32[1,1024]{1,0:T(1,128)} %bitcast.12), custom_call_target="tpu_custom_call" | custom-call | tf_op jit(solution)/shard_map/pallas_call | solution.py:254
  1.5 4.7 %collective-permute-start.2 = (f32[96,128]{1,0:T(8,128)S(1)}, f32[96,128]{1,0:T(8,128)S(1)}, u32[]{:S(2)}, u32[]{:S(2)}) collective-permute-start(f32[96,128]{1,0:T(8,128)S(1)} %get-tuple-element.45.refs_0_), channel_id=1, source_target_pairs={{0,3},{1,0},{2,1},{3,2},{4,7},{5,4},{6,5},{7,6},{8,11},{9,8},{10,9... | collective-permute-start | bytes 147464 | tf_op jit(solution)/shard_map/ppermute | solution.py:247
  6.2 0.0 collective-permute-start.1
  6.2 0.7 %collective-permute-start = (f32[96,128]{1,0:T(8,128)S(1)}, f32[96,128]{1,0:T(8,128)S(1)}, u32[]{:S(2)}, u32[]{:S(2)}) collective-permute-start(f32[96,128]{1,0:T(8,128)S(1)} %get-tuple-element.45.refs_0_), channel_id=1, source_target_pairs={{0,1},{1,2},{2,3},{3,0},{4,5},{5,6},{6,7},{7,4},{8,9},{9,10},{10,1... | collective-permute-start | bytes 147464 | tf_op jit(solution)/shard_map/ppermute | solution.py:247
  6.9 1.5 %collective-permute-start.3 = (f32[4,1024]{1,0:T(4,128)S(1)}, f32[4,1024]{1,0:T(4,128)S(1)}, u32[]{:S(2)}, u32[]{:S(2)}) collective-permute-start(f32[4,1024]{1,0:T(4,128)S(1)} %get-tuple-element.42.refs_0_.mine), channel_id=1, source_target_pairs={{0,16},{16,0},{1,17},{17,1},{2,18},{18,2},{3,19},{19,3},{4,20},{20... | collective-permute-start | bytes 49160 | tf_op jit(solution)/shard_map/ppermute | solution.py:247
  8.4 0.1 pad_add_fusion.place
  8.4 0.8 %collective-permute-done.3.refs_1_.other = f32[4,1024]{1,0:T(4,128)S(1)} collective-permute-done((f32[4,1024]{1,0:T(4,128)S(1)}, f32[4,1024]{1,0:T(4,128)S(1)}, u32[]{:S(2)}, u32[]{:S(2)}) %collective-permute-start.3) | collective-permute-done | bytes 16416 | tf_op jit(solution)/shard_map/ppermute | solution.py:247
  9.2 0.0 collective-permute-done.2.refs_3_
  9.2 1.5 %collective-permute-done.1.refs_2_ = f32[96,128]{1,0:T(8,128)S(1)} collective-permute-done((f32[96,128]{1,0:T(8,128)S(1)}, f32[96,128]{1,0:T(8,128)S(1)}, u32[]{:S(2)}, u32[]{:S(2)}) %collective-permute-start.1) | collective-permute-done | bytes 49184 | tf_op jit(solution)/shard_map/ppermute | solution.py:247
  10.7 0.1 collective-permute-done.refs_1_
  10.8 0.9 %shard_map.86 = (f32[264,128]{1,0:T(8,128)S(1)}, f32[264,128]{1,0:T(8,128)S(1)}, f32[264,128]{1,0:T(8,128)S(1)}, f32[264,128]{1,0:T(8,128)S(1)}) custom-call(s32[4]{0:T(128)S(1)} %pad_add_fusion.place, f32[96,128]{1,0:T(8,128)S(1)} %get-tuple-element.45.refs_0_, f32[96,128]{1,0:T(8,128)S(1)} %collective-permute-done.refs_1_, ...), custom_call_target="tpu_custom_call" | custom-call | tf_op jit(solution)/shard_map/pallas_call | solution.py:254
  11.7 1.4 %collective-permute-start.4 = (f32[264,128]{1,0:T(8,128)S(1)}, f32[264,128]{1,0:T(8,128)S(1)}, u32[]{:S(2)}, u32[]{:S(2)}) collective-permute-start(f32[264,128]{1,0:T(8,128)S(1)} %get-tuple-element.50), channel_id=1, source_target_pairs={{0,4},{4,8},{8,12},{12,0},{1,5},{5,9},{9,13},{13,1},{2,6},{6,10},{... | collective-permute-start | bytes 405512 | tf_op jit(solution)/shard_map/ppermute | solution.py:247
  13.1 2.6 %collective-permute-start.5 = (f32[264,128]{1,0:T(8,128)S(1)}, f32[264,128]{1,0:T(8,128)S(1)}, u32[]{:S(2)}, u32[]{:S(2)}) collective-permute-start(f32[264,128]{1,0:T(8,128)S(1)} %get-tuple-element.51), channel_id=1, source_target_pairs={{0,8},{4,12},{8,0},{12,4},{1,9},{5,13},{9,1},{13,5},{2,10},{6,14},... | collective-permute-start | bytes 405512 | tf_op jit(solution)/shard_map/ppermute | solution.py:247
  15.7 1.1 %collective-permute-start.6 = (f32[264,128]{1,0:T(8,128)S(1)}, f32[264,128]{1,0:T(8,128)S(1)}, u32[]{:S(2)}, u32[]{:S(2)}) collective-permute-start(f32[264,128]{1,0:T(8,128)S(1)} %get-tuple-element.52), channel_id=1, source_target_pairs={{0,12},{4,0},{8,4},{12,8},{1,13},{5,1},{9,5},{13,9},{2,14},{6,2},{... | collective-permute-start | bytes 405512 | tf_op jit(solution)/shard_map/ppermute | solution.py:247
  16.8 0.1 collective-permute-done.4.refs_1_
  16.9 3.0 %collective-permute-done.5.refs_2_ = f32[264,128]{1,0:T(8,128)S(1)} collective-permute-done((f32[264,128]{1,0:T(8,128)S(1)}, f32[264,128]{1,0:T(8,128)S(1)}, u32[]{:S(2)}, u32[]{:S(2)}) %collective-permute-start.5) | collective-permute-done | bytes 135200 | tf_op jit(solution)/shard_map/ppermute | solution.py:247
  19.9 0.7 %collective-permute-done.6.refs_3_ = f32[264,128]{1,0:T(8,128)S(1)} collective-permute-done((f32[264,128]{1,0:T(8,128)S(1)}, f32[264,128]{1,0:T(8,128)S(1)}, u32[]{:S(2)}, u32[]{:S(2)}) %collective-permute-start.6) | collective-permute-done | bytes 135200 | tf_op jit(solution)/shard_map/ppermute | solution.py:247
  20.7 1.3 %collective-permute-start.7 = (f32[528,128]{1,0:T(8,128)S(1)}, f32[528,128]{1,0:T(8,128)S(1)}, u32[]{:S(2)}, u32[]{:S(2)}) collective-permute-start(f32[528,128]{1,0:T(8,128)S(1)} %get-tuple-element.60.refs_2_), channel_id=1, source_target_pairs={{0,32},{32,64},{64,96},{96,0},{1,33},{33,65},{65,97},{97,1},{2,34}... | collective-permute-start | bytes 811016 | tf_op jit(solution)/shard_map/ppermute | solution.py:247
  22.0 1.5 %collective-permute-start.8 = (f32[528,128]{1,0:T(8,128)S(1)}, f32[528,128]{1,0:T(8,128)S(1)}, u32[]{:S(2)}, u32[]{:S(2)}) collective-permute-start(f32[528,128]{1,0:T(8,128)S(1)} %get-tuple-element.59.refs_3_), channel_id=1, source_target_pairs={{0,96},{32,0},{64,32},{96,64},{1,97},{33,1},{65,33},{97,65},{2,98}... | collective-permute-start | bytes 811016 | tf_op jit(solution)/shard_map/ppermute | solution.py:247
  23.4 2.4 %shard_map.88 = (bf16[1024,512]{1,0:T(8,128)(2,1)S(1)}, bf16[512,1024]{1,0:T(8,128)(2,1)S(1)}, f32[4,4,128,128]{3,2,1,0:T(8,128)S(1)}, f32[48,1024]{1,0:T(8,128)S(1)}) custom-call(s32[4]{0:T(128)S(1)} %pad_add_fusion.place, f32[4,1024]{1,0:T(4,128)S(1)} %get-tuple-element.42.refs_0_.mine, f32[4,1024]{1,0:T(4,128)S(1)} %collective-permute-done.3.refs_1_.other, ...), custom_call_target="tpu_custom_call" | custom-call | tf_op jit(solution)/shard_map/pallas_call | solution.py:254
  25.9 1.4 %collective-permute-done.7.refs_3_ = f32[528,128]{1,0:T(8,128)S(1)} collective-permute-done((f32[528,128]{1,0:T(8,128)S(1)}, f32[528,128]{1,0:T(8,128)S(1)}, u32[]{:S(2)}, u32[]{:S(2)}) %collective-permute-start.7) | collective-permute-done | bytes 270368 | tf_op jit(solution)/shard_map/ppermute | solution.py:247
  27.3 0.0 collective-permute-done.8.refs_4_
  27.3 1.5 %collective-permute-start.9 = (f32[528,128]{1,0:T(8,128)S(1)}, f32[528,128]{1,0:T(8,128)S(1)}, u32[]{:S(2)}, u32[]{:S(2)}) collective-permute-start(f32[528,128]{1,0:T(8,128)S(1)} %get-tuple-element.59.refs_3_), channel_id=1, source_target_pairs={{0,32},{32,64},{64,96},{96,0},{1,33},{33,65},{65,97},{97,1},{2,34}... | collective-permute-start | bytes 811016 | tf_op jit(solution)/shard_map/ppermute | solution.py:247
  28.8 1.2 %collective-permute-start.10 = (f32[528,128]{1,0:T(8,128)S(1)}, f32[528,128]{1,0:T(8,128)S(1)}, u32[]{:S(2)}, u32[]{:S(2)}) collective-permute-start(f32[528,128]{1,0:T(8,128)S(1)} %get-tuple-element.60.refs_2_), channel_id=1, source_target_pairs={{0,96},{32,0},{64,32},{96,64},{1,97},{33,1},{65,33},{97,65},{2,98}... | collective-permute-start | bytes 811016 | tf_op jit(solution)/shard_map/ppermute | solution.py:247
  30.0 0.3 collective-permute-start.11
  30.3 2.4 %collective-permute-start.12 = (f32[528,128]{1,0:T(8,128)S(1)}, f32[528,128]{1,0:T(8,128)S(1)}, u32[]{:S(2)}, u32[]{:S(2)}) collective-permute-start(f32[528,128]{1,0:T(8,128)S(1)} %collective-permute-done.8.refs_4_), channel_id=1, source_target_pairs={{0,96},{32,0},{64,32},{96,64},{1,97},{33,1},{65,33},{97,65},{2,98}... | collective-permute-start | bytes 811016 | tf_op jit(solution)/shard_map/ppermute | solution.py:247
  32.7 2.4 %shard_map.89 = (bf16[1024,512]{1,0:T(8,128)(2,1)S(1)}, bf16[512,1024]{1,0:T(8,128)(2,1)S(1)}, f32[4,4,128,128]{3,2,1,0:T(8,128)S(1)}, f32[48,1024]{1,0:T(8,128)S(1)}) custom-call(s32[4]{0:T(128)S(1)} %pad_add_fusion.place, f32[4,1024]{1,0:T(4,128)S(1)} %get-tuple-element.42.refs_0_.mine, f32[4,1024]{1,0:T(4,128)S(1)} %collective-permute-done.3.refs_1_.other, ...), custom_call_target="tpu_custom_call" | custom-call | tf_op jit(solution)/shard_map/pallas_call | solution.py:254
  35.1 0.0 collective-permute-done.9.refs_3_
  35.1 0.0 collective-permute-done.10.refs_4_
  35.1 2.5 %shard_map.90 = (bf16[1024,512]{1,0:T(8,128)(2,1)S(1)}, bf16[512,1024]{1,0:T(8,128)(2,1)S(1)}, f32[4,4,128,128]{3,2,1,0:T(8,128)S(1)}, f32[48,1024]{1,0:T(8,128)S(1)}) custom-call(s32[4]{0:T(128)S(1)} %pad_add_fusion.place, f32[4,1024]{1,0:T(4,128)S(1)} %get-tuple-element.42.refs_0_.mine, f32[4,1024]{1,0:T(4,128)S(1)} %collective-permute-done.3.refs_1_.other, ...), custom_call_target="tpu_custom_call" | custom-call | tf_op jit(solution)/shard_map/pallas_call | solution.py:254
  37.6 0.5 collective-permute-done.11.refs_3_
  38.1 0.3 collective-permute-done.12.refs_4_
  38.4 2.5 %shard_map.91 = (bf16[1024,512]{1,0:T(8,128)(2,1)S(1)}, bf16[512,1024]{1,0:T(8,128)(2,1)S(1)}, f32[4,4,128,128]{3,2,1,0:T(8,128)S(1)}, f32[48,1024]{1,0:T(8,128)S(1)}) custom-call(s32[4]{0:T(128)S(1)} %pad_add_fusion.place, f32[4,1024]{1,0:T(4,128)S(1)} %get-tuple-element.42.refs_0_.mine, f32[4,1024]{1,0:T(4,128)S(1)} %collective-permute-done.3.refs_1_.other, ...), custom_call_target="tpu_custom_call" | custom-call | tf_op jit(solution)/shard_map/pallas_call | solution.py:254
  40.9 5.3 %collective-permute-start.13 = (f32[48,1024]{1,0:T(8,128)S(1)}, f32[48,1024]{1,0:T(8,128)S(1)}, u32[]{:S(2)}, u32[]{:S(2)}) collective-permute-start(f32[48,1024]{1,0:T(8,128)S(1)} %get-tuple-element.62.sums), channel_id=1, source_target_pairs={{0,16},{16,0},{1,17},{17,1},{2,18},{18,2},{3,19},{19,3},{4,20},{20... | collective-permute-start | bytes 589832 | tf_op jit(solution)/shard_map/ppermute | solution.py:247
  46.2 1.1 %collective-permute-done.13.received = f32[48,1024]{1,0:T(8,128)S(1)} collective-permute-done((f32[48,1024]{1,0:T(8,128)S(1)}, f32[48,1024]{1,0:T(8,128)S(1)}, u32[]{:S(2)}, u32[]{:S(2)}) %collective-permute-start.13) | collective-permute-done | bytes 196640 | tf_op jit(solution)/shard_map/ppermute | solution.py:247
  47.3 4.0 %shard_map.92 = (f32[4,1024]{1,0:T(4,128)S(1)}, f32[24,1024]{1,0:T(8,128)S(1)}, f32[24,1024]{1,0:T(8,128)S(1)}) custom-call(f32[4,1024]{1,0:T(4,128)S(1)} %get-tuple-element.42.refs_0_.mine, f32[4,1024]{1,0:T(4,128)S(1)} %collective-permute-done.3.refs_1_.other, f32[48,1024]{1,0:T(8,128)S(1)} %get-tuple-element.62.sums, ...), custom_call_target="tpu_custom_call" | custom-call | tf_op jit(solution)/shard_map/pallas_call | solution.py:254
  51.3 0.5 collective-permute-start.14
  51.8 0.9 %collective-permute-done.14.received = f32[24,1024]{1,0:T(8,128)S(1)} collective-permute-done((f32[24,1024]{1,0:T(8,128)S(1)}, f32[24,1024]{1,0:T(8,128)S(1)}, u32[]{:S(2)}, u32[]{:S(2)}) %collective-permute-start.14) | collective-permute-done | bytes 98336 | tf_op jit(solution)/shard_map/ppermute | solution.py:247
  52.7 0.7 %shard_map.93 = (f32[3,1024]{1,0:T(4,128)}, f32[1,1024]{1,0:T(1,128)}, f32[16,1024]{1,0:T(8,128)}) custom-call(f32[4,1024]{1,0:T(4,128)S(1)} %get-tuple-element.75.state, f32[24,1024]{1,0:T(8,128)S(1)} %get-tuple-element.76.own, f32[24,1024]{1,0:T(8,128)S(1)} %collective-permute-done.14.received), custom_call_target="tpu_custom_call" | custom-call | tf_op jit(solution)/shard_map/pallas_call | solution.py:254
  (1 shorter events, 0.0 us)
Async XLA Ops:
  1.5 7.7 %collective-permute-start.2 = (f32[96,128]{1,0:T(8,128)S(1)}, f32[96,128]{1,0:T(8,128)S(1)}, u32[]{:S(2)}, u32[]{:S(2)}) collective-permute-start(f32[96,128]{1,0:T(8,128)S(1)} %get-tuple-element.45.refs_0_), channel_id=1, source_target_pairs={{0,3},{1,0},{2,1},{3,2},{4,7},{5,4},{6,5},{7,6},{8,11},{9,8},{10,9... | collective-permute-start | bytes 147464 | tf_op jit(solution)/shard_map/ppermute | solution.py:247
  6.2 4.5 %collective-permute-start.1 = (f32[96,128]{1,0:T(8,128)S(1)}, f32[96,128]{1,0:T(8,128)S(1)}, u32[]{:S(2)}, u32[]{:S(2)}) collective-permute-start(f32[96,128]{1,0:T(8,128)S(1)} %get-tuple-element.45.refs_0_), channel_id=1, source_target_pairs={{0,2},{1,3},{2,0},{3,1},{4,6},{5,7},{6,4},{7,5},{8,10},{9,11},{10,... | collective-permute-start | bytes 147464 | tf_op jit(solution)/shard_map/ppermute | solution.py:247
  6.2 4.7 %collective-permute-start = (f32[96,128]{1,0:T(8,128)S(1)}, f32[96,128]{1,0:T(8,128)S(1)}, u32[]{:S(2)}, u32[]{:S(2)}) collective-permute-start(f32[96,128]{1,0:T(8,128)S(1)} %get-tuple-element.45.refs_0_), channel_id=1, source_target_pairs={{0,1},{1,2},{2,3},{3,0},{4,5},{5,6},{6,7},{7,4},{8,9},{9,10},{10,1... | collective-permute-start | bytes 147464 | tf_op jit(solution)/shard_map/ppermute | solution.py:247
  6.9 2.4 %collective-permute-start.3 = (f32[4,1024]{1,0:T(4,128)S(1)}, f32[4,1024]{1,0:T(4,128)S(1)}, u32[]{:S(2)}, u32[]{:S(2)}) collective-permute-start(f32[4,1024]{1,0:T(4,128)S(1)} %get-tuple-element.42.refs_0_.mine), channel_id=1, source_target_pairs={{0,16},{16,0},{1,17},{17,1},{2,18},{18,2},{3,19},{19,3},{4,20},{20... | collective-permute-start | bytes 49160 | tf_op jit(solution)/shard_map/ppermute | solution.py:247
  11.7 5.2 %collective-permute-start.4 = (f32[264,128]{1,0:T(8,128)S(1)}, f32[264,128]{1,0:T(8,128)S(1)}, u32[]{:S(2)}, u32[]{:S(2)}) collective-permute-start(f32[264,128]{1,0:T(8,128)S(1)} %get-tuple-element.50), channel_id=1, source_target_pairs={{0,4},{4,8},{8,12},{12,0},{1,5},{5,9},{9,13},{13,1},{2,6},{6,10},{... | collective-permute-start | bytes 405512 | tf_op jit(solution)/shard_map/ppermute | solution.py:247
  13.1 6.8 %collective-permute-start.5 = (f32[264,128]{1,0:T(8,128)S(1)}, f32[264,128]{1,0:T(8,128)S(1)}, u32[]{:S(2)}, u32[]{:S(2)}) collective-permute-start(f32[264,128]{1,0:T(8,128)S(1)} %get-tuple-element.51), channel_id=1, source_target_pairs={{0,8},{4,12},{8,0},{12,4},{1,9},{5,13},{9,1},{13,5},{2,10},{6,14},... | collective-permute-start | bytes 405512 | tf_op jit(solution)/shard_map/ppermute | solution.py:247
  15.7 4.9 %collective-permute-start.6 = (f32[264,128]{1,0:T(8,128)S(1)}, f32[264,128]{1,0:T(8,128)S(1)}, u32[]{:S(2)}, u32[]{:S(2)}) collective-permute-start(f32[264,128]{1,0:T(8,128)S(1)} %get-tuple-element.52), channel_id=1, source_target_pairs={{0,12},{4,0},{8,4},{12,8},{1,13},{5,1},{9,5},{13,9},{2,14},{6,2},{... | collective-permute-start | bytes 405512 | tf_op jit(solution)/shard_map/ppermute | solution.py:247
  20.7 6.6 %collective-permute-start.7 = (f32[528,128]{1,0:T(8,128)S(1)}, f32[528,128]{1,0:T(8,128)S(1)}, u32[]{:S(2)}, u32[]{:S(2)}) collective-permute-start(f32[528,128]{1,0:T(8,128)S(1)} %get-tuple-element.60.refs_2_), channel_id=1, source_target_pairs={{0,32},{32,64},{64,96},{96,0},{1,33},{33,65},{65,97},{97,1},{2,34}... | collective-permute-start | bytes 811016 | tf_op jit(solution)/shard_map/ppermute | solution.py:247
  22.0 5.3 %collective-permute-start.8 = (f32[528,128]{1,0:T(8,128)S(1)}, f32[528,128]{1,0:T(8,128)S(1)}, u32[]{:S(2)}, u32[]{:S(2)}) collective-permute-start(f32[528,128]{1,0:T(8,128)S(1)} %get-tuple-element.59.refs_3_), channel_id=1, source_target_pairs={{0,96},{32,0},{64,32},{96,64},{1,97},{33,1},{65,33},{97,65},{2,98}... | collective-permute-start | bytes 811016 | tf_op jit(solution)/shard_map/ppermute | solution.py:247
  27.3 7.8 %collective-permute-start.9 = (f32[528,128]{1,0:T(8,128)S(1)}, f32[528,128]{1,0:T(8,128)S(1)}, u32[]{:S(2)}, u32[]{:S(2)}) collective-permute-start(f32[528,128]{1,0:T(8,128)S(1)} %get-tuple-element.59.refs_3_), channel_id=1, source_target_pairs={{0,32},{32,64},{64,96},{96,0},{1,33},{33,65},{65,97},{97,1},{2,34}... | collective-permute-start | bytes 811016 | tf_op jit(solution)/shard_map/ppermute | solution.py:247
  28.8 6.3 %collective-permute-start.10 = (f32[528,128]{1,0:T(8,128)S(1)}, f32[528,128]{1,0:T(8,128)S(1)}, u32[]{:S(2)}, u32[]{:S(2)}) collective-permute-start(f32[528,128]{1,0:T(8,128)S(1)} %get-tuple-element.60.refs_2_), channel_id=1, source_target_pairs={{0,96},{32,0},{64,32},{96,64},{1,97},{33,1},{65,33},{97,65},{2,98}... | collective-permute-start | bytes 811016 | tf_op jit(solution)/shard_map/ppermute | solution.py:247
  30.0 8.1 %collective-permute-start.11 = (f32[528,128]{1,0:T(8,128)S(1)}, f32[528,128]{1,0:T(8,128)S(1)}, u32[]{:S(2)}, u32[]{:S(2)}) collective-permute-start(f32[528,128]{1,0:T(8,128)S(1)} %collective-permute-done.7.refs_3_), channel_id=1, source_target_pairs={{0,32},{32,64},{64,96},{96,0},{1,33},{33,65},{65,97},{97,1},{2,34}... | collective-permute-start | bytes 811016 | tf_op jit(solution)/shard_map/ppermute | solution.py:247
  30.3 8.1 %collective-permute-start.12 = (f32[528,128]{1,0:T(8,128)S(1)}, f32[528,128]{1,0:T(8,128)S(1)}, u32[]{:S(2)}, u32[]{:S(2)}) collective-permute-start(f32[528,128]{1,0:T(8,128)S(1)} %collective-permute-done.8.refs_4_), channel_id=1, source_target_pairs={{0,96},{32,0},{64,32},{96,64},{1,97},{33,1},{65,33},{97,65},{2,98}... | collective-permute-start | bytes 811016 | tf_op jit(solution)/shard_map/ppermute | solution.py:247
  40.9 6.4 %collective-permute-start.13 = (f32[48,1024]{1,0:T(8,128)S(1)}, f32[48,1024]{1,0:T(8,128)S(1)}, u32[]{:S(2)}, u32[]{:S(2)}) collective-permute-start(f32[48,1024]{1,0:T(8,128)S(1)} %get-tuple-element.62.sums), channel_id=1, source_target_pairs={{0,16},{16,0},{1,17},{17,1},{2,18},{18,2},{3,19},{19,3},{4,20},{20... | collective-permute-start | bytes 589832 | tf_op jit(solution)/shard_map/ppermute | solution.py:247
  51.3 1.4 %collective-permute-start.14 = (f32[24,1024]{1,0:T(8,128)S(1)}, f32[24,1024]{1,0:T(8,128)S(1)}, u32[]{:S(2)}, u32[]{:S(2)}) collective-permute-start(f32[24,1024]{1,0:T(8,128)S(1)} %get-tuple-element.77), channel_id=1, source_target_pairs={{0,16},{16,0},{1,17},{17,1},{2,18},{18,2},{3,19},{19,3},{4,20},{20... | collective-permute-start | bytes 294920 | tf_op jit(solution)/shard_map/ppermute | solution.py:247

commit v15 on v13

--- a/solution.py
+++ b/solution.py
@@ -275,9 +275,9 @@
     )
     other = step(state, "core", 1)
     along_z = [payload] + [step(payload, "z", k) for k in range(1, 4)]
-    *along_z, other = lax.optimization_barrier((*along_z, other))
     to_y = call(functools.partial(merge_z, slots, domain), [f32(4 * domain + 8, LANES)] * 4, place, *along_z)
     along_y = [step(to_y[k], "y", k) if k else to_y[k] for k in range(4)]
+    *along_y, other = lax.optimization_barrier((*along_y, other))
     low, high = call(merge_y, [f32(8 * domain + 16, LANES)] * 2, *along_y)
     below_low, above_high = step(low, "x", 1), step(high, "x", -1)
     below_high, above_low = step(high, "x", 1), step(low, "x", -1)

time: 52.9 us -> 52.9 us (level)
  waiting for transfers between devices: 13.3 us -> 11.9 us
  starting transfers between devices: 22.3 us -> 23.7 us
    ppermute x15, waiting for transfers between devices: 13.3 us -> 11.9 us  [step(): lax.ppermute(value, axis, [(i, (i + by) % size) for i in range(size)])]
    ppermute x15, starting transfers between devices: 22.3 us -> 23.7 us  [step(): lax.ppermute(value, axis, [(i, (i + by) % size) for i in range(size)])]
  transfers between devices with their start and end apart: 15 -> 15, of which waited for: 11 -> 10; matrix products, arithmetic and copies ran while one was open for 0% -> 0% of each run, Pallas kernels for 14% -> 14%
where the time goes in v15:
time: 52.9 us; the launch traced here: 52.7 us
  starting transfers between devices  23.7 us (45%)
  Pallas kernels  16.3 us (31%)
  waiting for transfers between devices  11.9 us (22%)
  between operations  0.72 us (1%)
    ppermute x15, starting transfers between devices, step(): lax.ppermute(value, axis, [(i, (i + by) % size) for i in range(size)])  23.7 us
    pallas_call x9, Pallas kernels, call(): pl.pallas_call(fn, in_specs=specs, out_specs=out_specs, out_shape=outs, s...  16.3 us
    ppermute x15, waiting for transfers between devices, step(): lax.ppermute(value, axis, [(i, (i + by) % size) for i in range(size)])  11.9 us
  transfers between devices with their start and end apart: 15, of which 10 were waited for; matrix products, arithmetic and copies ran while one was open for 0% of the time, Pallas kernels for 14%

profile of v15, /device:TPU:1, one launch (start us, length us, event | category | flops | bytes accessed | tf_op | source)
XLA Modules:
  0.0 52.7 jit_solution(7739164762920950330)
XLA Ops:
  0.6 0.9 %shard_map.85 = (f32[96,128]{1,0:T(8,128)S(1)}, f32[4,1024]{1,0:T(4,128)S(1)}) custom-call(f32[3,2048]{1,0:T(4,128)} %positions.1, f32[16,128]{1,0:T(8,128)} %bitcast.9, s32[16,128]{1,0:T(8,128)} %bitcast.10, s32[16,128]{1,0:T(8,128)} %bitcast.11, f32[3,1024]{1,0:T(4,128)} %centers.1, f32[1,1024]{1,0:T(1,128)} %bitcast.12), custom_call_target="tpu_custom_call" | custom-call | tf_op jit(solution)/shard_map/pallas_call | solution.py:254
  1.5 4.7 %collective-permute-start.2 = (f32[96,128]{1,0:T(8,128)S(1)}, f32[96,128]{1,0:T(8,128)S(1)}, u32[]{:S(2)}, u32[]{:S(2)}) collective-permute-start(f32[96,128]{1,0:T(8,128)S(1)} %get-tuple-element.41.refs_0_), channel_id=1, source_target_pairs={{0,3},{1,0},{2,1},{3,2},{4,7},{5,4},{6,5},{7,6},{8,11},{9,8},{10,9... | collective-permute-start | bytes 147464 | tf_op jit(solution)/shard_map/ppermute | solution.py:247
  6.2 0.0 collective-permute-start.1
  6.2 0.7 %collective-permute-start = (f32[96,128]{1,0:T(8,128)S(1)}, f32[96,128]{1,0:T(8,128)S(1)}, u32[]{:S(2)}, u32[]{:S(2)}) collective-permute-start(f32[96,128]{1,0:T(8,128)S(1)} %get-tuple-element.41.refs_0_), channel_id=1, source_target_pairs={{0,1},{1,2},{2,3},{3,0},{4,5},{5,6},{6,7},{7,4},{8,9},{9,10},{10,1... | collective-permute-start | bytes 147464 | tf_op jit(solution)/shard_map/ppermute | solution.py:247
  6.9 0.1 pad_add_fusion.place
  6.9 0.4 collective-permute-done.2.refs_3_
  7.3 3.4 %collective-permute-done.1.refs_2_ = f32[96,128]{1,0:T(8,128)S(1)} collective-permute-done((f32[96,128]{1,0:T(8,128)S(1)}, f32[96,128]{1,0:T(8,128)S(1)}, u32[]{:S(2)}, u32[]{:S(2)}) %collective-permute-start.1) | collective-permute-done | bytes 49184 | tf_op jit(solution)/shard_map/ppermute | solution.py:247
  10.7 0.1 collective-permute-done.refs_1_
  10.8 0.9 %shard_map.86 = (f32[264,128]{1,0:T(8,128)S(1)}, f32[264,128]{1,0:T(8,128)S(1)}, f32[264,128]{1,0:T(8,128)S(1)}, f32[264,128]{1,0:T(8,128)S(1)}) custom-call(s32[4]{0:T(128)S(1)} %pad_add_fusion.place, f32[96,128]{1,0:T(8,128)S(1)} %get-tuple-element.41.refs_0_, f32[96,128]{1,0:T(8,128)S(1)} %collective-permute-done.refs_1_, ...), custom_call_target="tpu_custom_call" | custom-call | tf_op jit(solution)/shard_map/pallas_call | solution.py:254
  11.7 1.4 %collective-permute-start.3 = (f32[264,128]{1,0:T(8,128)S(1)}, f32[264,128]{1,0:T(8,128)S(1)}, u32[]{:S(2)}, u32[]{:S(2)}) collective-permute-start(f32[264,128]{1,0:T(8,128)S(1)} %get-tuple-element.43), channel_id=1, source_target_pairs={{0,4},{4,8},{8,12},{12,0},{1,5},{5,9},{9,13},{13,1},{2,6},{6,10},{... | collective-permute-start | bytes 405512 | tf_op jit(solution)/shard_map/ppermute | solution.py:247
  13.1 2.6 %collective-permute-start.4 = (f32[264,128]{1,0:T(8,128)S(1)}, f32[264,128]{1,0:T(8,128)S(1)}, u32[]{:S(2)}, u32[]{:S(2)}) collective-permute-start(f32[264,128]{1,0:T(8,128)S(1)} %get-tuple-element.44), channel_id=1, source_target_pairs={{0,8},{4,12},{8,0},{12,4},{1,9},{5,13},{9,1},{13,5},{2,10},{6,14},... | collective-permute-start | bytes 405512 | tf_op jit(solution)/shard_map/ppermute | solution.py:247
  15.7 1.1 %collective-permute-start.5 = (f32[264,128]{1,0:T(8,128)S(1)}, f32[264,128]{1,0:T(8,128)S(1)}, u32[]{:S(2)}, u32[]{:S(2)}) collective-permute-start(f32[264,128]{1,0:T(8,128)S(1)} %get-tuple-element.45), channel_id=1, source_target_pairs={{0,12},{4,0},{8,4},{12,8},{1,13},{5,1},{9,5},{13,9},{2,14},{6,2},{... | collective-permute-start | bytes 405512 | tf_op jit(solution)/shard_map/ppermute | solution.py:247
  16.8 2.9 %collective-permute-start.6 = (f32[4,1024]{1,0:T(4,128)S(1)}, f32[4,1024]{1,0:T(4,128)S(1)}, u32[]{:S(2)}, u32[]{:S(2)}) collective-permute-start(f32[4,1024]{1,0:T(4,128)S(1)} %get-tuple-element.40.refs_0_.mine), channel_id=1, source_target_pairs={{0,16},{16,0},{1,17},{17,1},{2,18},{18,2},{3,19},{19,3},{4,20},{20... | collective-permute-start | bytes 49160 | tf_op jit(solution)/shard_map/ppermute | solution.py:247
  19.7 0.8 %collective-permute-done.6.refs_1_.other = f32[4,1024]{1,0:T(4,128)S(1)} collective-permute-done((f32[4,1024]{1,0:T(4,128)S(1)}, f32[4,1024]{1,0:T(4,128)S(1)}, u32[]{:S(2)}, u32[]{:S(2)}) %collective-permute-start.6) | collective-permute-done | bytes 16416 | tf_op jit(solution)/shard_map/ppermute | solution.py:247
  20.6 0.0 collective-permute-done.3.refs_1_
  20.6 0.0 collective-permute-done.4.refs_2_
  20.6 0.1 collective-permute-done.5.refs_3_
  20.7 1.3 %collective-permute-start.7 = (f32[528,128]{1,0:T(8,128)S(1)}, f32[528,128]{1,0:T(8,128)S(1)}, u32[]{:S(2)}, u32[]{:S(2)}) collective-permute-start(f32[528,128]{1,0:T(8,128)S(1)} %get-tuple-element.51.refs_2_), channel_id=1, source_target_pairs={{0,32},{32,64},{64,96},{96,0},{1,33},{33,65},{65,97},{97,1},{2,34}... | collective-permute-start | bytes 811016 | tf_op jit(solution)/shard_map/ppermute | solution.py:247
  22.0 1.5 %collective-permute-start.8 = (f32[528,128]{1,0:T(8,128)S(1)}, f32[528,128]{1,0:T(8,128)S(1)}, u32[]{:S(2)}, u32[]{:S(2)}) collective-permute-start(f32[528,128]{1,0:T(8,128)S(1)} %get-tuple-element.52.refs_3_), channel_id=1, source_target_pairs={{0,96},{32,0},{64,32},{96,64},{1,97},{33,1},{65,33},{97,65},{2,98}... | collective-permute-start | bytes 811016 | tf_op jit(solution)/shard_map/ppermute | solution.py:247
  23.4 1.3 %collective-permute-start.10 = (f32[528,128]{1,0:T(8,128)S(1)}, f32[528,128]{1,0:T(8,128)S(1)}, u32[]{:S(2)}, u32[]{:S(2)}) collective-permute-start(f32[528,128]{1,0:T(8,128)S(1)} %get-tuple-element.51.refs_2_), channel_id=1, source_target_pairs={{0,96},{32,0},{64,32},{96,64},{1,97},{33,1},{65,33},{97,65},{2,98}... | collective-permute-start | bytes 811016 | tf_op jit(solution)/shard_map/ppermute | solution.py:247
  24.7 0.2 collective-permute-start.9
  24.9 2.4 %shard_map.88 = (bf16[1024,512]{1,0:T(8,128)(2,1)S(1)}, bf16[512,1024]{1,0:T(8,128)(2,1)S(1)}, f32[4,4,128,128]{3,2,1,0:T(8,128)S(1)}, f32[48,1024]{1,0:T(8,128)S(1)}) custom-call(s32[4]{0:T(128)S(1)} %pad_add_fusion.place, f32[4,1024]{1,0:T(4,128)S(1)} %get-tuple-element.40.refs_0_.mine, f32[4,1024]{1,0:T(4,128)S(1)} %collective-permute-done.6.refs_1_.other, ...), custom_call_target="tpu_custom_call" | custom-call | tf_op jit(solution)/shard_map/pallas_call | solution.py:254
  27.3 0.0 collective-permute-done.7.refs_3_
  27.3 0.0 collective-permute-done.8.refs_4_
  27.4 1.4 %collective-permute-start.11 = (f32[528,128]{1,0:T(8,128)S(1)}, f32[528,128]{1,0:T(8,128)S(1)}, u32[]{:S(2)}, u32[]{:S(2)}) collective-permute-start(f32[528,128]{1,0:T(8,128)S(1)} %collective-permute-done.7.refs_3_), channel_id=1, source_target_pairs={{0,32},{32,64},{64,96},{96,0},{1,33},{33,65},{65,97},{97,1},{2,34}... | collective-permute-start | bytes 811016 | tf_op jit(solution)/shard_map/ppermute | solution.py:247
  28.8 1.3 %collective-permute-start.12 = (f32[528,128]{1,0:T(8,128)S(1)}, f32[528,128]{1,0:T(8,128)S(1)}, u32[]{:S(2)}, u32[]{:S(2)}) collective-permute-start(f32[528,128]{1,0:T(8,128)S(1)} %collective-permute-done.8.refs_4_), channel_id=1, source_target_pairs={{0,96},{32,0},{64,32},{96,64},{1,97},{33,1},{65,33},{97,65},{2,98}... | collective-permute-start | bytes 811016 | tf_op jit(solution)/shard_map/ppermute | solution.py:247
  30.1 2.4 %shard_map.89 = (bf16[1024,512]{1,0:T(8,128)(2,1)S(1)}, bf16[512,1024]{1,0:T(8,128)(2,1)S(1)}, f32[4,4,128,128]{3,2,1,0:T(8,128)S(1)}, f32[48,1024]{1,0:T(8,128)S(1)}) custom-call(s32[4]{0:T(128)S(1)} %pad_add_fusion.place, f32[4,1024]{1,0:T(4,128)S(1)} %get-tuple-element.40.refs_0_.mine, f32[4,1024]{1,0:T(4,128)S(1)} %collective-permute-done.6.refs_1_.other, ...), custom_call_target="tpu_custom_call" | custom-call | tf_op jit(solution)/shard_map/pallas_call | solution.py:254
  32.5 0.2 collective-permute-done.10.refs_4_
  32.7 1.7 %collective-permute-done.9.refs_3_ = f32[528,128]{1,0:T(8,128)S(1)} collective-permute-done((f32[528,128]{1,0:T(8,128)S(1)}, f32[528,128]{1,0:T(8,128)S(1)}, u32[]{:S(2)}, u32[]{:S(2)}) %collective-permute-start.9) | collective-permute-done | bytes 270368 | tf_op jit(solution)/shard_map/ppermute | solution.py:247
  34.4 2.5 %shard_map.90 = (bf16[1024,512]{1,0:T(8,128)(2,1)S(1)}, bf16[512,1024]{1,0:T(8,128)(2,1)S(1)}, f32[4,4,128,128]{3,2,1,0:T(8,128)S(1)}, f32[48,1024]{1,0:T(8,128)S(1)}) custom-call(s32[4]{0:T(128)S(1)} %pad_add_fusion.place, f32[4,1024]{1,0:T(4,128)S(1)} %get-tuple-element.40.refs_0_.mine, f32[4,1024]{1,0:T(4,128)S(1)} %collective-permute-done.6.refs_1_.other, ...), custom_call_target="tpu_custom_call" | custom-call | tf_op jit(solution)/shard_map/pallas_call | solution.py:254
  36.9 3.2 %collective-permute-done.11.refs_3_ = f32[528,128]{1,0:T(8,128)S(1)} collective-permute-done((f32[528,128]{1,0:T(8,128)S(1)}, f32[528,128]{1,0:T(8,128)S(1)}, u32[]{:S(2)}, u32[]{:S(2)}) %collective-permute-start.11) | collective-permute-done | bytes 270368 | tf_op jit(solution)/shard_map/ppermute | solution.py:247
  40.1 0.0 collective-permute-done.12.refs_4_
  40.1 2.5 %shard_map.91 = (bf16[1024,512]{1,0:T(8,128)(2,1)S(1)}, bf16[512,1024]{1,0:T(8,128)(2,1)S(1)}, f32[4,4,128,128]{3,2,1,0:T(8,128)S(1)}, f32[48,1024]{1,0:T(8,128)S(1)}) custom-call(s32[4]{0:T(128)S(1)} %pad_add_fusion.place, f32[4,1024]{1,0:T(4,128)S(1)} %get-tuple-element.40.refs_0_.mine, f32[4,1024]{1,0:T(4,128)S(1)} %collective-permute-done.6.refs_1_.other, ...), custom_call_target="tpu_custom_call" | custom-call | tf_op jit(solution)/shard_map/pallas_call | solution.py:254
  42.6 2.9 %collective-permute-start.13 = (f32[48,1024]{1,0:T(8,128)S(1)}, f32[48,1024]{1,0:T(8,128)S(1)}, u32[]{:S(2)}, u32[]{:S(2)}) collective-permute-start(f32[48,1024]{1,0:T(8,128)S(1)} %get-tuple-element.58.sums), channel_id=1, source_target_pairs={{0,16},{16,0},{1,17},{17,1},{2,18},{18,2},{3,19},{19,3},{4,20},{20... | collective-permute-start | bytes 589832 | tf_op jit(solution)/shard_map/ppermute | solution.py:247
  45.5 1.1 %collective-permute-done.13.received = f32[48,1024]{1,0:T(8,128)S(1)} collective-permute-done((f32[48,1024]{1,0:T(8,128)S(1)}, f32[48,1024]{1,0:T(8,128)S(1)}, u32[]{:S(2)}, u32[]{:S(2)}) %collective-permute-start.13) | collective-permute-done | bytes 196640 | tf_op jit(solution)/shard_map/ppermute | solution.py:247
  46.6 4.0 %shard_map.92 = (f32[4,1024]{1,0:T(4,128)S(1)}, f32[24,1024]{1,0:T(8,128)S(1)}, f32[24,1024]{1,0:T(8,128)S(1)}) custom-call(f32[4,1024]{1,0:T(4,128)S(1)} %get-tuple-element.40.refs_0_.mine, f32[4,1024]{1,0:T(4,128)S(1)} %collective-permute-done.6.refs_1_.other, f32[48,1024]{1,0:T(8,128)S(1)} %get-tuple-element.58.sums, ...), custom_call_target="tpu_custom_call" | custom-call | tf_op jit(solution)/shard_map/pallas_call | solution.py:254
  50.6 0.5 collective-permute-start.14
  51.1 0.9 %collective-permute-done.14.received = f32[24,1024]{1,0:T(8,128)S(1)} collective-permute-done((f32[24,1024]{1,0:T(8,128)S(1)}, f32[24,1024]{1,0:T(8,128)S(1)}, u32[]{:S(2)}, u32[]{:S(2)}) %collective-permute-start.14) | collective-permute-done | bytes 98336 | tf_op jit(solution)/shard_map/ppermute | solution.py:247
  52.0 0.7 %shard_map.93 = (f32[3,1024]{1,0:T(4,128)}, f32[1,1024]{1,0:T(1,128)}, f32[16,1024]{1,0:T(8,128)}) custom-call(f32[4,1024]{1,0:T(4,128)S(1)} %get-tuple-element.71.state, f32[24,1024]{1,0:T(8,128)S(1)} %get-tuple-element.72.own, f32[24,1024]{1,0:T(8,128)S(1)} %collective-permute-done.14.received), custom_call_target="tpu_custom_call" | custom-call | tf_op jit(solution)/shard_map/pallas_call | solution.py:254
  (1 shorter events, 0.0 us)
Async XLA Ops:
  1.5 5.8 %collective-permute-start.2 = (f32[96,128]{1,0:T(8,128)S(1)}, f32[96,128]{1,0:T(8,128)S(1)}, u32[]{:S(2)}, u32[]{:S(2)}) collective-permute-start(f32[96,128]{1,0:T(8,128)S(1)} %get-tuple-element.41.refs_0_), channel_id=1, source_target_pairs={{0,3},{1,0},{2,1},{3,2},{4,7},{5,4},{6,5},{7,6},{8,11},{9,8},{10,9... | collective-permute-start | bytes 147464 | tf_op jit(solution)/shard_map/ppermute | solution.py:247
  6.2 4.5 %collective-permute-start.1 = (f32[96,128]{1,0:T(8,128)S(1)}, f32[96,128]{1,0:T(8,128)S(1)}, u32[]{:S(2)}, u32[]{:S(2)}) collective-permute-start(f32[96,128]{1,0:T(8,128)S(1)} %get-tuple-element.41.refs_0_), channel_id=1, source_target_pairs={{0,2},{1,3},{2,0},{3,1},{4,6},{5,7},{6,4},{7,5},{8,10},{9,11},{10,... | collective-permute-start | bytes 147464 | tf_op jit(solution)/shard_map/ppermute | solution.py:247
  6.2 4.7 %collective-permute-start = (f32[96,128]{1,0:T(8,128)S(1)}, f32[96,128]{1,0:T(8,128)S(1)}, u32[]{:S(2)}, u32[]{:S(2)}) collective-permute-start(f32[96,128]{1,0:T(8,128)S(1)} %get-tuple-element.41.refs_0_), channel_id=1, source_target_pairs={{0,1},{1,2},{2,3},{3,0},{4,5},{5,6},{6,7},{7,4},{8,9},{9,10},{10,1... | collective-permute-start | bytes 147464 | tf_op jit(solution)/shard_map/ppermute | solution.py:247
  11.7 8.8 %collective-permute-start.3 = (f32[264,128]{1,0:T(8,128)S(1)}, f32[264,128]{1,0:T(8,128)S(1)}, u32[]{:S(2)}, u32[]{:S(2)}) collective-permute-start(f32[264,128]{1,0:T(8,128)S(1)} %get-tuple-element.43), channel_id=1, source_target_pairs={{0,4},{4,8},{8,12},{12,0},{1,5},{5,9},{9,13},{13,1},{2,6},{6,10},{... | collective-permute-start | bytes 405512 | tf_op jit(solution)/shard_map/ppermute | solution.py:247
  13.1 7.5 %collective-permute-start.4 = (f32[264,128]{1,0:T(8,128)S(1)}, f32[264,128]{1,0:T(8,128)S(1)}, u32[]{:S(2)}, u32[]{:S(2)}) collective-permute-start(f32[264,128]{1,0:T(8,128)S(1)} %get-tuple-element.44), channel_id=1, source_target_pairs={{0,8},{4,12},{8,0},{12,4},{1,9},{5,13},{9,1},{13,5},{2,10},{6,14},... | collective-permute-start | bytes 405512 | tf_op jit(solution)/shard_map/ppermute | solution.py:247
  15.7 4.9 %collective-permute-start.5 = (f32[264,128]{1,0:T(8,128)S(1)}, f32[264,128]{1,0:T(8,128)S(1)}, u32[]{:S(2)}, u32[]{:S(2)}) collective-permute-start(f32[264,128]{1,0:T(8,128)S(1)} %get-tuple-element.45), channel_id=1, source_target_pairs={{0,12},{4,0},{8,4},{12,8},{1,13},{5,1},{9,5},{13,9},{2,14},{6,2},{... | collective-permute-start | bytes 405512 | tf_op jit(solution)/shard_map/ppermute | solution.py:247
  16.8 3.8 %collective-permute-start.6 = (f32[4,1024]{1,0:T(4,128)S(1)}, f32[4,1024]{1,0:T(4,128)S(1)}, u32[]{:S(2)}, u32[]{:S(2)}) collective-permute-start(f32[4,1024]{1,0:T(4,128)S(1)} %get-tuple-element.40.refs_0_.mine), channel_id=1, source_target_pairs={{0,16},{16,0},{1,17},{17,1},{2,18},{18,2},{3,19},{19,3},{4,20},{20... | collective-permute-start | bytes 49160 | tf_op jit(solution)/shard_map/ppermute | solution.py:247
  20.7 6.6 %collective-permute-start.7 = (f32[528,128]{1,0:T(8,128)S(1)}, f32[528,128]{1,0:T(8,128)S(1)}, u32[]{:S(2)}, u32[]{:S(2)}) collective-permute-start(f32[528,128]{1,0:T(8,128)S(1)} %get-tuple-element.51.refs_2_), channel_id=1, source_target_pairs={{0,32},{32,64},{64,96},{96,0},{1,33},{33,65},{65,97},{97,1},{2,34}... | collective-permute-start | bytes 811016 | tf_op jit(solution)/shard_map/ppermute | solution.py:247
  22.0 5.4 %collective-permute-start.8 = (f32[528,128]{1,0:T(8,128)S(1)}, f32[528,128]{1,0:T(8,128)S(1)}, u32[]{:S(2)}, u32[]{:S(2)}) collective-permute-start(f32[528,128]{1,0:T(8,128)S(1)} %get-tuple-element.52.refs_3_), channel_id=1, source_target_pairs={{0,96},{32,0},{64,32},{96,64},{1,97},{33,1},{65,33},{97,65},{2,98}... | collective-permute-start | bytes 811016 | tf_op jit(solution)/shard_map/ppermute | solution.py:247
  23.4 9.3 %collective-permute-start.10 = (f32[528,128]{1,0:T(8,128)S(1)}, f32[528,128]{1,0:T(8,128)S(1)}, u32[]{:S(2)}, u32[]{:S(2)}) collective-permute-start(f32[528,128]{1,0:T(8,128)S(1)} %get-tuple-element.51.refs_2_), channel_id=1, source_target_pairs={{0,96},{32,0},{64,32},{96,64},{1,97},{33,1},{65,33},{97,65},{2,98}... | collective-permute-start | bytes 811016 | tf_op jit(solution)/shard_map/ppermute | solution.py:247
  24.7 9.7 %collective-permute-start.9 = (f32[528,128]{1,0:T(8,128)S(1)}, f32[528,128]{1,0:T(8,128)S(1)}, u32[]{:S(2)}, u32[]{:S(2)}) collective-permute-start(f32[528,128]{1,0:T(8,128)S(1)} %get-tuple-element.52.refs_3_), channel_id=1, source_target_pairs={{0,32},{32,64},{64,96},{96,0},{1,33},{33,65},{65,97},{97,1},{2,34}... | collective-permute-start | bytes 811016 | tf_op jit(solution)/shard_map/ppermute | solution.py:247
  27.4 12.7 %collective-permute-start.11 = (f32[528,128]{1,0:T(8,128)S(1)}, f32[528,128]{1,0:T(8,128)S(1)}, u32[]{:S(2)}, u32[]{:S(2)}) collective-permute-start(f32[528,128]{1,0:T(8,128)S(1)} %collective-permute-done.7.refs_3_), channel_id=1, source_target_pairs={{0,32},{32,64},{64,96},{96,0},{1,33},{33,65},{65,97},{97,1},{2,34}... | collective-permute-start | bytes 811016 | tf_op jit(solution)/shard_map/ppermute | solution.py:247
  28.8 11.3 %collective-permute-start.12 = (f32[528,128]{1,0:T(8,128)S(1)}, f32[528,128]{1,0:T(8,128)S(1)}, u32[]{:S(2)}, u32[]{:S(2)}) collective-permute-start(f32[528,128]{1,0:T(8,128)S(1)} %collective-permute-done.8.refs_4_), channel_id=1, source_target_pairs={{0,96},{32,0},{64,32},{96,64},{1,97},{33,1},{65,33},{97,65},{2,98}... | collective-permute-start | bytes 811016 | tf_op jit(solution)/shard_map/ppermute | solution.py:247
  42.6 4.0 %collective-permute-start.13 = (f32[48,1024]{1,0:T(8,128)S(1)}, f32[48,1024]{1,0:T(8,128)S(1)}, u32[]{:S(2)}, u32[]{:S(2)}) collective-permute-start(f32[48,1024]{1,0:T(8,128)S(1)} %get-tuple-element.58.sums), channel_id=1, source_target_pairs={{0,16},{16,0},{1,17},{17,1},{2,18},{18,2},{3,19},{19,3},{4,20},{20... | collective-permute-start | bytes 589832 | tf_op jit(solution)/shard_map/ppermute | solution.py:247
  50.6 1.4 %collective-permute-start.14 = (f32[24,1024]{1,0:T(8,128)S(1)}, f32[24,1024]{1,0:T(8,128)S(1)}, u32[]{:S(2)}, u32[]{:S(2)}) collective-permute-start(f32[24,1024]{1,0:T(8,128)S(1)} %get-tuple-element.73), channel_id=1, source_target_pairs={{0,16},{16,0},{1,17},{17,1},{2,18},{18,2},{3,19},{19,3},{4,20},{20... | collective-permute-start | bytes 294920 | tf_op jit(solution)/shard_map/ppermute | solution.py:247
